TPU v7x, 32 devices: a whole 2x2x4 slice. The times are simulated.
32 devices in a mesh: batch: 8 (over y, x, core), tensor: 4 (over z).
Axes of the slice: x: 2, y: 2, z: 4, core: 2. Of those that a mesh axis runs over, the one named last changes fastest.
Arguments:
- tokens: bfloat16 [8192, 2048], P('batch', 'tensor'), may hold values from -6 to 6
- doc_lengths: int32 [8], replicated, may hold values from 1 to 8192, as said below
- norm1_gain: float32 [2048], P('tensor'), may hold values from 0.1 to 1.9
- w_query: bfloat16 [2048, 256], P(None, 'tensor'), may hold values from -0.125 to 0.125
- w_key: bfloat16 [2048, 256], P(None, 'tensor'), may hold values from -0.125 to 0.125
- w_value: bfloat16 [2048, 2048], P(None, 'tensor'), may hold values from -0.125 to 0.125
- w_out: bfloat16 [2048, 2048], P('tensor'), may hold values from -1 to 1
- norm2_gain: float32 [2048], P('tensor'), may hold values from 0.1 to 1.9
- w_gate: bfloat16 [2048, 5504], P(None, 'tensor'), may hold values from -0.125 to 0.125
- w_up: bfloat16 [2048, 5504], P(None, 'tensor'), may hold values from -0.125 to 0.125
- w_down: bfloat16 [5504, 2048], P('tensor'), may hold values from -0.078125 to 0.078125
- cotangent: bfloat16 [8192, 2048], P('batch', 'tensor'), may hold values from -6 to 6
Outputs:
- output: bfloat16 [8192, 2048], P('batch', 'tensor')
- grad_tokens: float32 [8192, 2048], P('batch', 'tensor')
- grad_norm1_gain: float32 [2048], P('tensor')
- grad_w_query: float32 [2048, 256], P(None, 'tensor')
- grad_w_key: float32 [2048, 256], P(None, 'tensor')
- grad_w_value: float32 [2048, 2048], P(None, 'tensor')
- grad_w_out: float32 [2048, 2048], P('tensor')
- grad_norm2_gain: float32 [2048], P('tensor')
- grad_w_gate: float32 [2048, 5504], P(None, 'tensor')
- grad_w_up: float32 [2048, 5504], P(None, 'tensor')
- grad_w_down: float32 [5504, 2048], P('tensor')
Inputs may be any that keep to these rules, and one draw needn't show every extreme that they name: `doc_lengths`: the lengths sum to 8192; the second document starts before token 1024 and has at least 7169 tokens.
All inputs are finite; a program needn't handle non-finite values.
Results may differ from a plain program's by a relative error of at most 0.01.
Values may be sent and summed in bfloat16 or wider, within the bound.
No kernel may reach another device: no remote copies, remote signals or barrier semaphores. Data moves between devices by JAX's collectives and lax.ppermute only.
A program may use at most 256 MiB of HBM per device.

v0:
```python
import math

import jax
import jax.numpy as jnp
from jax import lax
from jax.sharding import PartitionSpec as P

FEAT = 16
HV = 128


EPSILON = 1e-05
HIGHEST = lax.Precision.HIGHEST


def carried_in(part, axis, combine, identity, reverse):
    count = lax.axis_size(axis)
    place = lax.axis_index(axis)
    ahead = count - 1 - place if reverse else place
    gathered = jax.tree.map(lambda a: lax.all_gather(a, axis), part)
    state = jax.tree.map(lambda a, e: jnp.zeros_like(a) + jnp.asarray(e, a.dtype), part, identity)

    def one(turn, state):
        source = count - 1 - turn if reverse else turn
        return combine(
            state, jax.tree.map(lambda a: lax.dynamic_index_in_dim(a, source, 0, False), gathered)
        )

    return lax.fori_loop(0, ahead, one, state)


def taylor(values):
    width = values.shape[-1]
    root = width**0.25
    single = jnp.ones(values.shape[:-1] + (1,), values.dtype)
    square = (values[..., :, None] * values[..., None, :]).reshape(
        values.shape[:-1] + (width * width,)
    )
    return jnp.concatenate(
        [single, values / root, square / (math.sqrt(2.0) * root * root)], axis=-1
    )


def local_mix(queries, keys_in, values_in, prior_sum, prior_norm, allowed, opened):
    width = queries.shape[-1]
    scores = jnp.einsum("thf,shf->hts", queries, keys_in, precision=HIGHEST) / math.sqrt(width)
    weights = (1.0 + scores + 0.5 * scores * scores) * allowed[None]
    numer = jnp.einsum("hts,shv->thv", weights, values_in, precision=HIGHEST)
    denom = jnp.transpose(jnp.sum(weights, axis=2))
    feats = taylor(queries)
    numer = (
        numer
        + jnp.einsum("thr,hrv->thv", feats, prior_sum, precision=HIGHEST) * opened[:, None, None]
    )
    denom = denom + jnp.einsum("thr,hr->th", feats, prior_norm, precision=HIGHEST) * opened[:, None]
    return numer / denom[:, :, None]


def carry_out(keys_in, values_in, tail_mask):
    feats = taylor(keys_in) * tail_mask[:, None, None]
    return (jnp.einsum("thr,thv->hrv", feats, values_in, precision=HIGHEST), jnp.sum(feats, axis=0))


def reset_combine(earlier, later):
    keep = 1.0 - later[2]
    return (
        later[0] + keep * earlier[0],
        later[1] + keep * earlier[1],
        jnp.maximum(earlier[2], later[2]),
    )


def row_scale(inputs):
    partial_sum = jnp.sum(inputs * inputs, axis=1)
    total = lax.psum(partial_sum, "tensor")
    full_width = inputs.shape[1] * lax.axis_size("tensor")
    return lax.rsqrt(total / full_width + EPSILON)[:, None]


def norm_back(grad_normed, inputs, scale, gain):
    scaled = grad_normed * gain[None, :]
    local_dot = jnp.sum(scaled * inputs, axis=1)
    total = lax.psum(local_dot, "tensor")
    full_width = inputs.shape[1] * lax.axis_size("tensor")
    return scale * scaled - inputs * scale * scale * scale * (total / full_width)[:, None]


def spread(normed):
    return lax.all_gather(normed, "tensor", axis=1, tiled=True)


def combine_heads(partial_out):
    return lax.psum_scatter(partial_out, "tensor", scatter_dimension=1, tiled=True)


def widen_grad(grad_low):
    return lax.all_gather(grad_low, "tensor", axis=1, tiled=True)


def narrow_grad(partial_grad):
    return lax.psum_scatter(partial_grad, "tensor", scatter_dimension=1, tiled=True)


def project(left, right):
    return jnp.dot(left, right, preferred_element_type=jnp.float32)


def project_left(left, right):
    return jnp.einsum("ti,tj->ij", left, right, preferred_element_type=jnp.float32)


def project_back(left, right):
    return jnp.einsum("ti,ji->tj", left, right, preferred_element_type=jnp.float32)


def local(
    tokens,
    doc_lengths,
    norm1_gain,
    w_query,
    w_key,
    w_value,
    w_out,
    norm2_gain,
    w_gate,
    w_up,
    w_down,
    cotangent,
):
    token_count = tokens.shape[0]
    head_count = w_value.shape[1] // HV
    begin_here = lax.axis_index("batch") * token_count
    position = begin_here + jnp.arange(token_count, dtype=jnp.int32)
    doc_ends = jnp.cumsum(doc_lengths)
    doc_begins = doc_ends - doc_lengths
    segment = jnp.sum((position[:, None] >= doc_begins[None, :]).astype(jnp.int32), axis=1) - 1
    doc_index = jnp.arange(doc_lengths.shape[0], dtype=jnp.int32)
    first_begin = jnp.sum(jnp.where(doc_index == segment[0], doc_begins, 0))
    last_begin = jnp.sum(jnp.where(doc_index == segment[-1], doc_begins, 0))
    opened = ((segment == segment[0]) & (first_begin < begin_here)).astype(jnp.float32)
    tail_mask = (segment == segment[-1]).astype(jnp.float32)
    restart = (last_begin >= begin_here).astype(jnp.float32)
    allowed = (
        (position[:, None] >= position[None, :]) & (segment[:, None] == segment[None, :])
    ).astype(jnp.float32)
    inputs = tokens.astype(jnp.float32)
    scale_one = row_scale(inputs)
    normed_one = (inputs * scale_one * norm1_gain[None, :]).astype(jnp.bfloat16)
    normed_full = spread(normed_one)
    query_low = project(normed_full, w_query).astype(jnp.bfloat16)
    key_low = project(normed_full, w_key).astype(jnp.bfloat16)
    value_low = project(normed_full, w_value).astype(jnp.bfloat16)
    query_heads = query_low.astype(jnp.float32).reshape(token_count, head_count, FEAT)
    key_heads = key_low.astype(jnp.float32).reshape(token_count, head_count, FEAT)
    value_heads = value_low.astype(jnp.float32).reshape(token_count, head_count, HV)

    def carrying(key_in, value_in):
        return carry_out(key_in, value_in, tail_mask)

    carry_pair, pull_carry = jax.vjp(carrying, key_heads, value_heads)
    identity = (
        jnp.zeros_like(carry_pair[0]),
        jnp.zeros_like(carry_pair[1]),
        jnp.zeros((), jnp.float32),
    )
    prior_sum, prior_norm, prior_flag = carried_in(
        (carry_pair[0], carry_pair[1], restart), "batch", reset_combine, identity, False
    )

    def mixing(query_in, key_in, value_in, sum_in, norm_in):
        return local_mix(query_in, key_in, value_in, sum_in, norm_in, allowed, opened)

    mixed, pull_mix = jax.vjp(mixing, query_heads, key_heads, value_heads, prior_sum, prior_norm)
    mixed_low = mixed.reshape(token_count, head_count * HV).astype(jnp.bfloat16)
    hidden = inputs + combine_heads(project(mixed_low, w_out))
    scale_two = row_scale(hidden)
    normed_two = (hidden * scale_two * norm2_gain[None, :]).astype(jnp.bfloat16)
    normed_two_full = spread(normed_two)
    gate = project(normed_two_full, w_gate)
    up_proj = project(normed_two_full, w_up)
    sigmoid_gate = jax.nn.sigmoid(gate)
    silu_gate = gate * sigmoid_gate
    inner = (silu_gate * up_proj).astype(jnp.bfloat16)
    output = (hidden + combine_heads(project(inner, w_down))).astype(jnp.bfloat16)
    grad_top = cotangent.astype(jnp.float32)
    grad_top_full = widen_grad(cotangent)
    grad_w_down = project_left(inner, grad_top_full)
    grad_inner = project_back(grad_top_full, w_down)
    grad_gate_low = (
        grad_inner * up_proj * sigmoid_gate * (1.0 + gate * (1.0 - sigmoid_gate))
    ).astype(jnp.bfloat16)
    grad_up_low = (grad_inner * silu_gate).astype(jnp.bfloat16)
    grad_w_gate = project_left(normed_two_full, grad_gate_low)
    grad_w_up = project_left(normed_two_full, grad_up_low)
    grad_normed_two = narrow_grad(
        project_back(grad_gate_low, w_gate) + project_back(grad_up_low, w_up)
    )
    grad_gain_two = jnp.sum(grad_normed_two * hidden * scale_two, axis=0)
    grad_hidden = grad_top + norm_back(grad_normed_two, hidden, scale_two, norm2_gain)
    grad_hidden_full = widen_grad(grad_hidden.astype(jnp.bfloat16))
    grad_w_out = project_left(mixed_low, grad_hidden_full)
    grad_mixed = project_back(grad_hidden_full, w_out)
    grad_query, grad_key_one, grad_value_one, grad_prior_sum, grad_prior_norm = pull_mix(
        grad_mixed.reshape(token_count, head_count, HV)
    )
    grad_carry_sum, grad_carry_norm, grad_flag = carried_in(
        (grad_prior_sum, grad_prior_norm, restart), "batch", reset_combine, identity, True
    )
    grad_key_two, grad_value_two = pull_carry((grad_carry_sum, grad_carry_norm))
    grad_query_low = grad_query.reshape(token_count, head_count * FEAT).astype(jnp.bfloat16)
    grad_key_low = (
        (grad_key_one + grad_key_two).reshape(token_count, head_count * FEAT).astype(jnp.bfloat16)
    )
    grad_value_low = (
        (grad_value_one + grad_value_two).reshape(token_count, head_count * HV).astype(jnp.bfloat16)
    )
    grad_w_query = project_left(normed_full, grad_query_low)
    grad_w_key = project_left(normed_full, grad_key_low)
    grad_w_value = project_left(normed_full, grad_value_low)
    grad_normed_one = narrow_grad(
        project_back(grad_query_low, w_query)
        + project_back(grad_key_low, w_key)
        + project_back(grad_value_low, w_value)
    )
    grad_gain_one = jnp.sum(grad_normed_one * inputs * scale_one, axis=0)
    grad_tokens = grad_hidden + norm_back(grad_normed_one, inputs, scale_one, norm1_gain)
    (
        grad_w_query,
        grad_w_key,
        grad_w_value,
        grad_w_out,
        grad_gain_one,
        grad_w_gate,
        grad_w_up,
        grad_w_down,
        grad_gain_two,
    ) = lax.psum(
        (
            grad_w_query,
            grad_w_key,
            grad_w_value,
            grad_w_out,
            grad_gain_one,
            grad_w_gate,
            grad_w_up,
            grad_w_down,
            grad_gain_two,
        ),
        "batch",
    )
    return (
        output,
        grad_tokens,
        grad_gain_one,
        grad_w_query,
        grad_w_key,
        grad_w_value,
        grad_w_out,
        grad_gain_two,
        grad_w_gate,
        grad_w_up,
        grad_w_down,
    )


def solution(mesh):
    in_specs = (
        P("batch", "tensor"),
        P(),
        P("tensor"),
        P(None, "tensor"),
        P(None, "tensor"),
        P(None, "tensor"),
        P("tensor", None),
        P("tensor"),
        P(None, "tensor"),
        P(None, "tensor"),
        P("tensor", None),
        P("batch", "tensor"),
    )
    out_specs = (
        P("batch", "tensor"),
        P("batch", "tensor"),
        P("tensor"),
        P(None, "tensor"),
        P(None, "tensor"),
        P(None, "tensor"),
        P("tensor", None),
        P("tensor"),
        P(None, "tensor"),
        P(None, "tensor"),
        P("tensor", None),
    )
    return jax.shard_map(local, mesh=mesh, in_specs=in_specs, out_specs=out_specs, check_vma=False)
```

profile of v0, /device:TPU:0, one launch (start us, length us, event | category | flops | bytes accessed | tf_op | source)
XLA Modules:
  0.0 1820.0 jit_solution(16739856377201930565)
XLA Ops:
  8.9 13.5 psum.91
  23.0 2.5 fusion.5
  30.9 73.7 %all-gather.13.cloned.1.call-done = bf16[1024,2048]{1,0:T(8,128)(2,1)} async-done(((bf16[1024,512]{1,0:T(8,128)(2,1)}), bf16[1024,2048]{1,0:T(8,128)(2,1)}) %all-gather.13.cloned.1.call-update) | async-done | bytes 4194320 | tf_op jit(solution)/shard_map/all_gather | solution.py:89
  104.6 3.7 bitcast_convert_fusion
  109.7 2.4 convolution_convert_fusion
  112.2 3.6 fusion.51
  120.2 14.5 all-reduce
  135.3 5.0 fusion.50
  140.4 9.1 all-gather.4
  150.9 2.6 multiply_multiply_fusion
  153.5 8.0 fusion.30
  161.6 13.6 fusion.31
  175.9 5.4 fusion.40
  181.9 6.6 fusion.20
  189.5 5.8 fusion.55
  195.4 159.3 %reduce-scatter.5.cloned.1.call-done = f32[1024,512]{1,0:T(8,128)} async-done(((f32[1024,2048]{1,0:T(8,128)}), f32[1024,512]{1,0:T(8,128)}) %reduce-scatter.5.cloned.1.call-update) | async-done | bytes 2097168 | tf_op jit(solution)/shard_map/reduce_scatter | solution.py:93
  354.7 3.2 multiply_reduce_fusion.6
  357.9 11.1 psum.92
  369.0 2.8 multiply_convert_fusion.3
  372.7 78.5 %all-gather.15.cloned.1.call-done = bf16[1024,2048]{1,0:T(8,128)(2,1)} async-done(((bf16[1024,512]{1,0:T(8,128)(2,1)}), bf16[1024,2048]{1,0:T(8,128)(2,1)}) %all-gather.15.cloned.1.call-update) | async-done | bytes 4194320 | tf_op jit(solution)/shard_map/all_gather | solution.py:89
  451.2 11.5 fusion.57
  462.7 9.6 fusion.56
  472.2 59.7 %all-gather.17.cloned.1.call-done = bf16[1024,2048]{1,0:T(8,128)(2,1)} async-done(((bf16[1024,512]{1,0:T(8,128)(2,1)}), bf16[1024,2048]{1,0:T(8,128)(2,1)}) %all-gather.17.cloned.1.call-update) | async-done | bytes 4194320 | tf_op jit(solution)/shard_map/all_gather | solution.py:97
  531.9 14.8 multiply_convert_fusion
  546.7 11.0 fusion.59
  557.8 11.5 convolution_add_fusion
  569.3 143.1 %reduce-scatter.9.cloned.1.call-done = f32[1024,512]{1,0:T(8,128)} async-done(((f32[1024,2048]{1,0:T(8,128)}), f32[1024,512]{1,0:T(8,128)}) %reduce-scatter.9.cloned.1.call-update) | async-done | bytes 2097168 | tf_op jit(solution)/shard_map/reduce_scatter | solution.py:101
  712.4 3.4 multiply_reduce_fusion.4
  715.8 11.8 psum.93
  728.9 3.9 fusion.52
  732.9 79.2 %all-gather.19.cloned.1.call-done = bf16[1024,2048]{1,0:T(8,128)(2,1)} async-done(((bf16[1024,512]{1,0:T(8,128)(2,1)}), bf16[1024,2048]{1,0:T(8,128)(2,1)}) %all-gather.19.cloned.1.call-update) | async-done | bytes 4194320 | tf_op jit(solution)/shard_map/all_gather | solution.py:97
  812.2 5.4 fusion.21
  818.9 5.5 fusion.17
  824.5 6.5 fusion.38
  831.0 9.1 all-gather.5
  840.1 4.2 add_bitcast_fusion
  846.8 2.5 multiply_reduce_fusion.3
  849.3 19.2 %fusion.1 = f32[4,1024,1024]{1,2,0:T(8,128)} fusion(f32[4,1024,1024]{1,2,0:T(8,128)} %get-tuple-element.248, bf16[1024,4,128]{0,2,1:T(8,128)(2,1)S(1)} %bitcast.200, f32[4,1024]{1,0:T(4,128)S(1)} %negate_bitcast_fusion, f32[1024,1024]{0,1:T(8,128)S(1)} %copy-done.19, f32[1024,4]{0,1:T(4,128)S(1)} %copy-done.55, f32[1024,512]{0,1:T(8,128)S(1)} %copy-done.28), kind=kOutput, calls=%fused_computation.6 | convolution fusion | flops 6484918272 | bytes 40927232 | tf_op jit(solution)/shard_map/transpose(jvp(hts,shv->thv))/dot_general | solution.py:48
  868.5 9.2 fusion.26
  877.7 4.7 fusion.60
  882.4 24.1 %fusion.14 = f32[4,128,1024]{2,1,0:T(8,128)} fusion(f32[4,1024,1024]{1,2,0:T(8,128)} %get-tuple-element.248, f32[1024,1024]{0,1:T(8,128)S(1)} %copy-done.20, f32[1024,4]{0,1:T(4,128)S(1)} %copy-done.55, f32[1024,512]{0,1:T(8,128)S(1)} %copy-done.28), kind=kOutput, calls=%fused_computation.44 | convolution fusion | flops 6468141056 | bytes 25182208 | tf_op jit(solution)/shard_map/transpose(jvp(hts,shv->thv))/dot_general | solution.py:48
  906.6 18.2 %while.31 = (s32[]{:T(128)}, f32[4,273,128]{2,1,0:T(8,128)S(1)}, f32[4,273]{1,0:T(4,128)S(1)}, s32[]{:T(128)}, f32[8,4,273,128]{3,2,1,0:T(8,128)}, /*index=5*/f3...) while((s32[]{:T(128)}, f32[4,273,128]{2,1,0:T(8,128)S(1)}, ...), condition=%wide.region_21.22_spmd, body=%wide.region_20.21_spmd.sunk | while | flops 281743 | bytes 1690627 | solution.py:29
  924.8 7.2 add_convert_fusion
  936.6 2.5 multiply_reduce_fusion.1
  939.2 5.8 fusion.61
  945.0 11.4 fusion.27
  956.5 10.4 add_add_fusion
  967.0 11.6 fusion.58
  978.7 11.3 fusion.64
  990.1 8.8 fusion.68
  998.9 9.0 fusion.67
  1010.3 4.4 fusion.63
  1016.3 4.5 fusion.62
  1020.9 87.8 %reduce-scatter.11.cloned.1.call-done = f32[1024,512]{1,0:T(8,128)} async-done(((f32[1024,2048]{1,0:T(8,128)}), f32[1024,512]{1,0:T(8,128)}) %reduce-scatter.11.cloned.1.call-update) | async-done | bytes 2097168 | tf_op jit(solution)/shard_map/reduce_scatter | solution.py:101
  1108.7 2.4 fusion.13
  1111.2 14.0 all-reduce.1
  1125.2 11.8 psum.94
  1137.1 119.3 %reduce-scatter.7.cloned.1.call-done = f32[1024,512]{1,0:T(8,128)} async-done(((f32[1024,2048]{1,0:T(8,128)}), f32[1024,512]{1,0:T(8,128)}) %reduce-scatter.7.cloned.1.call-update) | async-done | bytes 2097168 | tf_op jit(solution)/shard_map/reduce_scatter | solution.py:93
  1256.4 5.0 fusion.9
  1261.4 509.9 %all-reduce.5.cloned.1.call-done = (f32[2048,64]{0,1:T(8,128)}, f32[2048,64]{0,1:T(8,128)}, f32[2048,512]{1,0:T(8,128)}, f32[512,2048]{1,0:T(8,128)}, f32[2048,1...) async-done(((f32[2048,64]{0,1:T(8,128)}, f32[2048,64]{0,1:T(8,128)}, f32[2048,512]{1,0:T(8,128)}, f32[512,2048]{1,0:T(8,128)}, f32[2048,1376]{0,1:T(8,128)}, ...) | async-done | bytes 43253776 | tf_op jit(solution)/shard_map/psum | solution.py:237
  1775.0 4.8 copy.99
  1781.8 10.4 copy.101
  1792.2 10.4 copy.102
  1802.6 10.5 copy.103
  (221 shorter events, 50.3 us)
Async XLA Ops:
  7.2 182.4 %copy-start = (bf16[512,2048]{1,0:T(8,128)(2,1)S(1)}, bf16[512,2048]{1,0:T(8,128)(2,1)}, u32[]{:S(2)}) copy-start(bf16[512,2048]{1,0:T(8,128)(2,1)} %param.22) | copy-start | bytes 6291460
  7.2 18.4 %copy-start.61 = (s32[8]{0:T(128)S(1)}, s32[8]{0:T(128)}, u32[]{:S(2)}) copy-start(s32[8]{0:T(128)} %param.17) | copy-start | bytes 100
  7.2 97.4 %copy-start.31 = (bf16[2048,64]{0,1:T(8,128)(2,1)S(1)}, bf16[2048,64]{0,1:T(8,128)(2,1)}, u32[]{:S(2)}) copy-start(bf16[2048,64]{0,1:T(8,128)(2,1)} %param.20) | copy-start | bytes 786436
  7.2 97.4 %all-gather.13.cloned.1.call-start = ((), (), s32[]{:S(2)}) async-start(), calls=%async_computation.4 | async-start | bytes 5242880 | tf_op jit(solution)/shard_map/all_gather | solution.py:89
  25.5 149.7 %all-gather.21.cloned.1.call-start = ((), (), s32[]{:S(2)}) async-start(), calls=%async_computation.12 | async-start | bytes 5160960 | tf_op jit(solution)/shard_map/all_gather | solution.py:20
  30.9 104.4 %copy-start.44 = (f32[1024]{0:T(1024)}, f32[1024]{0:T(1024)S(1)}, u32[]{:S(2)}) copy-start(f32[1024]{0:T(1024)S(1)} %get-tuple-element.244) | copy-start | bytes 12292
  104.6 5.0 copy-start.2
  104.6 5.0 copy-start.59
  108.4 26.9 %copy-start.25 = (f32[1024,4,16]{0,2,1:T(8,128)}, f32[1024,4,16]{0,2,1:T(8,128)S(1)}, u32[]{:S(2)}) copy-start(f32[1024,4,16]{0,2,1:T(8,128)S(1)} %broadcast_multiply_fusion.1) | copy-start | bytes 786436
  112.1 22.5 %copy-start.37 = (bf16[1024,512]{0,1:T(8,128)(2,1)}, bf16[1024,512]{0,1:T(8,128)(2,1)S(1)}, u32[]{:S(2)}) copy-start(bf16[1024,512]{0,1:T(8,128)(2,1)S(1)} %convolution_convert_fusion) | copy-start | bytes 3145732
  115.8 238.9 %reduce-scatter.5.cloned.1.call-start = ((), (), s32[]{:S(2)}) async-start(), calls=%async_computation.5 | async-start | bytes 10485760 | tf_op jit(solution)/shard_map/reduce_scatter | solution.py:93
  134.7 14.8 copy-start.3
  134.7 14.8 copy-start.33
  135.3 26.3 %copy-start.18 = (f32[1024,1024]{0,1:T(8,128)}, f32[1024,1024]{0,1:T(8,128)S(1)}, u32[]{:S(2)}) copy-start(f32[1024,1024]{0,1:T(8,128)S(1)} %and_convert_fusion) | copy-start | bytes 12582916
  150.9 10.7 copy-start.29
  150.9 31.0 %copy-start.35 = (f32[1024,4,16]{0,2,1:T(8,128)}, f32[1024,4,16]{0,2,1:T(8,128)S(1)}, u32[]{:S(2)}) copy-start(f32[1024,4,16]{0,2,1:T(8,128)S(1)} %broadcast_multiply_fusion) | copy-start | bytes 786436
  153.5 8.1 copy-start.38
  161.6 13.6 copy-start.64
  175.7 12.9 copy-start.10
  175.7 6.3 copy-start.12
  181.9 6.6 copy-start.53
  195.3 159.4 %copy-start.8 = (bf16[1024,512]{1,0:T(8,128)(2,1)S(1)}, bf16[1024,512]{1,0:T(8,128)(2,1)}, u32[]{:S(2)}) copy-start(bf16[1024,512]{1,0:T(8,128)(2,1)} %param.16) | copy-start | bytes 3145732
  195.3 255.8 %all-gather.15.cloned.1.call-start = ((), (), s32[]{:S(2)}) async-start(), calls=%async_computation.6 | async-start | bytes 5242880 | tf_op jit(solution)/shard_map/all_gather | solution.py:89
  369.0 359.3 %copy-start.40 = (f32[1024]{0:T(1024)}, f32[1024]{0:T(1024)S(1)}, u32[]{:S(2)}) copy-start(f32[1024]{0:T(1024)S(1)} %add_rsqrt_fusion) | copy-start | bytes 12292
  371.9 160.0 %all-gather.17.cloned.1.call-start = ((), (), s32[]{:S(2)}) async-start(), calls=%async_computation.8 | async-start | bytes 5242880 | tf_op jit(solution)/shard_map/all_gather | solution.py:97
  372.5 340.0 %reduce-scatter.9.cloned.1.call-start = ((), (), s32[]{:S(2)}) async-start(), calls=%async_computation.9 | async-start | bytes 10485760 | tf_op jit(solution)/shard_map/reduce_scatter | solution.py:101
  451.2 11.5 copy-start.57
  546.7 11.0 copy-start.66
  546.7 11.0 copy-start.23
  569.3 159.7 %copy-start.15 = (bf16[1024,512]{1,0:T(8,128)(2,1)S(1)}, bf16[1024,512]{1,0:T(8,128)(2,1)}, u32[]{:S(2)}) copy-start(bf16[1024,512]{1,0:T(8,128)(2,1)} %param.27) | copy-start | bytes 3145732
  569.3 242.9 %all-gather.19.cloned.1.call-start = ((), (), s32[]{:S(2)}) async-start(), calls=%async_computation.10 | async-start | bytes 5242880 | tf_op jit(solution)/shard_map/all_gather | solution.py:97
  732.9 173.6 %all-gather.23.cloned.1.call-start = ((), (), s32[]{:S(2)}) async-start(), calls=%async_computation.13 | async-start | bytes 5160960 | tf_op jit(solution)/shard_map/all_gather | solution.py:20
  812.2 6.7 copy-start.13
  812.2 6.7 copy-start.36
  812.2 6.7 copy-start.51
  812.2 6.7 copy-start.54
  824.4 15.8 copy-start.11
  824.4 284.3 %reduce-scatter.11.cloned.1.call-start = ((), (), s32[]{:S(2)}) async-start(), calls=%async_computation.11 | async-start | bytes 10485760 | tf_op jit(solution)/shard_map/reduce_scatter | solution.py:101
  824.4 15.7 copy-start.28
  846.7 2.6 copy-start.55
  868.5 9.2 copy-start.34
  877.7 4.7 copy-start.20
  882.4 24.2 %copy-start.65 = (f32[8]{0:T(128)S(1)}, f32[8]{0:T(128)}, u32[]{:S(2)}) copy-start(f32[8]{0:T(128)} %all-reduce) | copy-start | bytes 100
  906.6 18.3 %copy-start.26 = (f32[1024,4,16]{0,2,1:T(8,128)S(1)}, f32[1024,4,16]{0,2,1:T(8,128)}, u32[]{:S(2)}) copy-start(f32[1024,4,16]{0,2,1:T(8,128)} %copy-done.25) | copy-start | bytes 786436
  906.6 18.3 %copy-start.45 = (f32[1024]{0:T(1024)S(1)}, f32[1024]{0:T(1024)}, u32[]{:S(2)}) copy-start(f32[1024]{0:T(1024)} %copy-done.44) | copy-start | bytes 12292
  939.2 5.8 copy-start.30
  945.0 11.5 copy-start.32
  966.9 289.4 %reduce-scatter.7.cloned.1.call-start = ((), (), s32[]{:S(2)}) async-start(), calls=%async_computation.7 | async-start | bytes 10485760 | tf_op jit(solution)/shard_map/reduce_scatter | solution.py:93
  978.6 792.6 %all-reduce.5.cloned.1.call-start = ((), (), s32[]{:S(2)}) async-start(), calls=%async_computation.14 | async-start | bytes 86507520 | tf_op jit(solution)/shard_map/psum | solution.py:237
  978.7 11.4 copy-start.24
  978.7 11.4 copy-start.58
  990.0 8.8 copy-start.67
  998.9 9.0 copy-start.4
  998.9 10.7 copy-start.63
  1020.8 87.9 %copy-start.9 = (bf16[1024,512]{1,0:T(8,128)(2,1)S(1)}, bf16[1024,512]{1,0:T(8,128)(2,1)}, u32[]{:S(2)}) copy-start(bf16[1024,512]{1,0:T(8,128)(2,1)} %param.16) | copy-start | bytes 3145732
  1020.8 87.9 %copy-start.43 = (f32[1024]{0:T(1024)S(1)}, f32[1024]{0:T(1024)}, u32[]{:S(2)}) copy-start(f32[1024]{0:T(1024)} %copy-done.42) | copy-start | bytes 12292
  1020.8 87.9 %copy-start.52 = (f32[512]{0:T(512)S(1)}, f32[512]{0:T(512)}, u32[]{:S(2)}) copy-start(f32[512]{0:T(512)} %param.18) | copy-start | bytes 6148
  1020.8 90.3 %copy-start.56 = (f32[512]{0:T(512)S(1)}, f32[512]{0:T(512)}, u32[]{:S(2)}) copy-start(f32[512]{0:T(512)} %get-tuple-element.187) | copy-start | bytes 6148
  1020.8 235.5 %copy-start.41 = (f32[1024]{0:T(1024)S(1)}, f32[1024]{0:T(1024)}, u32[]{:S(2)}) copy-start(f32[1024]{0:T(1024)} %copy-done.40) | copy-start | bytes 12292
  1020.8 235.5 %copy-start.47 = (f32[1024]{0:T(1024)S(1)}, f32[1024]{0:T(1024)}, u32[]{:S(2)}) copy-start(f32[1024]{0:T(1024)} %copy-done.46) | copy-start | bytes 12292
  1020.8 235.5 %copy-start.48 = (f32[512]{0:T(512)S(1)}, f32[512]{0:T(512)}, u32[]{:S(2)}) copy-start(f32[512]{0:T(512)} %param.23) | copy-start | bytes 6148
  1020.9 235.5 %copy-start.5 = (f32[1024,512]{1,0:T(8,128)S(1)}, f32[1024,512]{1,0:T(8,128)}, u32[]{:S(2)}) copy-start(f32[1024,512]{1,0:T(8,128)} %get-tuple-element.237) | copy-start | bytes 6291460
  1775.0 4.8 copy-start.22
  1802.6 10.5 copy-start.1
  (15 other events, 27.2 us)
Sparse Core Ops, SparseCore 0:
  25.6 78.9 all-gather.12
  115.9 37.1 all-gather.20
  195.5 159.1 reduce-scatter.4
  372.0 79.1 all-gather.14
  452.6 79.2 all-gather.16
  569.4 143.0 reduce-scatter.8
  733.0 79.1 all-gather.18
  824.5 37.0 all-gather.22
  967.0 141.6 reduce-scatter.10
  1110.9 145.3 reduce-scatter.6
  1262.7 508.5 all-reduce.4
where the time goes:
time: 1830 us; the launch traced here: 1820 us
  waiting for transfers between devices  1310 us (72%)
  matrix products  278 us (15%)
  blocking collectives  95 us (5%)
  local copies, waits for them, and re-layouts  59.1 us (3%)
  other arithmetic  54.7 us (3%)
    psum x1, waiting for transfers between devices, local(): lax.psum((grad_w_query, grad_w_key, grad_w_value, grad_w_out, grad_gain_o...  510 us
    reduce_scatter x2, waiting for transfers between devices, combine_heads(): lax.psum_scatter(partial_out, 'tensor', scatter_dimension=1, tiled=True)  279 us
    reduce_scatter x2, waiting for transfers between devices, narrow_grad(): lax.psum_scatter(partial_grad, 'tensor', scatter_dimension=1, tiled=True)  231 us
    all_gather x2, waiting for transfers between devices, spread(): return lax.all_gather(normed, 'tensor', axis=1, tiled=True)  152 us
    all_gather x2, waiting for transfers between devices, widen_grad(): return lax.all_gather(grad_low, 'tensor', axis=1, tiled=True)  139 us
    dot_general x7, matrix products, project_back(): jnp.einsum('ti,ji->tj', left, right, preferred_element_type=jnp.float32)  63.5 us
    dot_general x3, matrix products, local_mix(): numer = jnp.einsum('hts,shv->thv', weights, values_in, precision=HIGHEST)  56.9 us
    unnamed x146, local copies, waits for them, and re-layouts  53.8 us
  transfers between devices with their start and end apart: 11, of which 9 were waited for; matrix products, arithmetic and copies ran while one was open for 11% of the time, Pallas kernels for 0%

commit v1 on v0

v1 whole, which is shorter than its diff:
```python
import functools
import math

import jax
import jax.numpy as jnp
import numpy as np
from jax import lax
from jax.experimental import pallas as pl
from jax.experimental.pallas import tpu as pltpu
from jax.sharding import PartitionSpec as P

FEAT = 16
HV = 128
EPSILON = 1e-05
WIDE = 256
ROWS = 160
STRIP = 256
LOW = jnp.bfloat16
F32 = jnp.float32


def feature_table():
    table = np.zeros((8, WIDE), np.float32)
    table[0:2] = -1.0
    at = 0
    for i in range(FEAT + 1):
        for j in range(i, FEAT + 1):
            table[0, at] = i if i < FEAT else -1
            table[1, at] = j if j < FEAT else -1
            table[2, at] = float(i == FEAT)
            table[3, at] = float(j == FEAT)
            table[4, at] = 0.5 if i == j and i < FEAT else 1.0
            at += 1
    return table


def nt(a, b):
    return lax.dot_general(a, b, (((1,), (1,)), ((), ())), preferred_element_type=F32)


def tn(a, b):
    return lax.dot_general(a, b, (((0,), (0,)), ((), ())), preferred_element_type=F32)


def nn(a, b):
    return lax.dot_general(a, b, (((1,), (0,)), ((), ())), preferred_element_type=F32)


def pickers(table, head, lanes):
    lane = lax.broadcasted_iota(jnp.int32, (lanes, WIDE), 0).astype(F32)
    base = (head * FEAT).astype(F32)
    first, second = table[0:1, :], table[1:2, :]
    one = jnp.where((lane == base + first) & (first >= 0), 0.5, 0.0).astype(LOW)
    two = jnp.where((lane == base + second) & (second >= 0), 0.5, 0.0).astype(LOW)
    return one, two


def head_lanes(head, lanes):
    lane = lax.broadcasted_iota(jnp.int32, (1, lanes), 1)
    return (lane >= head * FEAT) & (lane < (head + 1) * FEAT)


def factors(z, table, one, two):
    return nn(z, one) + table[2:3, :], nn(z, two) + table[3:4, :]


def pad_state(state):
    return jnp.concatenate([state, jnp.zeros((WIDE - ROWS, HV), state.dtype)], axis=0)


def state_body(k_ref, v_ref, tail_ref, table_ref, sum_ref, norm_ref):
    head = pl.program_id(0)
    table = table_ref[...]
    one, two = pickers(table, head, k_ref.shape[1])
    left, right = factors(k_ref[...], table, one, two)
    feats = (left * right * table[4:5, :] * tail_ref[...]).astype(LOW)
    sum_ref[0] = tn(feats, v_ref[...])[:ROWS].astype(sum_ref.dtype)
    norm_ref[0] = nn(jnp.ones((8, feats.shape[0]), LOW), feats)


def masked_weights(scores, segc, segr, row0, width):
    rows = scores.shape[0]
    row = row0 + lax.broadcasted_iota(jnp.int32, (rows, width), 0)
    col = lax.broadcasted_iota(jnp.int32, (rows, width), 1)
    return (row >= col) & (segc == segr)


def inner_body(q_ref, k_ref, v_ref, segc_ref, segr_ref, numer_ref, denom_ref):
    head = pl.program_id(0)
    tokens, lanes = q_ref.shape
    mine = head_lanes(head, lanes)
    for row0 in range(0, tokens, STRIP):
        width = row0 + STRIP
        query = jnp.where(mine, q_ref[pl.ds(row0, STRIP), :] * LOW(0.25), LOW(0.0))
        scores = nt(query, k_ref[pl.ds(0, width), :])
        keep = masked_weights(scores, segc_ref[pl.ds(row0, STRIP), :], segr_ref[:, pl.ds(0, width)], row0, width)
        weights = jnp.where(keep, 1.0 + scores * (1.0 + 0.5 * scores), 0.0).astype(LOW)
        wide = jnp.concatenate([v_ref[pl.ds(0, width), :], jnp.ones((width, HV), LOW)], axis=1)
        both = nn(weights, wide)
        numer_ref[pl.ds(row0, STRIP), :] = both[:, :HV]
        denom_ref[pl.ds(row0, STRIP), :] = both[:, HV:]


def merge_body(q_ref, numer_ref, denom_ref, sum_ref, norm_ref, open_ref, table_ref, y_ref, total_ref):
    head = pl.program_id(0)
    table = table_ref[...]
    one, two = pickers(table, head, q_ref.shape[1])
    left, right = factors(q_ref[...], table, one, two)
    feats = (left * right * open_ref[...]).astype(LOW)
    norm = jnp.broadcast_to(norm_ref[0][0:1, :], (HV, WIDE))
    norm_high = norm.astype(LOW)
    norm_rest = (norm - norm_high.astype(F32)).astype(LOW)
    total = denom_ref[...] + nt(feats, norm_high) + nt(feats, norm_rest)
    numer = numer_ref[...] + nn(feats, pad_state(sum_ref[0].astype(LOW)))
    total_ref[...] = total
    y_ref[...] = (numer / total).astype(LOW)


def pull_state_body(q_ref, dy_ref, y_ref, total_ref, open_ref, table_ref, wide_ref, sum_ref, norm_ref):
    head = pl.program_id(0)
    table = table_ref[...]
    one, two = pickers(table, head, q_ref.shape[1])
    left, right = factors(q_ref[...], table, one, two)
    feats = (left * right * open_ref[...]).astype(LOW)
    inverse = 1.0 / total_ref[...]
    dy = dy_ref[...]
    dnumer = (dy * inverse).astype(LOW)
    ddenom = -jnp.sum(dy * y_ref[...].astype(F32), axis=1, keepdims=True) * inverse
    ddenom = jnp.where(lax.broadcasted_iota(jnp.int32, ddenom.shape, 1) < 8, ddenom, 0.0).astype(LOW)
    wide_ref[...] = jnp.concatenate([dnumer, ddenom], axis=1)
    sum_ref[0] = tn(feats, dnumer)[:ROWS].astype(sum_ref.dtype)
    norm_ref[0] = tn(ddenom, feats)[:8]


def pull_inner_body(
    q_ref, k_ref, v_ref, segc_ref, segr_ref, wide_ref, sum_ref, norm_ref, open_ref, table_ref,
    dq_ref, dk_ref, dv_ref, dq_acc, dk_acc,
):
    head = pl.program_id(0)
    last = pl.num_programs(0) - 1
    tokens, lanes = q_ref.shape
    mine = head_lanes(head, lanes)

    @pl.when(head == 0)
    def _():
        dq_acc[...] = jnp.zeros_like(dq_acc)
        dk_acc[...] = jnp.zeros_like(dk_acc)

    dv_ref[...] = jnp.zeros_like(dv_ref)
    table = table_ref[...]
    one, two = pickers(table, head, lanes)
    state = pad_state(sum_ref[0].astype(LOW))
    norm = norm_ref[0][0:1, :]
    single = (lax.broadcasted_iota(jnp.int32, (1, HV), 1) < 1).astype(LOW)
    for row0 in range(0, tokens, STRIP):
        width = row0 + STRIP
        rows = pl.ds(row0, STRIP)
        query = jnp.where(mine, q_ref[rows, :] * LOW(0.25), LOW(0.0))
        keys = jnp.where(mine, k_ref[pl.ds(0, width), :] * LOW(0.25), LOW(0.0))
        scores = nt(query, k_ref[pl.ds(0, width), :])
        keep = masked_weights(scores, segc_ref[rows, :], segr_ref[:, pl.ds(0, width)], row0, width)
        weights = jnp.where(keep, 1.0 + scores * (1.0 + 0.5 * scores), 0.0).astype(LOW)
        dwide = wide_ref[rows, :]
        ones = jnp.broadcast_to(single, (width, HV))
        wide = jnp.concatenate([v_ref[pl.ds(0, width), :], ones], axis=1)
        dscores = jnp.where(keep, nt(dwide, wide) * (1.0 + scores), 0.0).astype(LOW)
        dv_ref[pl.ds(0, width), :] += tn(weights, dwide[:, :HV])
        dk_acc[pl.ds(0, width), :] += tn(dscores, query)
        left, right = factors(q_ref[rows, :], table, one, two)
        pulled = nt(dwide[:, :HV], state) + dwide[:, HV : HV + 1].astype(F32) * norm
        pulled = pulled * open_ref[rows, :]
        dq_acc[rows, :] += nn(dscores, keys) + nt((pulled * right).astype(LOW), one) + nt((pulled * left).astype(LOW), two)

    @pl.when(head == last)
    def _():
        dq_ref[...] = dq_acc[...].astype(dq_ref.dtype)
        dk_ref[...] = dk_acc[...]


def pull_carry_body(k_ref, v_ref, tail_ref, sum_ref, norm_ref, dk_in_ref, dv_in_ref, table_ref, dk_ref, dv_ref, dk_acc):
    head = pl.program_id(0)

    @pl.when(head == 0)
    def _():
        dk_acc[...] = dk_in_ref[...]

    table = table_ref[...]
    one, two = pickers(table, head, k_ref.shape[1])
    left, right = factors(k_ref[...], table, one, two)
    scale = table[4:5, :] * tail_ref[...]
    state = pad_state(sum_ref[0].astype(LOW))
    dv_ref[...] = (dv_in_ref[...] + nn((left * right * scale).astype(LOW), state)).astype(dv_ref.dtype)
    pulled = (nt(v_ref[...], state) + norm_ref[0][0:1, :]) * scale
    dk_acc[...] += nt((pulled * right).astype(LOW), one) + nt((pulled * left).astype(LOW), two)

    @pl.when(head == pl.num_programs(0) - 1)
    def _():
        dk_ref[...] = dk_acc[...].astype(dk_ref.dtype)


def shape(dims, kind):
    return jax.ShapeDtypeStruct(dims, kind)


class Mixer:
    def __init__(self, tokens, heads):
        self.tokens, self.heads = tokens, heads
        lanes = heads * FEAT
        self.full = lambda a, b: pl.BlockSpec((a, b), lambda h: (0, 0))
        self.thin = self.full(tokens, lanes)
        self.column = self.full(tokens, 1)
        self.row = self.full(1, tokens)
        self.table = self.full(8, WIDE)
        self.head = pl.BlockSpec((tokens, HV), lambda h: (0, h))
        self.pair = pl.BlockSpec((tokens, 2 * HV), lambda h: (0, h))
        self.sum = pl.BlockSpec((1, ROWS, HV), lambda h: (h, 0, 0))
        self.norm = pl.BlockSpec((1, 8, WIDE), lambda h: (h, 0, 0))
        self.thin_shape = lambda kind: shape((tokens, lanes), kind)
        self.head_shape = lambda kind: shape((tokens, heads * HV), kind)
        self.state_shapes = [shape((heads, ROWS, HV), F32), shape((heads, 8, WIDE), F32)]
        self.acc = pltpu.VMEM((tokens, lanes), F32)

    def call(self, body, name, in_specs, out_specs, out_shape, scratch, micros, *args):
        return pl.pallas_call(
            body,
            grid=(self.heads,),
            in_specs=in_specs,
            out_specs=out_specs,
            out_shape=out_shape,
            scratch_shapes=scratch,
            name=name,
            compiler_params=pltpu.CompilerParams(
                dimension_semantics=("arbitrary",), vmem_limit_bytes=48 * 1024 * 1024
            ),
            cost_estimate=pl.CostEstimate(
                flops=int(micros * 1e-6 * 1e15), bytes_accessed=1 << 20, transcendentals=0
            ),
        )(*args)

    def state(self, k, v, tail, table):
        return self.call(
            state_body, "mix_state", [self.thin, self.head, self.column, self.table],
            [self.sum, self.norm], self.state_shapes, [], 4, k, v, tail, table,
        )

    def inner(self, q, k, v, segc, segr):
        return self.call(
            inner_body, "mix_inner", [self.thin, self.thin, self.head, self.column, self.row],
            [self.head, self.head], [self.head_shape(F32)] * 2, [], 10, q, k, v, segc, segr,
        )

    def merge(self, q, numer, denom, total, norm, opened, table):
        return self.call(
            merge_body, "mix_merge",
            [self.thin, self.head, self.head, self.sum, self.norm, self.column, self.table],
            [self.head, self.head], [self.head_shape(LOW), self.head_shape(F32)], [], 5,
            q, numer, denom, total, norm, opened, table,
        )

    def pull_state(self, q, dy, y, total, opened, table):
        return self.call(
            pull_state_body, "mix_pull_state",
            [self.thin, self.head, self.head, self.head, self.column, self.table],
            [self.pair, self.sum, self.norm],
            [shape((self.tokens, self.heads * 2 * HV), LOW)] + self.state_shapes, [], 5,
            q, dy, y, total, opened, table,
        )

    def pull_inner(self, q, k, v, segc, segr, wide, total, norm, opened, table):
        return self.call(
            pull_inner_body, "mix_pull_inner",
            [self.thin, self.thin, self.head, self.column, self.row, self.pair, self.sum, self.norm, self.column, self.table],
            [self.thin, self.thin, self.head],
            [self.thin_shape(LOW), self.thin_shape(F32), self.head_shape(F32)],
            [self.acc, self.acc], 20, q, k, v, segc, segr, wide, total, norm, opened, table,
        )

    def pull_carry(self, k, v, tail, total, norm, dk, dv, table):
        return self.call(
            pull_carry_body, "mix_pull_carry",
            [self.thin, self.head, self.column, self.sum, self.norm, self.thin, self.head, self.table],
            [self.thin, self.head], [self.thin_shape(LOW), self.head_shape(LOW)], [self.acc], 6,
            k, v, tail, total, norm, dk, dv, table,
        )


def outside(part, reverse):
    count, place = lax.axis_size("batch"), lax.axis_index("batch")
    total = list(part)
    before = [jnp.zeros_like(a) for a in part]
    bit = 1
    while bit < count:
        pairs = [(i, i ^ bit) for i in range(count)]
        low = total[0].astype(LOW)
        other = [lax.ppermute(low, "batch", pairs).astype(F32), lax.ppermute(total[1], "batch", pairs)]
        upper = (place & bit) != 0
        take = jnp.logical_not(upper) if reverse else upper
        before = [a + jnp.where(take, b, 0.0) for a, b in zip(before, other)]
        total = [a + b for a, b in zip(total, other)]
        bit *= 2
    return before


def widen(part):
    return lax.all_gather(part, "tensor", axis=1, tiled=True)


def narrow(part):
    return lax.psum_scatter(part, "tensor", scatter_dimension=1, tiled=True)


def project(left, right):
    return jnp.dot(left, right, preferred_element_type=F32)


def project_left(left, right):
    return jnp.einsum("ti,tj->ij", left, right, preferred_element_type=F32)


def project_back(left, right):
    return jnp.einsum("ti,ji->tj", left, right, preferred_element_type=F32)


def local(
    tokens, doc_lengths, norm1_gain, w_query, w_key, w_value, w_out, norm2_gain, w_gate, w_up, w_down, cotangent,
):
    count, slice_width = tokens.shape
    heads = w_value.shape[1] // HV
    lanes = heads * FEAT
    width = w_query.shape[0]
    begin_here = lax.axis_index("batch") * count
    position = begin_here + jnp.arange(count, dtype=jnp.int32)
    doc_index = jnp.arange(doc_lengths.shape[0], dtype=jnp.int32)
    doc_begins = jnp.sum(jnp.where(doc_index[None, :] < doc_index[:, None], doc_lengths[None, :], 0), axis=1)
    segment = jnp.sum((position[:, None] >= doc_begins[None, :]).astype(jnp.int32), axis=1) - 1
    head_seg, tail_seg = segment[0], segment[-1]
    first_begin = jnp.sum(jnp.where(doc_index == head_seg, doc_begins, 0))
    opened = ((segment == head_seg) & (first_begin < begin_here)).astype(F32)[:, None]
    tail = (segment == tail_seg).astype(F32)[:, None]
    segc, segr = segment[:, None], segment[None, :]
    table = jnp.asarray(feature_table())
    mixer = Mixer(count, heads)

    gains = lax.all_gather(jnp.stack([norm1_gain, norm2_gain]), "tensor", axis=1, tiled=True)
    x_full = widen(tokens)
    c_full = widen(cotangent)
    inputs = tokens.astype(F32)
    x_wide = x_full.astype(F32)
    scale_one = lax.rsqrt(jnp.mean(x_wide * x_wide, axis=1, keepdims=True) + EPSILON)
    normed_one = (x_wide * scale_one * gains[0:1]).astype(LOW)
    w_mix = jnp.concatenate([w_query, w_key, w_value], axis=1)
    mixed_in = project(normed_one, w_mix).astype(LOW)
    q, k, v = mixed_in[:, :lanes], mixed_in[:, lanes : 2 * lanes], mixed_in[:, 2 * lanes :]

    carry = mixer.state(k, v, tail, table)
    prior = outside(carry, False)
    numer, denom = mixer.inner(q, k, v, segc, segr)
    y, total = mixer.merge(q, numer, denom, *prior, opened, table)

    hidden = inputs + narrow(project(y, w_out).astype(LOW)).astype(F32)
    hidden_full = widen(hidden.astype(LOW)).astype(F32)
    scale_two = lax.rsqrt(jnp.mean(hidden_full * hidden_full, axis=1, keepdims=True) + EPSILON)
    normed_two = (hidden_full * scale_two * gains[1:2]).astype(LOW)
    gate = project(normed_two, w_gate)
    up = project(normed_two, w_up)
    sig = jax.nn.sigmoid(gate)
    silu = gate * sig
    inner = (silu * up).astype(LOW)
    output = (hidden + narrow(project(inner, w_down).astype(LOW)).astype(F32)).astype(LOW)

    dinner = project_back(c_full, w_down)
    dgate = (dinner * up * sig * (1.0 + gate * (1.0 - sig))).astype(LOW)
    dup = (dinner * silu).astype(LOW)
    dot_two = lax.psum(
        jnp.sum(dgate.astype(F32) * gate + dup.astype(F32) * up, axis=1, keepdims=True), "tensor"
    )
    dnormed_two = narrow((project_back(dgate, w_gate) + project_back(dup, w_up)).astype(LOW)).astype(F32)
    grad_hidden = (
        cotangent.astype(F32)
        + scale_two * norm2_gain[None, :] * dnormed_two
        - hidden * (scale_two * scale_two * dot_two / width)
    )
    dh_full = widen(grad_hidden.astype(LOW))
    dy = project_back(dh_full, w_out)
    wide, dsum, dnorm = mixer.pull_state(q, dy, y, total, opened, table)
    after = outside([dsum, dnorm], True)
    dq, dk, dv = mixer.pull_inner(q, k, v, segc, segr, wide, *prior, opened, table)
    dk, dv = mixer.pull_carry(k, v, tail, *after, dk, dv, table)
    dmix = jnp.concatenate([dq, dk, dv], axis=1)
    dot_one = lax.psum(
        jnp.sum(dmix.astype(F32) * mixed_in.astype(F32), axis=1, keepdims=True), "tensor"
    )
    dnormed_one = narrow(project_back(dmix, w_mix).astype(LOW)).astype(F32)
    grad_tokens = (
        grad_hidden
        + scale_one * norm1_gain[None, :] * dnormed_one
        - inputs * (scale_one * scale_one * dot_one / width)
    )

    grad_w_down = project_left(inner, c_full)
    grad_w_gate = project_left(normed_two, dgate)
    grad_w_up = project_left(normed_two, dup)
    grad_w_out = project_left(y, dh_full)
    grad_w_mix = project_left(normed_one, dmix)
    gain_one = jnp.sum(grad_w_mix * w_mix.astype(F32), axis=1)
    gain_two = jnp.sum(grad_w_gate * w_gate.astype(F32) + grad_w_up * w_up.astype(F32), axis=1)
    gain_grads = lax.psum(jnp.stack([gain_one, gain_two]), ("batch", "tensor")) / gains
    gain_grads = lax.dynamic_slice_in_dim(gain_grads, lax.axis_index("tensor") * slice_width, slice_width, 1)
    ffn = lax.psum([g.astype(LOW) for g in (grad_w_down, grad_w_gate, grad_w_up)], "batch")
    mix = lax.psum([g.astype(LOW) for g in (grad_w_out, grad_w_mix)], "batch")
    grad_w_down, grad_w_gate, grad_w_up = [g.astype(F32) for g in ffn]
    grad_w_out, grad_w_mix = [g.astype(F32) for g in mix]
    return (
        output,
        grad_tokens,
        gain_grads[0],
        grad_w_mix[:, :lanes],
        grad_w_mix[:, lanes : 2 * lanes],
        grad_w_mix[:, 2 * lanes :],
        grad_w_out,
        gain_grads[1],
        grad_w_gate,
        grad_w_up,
        grad_w_down,
    )


def solution(mesh):
    rows, cols = P("tensor", None), P(None, "tensor")
    both, one = P("batch", "tensor"), P("tensor")
    in_specs = (both, P(), one, cols, cols, cols, rows, one, cols, cols, rows, both)
    out_specs = (both, both, one, cols, cols, cols, rows, one, cols, cols, rows)
    return jax.shard_map(local, mesh=mesh, in_specs=in_specs, out_specs=out_specs, check_vma=False)
```

time: 1830 us -> 1080 us (0.59)
  waiting for transfers between devices: 1310 us -> 707 us
  matrix products: 278 us -> 135 us
  Pallas kernels: 0 us -> 41.7 us
  local copies, waits for them, and re-layouts: 59.1 us -> 29.2 us
    reduce_scatter x4, waiting for transfers between devices: 510 us -> 141 us  [narrow(): return lax.psum_scatter(part, 'tensor', scatter_dimension=1, tiled=True)]
    psum x1, waiting for transfers between devices: 510 us -> 273 us  [local(): mix = lax.psum([g.astype(LOW) for g in (grad_w_out, grad_w_mix)], 'batch')]
    dot_general x35 -> x15, matrix products: 278 us -> 135 us  [the longest x5 50.2 us: project_left(): return jnp.einsum('ti,tj->ij', left, right, preferred_element_type=F32)]
    pallas_call x0 -> x6, Pallas kernels: none -> 41.7 us  [call(): pl.pallas_call(body, grid=(self.heads,), in_specs=in_specs, out_specs=out...]
    unnamed x146 -> x128, local copies, waits for them, and re-layouts: 53.8 us -> 20 us
    convert_element_type x5 -> x13, other arithmetic: 11.1 us -> 35.5 us  [the longest x3 20.5 us: local(): grad_w_down, grad_w_gate, grad_w_up = [g.astype(F32) for g in ffn]]
    all_gather x6 -> x4, waiting for transfers between devices: 291 us -> 280 us  [widen(): return lax.all_gather(part, 'tensor', axis=1, tiled=True)]
    psum x5 -> x3, blocking collectives: 62.3 us -> 61.6 us  [the longest x1 42.6 us: local(): lax.psum(jnp.stack([gain_one, gain_two]), ('batch', 'tensor')) / gains]
  transfers between devices with their start and end apart: 11 -> 21, of which waited for: 9 -> 14; matrix products, arithmetic and copies ran while one was open for 11% -> 10% of each run, Pallas kernels for 0% -> 3%
where the time goes in v1:
time: 1080 us; the launch traced here: 1070 us
  waiting for transfers between devices  707 us (65%)
  matrix products  135 us (12%)
  blocking collectives  76.9 us (7%)
  other arithmetic  53.1 us (5%)
  Pallas kernels  41.7 us (4%)
  local copies, waits for them, and re-layouts  29.2 us (3%)
  between operations  15.7 us (1%)
    all_gather x4, waiting for transfers between devices, widen(): return lax.all_gather(part, 'tensor', axis=1, tiled=True)  280 us
    psum x1, waiting for transfers between devices, local(): mix = lax.psum([g.astype(LOW) for g in (grad_w_out, grad_w_mix)], 'batch')  273 us
    reduce_scatter x4, waiting for transfers between devices, narrow(): return lax.psum_scatter(part, 'tensor', scatter_dimension=1, tiled=True)  141 us
    dot_general x5, matrix products, project_left(): return jnp.einsum('ti,tj->ij', left, right, preferred_element_type=F32)  50.2 us
    dot_general x5, matrix products, project(): return jnp.dot(left, right, preferred_element_type=F32)  45.9 us
    psum x1, blocking collectives, local(): lax.psum(jnp.stack([gain_one, gain_two]), ('batch', 'tensor')) / gains  42.6 us
    pallas_call x6, Pallas kernels, call(): pl.pallas_call(body, grid=(self.heads,), in_specs=in_specs, out_specs=out...  41.7 us
    dot_general x5, matrix products, project_back(): return jnp.einsum('ti,ji->tj', left, right, preferred_element_type=F32)  39.1 us
  transfers between devices with their start and end apart: 21, of which 14 were waited for; matrix products, arithmetic and copies ran while one was open for 10% of the time, Pallas kernels for 3%

profile of v1, /device:TPU:0, one launch (start us, length us, event | category | flops | bytes accessed | tf_op | source)
XLA Modules:
  0.0 1068.8 jit_solution(12073381546807070057)
XLA Ops:
  9.5 1.3 fusion.20
  11.6 4.0 copy.41
  15.6 15.3 %all_gather.16 = f32[2,2048]{1,0:T(2,128)S(1)} all-gather(f32[2,512]{1,0:T(2,128)S(1)} %pad_maximum_fusion.3), channel_id=1, replica_groups=mesh['batch'=8,'tensor'=4] {'tensor'}, dimensions={1}, use_global_device_ids=true | all-gather | bytes 20480 | tf_op jit(solution)/shard_map/all_gather | solution.py:344
  30.9 2.2 and_convert_fusion
  33.7 59.5 %all-gather.5.cloned.1.call-done = bf16[1024,2048]{1,0:T(8,128)(2,1)} async-done(((bf16[1024,512]{1,0:T(8,128)(2,1)}), bf16[1024,2048]{1,0:T(8,128)(2,1)}) %all-gather.5.cloned.1.call-update) | async-done | bytes 4194320 | tf_op jit(solution)/shard_map/all_gather | solution.py:305
  93.2 3.2 fusion
  97.1 5.1 convolution_convert_fusion.5
  103.3 3.2 mix_state.1
  108.7 1.5 collective-permute-start.4
  110.1 1.0 fusion.18
  111.7 1.2 copy-done.3
  114.9 5.8 mix_inner.1
  120.6 1.3 copy-done.23
  122.0 1.5 collective-permute-start.5
  123.5 1.0 fusion.14
  126.0 4.2 collective-permute-done.2
  130.2 1.0 fusion.13.sum_ref
  131.2 5.7 mix_merge.1
  136.9 1.3 copy-done.21
  138.2 4.4 convolution_convert_fusion.3
  142.6 1.0 copy-done.18
  144.4 74.0 %reduce-scatter.5.cloned.1.call-done = bf16[1024,512]{1,0:T(8,128)(2,1)} async-done(((bf16[1024,2048]{1,0:T(8,128)(2,1)}), bf16[1024,512]{1,0:T(8,128)(2,1)}) %reduce-scatter.5.cloned.1.call-update) | async-done | bytes 1048592 | tf_op jit(solution)/shard_map/reduce_scatter | solution.py:309
  218.5 2.8 fusion.8
  221.5 79.9 %all-gather.9.cloned.1.call-done = bf16[1024,2048]{1,0:T(8,128)(2,1)} async-done(((bf16[1024,512]{1,0:T(8,128)(2,1)}), bf16[1024,2048]{1,0:T(8,128)(2,1)}) %all-gather.9.cloned.1.call-update) | async-done | bytes 4194320 | tf_op jit(solution)/shard_map/all_gather | solution.py:305
  301.4 10.8 %fusion.39 = f32[1024,1376]{0,1:T(8,128)} fusion(bf16[1024,2048]{1,0:T(8,128)(2,1)} %all-gather.9.cloned.1.call-done, bf16[1376,2048]{1,0:T(8,128)(2,1)} %param.23), kind=kOutput, calls=%fused_computation.83 | convolution fusion | flops 5771362304 | bytes 15466496 | tf_op jit(solution)/shard_map/ti,ji->tj/dot_general | solution.py:321
  312.2 70.6 %all-gather.7.cloned.1.call-done = bf16[1024,2048]{1,0:T(8,128)(2,1)} async-done(((bf16[1024,512]{1,0:T(8,128)(2,1)}), bf16[1024,2048]{1,0:T(8,128)(2,1)}) %all-gather.7.cloned.1.call-update) | async-done | bytes 4194320 | tf_op jit(solution)/shard_map/all_gather | solution.py:305
  382.8 3.2 fusion.3
  386.3 10.1 fusion.30
  396.4 15.1 %add_reduce_fusion.1 = (f32[1024]{0:T(1024)S(1)}, bf16[1024,1376]{0,1:T(8,128)(2,1)}, bf16[1024,1376]{0,1:T(8,128)(2,1)}, bf16[1024,1376]{0,1:T(8,128)(2,1)}) fusion(f32[1024,1376]{0,1:T(8,128)} %fusion.30, f32[1024,1376]{0,1:T(8,128)} %fusion.39, bf16[2048,1376]{0,1:T(8,128)(2,1)S(1)} %bitcast.67, bf16[1024,2048]{1,0:T(8,128)(2,1)S(1)} %copy-done.28, ...), kind=kOutput, calls=%fused_computation.13 | convolution fusion | flops 5809339392 | bytes 29573120 | tf_op jit(solution)/shard_map/dot_general | solution.py:313
  411.6 8.8 fusion.40
  420.4 8.4 add_convert_fusion
  428.9 9.1 psum.56
  438.0 66.4 %reduce-scatter.9.cloned.1.call-done = bf16[1024,512]{1,0:T(8,128)(2,1)} async-done(((bf16[1024,2048]{1,0:T(8,128)(2,1)}), bf16[1024,512]{1,0:T(8,128)(2,1)}) %reduce-scatter.9.cloned.1.call-update) | async-done | bytes 1048592 | tf_op jit(solution)/shard_map/reduce_scatter | solution.py:309
  504.4 3.9 fusion.23
  508.3 11.1 %convolution_convert_fusion.2 = bf16[1024,2048]{1,0:T(8,128)(2,1)} fusion(bf16[1024,1376]{0,1:T(8,128)(2,1)} %get-tuple-element.94, bf16[1376,2048]{1,0:T(8,128)(2,1)} %param.23), kind=kOutput, calls=%fused_computation.21 | convolution fusion | flops 5773459456 | bytes 12648448 | tf_op jit(solution)/shard_map/dot_general | solution.py:313
  519.6 70.1 %all-gather.11.cloned.1.call-done = bf16[1024,2048]{1,0:T(8,128)(2,1)} async-done(((bf16[1024,512]{1,0:T(8,128)(2,1)}), bf16[1024,2048]{1,0:T(8,128)(2,1)}) %all-gather.11.cloned.1.call-update) | async-done | bytes 4194320 | tf_op jit(solution)/shard_map/all_gather | solution.py:305
  589.6 6.0 fusion.41.dy_ref
  595.7 5.5 mix_pull_state.1
  601.2 1.3 copy-done.22
  604.6 1.4 collective-permute-start.10
  606.7 0.9 copy-done.10
  608.6 16.2 %mix_pull_inner.1 = (bf16[1024,64]{1,0:T(8,128)(2,1)S(1)}, f32[1024,64]{1,0:T(8,128)S(1)}, f32[1024,512]{1,0:T(8,128)S(1)}) custom-call(bf16[1024,64]{1,0:T(8,128)(2,1)S(1)} %copy-done.14, bf16[1024,64]{1,0:T(8,128)(2,1)S(1)} %copy-done.10, bf16[1024,512]{1,0:T(8,128)(2,1)S(1)} %copy-done.4, s32[1024,1]{1,0:T(8,128)S(1)} %copy.43.segc_ref, ...), custom_call_target="tpu_custom_call" | custom-call | flops 20000000000 | bytes 1048576 | tf_op jit(solution)/shard_map/mix_pull_inner/pallas_call | solution.py:224
  624.8 1.5 collective-permute-start.11
  627.1 2.0 collective-permute-done.11
  629.1 3.2 collective-permute-done.8
  632.5 5.4 mix_pull_carry.1
  637.9 5.1 convolution_convert_fusion.1
  643.1 10.6 convolution_convert_fusion
  653.7 9.1 fusion.24
  662.8 19.3 %fusion.32 = (bf16[2048,1376]{0,1:T(8,128)(2,1)}, f32[2048]{0:T(1024)S(1)}, bf16[2048,1376]{0,1:T(8,128)(2,1)}) fusion(bf16[2048,1376]{0,1:T(8,128)(2,1)} %param.22, f32[2048,1376]{0,1:T(8,128)} %fusion.24, bf16[2048,1376]{0,1:T(8,128)(2,1)} %param.21, bf16[1024,1376]{0,1:T(8,128)(2,1)S(1)} %copy-done.53, ...), kind=kOutput, calls=%fused_computation.76 | convolution fusion | flops 5802293248 | bytes 40849408 | tf_op jit(solution)/shard_map/ti,tj->ij/dot_general | solution.py:317
  682.2 6.0 convolution_convert_fusion.4
  688.2 5.2 fusion.33
  693.5 2.0 multiply_reduce_fusion.1
  695.5 9.9 psum.57
  705.4 42.6 %psum.58 = f32[2,2048]{1,0:T(2,128)S(1)} all-reduce(f32[2,2048]{1,0:T(2,128)S(1)} %pad_maximum_fusion.2), channel_id=1, replica_groups=mesh['batch'=8,'tensor'=4] {'batch','tensor'}, use_global_device_ids=true, to_apply=%region_15.16 | all-reduce | flops 4096 | bytes 32768 | tf_op jit(solution)/shard_map/psum | solution.py:407
  749.4 4.5 fusion.7
  754.0 272.8 %all-reduce.3.cloned.1.call-done = (bf16[2048,640]{0,1:T(8,128)(2,1)}, bf16[512,2048]{1,0:T(8,128)(2,1)}, bf16[2048,1376]{0,1:T(8,128)(2,1)}, bf16[2048,1376]{0,1:T(8,128)(2,1)}, bf16[1376,2048]{1,0:T(8,128)(2,1)}) async-done(((bf16[2048,640]{0,1:T(8,128)(2,1)}, bf16[512,2048]{1,0:T(8,128)(2,1)}, bf16[2048,1376]{0,1:T(8,128)(2,1)}, bf16[2048,1376]{0,1:T(8,128)(2,1)}, bf16[1376,2048]{1,0:T(8,128)(2,1)}), ...) | async-done | bytes 21626896 | tf_op jit(solution)/shard_map/psum | solution.py:410
  1026.8 2.1 fusion.34
  1028.9 4.1 slice.56
  1033.0 5.5 copy.49
  1038.5 2.7 convert_element_type.219
  1041.2 8.7 convert_element_type.221
  1049.9 5.9 convert_element_type.223
  1055.8 5.9 convert_element_type.225
  (189 shorter events, 18.7 us)
Async XLA Ops:
  7.2 131.0 %copy-start = (bf16[512,2048]{1,0:T(8,128)(2,1)S(1)}, bf16[512,2048]{1,0:T(8,128)(2,1)}, u32[]{:S(2)}) copy-start(bf16[512,2048]{1,0:T(8,128)(2,1)} %param.19) | copy-start | bytes 6291460
  7.2 8.4 copy-start.42
  7.2 8.4 copy-start.36
  7.2 86.0 %all-gather.5.cloned.1.call-start = ((), (), s32[]{:S(2)}) async-start(), calls=%async_computation.4 | async-start | bytes 5242880 | tf_op jit(solution)/shard_map/all_gather | solution.py:305
  8.0 210.5 %reduce-scatter.5.cloned.1.call-start = ((), (), s32[]{:S(2)}) async-start(), calls=%async_computation.5 | async-start | bytes 5242880 | tf_op jit(solution)/shard_map/reduce_scatter | solution.py:309
  11.6 85.4 %copy-start.48 = (bf16[2048,64]{0,1:T(8,128)(2,1)S(1)}, bf16[2048,64]{0,1:T(8,128)(2,1)}, u32[]{:S(2)}) copy-start(bf16[2048,64]{0,1:T(8,128)(2,1)} %param.17) | copy-start | bytes 786436
  33.7 68.5 %copy-start.44 = (f32[1,2048]{1,0:T(1,128)}, f32[1,2048]{1,0:T(1,128)S(1)}, u32[]{:S(2)}) copy-start(f32[1,2048]{1,0:T(1,128)S(1)} %get-tuple-element.106) | copy-start | bytes 24580
  97.1 6.3 copy-start.17
  107.3 2.9 collective-permute-start
  107.3 1.4 collective-permute-start.3
  108.7 13.3 %collective-permute-start.4 = (f32[4,8,256]{2,1,0:T(8,128)S(1)}, f32[4,8,256]{2,1,0:T(8,128)S(1)}, u32[]{:S(2)}, u32[]{:S(2)}) collective-permute-start(f32[4,8,256]{2,1,0:T(8,128)S(1)} %add.174), channel_id=1, source_target_pairs={{0,8},{4,12},{8,0},{12,4},{16,24},{20,28},{24,16},{28,20},{1,9},{5... | collective-permute-start | bytes 98312 | tf_op jit(solution)/shard_map/ppermute | solution.py:295
  111.1 12.4 %collective-permute-start.1 = (bf16[4,160,128]{2,1,0:T(8,128)(2,1)S(1)}, bf16[4,160,128]{2,1,0:T(8,128)(2,1)S(1)}, u32[]{:S(2)}, u32[]{:S(2)}) collective-permute-start(bf16[4,160,128]{2,1,0:T(8,128)(2,1)S(1)} %fusion.18), channel_id=1, source_target_pairs={{0,8},{4,12},{8,0},{12,4},{16,24},{20,28},{24,16},{28,20},{1,9},{5... | collective-permute-start | bytes 491528 | tf_op jit(solution)/shard_map/ppermute | solution.py:295
  114.9 16.4 %copy-start.5 = (f32[1024,1]{1,0:T(8,128)S(1)}, f32[1024,1]{1,0:T(8,128)}, u32[]{:S(2)}) copy-start(f32[1024,1]{1,0:T(8,128)} %get-tuple-element.103.open_ref) | copy-start | bytes 12292
  122.0 4.0 collective-permute-start.5
  124.5 5.7 collective-permute-start.2
  143.7 157.7 %all-gather.9.cloned.1.call-start = ((), (), s32[]{:S(2)}) async-start(), calls=%async_computation.8 | async-start | bytes 5242880 | tf_op jit(solution)/shard_map/all_gather | solution.py:305
  144.4 238.4 %all-gather.7.cloned.1.call-start = ((), (), s32[]{:S(2)}) async-start(), calls=%async_computation.6 | async-start | bytes 5242880 | tf_op jit(solution)/shard_map/all_gather | solution.py:305
  221.3 283.1 %reduce-scatter.9.cloned.1.call-start = ((), (), s32[]{:S(2)}) async-start(), calls=%async_computation.9 | async-start | bytes 5242880 | tf_op jit(solution)/shard_map/reduce_scatter | solution.py:309
  312.2 73.8 %copy-start.46 = (f32[1,2048]{1,0:T(1,128)S(1)}, f32[1,2048]{1,0:T(1,128)}, u32[]{:S(2)}) copy-start(f32[1,2048]{1,0:T(1,128)} %get-tuple-element.105) | copy-start | bytes 24580
  382.8 13.6 %slice-start.6 = ((s8[5636096]{0:T(1024)(128)(4,1)}), s8[4194304]{0:T(1024)(128)(4,1)S(1)}, s32[]{:S(2)}) async-start(s8[5636096]{0:T(1024)(128)(4,1)} %bitcast.66), calls=%async_computation.19 | async-start | bytes 8388608
  386.3 10.1 slice-start.7
  386.3 25.3 %slice-start.4 = ((s8[5636096]{0:T(1024)(128)(4,1)}), s8[4194304]{0:T(1024)(128)(4,1)S(1)}, s32[]{:S(2)}) async-start(s8[5636096]{0:T(1024)(128)(4,1)} %bitcast.64), calls=%async_computation.17 | async-start | bytes 8388608
  396.4 15.2 %slice-start.5 = ((s8[5636096]{0:T(1024)(128)(4,1)}), s8[1441792]{0:T(1024)(128)(4,1)S(1)}, s32[]{:S(2)}) async-start(s8[5636096]{0:T(1024)(128)(4,1)} %bitcast.64), calls=%async_computation.18 | async-start | bytes 2883584
  411.6 8.8 copy-start.52
  428.8 75.6 %copy-start.37 = (f32[512]{0:T(512)S(1)}, f32[512]{0:T(512)}, u32[]{:S(2)}) copy-start(f32[512]{0:T(512)} %param.20) | copy-start | bytes 6148
  428.8 160.8 %all-gather.11.cloned.1.call-start = ((), (), s32[]{:S(2)}) async-start(), calls=%async_computation.10 | async-start | bytes 5242880 | tf_op jit(solution)/shard_map/all_gather | solution.py:305
  438.0 81.5 %copy-start.34 = (f32[1024,1]{0,1:T(1,128)}, f32[1024,1]{0,1:T(1,128)S(1)}, u32[]{:S(2)}) copy-start(f32[1024,1]{0,1:T(1,128)S(1)} %multiply_multiply_fusion.1) | copy-start | bytes 12292
  508.3 241.0 %reduce-scatter.7.cloned.1.call-start = ((), (), s32[]{:S(2)}) async-start(), calls=%async_computation.7 | async-start | bytes 5242880 | tf_op jit(solution)/shard_map/reduce_scatter | solution.py:309
  519.5 229.9 %reduce-scatter.11.cloned.1.call-start = ((), (), s32[]{:S(2)}) async-start(), calls=%async_computation.11 | async-start | bytes 5242880 | tf_op jit(solution)/shard_map/reduce_scatter | solution.py:309
  589.6 6.0 copy-start.6
  589.6 6.0 copy-start.13
  589.6 6.0 copy-start.19
  595.7 11.0 %copy-start.4 = (bf16[1024,512]{1,0:T(8,128)(2,1)S(1)}, bf16[1024,512]{1,0:T(8,128)(2,1)}, u32[]{:S(2)}) copy-start(bf16[1024,512]{1,0:T(8,128)(2,1)} %copy-done.2) | copy-start | bytes 3145732
  595.7 11.0 %copy-start.7 = (f32[1024,1]{1,0:T(8,128)S(1)}, f32[1024,1]{1,0:T(8,128)}, u32[]{:S(2)}) copy-start(f32[1024,1]{1,0:T(8,128)} %get-tuple-element.103.open_ref) | copy-start | bytes 12292
  603.2 2.8 collective-permute-start.6
  603.2 1.4 collective-permute-start.9
  604.6 20.2 %collective-permute-start.10 = (f32[4,8,256]{2,1,0:T(8,128)S(1)}, f32[4,8,256]{2,1,0:T(8,128)S(1)}, u32[]{:S(2)}, u32[]{:S(2)}) collective-permute-start(f32[4,8,256]{2,1,0:T(8,128)S(1)} %add.190), channel_id=1, source_target_pairs={{0,8},{4,12},{8,0},{12,4},{16,24},{20,28},{24,16},{28,20},{1,9},{5... | collective-permute-start | bytes 98312 | tf_op jit(solution)/shard_map/ppermute | solution.py:295
  606.0 20.3 %collective-permute-start.7 = (bf16[4,160,128]{2,1,0:T(8,128)(2,1)S(1)}, bf16[4,160,128]{2,1,0:T(8,128)(2,1)S(1)}, u32[]{:S(2)}, u32[]{:S(2)}) collective-permute-start(bf16[4,160,128]{2,1,0:T(8,128)(2,1)S(1)} %fusion.19), channel_id=1, source_target_pairs={{0,8},{4,12},{8,0},{12,4},{16,24},{20,28},{24,16},{28,20},{1,9},{5... | collective-permute-start | bytes 491528 | tf_op jit(solution)/shard_map/ppermute | solution.py:295
  608.6 23.8 %copy-start.11 = (bf16[1024,64]{1,0:T(8,128)(2,1)S(1)}, bf16[1024,64]{1,0:T(8,128)(2,1)}, u32[]{:S(2)}) copy-start(bf16[1024,64]{1,0:T(8,128)(2,1)} %copy-done.8) | copy-start | bytes 393220
  624.8 13.0 %copy-start.15 = (bf16[1024,64]{1,0:T(8,128)(2,1)}, bf16[1024,64]{1,0:T(8,128)(2,1)S(1)}, u32[]{:S(2)}) copy-start(bf16[1024,64]{1,0:T(8,128)(2,1)S(1)} %get-tuple-element.32) | copy-start | bytes 393220
  624.8 4.3 collective-permute-start.11
  626.4 6.0 collective-permute-start.8
  643.0 10.7 %copy-start.47 = (f32[1,2048]{1,0:T(1,128)S(1)}, f32[1,2048]{1,0:T(1,128)}, u32[]{:S(2)}) copy-start(f32[1,2048]{1,0:T(1,128)} %get-tuple-element.105) | copy-start | bytes 24580
  643.0 383.8 %all-reduce.3.cloned.1.call-start = ((), (), s32[]{:S(2)}) async-start(), calls=%async_computation.12 | async-start | bytes 43253760 | tf_op jit(solution)/shard_map/psum | solution.py:410
  643.0 10.6 copy-start.29
  643.1 10.6 copy-start.54
  653.7 9.1 copy-start.53
  662.8 19.3 %copy-start.20 = (bf16[1024,512]{1,0:T(8,128)(2,1)S(1)}, bf16[1024,512]{1,0:T(8,128)(2,1)}, u32[]{:S(2)}) copy-start(bf16[1024,512]{1,0:T(8,128)(2,1)} %copy-done.18) | copy-start | bytes 3145732
  682.1 6.1 copy-start.16
  682.1 6.1 copy-start.27
  682.1 6.1 copy-start.32
  682.1 6.1 copy-start.40
  682.1 6.1 copy-start.45
  682.2 6.1 copy-start.51
  693.4 55.8 %copy-start.41 = (f32[1024]{0:T(1024)S(1)}, f32[1024]{0:T(1024)}, u32[]{:S(2)}) copy-start(f32[1024]{0:T(1024)} %get-tuple-element.109) | copy-start | bytes 12292
  693.4 56.0 %copy-start.24 = (bf16[1024,512]{1,0:T(8,128)(2,1)S(1)}, bf16[1024,512]{1,0:T(8,128)(2,1)}, u32[]{:S(2)}) copy-start(bf16[1024,512]{1,0:T(8,128)(2,1)} %param.13) | copy-start | bytes 3145732
  693.4 56.0 %copy-start.35 = (f32[1024,1]{0,1:T(1,128)S(1)}, f32[1024,1]{0,1:T(1,128)}, u32[]{:S(2)}) copy-start(f32[1024,1]{0,1:T(1,128)} %copy-done.34) | copy-start | bytes 12292
  693.4 56.0 %copy-start.38 = (f32[512]{0:T(512)S(1)}, f32[512]{0:T(512)}, u32[]{:S(2)}) copy-start(f32[512]{0:T(512)} %param.20) | copy-start | bytes 6148
  693.4 56.0 %copy-start.43 = (f32[512]{0:T(512)S(1)}, f32[512]{0:T(512)}, u32[]{:S(2)}) copy-start(f32[512]{0:T(512)} %param.15) | copy-start | bytes 6148
  1038.5 11.4 %slice-start.2 = ((s8[5636096]{0:T(1024)(128)(4,1)}), s8[4194304]{0:T(1024)(128)(4,1)S(1)}, s32[]{:S(2)}) async-start(s8[5636096]{0:T(1024)(128)(4,1)} %bitcast.43), calls=%async_computation.15 | async-start | bytes 8388608
  1041.2 8.7 slice-start.3
  1041.2 14.6 %slice-start = ((s8[5636096]{0:T(1024)(128)(4,1)}), s8[4194304]{0:T(1024)(128)(4,1)S(1)}, s32[]{:S(2)}) async-start(s8[5636096]{0:T(1024)(128)(4,1)} %bitcast.41), calls=%async_computation.13 | async-start | bytes 8388608
  1049.9 5.9 slice-start.1
  1055.8 5.9 copy-start.1
  (20 other events, 54.4 us)
Sparse Core Ops, SparseCore 0:
  9.6 83.5 all-gather.4
  143.8 74.6 reduce-scatter.4
  220.1 81.2 all-gather.8
  303.5 79.2 all-gather.6
  428.9 75.4 reduce-scatter.8
  508.4 81.1 all-gather.10
  592.5 75.2 reduce-scatter.6
  670.8 78.5 reduce-scatter.10
  754.7 272.0 all-reduce.2

commit v2 on v1

--- a/solution.py
+++ b/solution.py
@@ -15,6 +15,7 @@
 WIDE = 256
 ROWS = 160
 STRIP = 256
+CHUNKS = 2
 LOW = jnp.bfloat16
 F32 = jnp.float32
 
@@ -116,14 +117,15 @@
     y_ref[...] = (numer / total).astype(LOW)
 
 
-def pull_state_body(q_ref, dy_ref, y_ref, total_ref, open_ref, table_ref, wide_ref, sum_ref, norm_ref):
+def pull_state_body(q_ref, y_ref, total_ref, open_ref, table_ref, *refs):
+    *dy_refs, wide_ref, sum_ref, norm_ref = refs
     head = pl.program_id(0)
     table = table_ref[...]
     one, two = pickers(table, head, q_ref.shape[1])
     left, right = factors(q_ref[...], table, one, two)
     feats = (left * right * open_ref[...]).astype(LOW)
     inverse = 1.0 / total_ref[...]
-    dy = dy_ref[...]
+    dy = jnp.concatenate([r[...] for r in dy_refs], axis=0)
     dnumer = (dy * inverse).astype(LOW)
     ddenom = -jnp.sum(dy * y_ref[...].astype(F32), axis=1, keepdims=True) * inverse
     ddenom = jnp.where(lax.broadcasted_iota(jnp.int32, ddenom.shape, 1) < 8, ddenom, 0.0).astype(LOW)
@@ -260,10 +262,11 @@
     def pull_state(self, q, dy, y, total, opened, table):
         return self.call(
             pull_state_body, "mix_pull_state",
-            [self.thin, self.head, self.head, self.head, self.column, self.table],
+            [self.thin, self.head, self.head, self.column, self.table]
+            + [pl.BlockSpec((d.shape[0], HV), lambda h: (0, h)) for d in dy],
             [self.pair, self.sum, self.norm],
             [shape((self.tokens, self.heads * 2 * HV), LOW)] + self.state_shapes, [], 5,
-            q, dy, y, total, opened, table,
+            q, y, total, opened, table, *dy,
         )
 
     def pull_inner(self, q, k, v, segc, segr, wide, total, norm, opened, table):
@@ -301,24 +304,337 @@
     return before
 
 
+def padded(width):
+    return -(-width // 16) * 16
+
+
+def batch_orders():
+    count = lax.axis_size("batch")
+    bits = [1 << b for b in range(count.bit_length() - 1)]
+    return bits[:1] + bits[1:], bits[:1] + bits[:0:-1]
+
+
+def block_order():
+    count = lax.axis_size("batch")
+    first, second = batch_orders()
+    relative, places = [], []
+    for step in range(count):
+        at = sum(bit for n, bit in enumerate(first) if step >> (len(first) - 1 - n) & 1)
+        relative.append(at)
+        places.append(sum(1 << (len(second) - 1 - n) for n, bit in enumerate(second) if at & bit))
+    blocks = jnp.asarray(np.array(relative, np.int32)) ^ lax.axis_index("batch").astype(jnp.int32)
+    return blocks, places
+
+
+def cost(micros):
+    return pl.CostEstimate(flops=int(micros * 1e9), bytes_accessed=1 << 20, transcendentals=0)
+
+
+BIG = pltpu.CompilerParams(dimension_semantics=("arbitrary",), vmem_limit_bytes=56 * 1024 * 1024)
+
+
+def grad_blocks_body(blocks, swap, *refs, groups):
+    out_a, out_b = refs[-2:]
+    refs = list(refs[:-2])
+    at = 0
+    for rows, parts in groups:
+        value = None
+        for _ in range(parts):
+            term = nn(refs[1][...], refs[0][...])
+            refs = refs[2:]
+            value = term if value is None else value + term
+        for n, out in enumerate((out_a, out_b)):
+            half = value[n * rows // 2 : (n + 1) * rows // 2].astype(LOW)
+            gap = padded(rows // 2) - rows // 2
+            if gap:
+                half = jnp.concatenate([half, jnp.zeros((gap, half.shape[1]), LOW)], axis=0)
+            out[0, at : at + padded(rows // 2), :] = half
+        at += padded(rows // 2)
+
+
+def grad_blocks(name, groups, far, micros):
+    count = lax.axis_size("batch")
+    split = count // 2
+    width = groups[0][0][0].shape[1]
+    columns = width // count
+    blocks, places = block_order()
+    base = split if far else 0
+    in_specs, operands, kinds, rows = [], [], [], 0
+    for parts in groups:
+        for left, right in parts:
+            in_specs.append(pl.BlockSpec((left.shape[0], columns), lambda s, b, w: (0, b[s])))
+            in_specs.append(pl.BlockSpec(right.shape, lambda s, b, w: (0, 0)))
+            operands += [left, right]
+        kinds.append((parts[0][1].shape[0], len(parts)))
+        rows += padded(parts[0][1].shape[0] // 2)
+    size = (1, rows, columns)
+    return pl.pallas_call(
+        functools.partial(grad_blocks_body, groups=tuple(kinds)),
+        grid_spec=pltpu.PrefetchScalarGridSpec(
+            num_scalar_prefetch=2,
+            grid=(split,),
+            in_specs=in_specs,
+            out_specs=[
+                pl.BlockSpec(size, lambda s, b, w: (s, 0, 0)),
+                pl.BlockSpec(size, lambda s, b, w: (w[s], 0, 0)),
+            ],
+        ),
+        out_shape=[shape((split, rows, columns), LOW)] * 2,
+        name=name,
+        compiler_params=BIG,
+        cost_estimate=cost(micros),
+    )(
+        blocks[base : base + split],
+        jnp.asarray(np.array(places[base : base + split], np.int32) - base),
+        *operands,
+    )
+
+
+def flip(value, bit):
+    return lax.ppermute(value, "batch", [(i, i ^ bit) for i in range(lax.axis_size("batch"))])
+
+
+def added(one, other):
+    return (one.astype(F32) + other.astype(F32)).astype(LOW)
+
+
+class Exchange:
+    def __init__(self, far):
+        self.orders = batch_orders()
+        self.steps = len(self.orders[0])
+        self.away, self.near, self.came = [[f] for f in far], None, [[], []]
+        self.step = 0
+
+    def get(self):
+        return [self.away, self.near, self.came]
+
+    def put(self, values):
+        self.away, self.near, self.came = values
+
+    def send(self, limit=None):
+        n = self.step
+        if n == 2 * self.steps:
+            return
+        for half, order in enumerate(self.orders):
+            bit = order[n if n < self.steps else 2 * self.steps - 1 - n]
+            first = len(self.came[half])
+            last = len(self.away[half]) if limit is None else first + limit
+            self.came[half] += [flip(a, bit) for a in self.away[half][first:last]]
+
+    def take(self):
+        n = self.step
+        if n == 2 * self.steps:
+            return
+        self.step += 1
+        if n < self.steps:
+            half = self.near[0].shape[0] // 2
+            pairs = [(k, c[0]) for k, c in zip(self.near, self.came)]
+            if half:
+                self.away = [[added(k[half:], c[half:])] for k, c in pairs]
+                self.near = [added(k[:half], c[:half]) for k, c in pairs]
+            else:
+                self.near = [added(k, c) for k, c in pairs]
+                self.away = [[k] for k in self.near]
+        else:
+            self.away = [a + c for a, c in zip(self.away, self.came)]
+        self.came = [[], []]
+
+    def run(self):
+        while self.step < 2 * self.steps:
+            self.send()
+            self.take()
+        return self.away
+
+
+def place_body(blocks, table, *refs, outs, count):
+    step = pl.program_id(0)
+    pieces = count
+    chosen = []
+    for n in range(2):
+        which = table[n, step]
+        group = refs[n * pieces : (n + 1) * pieces]
+        value = group[0][0]
+        for m in range(1, pieces):
+            value = jnp.where(which == m, group[m][0], value)
+        chosen.append(value)
+    results = refs[2 * pieces :]
+    for start, rows, targets in outs:
+        both = jnp.concatenate([c[start : start + rows // 2].astype(F32) for c in chosen], axis=0)
+        for index, first, size, turned in targets:
+            part = both[first : first + size]
+            results[index][...] = part.T if turned else part
+
+
+def place_blocks(name, pieces, outs, width, micros):
+    count = lax.axis_size("batch")
+    columns = width // count
+    blocks, places = block_order()
+    table = np.array([list(range(count)), places], np.int32)
+    size = pieces[0][0].shape[1:]
+    piece = pl.BlockSpec((1,) + size, lambda s, b, t: (0, 0, 0), pipeline_mode=pl.Buffered(1))
+    out_specs, out_shape, layout, start = [], [], [], 0
+    for rows, targets in outs:
+        listed = []
+        for first, used, turned in targets:
+            listed.append((len(out_shape), first, used, turned))
+            if turned:
+                out_specs.append(pl.BlockSpec((columns, used), lambda s, b, t: (b[s], 0)))
+                out_shape.append(shape((width, used), F32))
+            else:
+                out_specs.append(pl.BlockSpec((used, columns), lambda s, b, t: (0, b[s])))
+                out_shape.append(shape((used, width), F32))
+        layout.append((start, rows, tuple(listed)))
+        start += padded(rows // 2)
+    return pl.pallas_call(
+        functools.partial(place_body, outs=tuple(layout), count=count),
+        grid_spec=pltpu.PrefetchScalarGridSpec(
+            num_scalar_prefetch=2,
+            grid=(count,),
+            in_specs=[piece] * (2 * count),
+            out_specs=out_specs,
+        ),
+        out_shape=out_shape,
+        name=name,
+        compiler_params=BIG,
+        cost_estimate=cost(micros),
+    )(blocks, jnp.asarray(table), *pieces[0], *pieces[1])
+
+
+def batch_sum(value):
+    bit = 1
+    while bit < lax.axis_size("batch"):
+        value = value + flip(value, bit)
+        bit *= 2
+    return value
+
+
+def after(values, *others):
+    return lax.optimization_barrier((values, others))[0]
+
+
+def lock(*items):
+    values = lax.optimization_barrier([i.get() if hasattr(i, "get") else i for i in items])
+    for item, value in zip(items, values):
+        if hasattr(item, "put"):
+            item.put(value)
+    return [v for i, v in zip(items, values) if not hasattr(i, "get")]
+
+
+class Gather:
+    def __init__(self, *parts):
+        self.right, self.left = [list(parts)], [list(parts)]
+        self.hops = 0
+        self.least = lax.axis_size("tensor") - 1
+
+    def get(self):
+        return [self.right, self.left]
+
+    def put(self, values):
+        self.right, self.left = values
+
+    def hop(self):
+        count = lax.axis_size("tensor")
+        self.hops += 1
+        to_right = [(k, k + 1) for k in range(self.hops - 1, count - 1)]
+        to_left = [(k, k - 1) for k in range(1, count - self.hops + 1)]
+        self.right.append([lax.ppermute(a, "tensor", to_right) for a in self.right[-1]])
+        self.left.append([lax.ppermute(a, "tensor", to_left) for a in self.left[-1]])
+
+    def run(self):
+        while self.hops < self.least:
+            self.hop()
+        return self
+
+    def pieces(self, n=0):
+        count, place = lax.axis_size("tensor"), lax.axis_index("tensor")
+        return [self.right[0][n]] + [
+            jnp.where(place + r < count, self.left[r][n], self.right[count - r][n]) for r in range(1, count)
+        ]
+
+    def total(self, n=0):
+        return sum(a[n] for a in self.right) + sum(a[n] for a in self.left[1:])
+
+
+class Scatter:
+    def __init__(self, make):
+        self.make, self.came, self.made = make, [], {}
+        self.left = lax.axis_size("tensor") - 1
+        self.prepare()
+
+    def prepare(self):
+        count = lax.axis_size("tensor")
+        for r in (self.left, (count - self.left) % count):
+            if r not in self.made:
+                self.made[r] = self.make(r)
+
+    def get(self):
+        return [self.came, self.made]
+
+    def put(self, values):
+        self.came, self.made = values
+
+    def hop(self):
+        count = lax.axis_size("tensor")
+        sends = [self.made[self.left], self.made[count - self.left]]
+        if self.came:
+            sends = [s + c.astype(F32) for s, c in zip(sends, self.came)]
+        sends = [s.astype(LOW) for s in sends]
+        self.came = [
+            lax.ppermute(sends[0], "tensor", [(k, k + 1) for k in range(0, count - self.left)]),
+            lax.ppermute(sends[1], "tensor", [(k, k - 1) for k in range(self.left, count)]),
+        ]
+        self.left -= 1
+        self.prepare()
+
+    def result(self):
+        return self.made[0] + self.came[0].astype(F32) + self.came[1].astype(F32)
+
+
+def copy_body(turn, in_ref, out_ref):
+    out_ref[...] = in_ref[...]
+
+
+def straighten(array):
+    count = lax.axis_size("tensor")
+    turn = (jnp.arange(count, dtype=jnp.int32) - lax.axis_index("tensor")) % count
+    size = (array.shape[0], array.shape[1] // count)
+    return pl.pallas_call(
+        copy_body,
+        grid_spec=pltpu.PrefetchScalarGridSpec(
+            num_scalar_prefetch=1,
+            grid=(count,),
+            in_specs=[pl.BlockSpec(size, lambda n, t: (0, t[n]))],
+            out_specs=pl.BlockSpec(size, lambda n, t: (0, n)),
+        ),
+        out_shape=shape(array.shape, array.dtype),
+        name="straighten",
+        compiler_params=BIG,
+        cost_estimate=cost(4),
+    )(turn, array)
+
+
 def widen(part):
     return lax.all_gather(part, "tensor", axis=1, tiled=True)
 
 
 def narrow(part):
-    return lax.psum_scatter(part, "tensor", scatter_dimension=1, tiled=True)
+    return lax.psum_scatter(part, "tensor", scatter_dimension=1, tiled=True).astype(F32)
 
 
 def project(left, right):
     return jnp.dot(left, right, preferred_element_type=F32)
 
 
-def project_left(left, right):
-    return jnp.einsum("ti,tj->ij", left, right, preferred_element_type=F32)
-
-
 def project_back(left, right):
     return jnp.einsum("ti,ji->tj", left, right, preferred_element_type=F32)
+
+
+def across(left, right):
+    return jnp.einsum("it,ij->tj", left, right, preferred_element_type=F32)
+
+
+def row_sum(values):
+    return jnp.sum(values, axis=1, keepdims=True)
 
 
 def local(
@@ -341,86 +657,190 @@
     table = jnp.asarray(feature_table())
     mixer = Mixer(count, heads)
 
+    size, place = lax.axis_size("tensor"), lax.axis_index("tensor")
+    half = count // 2
+    cut = lambda a: (a[:half], a[half:])
+    join = lambda *parts: jnp.concatenate(parts, axis=0)
+    c_a, c_b = cut(cotangent)
+    w_gate, w_up = w_gate.T, w_up.T
+    units = w_gate.shape[0]
+
+    x_full = widen(tokens)
     gains = lax.all_gather(jnp.stack([norm1_gain, norm2_gain]), "tensor", axis=1, tiled=True)
-    x_full = widen(tokens)
-    c_full = widen(cotangent)
-    inputs = tokens.astype(F32)
+    w_mix = jnp.concatenate([w_query, w_key, w_value], axis=1)
+    gather_c = Gather(cotangent)
+    x_full, gains, w_mix = lock(x_full, gains, w_mix, gather_c)
+
+    gather_c.hop()
     x_wide = x_full.astype(F32)
-    scale_one = lax.rsqrt(jnp.mean(x_wide * x_wide, axis=1, keepdims=True) + EPSILON)
+    scale_one = lax.rsqrt(row_sum(x_wide * x_wide) / width + EPSILON)
     normed_one = (x_wide * scale_one * gains[0:1]).astype(LOW)
-    w_mix = jnp.concatenate([w_query, w_key, w_value], axis=1)
     mixed_in = project(normed_one, w_mix).astype(LOW)
     q, k, v = mixed_in[:, :lanes], mixed_in[:, lanes : 2 * lanes], mixed_in[:, 2 * lanes :]
-
     carry = mixer.state(k, v, tail, table)
     prior = outside(carry, False)
     numer, denom = mixer.inner(q, k, v, segc, segr)
     y, total = mixer.merge(q, numer, denom, *prior, opened, table)
-
-    hidden = inputs + narrow(project(y, w_out).astype(LOW)).astype(F32)
-    hidden_full = widen(hidden.astype(LOW)).astype(F32)
-    scale_two = lax.rsqrt(jnp.mean(hidden_full * hidden_full, axis=1, keepdims=True) + EPSILON)
-    normed_two = (hidden_full * scale_two * gains[1:2]).astype(LOW)
-    gate = project(normed_two, w_gate)
-    up = project(normed_two, w_up)
-    sig = jax.nn.sigmoid(gate)
-    silu = gate * sig
-    inner = (silu * up).astype(LOW)
-    output = (hidden + narrow(project(inner, w_down).astype(LOW)).astype(F32)).astype(LOW)
-
-    dinner = project_back(c_full, w_down)
-    dgate = (dinner * up * sig * (1.0 + gate * (1.0 - sig))).astype(LOW)
-    dup = (dinner * silu).astype(LOW)
-    dot_two = lax.psum(
-        jnp.sum(dgate.astype(F32) * gate + dup.astype(F32) * up, axis=1, keepdims=True), "tensor"
+    columns = lambda w, r: lax.dynamic_slice_in_dim(w, ((place + r) % size) * slice_width, slice_width, 1)
+    scatter = Scatter(lambda r: project(y, columns(w_out, r)))
+    y, total = lock(y, total, gather_c, scatter)
+    while scatter.left:
+        scatter.hop()
+        if gather_c.hops < gather_c.least:
+            gather_c.hop()
+        lock(scatter, gather_c)
+    hidden = tokens.astype(F32) + scatter.result()
+    hidden_a, hidden_b = cut(hidden)
+    low_a, low_b = cut(hidden.astype(LOW))
+    hidden_a, hidden_b, low_a, low_b = lock(hidden_a, hidden_b, low_a, low_b)
+
+    wide_a = widen(low_a)
+    c_full = straighten(jnp.concatenate(gather_c.pieces(), axis=1))
+    ca_full, cb_full = cut(c_full)
+    dinner_a = project_back(w_down, ca_full)
+    dinner_b = project_back(w_down, cb_full)
+    wide_a, c_full, dinner_a, dinner_b = lock(wide_a, c_full, dinner_a, dinner_b)
+    ca_full, cb_full = cut(c_full)
+
+    def feed(wide, dinner):
+        wide32 = wide.astype(F32)
+        scale = lax.rsqrt(row_sum(wide32 * wide32) / width + EPSILON)
+        normed = (wide32 * scale * gains[1:2]).astype(LOW)
+        gate = project_back(w_gate, normed)
+        up = project_back(w_up, normed)
+        sig = jax.nn.sigmoid(gate)
+        silu = gate * sig
+        inner = (silu * up).astype(LOW)
+        dgate = (dinner * up * sig * (1.0 + gate * (1.0 - sig))).astype(LOW)
+        dup = (dinner * silu).astype(LOW)
+        pulled = (across(dgate, w_gate) + across(dup, w_up)).astype(LOW)
+        return scale, normed, inner, dgate, dup, pulled
+
+    wide_b = widen(low_b)
+    wide_b, (scale_a, normed_a, inner_a, dgate_a, dup_a, part) = lock(wide_b, feed(wide_a, dinner_a))
+
+    back_a = narrow(part)
+    scale_b, normed_b, inner_b, dgate_b, dup_b, part = feed(wide_b, dinner_b)
+    groups = [
+        [(normed_a, dgate_a), (normed_b, dgate_b)],
+        [(normed_a, dup_a), (normed_b, dup_b)],
+        [(ca_full, inner_a), (cb_full, inner_b)],
+    ]
+    ffn = Exchange(grad_blocks("grad_ffn_far", groups, True, 16))
+    back_a, scale_b, normed_b, inner_b, dgate_b, dup_b, part = lock(
+        back_a, scale_b, normed_b, inner_b, dgate_b, dup_b, part, ffn
     )
-    dnormed_two = narrow((project_back(dgate, w_gate) + project_back(dup, w_up)).astype(LOW)).astype(F32)
-    grad_hidden = (
-        cotangent.astype(F32)
-        + scale_two * norm2_gain[None, :] * dnormed_two
-        - hidden * (scale_two * scale_two * dot_two / width)
+
+    def turned(c, scale, back, hidden):
+        scaled = scale * back
+        return c.astype(F32) + norm2_gain[None, :] * scaled, jnp.sum(scaled * hidden, axis=0)
+
+    def spread(u, c, wide, scale, local_u, hidden):
+        u, wide = u.astype(F32), wide.astype(F32)
+        dot = row_sum((u - c.astype(F32)) * wide) * scale * scale / width
+        dh = (u - wide * dot).astype(LOW)
+        return dh, local_u - hidden * dot, project_back(dh, w_out)
+
+    back_b = narrow(part)
+    u_a, gain_a = turned(c_a, scale_a, back_a, hidden_a)
+    low_a = u_a.astype(LOW)
+    groups = [
+        [(normed_a, dgate_a), (normed_b, dgate_b)],
+        [(normed_a, dup_a), (normed_b, dup_b)],
+        [(ca_full, inner_a), (cb_full, inner_b)],
+    ]
+    ffn.send()
+    ffn.near = grad_blocks("grad_ffn_near", groups, False, 16)
+    ffn.take()
+    ffn.send()
+    back_b, u_a, gain_a, low_a, ffn.away, ffn.near = lock(back_b, u_a, gain_a, low_a, ffn.away, ffn.near)
+
+    wide_u = widen(low_a)
+    u_b, gain_b = turned(c_b, scale_b, back_b, hidden_b)
+    low_b = u_b.astype(LOW)
+    parts = [across(m, w_down).astype(LOW) for m in (inner_a, inner_b)]
+    wide_u, u_b, gain_b, low_b, parts = lock(wide_u, u_b, gain_b, low_b, parts, ffn)
+
+    wide_v = widen(low_b)
+    ffn.take()
+    ffn.send()
+    dh_a, grad_hidden_a, dy_a = spread(wide_u, ca_full, wide_a, scale_a, u_a, hidden_a)
+    ffn.take()
+    ffn.send()
+    wide_v, dh_a, grad_hidden_a, dy_a = lock(wide_v, dh_a, grad_hidden_a, dy_a, ffn)
+
+    down = narrow(join(*parts))
+    ffn.take()
+    ffn.send(1)
+    dh_b, grad_hidden_b, dy_b = spread(wide_v, cb_full, wide_b, scale_b, u_b, hidden_b)
+    wide, dsum, dnorm = mixer.pull_state(q, [dy_a, dy_b], y, total, opened, table)
+    wide, dsum, dnorm = lock(wide, dsum, dnorm, ffn)
+    following = outside([dsum, dnorm], True)
+    dq, dk, dv = mixer.pull_inner(q, k, v, segc, segr, wide, *prior, opened, table)
+    following, dq, dk, dv = lock(following, dq, dk, dv, ffn)
+    ffn.send()
+    dk, dv = mixer.pull_carry(k, v, tail, *following, dk, dv, table)
+    dmix = jnp.concatenate([dq, dk, dv], axis=1)
+    part = project_back(dmix, w_mix).astype(LOW)
+    down, part, dmix, dh_b, grad_hidden_b = lock(down, part, dmix, dh_b, grad_hidden_b)
+
+    back = narrow(part)
+    y_a, y_b = cut(y)
+    groups = [[(normed_one, dmix.T)], [(dh_a, y_a.T), (dh_b, y_b.T)]]
+    mix = Exchange(grad_blocks("grad_mix_far", groups, True, 5))
+    mix.send()
+    mix.near = grad_blocks("grad_mix_near", groups, False, 5)
+    dots = Gather(row_sum(dmix.astype(F32) * mixed_in.astype(F32)).reshape(count // 128, 128)).run()
+    lock(mix, ffn)
+    mix.take()
+    mix.send()
+    ffn.take()
+    ffn.send()
+    output = (join(hidden_a, hidden_b) + down).astype(LOW)
+    output = lock(mix, ffn, output, dots)[0]
+    mix.take()
+    mix.send()
+    ffn.take()
+    grad_w_gate, grad_w_up, grad_w_down = place_blocks(
+        "place_ffn", ffn.run(), [(units, [(0, units, False)])] * 3, width, 20
     )
-    dh_full = widen(grad_hidden.astype(LOW))
-    dy = project_back(dh_full, w_out)
-    wide, dsum, dnorm = mixer.pull_state(q, dy, y, total, opened, table)
-    after = outside([dsum, dnorm], True)
-    dq, dk, dv = mixer.pull_inner(q, k, v, segc, segr, wide, *prior, opened, table)
-    dk, dv = mixer.pull_carry(k, v, tail, *after, dk, dv, table)
-    dmix = jnp.concatenate([dq, dk, dv], axis=1)
-    dot_one = lax.psum(
-        jnp.sum(dmix.astype(F32) * mixed_in.astype(F32), axis=1, keepdims=True), "tensor"
+    mix.take()
+    mix.send()
+    mix.take()
+    mix.send()
+    back, grad_w_gate, grad_w_up, grad_w_down, output = lock(
+        back, grad_w_gate, grad_w_up, grad_w_down, output, mix
     )
-    dnormed_one = narrow(project_back(dmix, w_mix).astype(LOW)).astype(F32)
+    inputs = tokens.astype(F32)
+    gain_one = jnp.sum(back * inputs * scale_one, axis=0)
+    gain_grads = batch_sum(jnp.stack([gain_one, gain_a + gain_b]))
     grad_tokens = (
-        grad_hidden
-        + scale_one * norm1_gain[None, :] * dnormed_one
-        - inputs * (scale_one * scale_one * dot_one / width)
+        join(grad_hidden_a, grad_hidden_b)
+        + scale_one * norm1_gain[None, :] * back
+        - inputs * (scale_one * scale_one * dots.total().reshape(count, 1) / width)
     )
-
-    grad_w_down = project_left(inner, c_full)
-    grad_w_gate = project_left(normed_two, dgate)
-    grad_w_up = project_left(normed_two, dup)
-    grad_w_out = project_left(y, dh_full)
-    grad_w_mix = project_left(normed_one, dmix)
-    gain_one = jnp.sum(grad_w_mix * w_mix.astype(F32), axis=1)
-    gain_two = jnp.sum(grad_w_gate * w_gate.astype(F32) + grad_w_up * w_up.astype(F32), axis=1)
-    gain_grads = lax.psum(jnp.stack([gain_one, gain_two]), ("batch", "tensor")) / gains
-    gain_grads = lax.dynamic_slice_in_dim(gain_grads, lax.axis_index("tensor") * slice_width, slice_width, 1)
-    ffn = lax.psum([g.astype(LOW) for g in (grad_w_down, grad_w_gate, grad_w_up)], "batch")
-    mix = lax.psum([g.astype(LOW) for g in (grad_w_out, grad_w_mix)], "batch")
-    grad_w_down, grad_w_gate, grad_w_up = [g.astype(F32) for g in ffn]
-    grad_w_out, grad_w_mix = [g.astype(F32) for g in mix]
+    values = heads * HV
+    grad_w_query, grad_w_key, grad_w_value, grad_w_out = place_blocks(
+        "place_mix",
+        mix.run(),
+        [
+            (2 * lanes + values, [(0, lanes, False), (lanes, lanes, False), (2 * lanes, values, True)]),
+            (values, [(0, values, False)]),
+        ],
+        width,
+        5,
+    )
     return (
         output,
         grad_tokens,
         gain_grads[0],
-        grad_w_mix[:, :lanes],
-        grad_w_mix[:, lanes : 2 * lanes],
-        grad_w_mix[:, 2 * lanes :],
+        grad_w_query.T,
+        grad_w_key.T,
+        grad_w_value,
         grad_w_out,
         gain_grads[1],
-        grad_w_gate,
-        grad_w_up,
+        grad_w_gate.T,
+        grad_w_up.T,
         grad_w_down,
     )
 

time: 1080 us -> 775 us (0.72)
  waiting for transfers between devices: 707 us -> 322 us
  Pallas kernels: 41.7 us -> 121 us
  starting transfers between devices: 10.1 us -> 72.6 us
  blocking collectives: 76.9 us -> 14.9 us
  matrix products: 135 us -> 84 us
  other arithmetic: 53.1 us -> 93 us
  local copies, waits for them, and re-layouts: 29.2 us -> 42.1 us
    psum x1 -> x0, waiting for transfers between devices: 273 us -> none  [local(): mix = lax.psum([g.astype(LOW) for g in (grad_w_out, grad_w_mix)], 'batch')]
    ppermute x0 -> x61, waiting for transfers between devices: none -> 185 us  [the longest x43 113 us: flip(): lax.ppermute(value, 'batch', [(i, i ^ bit) for i in range(lax.axis_size('...]
    all_gather x4 -> x5, waiting for transfers between devices: 280 us -> 101 us  [widen(): return lax.all_gather(part, 'tensor', axis=1, tiled=True)]
    reduce_scatter x4, waiting for transfers between devices: 141 us -> 26.8 us  [narrow(): lax.psum_scatter(part, 'tensor', scatter_dimension=1, tiled=True)]
    pallas_call x0 -> x7, Pallas kernels: none -> 79 us  [the longest x4 47.6 us: grad_blocks(): pl.pallas_call(functools.partial(grad_blocks_body, groups=tuple(kinds)),...]
    psum x3 -> x0, blocking collectives: 61.6 us -> none  [the longest x1 42.6 us: local(): lax.psum(jnp.stack([gain_one, gain_two]), ('batch', 'tensor')) / gains]
    ppermute x0 -> x61, starting transfers between devices: none -> 61.2 us  [the longest x43 30.9 us: flip(): lax.ppermute(value, 'batch', [(i, i ^ bit) for i in range(lax.axis_size('...]
    dot_general x5, matrix products: 45.9 us -> 5.86 us  [project(): return jnp.dot(left, right, preferred_element_type=F32)]
  transfers between devices with their start and end apart: 21 -> 82, of which waited for: 14 -> 39; matrix products, arithmetic and copies ran while one was open for 10% -> 22% of each run, Pallas kernels for 3% -> 14%
where the time goes in v2:
time: 775 us; the launch traced here: 766 us
  waiting for transfers between devices  322 us (42%)
  Pallas kernels  121 us (16%)
  other arithmetic  93 us (12%)
  matrix products  84 us (11%)
  starting transfers between devices  72.6 us (9%)
  local copies, waits for them, and re-layouts  42.1 us (5%)
  between operations  16.4 us (2%)
  blocking collectives  14.9 us (2%)
    ppermute x43, waiting for transfers between devices, flip(): lax.ppermute(value, 'batch', [(i, i ^ bit) for i in range(lax.axis_size('...  113 us
    all_gather x5, waiting for transfers between devices, widen(): return lax.all_gather(part, 'tensor', axis=1, tiled=True)  101 us
    pallas_call x4, Pallas kernels, grad_blocks(): pl.pallas_call(functools.partial(grad_blocks_body, groups=tuple(kinds)),...  47.6 us
    dot_general x9, matrix products, project_back(): return jnp.einsum('ti,ji->tj', left, right, preferred_element_type=F32)  46.6 us
    ppermute x3, waiting for transfers between devices, hop(): lax.ppermute(sends[0], 'tensor', [(k, k + 1) for k in range(0, count - se...  43 us
    pallas_call x6, Pallas kernels, call(): pl.pallas_call(body, grid=(self.heads,), in_specs=in_specs, out_specs=out...  42.2 us
    dot_general x6, matrix products, across(): return jnp.einsum('it,ij->tj', left, right, preferred_element_type=F32)  31.5 us
    ppermute x43, starting transfers between devices, flip(): lax.ppermute(value, 'batch', [(i, i ^ bit) for i in range(lax.axis_size('...  30.9 us
  transfers between devices with their start and end apart: 82, of which 39 were waited for; matrix products, arithmetic and copies ran while one was open for 22% of the time, Pallas kernels for 14%

profile of v2, /device:TPU:0, one launch (start us, length us, event | category | flops | bytes accessed | tf_op | source)
XLA Modules:
  0.0 766.5 jit_solution(5184060028941916751)
XLA Ops:
  15.0 14.9 %all_gather.19 = f32[2,2048]{1,0:T(2,128)S(1)} all-gather(f32[2,512]{1,0:T(2,128)S(1)} %pad_maximum_fusion.4), channel_id=1, replica_groups=mesh['batch'=8,'tensor'=4] {'tensor'}, dimensions={1}, use_global_device_ids=true | all-gather | bytes 20480 | tf_op jit(solution)/shard_map/all_gather | solution.py:669
  32.3 3.9 pad_maximum_fusion.2
  36.3 57.0 %all-gather.6.cloned.1.call-done = bf16[1024,2048]{1,0:T(8,128)(2,1)} async-done(((bf16[1024,512]{1,0:T(8,128)(2,1)}), bf16[1024,2048]{1,0:T(8,128)(2,1)}) %all-gather.6.cloned.1.call-update) | async-done | bytes 4194320 | tf_op jit(solution)/shard_map/all_gather | solution.py:617
  93.2 3.2 fusion
  98.4 3.0 convolution_convert_fusion.3
  107.6 3.2 mix_state.1
  122.0 5.8 mix_inner.1
  133.1 4.0 collective-permute-done.2
  138.1 5.8 mix_merge.1
  147.2 5.6 collective-permute-start.8
  159.3 13.5 %collective-permute-done.8 = bf16[1024,512]{1,0:T(8,128)(2,1)} collective-permute-done((bf16[1024,512]{1,0:T(8,128)(2,1)}, bf16[1024,512]{1,0:T(8,128)(2,1)}, u32[]{:S(2)}, u32[]{:S(2)}) %collective-permute-start.8) | collective-permute-done | bytes 1048608 | tf_op jit(solution)/shard_map/ppermute | solution.py:583
  172.8 9.6 %collective-permute-done.11 = bf16[1024,512]{1,0:T(8,128)(2,1)} collective-permute-done((bf16[1024,512]{1,0:T(8,128)(2,1)}, bf16[1024,512]{1,0:T(8,128)(2,1)}, u32[]{:S(2)}, u32[]{:S(2)}) %collective-permute-start.11) | collective-permute-done | bytes 1048608 | tf_op jit(solution)/shard_map/ppermute | solution.py:541
  184.5 2.9 collective-permute-start.12
  190.2 16.6 %collective-permute-done.12 = bf16[1024,512]{1,0:T(8,128)(2,1)S(1)} collective-permute-done((bf16[1024,512]{1,0:T(8,128)(2,1)S(1)}, bf16[1024,512]{1,0:T(8,128)(2,1)S(1)}, u32[]{:S(2)}, u32[]{:S(2)}) %collective-permute-start.12) | collective-permute-done | bytes 1048608 | tf_op jit(solution)/shard_map/ppermute | solution.py:583
  206.8 5.9 collective-permute-done.15
  214.0 2.7 collective-permute-start.16
  221.4 12.9 %collective-permute-done.16 = bf16[1024,512]{1,0:T(8,128)(2,1)} collective-permute-done((bf16[1024,512]{1,0:T(8,128)(2,1)}, bf16[1024,512]{1,0:T(8,128)(2,1)}, u32[]{:S(2)}, u32[]{:S(2)}) %collective-permute-start.16) | collective-permute-done | bytes 1048608 | tf_op jit(solution)/shard_map/ppermute | solution.py:583
  234.3 6.5 collective-permute-done.17
  251.6 5.6 straighten.1
  257.2 8.1 %convolution_bitcast_fusion.5 = f32[1376,512]{1,0:T(8,128)} fusion(bf16[1376,2048]{1,0:T(8,128)(2,1)} %param.35, bf16[1024,2048]{1,0:T(8,128)(2,1)} %straighten.1), kind=kOutput, calls=%fused_computation.41 | convolution fusion | flops 2885681152 | bytes 10551296 | tf_op jit(solution)/shard_map/ti,ji->tj/dot_general | solution.py:629
  265.3 4.7 convolution_bitcast_fusion.4
  270.6 19.5 %all-gather.10.cloned.1.call-done = bf16[512,2048]{1,0:T(8,128)(2,1)} async-done(((bf16[512,512]{1,0:T(8,128)(2,1)}), bf16[512,2048]{1,0:T(8,128)(2,1)}) %all-gather.10.cloned.1.call-update) | async-done | bytes 2097168 | tf_op jit(solution)/shard_map/all_gather | solution.py:617
  292.9 6.2 convolution_bitcast_fusion.2
  299.2 5.4 multiply_convert_fusion.3
  304.6 3.5 fusion.58
  308.1 4.6 add_convert_fusion.5
  312.8 24.1 %all-gather.8.cloned.1.call-done = bf16[512,2048]{1,0:T(8,128)(2,1)} async-done(((bf16[512,512]{1,0:T(8,128)(2,1)}), bf16[512,2048]{1,0:T(8,128)(2,1)}) %all-gather.8.cloned.1.call-update) | async-done | bytes 2097168 | tf_op jit(solution)/shard_map/all_gather | solution.py:617
  340.0 6.4 convolution_bitcast_fusion
  349.4 5.4 multiply_convert_fusion
  354.9 3.5 fusion.59
  358.4 4.6 add_convert_fusion.4
  363.0 15.9 %grad_ffn_far.1 = (bf16[4,2064,256]{2,1,0:T(8,128)(2,1)}, bf16[4,2064,256]{2,1,0:T(8,128)(2,1)}) custom-call(s32[4]{0:T(128)} %get-tuple-element.452.blocks, s32[4]{0:T(128)} %constant.83.clone.swap, bf16[512,2048]{1,0:T(8,128)(2,1)} %copy-done.68, bf16[1376,512]{1,0:T(8,128)(2,1)} %copy-done.111, bf16[512,2048]{1,0:T(8,128)(2,1)} %copy-done.69, ...), custom_call_target="tpu_custom_call" | custom-call | flops 16000000000 | bytes 1048576 | tf_op jit(solution)/shard_map/grad_ffn_far/pallas_call | solution.py:371
  378.9 3.3 reduce-scatter.5.cloned.1.call-done
  385.4 3.2 fusion.48
  388.6 16.2 %grad_ffn_near.1 = (bf16[4,2064,256]{2,1,0:T(8,128)(2,1)}, bf16[4,2064,256]{2,1,0:T(8,128)(2,1)}) custom-call(s32[4]{0:T(128)} %get-tuple-element.451.blocks, s32[4]{0:T(128)} %constant.83.clone.swap, bf16[512,2048]{1,0:T(8,128)(2,1)} %copy-done.68, bf16[1376,512]{1,0:T(8,128)(2,1)} %copy-done.111, bf16[512,2048]{1,0:T(8,128)(2,1)} %copy-done.69, ...), custom_call_target="tpu_custom_call" | custom-call | flops 16000000000 | bytes 1048576 | tf_op jit(solution)/shard_map/grad_ffn_near/pallas_call | solution.py:371
  404.8 23.5 %reduce-scatter.7.cloned.1.call-done = bf16[512,512]{1,0:T(8,128)(2,1)} async-done(((bf16[512,2048]{1,0:T(8,128)(2,1)}), bf16[512,512]{1,0:T(8,128)(2,1)}) %reduce-scatter.7.cloned.1.call-update) | async-done | bytes 524304 | tf_op jit(solution)/shard_map/reduce_scatter | solution.py:621
  430.4 5.4 add_convert_fusion.1
  436.6 4.1 add_convert_fusion
  443.8 7.9 %convolution_convert_fusion.2 = bf16[512,2048]{1,0:T(8,128)(2,1)} fusion(bf16[1376,512]{1,0:T(8,128)(2,1)} %get-tuple-element.268.refs_9_, bf16[1376,2048]{1,0:T(8,128)(2,1)} %param.35), kind=kOutput, calls=%fused_computation.46 | convolution fusion | flops 2886729728 | bytes 9142272 | tf_op jit(solution)/shard_map/it,ij->tj/dot_general | solution.py:633
  451.8 7.4 convolution_convert_fusion.1
  460.6 28.1 %collective-permute-done.20 = bf16[2,2064,256]{2,1,0:T(8,128)(2,1)} collective-permute-done((bf16[2,2064,256]{2,1,0:T(8,128)(2,1)}, bf16[2,2064,256]{2,1,0:T(8,128)(2,1)}, u32[]{:S(2)}, u32[]{:S(2)}) %collective-permute-start.20) | collective-permute-done | bytes 2113568 | tf_op jit(solution)/shard_map/ppermute | solution.py:394
  490.1 2.9 add_convert_fusion.10
  494.5 2.9 add_convert_fusion.7
  497.8 2.7 fusion.8
  503.2 13.8 %collective-permute-done.22 = bf16[1,2064,256]{2,1,0:T(8,128)(2,1)} collective-permute-done((bf16[1,2064,256]{2,1,0:T(8,128)(2,1)}, bf16[1,2064,256]{2,1,0:T(8,128)(2,1)}, u32[]{:S(2)}, u32[]{:S(2)}) %collective-permute-start.22) | collective-permute-done | bytes 1056800 | tf_op jit(solution)/shard_map/ppermute | solution.py:394
  528.6 13.6 %collective-permute-done.24.refs_1_ = bf16[1,2064,256]{2,1,0:T(8,128)(2,1)S(1)} collective-permute-done((bf16[1,2064,256]{2,1,0:T(8,128)(2,1)S(1)}, bf16[1,2064,256]{2,1,0:T(8,128)(2,1)S(1)}, u32[]{:S(2)}, u32[]{:S(2)}) %collective-permute-start.24) | collective-permute-done | bytes 1056800 | tf_op jit(solution)/shard_map/ppermute | solution.py:394
  543.2 3.4 collective-permute-done.25.refs_9_
  547.8 3.8 fusion.12
  555.1 5.9 mix_pull_state.1
  561.0 7.4 collective-permute-done.26.refs_2_
  573.5 16.1 %mix_pull_inner.1 = (bf16[1024,64]{1,0:T(8,128)(2,1)S(1)}, f32[1024,64]{1,0:T(8,128)S(1)}, f32[1024,512]{1,0:T(8,128)S(1)}) custom-call(bf16[1024,64]{1,0:T(8,128)(2,1)S(1)} %copy-done.15, bf16[1024,64]{1,0:T(8,128)(2,1)S(1)} %copy.104.k_ref, bf16[1024,512]{1,0:T(8,128)(2,1)S(1)} %copy-done.5, s32[1024,1]{1,0:T(8,128)S(1)} %copy-done.2, ...), custom_call_target="tpu_custom_call" | custom-call | flops 20000000000 | bytes 1048576 | tf_op jit(solution)/shard_map/mix_pull_inner/pallas_call | solution.py:226
  594.0 2.7 collective-permute-done.30
  596.8 5.3 mix_pull_carry.1
  610.4 6.8 convolution_convert_fusion
  617.2 2.8 convert_element_type.447
  624.9 7.9 %grad_mix_far.1 = (bf16[4,576,256]{2,1,0:T(8,128)(2,1)}, bf16[4,576,256]{2,1,0:T(8,128)(2,1)}) custom-call(s32[4]{0:T(128)} %get-tuple-element.452.blocks, s32[4]{0:T(128)} %constant.83.clone.swap, bf16[1024,2048]{1,0:T(8,128)(2,1)} %copy-done.55, bf16[640,1024]{1,0:T(8,128)(2,1)} %bitcast.86, bf16[512,2048]{1,0:T(8,128)(2,1)} %copy-done.66, ...), custom_call_target="tpu_custom_call" | custom-call | flops 5000000000 | bytes 1048576 | tf_op jit(solution)/shard_map/grad_mix_far/pallas_call | solution.py:371
  636.1 11.9 %collective-permute-done.36.refs_3_ = bf16[1,2064,256]{2,1,0:T(8,128)(2,1)} collective-permute-done((bf16[1,2064,256]{2,1,0:T(8,128)(2,1)}, bf16[1,2064,256]{2,1,0:T(8,128)(2,1)}, u32[]{:S(2)}, u32[]{:S(2)}) %collective-permute-start.36) | collective-permute-done | bytes 1056800 | tf_op jit(solution)/shard_map/ppermute | solution.py:394
  650.0 5.2 collective-permute-done.51
  656.5 7.6 grad_mix_near.1
  673.7 11.1 %collective-permute-done.38 = bf16[2,576,256]{2,1,0:T(8,128)(2,1)S(1)} collective-permute-done((bf16[2,576,256]{2,1,0:T(8,128)(2,1)S(1)}, bf16[2,576,256]{2,1,0:T(8,128)(2,1)S(1)}, u32[]{:S(2)}, u32[]{:S(2)}) %collective-permute-start.38) | collective-permute-done | bytes 589856 | tf_op jit(solution)/shard_map/ppermute | solution.py:394
  696.8 6.1 collective-permute-done.54
  708.7 5.3 collective-permute-done.55.refs_1_
  716.9 17.8 %place_ffn.1 = (f32[1376,2048]{1,0:T(8,128)}, f32[1376,2048]{1,0:T(8,128)}, f32[1376,2048]{1,0:T(8,128)}) custom-call(s32[8]{0:T(128)} %copy-done.89, s32[2,8]{1,0:T(2,128)} %constant.84.clone.table, bf16[1,2064,256]{2,1,0:T(8,128)(2,1)} %copy-done.73, bf16[1,2064,256]{2,1,0:T(8,128)(2,1)} %copy-done.90, ...), custom_call_target="tpu_custom_call" | custom-call | flops 20000000000 | bytes 1048576 | tf_op jit(solution)/shard_map/place_ffn/pallas_call | solution.py:488
  751.7 8.0 %place_mix.1 = (f32[64,2048]{1,0:T(8,128)}, f32[64,2048]{1,0:T(8,128)}, f32[2048,512]{1,0:T(8,128)}, f32[512,2048]{1,0:T(8,128)}) custom-call(s32[8]{0:T(128)} %copy-done.89, s32[2,8]{1,0:T(2,128)} %constant.84.clone.table, bf16[1,576,256]{2,1,0:T(8,128)(2,1)} %add_convert_fusion.23.refs_0_, bf16[1,576,256]{2,1,0:T(8,128)(2,1)} %collective-permute-done.55.refs_1_, ...), custom_call_target="tpu_custom_call" | custom-call | flops 5000000000 | bytes 1048576 | tf_op jit(solution)/shard_map/place_mix/pallas_call | solution.py:488
  (504 shorter events, 185.3 us)
Async XLA Ops:
  7.2 86.0 %all-gather.6.cloned.1.call-start = ((), (), s32[]{:S(2)}) async-start(), calls=%async_computation.4 | async-start | bytes 5242880 | tf_op jit(solution)/shard_map/all_gather | solution.py:617
  8.0 282.1 %all-gather.10.cloned.1.call-start = ((), (), s32[]{:S(2)}) async-start(), calls=%async_computation.6 | async-start | bytes 2621440 | tf_op jit(solution)/shard_map/all_gather | solution.py:617
  111.5 6.8 collective-permute-start
  112.9 33.1 %collective-permute-start.6 = (bf16[1024,512]{1,0:T(8,128)(2,1)}, bf16[1024,512]{1,0:T(8,128)(2,1)}, u32[]{:S(2)}, u32[]{:S(2)}) collective-permute-start(bf16[1024,512]{1,0:T(8,128)(2,1)} %param.36), channel_id=1, source_target_pairs={{0,1},{1,2},{2,3},{4,5},{5,6},{6,7},{8,9},{9,10},{10,11},{12,13},{... | collective-permute-start | bytes 3145736 | tf_op jit(solution)/shard_map/ppermute | solution.py:540
  115.1 30.8 %collective-permute-start.7 = (bf16[1024,512]{1,0:T(8,128)(2,1)}, bf16[1024,512]{1,0:T(8,128)(2,1)}, u32[]{:S(2)}, u32[]{:S(2)}) collective-permute-start(bf16[1024,512]{1,0:T(8,128)(2,1)} %param.36), channel_id=1, source_target_pairs={{1,0},{2,1},{3,2},{5,4},{6,5},{7,6},{9,8},{10,9},{11,10},{13,12},{... | collective-permute-start | bytes 3145736 | tf_op jit(solution)/shard_map/ppermute | solution.py:541
  116.7 12.4 %collective-permute-start.4 = (f32[4,8,256]{2,1,0:T(8,128)S(1)}, f32[4,8,256]{2,1,0:T(8,128)S(1)}, u32[]{:S(2)}, u32[]{:S(2)}) collective-permute-start(f32[4,8,256]{2,1,0:T(8,128)S(1)} %add.323), channel_id=1, source_target_pairs={{0,8},{4,12},{8,0},{12,4},{16,24},{20,28},{24,16},{28,20},{1,9},{5... | collective-permute-start | bytes 98312 | tf_op jit(solution)/shard_map/ppermute | solution.py:298
  119.2 11.5 %collective-permute-start.1 = (bf16[4,160,128]{2,1,0:T(8,128)(2,1)S(1)}, bf16[4,160,128]{2,1,0:T(8,128)(2,1)S(1)}, u32[]{:S(2)}, u32[]{:S(2)}) collective-permute-start(bf16[4,160,128]{2,1,0:T(8,128)(2,1)S(1)} %fusion.35), channel_id=1, source_target_pairs={{0,8},{4,12},{8,0},{12,4},{16,24},{20,28},{24,16},{28,20},{1,9},{5... | collective-permute-start | bytes 491528 | tf_op jit(solution)/shard_map/ppermute | solution.py:298
  131.7 5.4 collective-permute-start.2
  147.2 25.6 %collective-permute-start.8 = (bf16[1024,512]{1,0:T(8,128)(2,1)}, bf16[1024,512]{1,0:T(8,128)(2,1)}, u32[]{:S(2)}, u32[]{:S(2)}) collective-permute-start(bf16[1024,512]{1,0:T(8,128)(2,1)} %convert_element_type.402), channel_id=1, source_target_pairs={{0,1},{4,5},{8,9},{12,13},{16,17},{20,21},{24,25},{28,29}} | collective-permute-start | bytes 3145736 | tf_op jit(solution)/shard_map/ppermute | solution.py:583
  153.9 18.9 %collective-permute-start.9 = (bf16[1024,512]{1,0:T(8,128)(2,1)}, bf16[1024,512]{1,0:T(8,128)(2,1)}, u32[]{:S(2)}, u32[]{:S(2)}) collective-permute-start(bf16[1024,512]{1,0:T(8,128)(2,1)} %convert_element_type.403), channel_id=1, source_target_pairs={{3,2},{7,6},{11,10},{15,14},{19,18},{23,22},{27,26},{31,30}} | collective-permute-start | bytes 3145736 | tf_op jit(solution)/shard_map/ppermute | solution.py:584
  155.6 17.1 %collective-permute-start.10 = (bf16[1024,512]{1,0:T(8,128)(2,1)}, bf16[1024,512]{1,0:T(8,128)(2,1)}, u32[]{:S(2)}, u32[]{:S(2)}) collective-permute-start(bf16[1024,512]{1,0:T(8,128)(2,1)} %collective-permute-done.6), channel_id=1, source_target_pairs={{1,2},{2,3},{5,6},{6,7},{9,10},{10,11},{13,14},{14,15},{17,18},{18... | collective-permute-start | bytes 3145736 | tf_op jit(solution)/shard_map/ppermute | solution.py:540
  157.2 25.1 %collective-permute-start.11 = (bf16[1024,512]{1,0:T(8,128)(2,1)}, bf16[1024,512]{1,0:T(8,128)(2,1)}, u32[]{:S(2)}, u32[]{:S(2)}) collective-permute-start(bf16[1024,512]{1,0:T(8,128)(2,1)} %collective-permute-done.7), channel_id=1, source_target_pairs={{1,0},{2,1},{5,4},{6,5},{9,8},{10,9},{13,12},{14,13},{17,16},{18,1... | collective-permute-start | bytes 3145736 | tf_op jit(solution)/shard_map/ppermute | solution.py:541
  184.5 22.3 %collective-permute-start.12 = (bf16[1024,512]{1,0:T(8,128)(2,1)S(1)}, bf16[1024,512]{1,0:T(8,128)(2,1)S(1)}, u32[]{:S(2)}, u32[]{:S(2)}) collective-permute-start(bf16[1024,512]{1,0:T(8,128)(2,1)S(1)} %get-tuple-element.434), channel_id=1, source_target_pairs={{0,1},{1,2},{4,5},{5,6},{8,9},{9,10},{12,13},{13,14},{16,17},{17,1... | collective-permute-start | bytes 3145736 | tf_op jit(solution)/shard_map/ppermute | solution.py:583
  187.4 19.4 %collective-permute-start.13 = (bf16[1024,512]{1,0:T(8,128)(2,1)S(1)}, bf16[1024,512]{1,0:T(8,128)(2,1)S(1)}, u32[]{:S(2)}, u32[]{:S(2)}) collective-permute-start(bf16[1024,512]{1,0:T(8,128)(2,1)S(1)} %get-tuple-element.433), channel_id=1, source_target_pairs={{2,1},{3,2},{6,5},{7,6},{10,9},{11,10},{14,13},{15,14},{18,17},{19... | collective-permute-start | bytes 3145736 | tf_op jit(solution)/shard_map/ppermute | solution.py:584
  188.1 18.7 %collective-permute-start.14 = (bf16[1024,512]{1,0:T(8,128)(2,1)}, bf16[1024,512]{1,0:T(8,128)(2,1)S(1)}, u32[]{:S(2)}, u32[]{:S(2)}) collective-permute-start(bf16[1024,512]{1,0:T(8,128)(2,1)} %collective-permute-done.10), channel_id=1, source_target_pairs={{2,3},{6,7},{10,11},{14,15},{18,19},{22,23},{26,27},{30,31}} | collective-permute-start | bytes 3145736 | tf_op jit(solution)/shard_map/ppermute | solution.py:540
  188.9 23.8 %collective-permute-start.15 = (bf16[1024,512]{1,0:T(8,128)(2,1)}, bf16[1024,512]{1,0:T(8,128)(2,1)S(1)}, u32[]{:S(2)}, u32[]{:S(2)}) collective-permute-start(bf16[1024,512]{1,0:T(8,128)(2,1)} %collective-permute-done.11), channel_id=1, source_target_pairs={{1,0},{5,4},{9,8},{13,12},{17,16},{21,20},{25,24},{29,28}} | collective-permute-start | bytes 3145736 | tf_op jit(solution)/shard_map/ppermute | solution.py:541
  214.0 20.3 %collective-permute-start.16 = (bf16[1024,512]{1,0:T(8,128)(2,1)}, bf16[1024,512]{1,0:T(8,128)(2,1)}, u32[]{:S(2)}, u32[]{:S(2)}) collective-permute-start(bf16[1024,512]{1,0:T(8,128)(2,1)} %add_convert_fusion.13), channel_id=1, source_target_pairs={{0,1},{1,2},{2,3},{4,5},{5,6},{6,7},{8,9},{9,10},{10,11},{12,13},{... | collective-permute-start | bytes 3145736 | tf_op jit(solution)/shard_map/ppermute | solution.py:583
  218.1 22.7 %collective-permute-start.17 = (bf16[1024,512]{1,0:T(8,128)(2,1)}, bf16[1024,512]{1,0:T(8,128)(2,1)}, u32[]{:S(2)}, u32[]{:S(2)}) collective-permute-start(bf16[1024,512]{1,0:T(8,128)(2,1)} %add_convert_fusion.12), channel_id=1, source_target_pairs={{1,0},{2,1},{3,2},{5,4},{6,5},{7,6},{9,8},{10,9},{11,10},{13,12},{... | collective-permute-start | bytes 3145736 | tf_op jit(solution)/shard_map/ppermute | solution.py:584
  245.5 91.4 %all-gather.8.cloned.1.call-start = ((), (), s32[]{:S(2)}) async-start(), calls=%async_computation.5 | async-start | bytes 2621440 | tf_op jit(solution)/shard_map/all_gather | solution.py:617
  270.1 112.1 %reduce-scatter.5.cloned.1.call-start = ((), (), s32[]{:S(2)}) async-start(), calls=%async_computation.7 | async-start | bytes 2621440 | tf_op jit(solution)/shard_map/reduce_scatter | solution.py:621
  336.9 91.3 %reduce-scatter.7.cloned.1.call-start = ((), (), s32[]{:S(2)}) async-start(), calls=%async_computation.8 | async-start | bytes 2621440 | tf_op jit(solution)/shard_map/reduce_scatter | solution.py:621
  384.3 46.0 %collective-permute-start.18 = (bf16[4,2064,256]{2,1,0:T(8,128)(2,1)}, bf16[4,2064,256]{2,1,0:T(8,128)(2,1)}, u32[]{:S(2)}, u32[]{:S(2)}) collective-permute-start(bf16[4,2064,256]{2,1,0:T(8,128)(2,1)} %get-tuple-element.280), channel_id=1, source_target_pairs={{0,4},{4,0},{8,12},{12,8},{16,20},{20,16},{24,28},{28,24},{1,5},{5... | collective-permute-start | bytes 12681224 | tf_op jit(solution)/shard_map/ppermute | solution.py:394
  384.4 105.6 %all-gather.12.cloned.1.call-start = ((), (), s32[]{:S(2)}) async-start(), calls=%async_computation.9 | async-start | bytes 2621440 | tf_op jit(solution)/shard_map/all_gather | solution.py:617
  384.8 51.0 %collective-permute-start.19 = (bf16[4,2064,256]{2,1,0:T(8,128)(2,1)}, bf16[4,2064,256]{2,1,0:T(8,128)(2,1)}, u32[]{:S(2)}, u32[]{:S(2)}) collective-permute-start(bf16[4,2064,256]{2,1,0:T(8,128)(2,1)} %get-tuple-element.282), channel_id=1, source_target_pairs={{0,4},{4,0},{8,12},{12,8},{16,20},{20,16},{24,28},{28,24},{1,5},{5... | collective-permute-start | bytes 12681224 | tf_op jit(solution)/shard_map/ppermute | solution.py:394
  440.8 105.8 %all-gather.14.cloned.1.call-start = ((), (), s32[]{:S(2)}) async-start(), calls=%async_computation.11 | async-start | bytes 2621440 | tf_op jit(solution)/shard_map/all_gather | solution.py:617
  440.8 47.9 %collective-permute-start.20 = (bf16[2,2064,256]{2,1,0:T(8,128)(2,1)}, bf16[2,2064,256]{2,1,0:T(8,128)(2,1)}, u32[]{:S(2)}, u32[]{:S(2)}) collective-permute-start(bf16[2,2064,256]{2,1,0:T(8,128)(2,1)} %get-tuple-element.416), channel_id=1, source_target_pairs={{0,8},{4,12},{8,0},{12,4},{16,24},{20,28},{24,16},{28,20},{1,9},{5... | collective-permute-start | bytes 6340616 | tf_op jit(solution)/shard_map/ppermute | solution.py:394
  442.4 47.6 %collective-permute-start.21 = (bf16[2,2064,256]{2,1,0:T(8,128)(2,1)}, bf16[2,2064,256]{2,1,0:T(8,128)(2,1)}, u32[]{:S(2)}, u32[]{:S(2)}) collective-permute-start(bf16[2,2064,256]{2,1,0:T(8,128)(2,1)} %get-tuple-element.414), channel_id=1, source_target_pairs={{0,16},{4,20},{8,24},{12,28},{16,0},{20,4},{24,8},{28,12},{1,17},{... | collective-permute-start | bytes 6340616 | tf_op jit(solution)/shard_map/ppermute | solution.py:394
  490.0 127.3 %reduce-scatter.9.cloned.1.call-start = ((), (), s32[]{:S(2)}) async-start(), calls=%async_computation.10 | async-start | bytes 5242880 | tf_op jit(solution)/shard_map/reduce_scatter | solution.py:621
  493.0 24.0 %collective-permute-start.22 = (bf16[1,2064,256]{2,1,0:T(8,128)(2,1)}, bf16[1,2064,256]{2,1,0:T(8,128)(2,1)}, u32[]{:S(2)}, u32[]{:S(2)}) collective-permute-start(bf16[1,2064,256]{2,1,0:T(8,128)(2,1)} %add_convert_fusion.10), channel_id=1, source_target_pairs={{0,16},{4,20},{8,24},{12,28},{16,0},{20,4},{24,8},{28,12},{1,17},{... | collective-permute-start | bytes 3170312 | tf_op jit(solution)/shard_map/ppermute | solution.py:394
  497.4 23.7 %collective-permute-start.23 = (bf16[1,2064,256]{2,1,0:T(8,128)(2,1)}, bf16[1,2064,256]{2,1,0:T(8,128)(2,1)}, u32[]{:S(2)}, u32[]{:S(2)}) collective-permute-start(bf16[1,2064,256]{2,1,0:T(8,128)(2,1)} %add_convert_fusion.7), channel_id=1, source_target_pairs={{0,8},{4,12},{8,0},{12,4},{16,24},{20,28},{24,16},{28,20},{1,9},{5... | collective-permute-start | bytes 3170312 | tf_op jit(solution)/shard_map/ppermute | solution.py:394
  503.2 231.6 %reduce-scatter.11.cloned.1.call-start = ((), (), s32[]{:S(2)}) async-start(), calls=%async_computation.12 | async-start | bytes 5242880 | tf_op jit(solution)/shard_map/reduce_scatter | solution.py:621
  519.3 22.9 %collective-permute-start.24 = (bf16[1,2064,256]{2,1,0:T(8,128)(2,1)S(1)}, bf16[1,2064,256]{2,1,0:T(8,128)(2,1)S(1)}, u32[]{:S(2)}, u32[]{:S(2)}) collective-permute-start(bf16[1,2064,256]{2,1,0:T(8,128)(2,1)S(1)} %add_convert_fusion.9.refs_0_), channel_id=1, source_target_pairs={{0,16},{4,20},{8,24},{12,28},{16,0},{20,4},{24,8},{28,12},{1,17},{... | collective-permute-start | bytes 3170312 | tf_op jit(solution)/shard_map/ppermute | solution.py:394
  523.2 23.3 %collective-permute-start.25 = (bf16[1,2064,256]{2,1,0:T(8,128)(2,1)S(1)}, bf16[1,2064,256]{2,1,0:T(8,128)(2,1)}, u32[]{:S(2)}, u32[]{:S(2)}) collective-permute-start(bf16[1,2064,256]{2,1,0:T(8,128)(2,1)S(1)} %add_convert_fusion.6.refs_8_), channel_id=1, source_target_pairs={{0,8},{4,12},{8,0},{12,4},{16,24},{20,28},{24,16},{28,20},{1,9},{5... | collective-permute-start | bytes 3170312 | tf_op jit(solution)/shard_map/ppermute | solution.py:394
  546.6 21.9 %collective-permute-start.26 = (bf16[1,2064,256]{2,1,0:T(8,128)(2,1)}, bf16[1,2064,256]{2,1,0:T(8,128)(2,1)}, u32[]{:S(2)}, u32[]{:S(2)}) collective-permute-start(bf16[1,2064,256]{2,1,0:T(8,128)(2,1)} %copy-done.73), channel_id=1, source_target_pairs={{0,8},{4,12},{8,0},{12,4},{16,24},{20,28},{24,16},{28,20},{1,9},{5... | collective-permute-start | bytes 3170312 | tf_op jit(solution)/shard_map/ppermute | solution.py:394
  547.1 21.4 %collective-permute-start.27 = (bf16[1,2064,256]{2,1,0:T(8,128)(2,1)}, bf16[1,2064,256]{2,1,0:T(8,128)(2,1)S(1)}, u32[]{:S(2)}, u32[]{:S(2)}) collective-permute-start(bf16[1,2064,256]{2,1,0:T(8,128)(2,1)} %copy-done.75), channel_id=1, source_target_pairs={{0,16},{4,20},{8,24},{12,28},{16,0},{20,4},{24,8},{28,12},{1,17},{... | collective-permute-start | bytes 3170312 | tf_op jit(solution)/shard_map/ppermute | solution.py:394
  571.2 18.4 %collective-permute-start.32 = (f32[4,8,256]{2,1,0:T(8,128)S(1)}, f32[4,8,256]{2,1,0:T(8,128)S(1)}, u32[]{:S(2)}, u32[]{:S(2)}) collective-permute-start(f32[4,8,256]{2,1,0:T(8,128)S(1)} %add.370), channel_id=1, source_target_pairs={{0,8},{4,12},{8,0},{12,4},{16,24},{20,28},{24,16},{28,20},{1,9},{5... | collective-permute-start | bytes 98312 | tf_op jit(solution)/shard_map/ppermute | solution.py:298
  572.2 18.7 %collective-permute-start.29 = (bf16[4,160,128]{2,1,0:T(8,128)(2,1)S(1)}, bf16[4,160,128]{2,1,0:T(8,128)(2,1)S(1)}, u32[]{:S(2)}, u32[]{:S(2)}) collective-permute-start(bf16[4,160,128]{2,1,0:T(8,128)(2,1)S(1)} %fusion.36), channel_id=1, source_target_pairs={{0,8},{4,12},{8,0},{12,4},{16,24},{20,28},{24,16},{28,20},{1,9},{5... | collective-permute-start | bytes 491528 | tf_op jit(solution)/shard_map/ppermute | solution.py:298
  590.9 5.8 collective-permute-start.30
  623.7 24.4 %collective-permute-start.36 = (bf16[1,2064,256]{2,1,0:T(8,128)(2,1)}, bf16[1,2064,256]{2,1,0:T(8,128)(2,1)}, u32[]{:S(2)}, u32[]{:S(2)}) collective-permute-start(bf16[1,2064,256]{2,1,0:T(8,128)(2,1)} %copy-done.90), channel_id=1, source_target_pairs={{0,8},{4,12},{8,0},{12,4},{16,24},{20,28},{24,16},{28,20},{1,9},{5... | collective-permute-start | bytes 3170312 | tf_op jit(solution)/shard_map/ppermute | solution.py:394
  632.8 33.3 %collective-permute-start.34 = (bf16[4,576,256]{2,1,0:T(8,128)(2,1)}, bf16[4,576,256]{2,1,0:T(8,128)(2,1)S(1)}, u32[]{:S(2)}, u32[]{:S(2)}) collective-permute-start(bf16[4,576,256]{2,1,0:T(8,128)(2,1)} %get-tuple-element.332), channel_id=1, source_target_pairs={{0,4},{4,0},{8,12},{12,8},{16,20},{20,16},{24,28},{28,24},{1,5},{5... | collective-permute-start | bytes 3538952 | tf_op jit(solution)/shard_map/ppermute | solution.py:394
  632.8 33.4 %collective-permute-start.35 = (bf16[4,576,256]{2,1,0:T(8,128)(2,1)}, bf16[4,576,256]{2,1,0:T(8,128)(2,1)S(1)}, u32[]{:S(2)}, u32[]{:S(2)}) collective-permute-start(bf16[4,576,256]{2,1,0:T(8,128)(2,1)} %get-tuple-element.333), channel_id=1, source_target_pairs={{0,4},{4,0},{8,12},{12,8},{16,20},{20,16},{24,28},{28,24},{1,5},{5... | collective-permute-start | bytes 3538952 | tf_op jit(solution)/shard_map/ppermute | solution.py:394
  633.3 32.8 %collective-permute-start.37 = (bf16[1,2064,256]{2,1,0:T(8,128)(2,1)}, bf16[1,2064,256]{2,1,0:T(8,128)(2,1)}, u32[]{:S(2)}, u32[]{:S(2)}) collective-permute-start(bf16[1,2064,256]{2,1,0:T(8,128)(2,1)} %collective-permute-done.25.refs_9_), channel_id=1, source_target_pairs={{0,16},{4,20},{8,24},{12,28},{16,0},{20,4},{24,8},{28,12},{1,17},{... | collective-permute-start | bytes 3170312 | tf_op jit(solution)/shard_map/ppermute | solution.py:394
  634.7 14.6 %collective-permute-start.48 = (f32[8,128]{1,0:T(8,128)S(1)}, f32[8,128]{1,0:T(8,128)S(1)}, u32[]{:S(2)}, u32[]{:S(2)}) collective-permute-start(f32[8,128]{1,0:T(8,128)S(1)} %bitcast.106), channel_id=1, source_target_pairs={{0,1},{1,2},{2,3},{4,5},{5,6},{6,7},{8,9},{9,10},{10,11},{12,13},{... | collective-permute-start | bytes 12296 | tf_op jit(solution)/shard_map/ppermute | solution.py:540
  648.0 7.2 collective-permute-start.51
  649.3 14.7 %collective-permute-start.49 = (f32[8,128]{1,0:T(8,128)S(1)}, f32[8,128]{1,0:T(8,128)S(1)}, u32[]{:S(2)}, u32[]{:S(2)}) collective-permute-start(f32[8,128]{1,0:T(8,128)S(1)} %collective-permute-done.48), channel_id=1, source_target_pairs={{1,2},{2,3},{5,6},{6,7},{9,10},{10,11},{13,14},{14,15},{17,18},{18... | collective-permute-start | bytes 12296 | tf_op jit(solution)/shard_map/ppermute | solution.py:540
  655.2 9.7 %collective-permute-start.52 = (f32[8,128]{1,0:T(8,128)S(1)}, f32[8,128]{1,0:T(8,128)S(1)}, u32[]{:S(2)}, u32[]{:S(2)}) collective-permute-start(f32[8,128]{1,0:T(8,128)S(1)} %collective-permute-done.51), channel_id=1, source_target_pairs={{1,0},{2,1},{5,4},{6,5},{9,8},{10,9},{13,12},{14,13},{17,16},{18,1... | collective-permute-start | bytes 12296 | tf_op jit(solution)/shard_map/ppermute | solution.py:541
  664.9 7.4 collective-permute-start.53
  666.2 19.8 %collective-permute-start.40 = (bf16[1,2064,256]{2,1,0:T(8,128)(2,1)S(1)}, bf16[1,2064,256]{2,1,0:T(8,128)(2,1)S(1)}, u32[]{:S(2)}, u32[]{:S(2)}) collective-permute-start(bf16[1,2064,256]{2,1,0:T(8,128)(2,1)S(1)} %copy-done.74), channel_id=1, source_target_pairs={{0,4},{4,0},{8,12},{12,8},{16,20},{20,16},{24,28},{28,24},{1,5},{5... | collective-permute-start | bytes 3170312 | tf_op jit(solution)/shard_map/ppermute | solution.py:394
  666.3 20.2 %collective-permute-start.41 = (bf16[1,2064,256]{2,1,0:T(8,128)(2,1)S(1)}, bf16[1,2064,256]{2,1,0:T(8,128)(2,1)S(1)}, u32[]{:S(2)}, u32[]{:S(2)}) collective-permute-start(bf16[1,2064,256]{2,1,0:T(8,128)(2,1)S(1)} %copy-done.91), channel_id=1, source_target_pairs={{0,4},{4,0},{8,12},{12,8},{16,20},{20,16},{24,28},{28,24},{1,5},{5... | collective-permute-start | bytes 3170312 | tf_op jit(solution)/shard_map/ppermute | solution.py:394
  666.8 21.2 %collective-permute-start.42 = (bf16[1,2064,256]{2,1,0:T(8,128)(2,1)}, bf16[1,2064,256]{2,1,0:T(8,128)(2,1)S(1)}, u32[]{:S(2)}, u32[]{:S(2)}) collective-permute-start(bf16[1,2064,256]{2,1,0:T(8,128)(2,1)} %collective-permute-done.26.refs_2_), channel_id=1, source_target_pairs={{0,4},{4,0},{8,12},{12,8},{16,20},{20,16},{24,28},{28,24},{1,5},{5... | collective-permute-start | bytes 3170312 | tf_op jit(solution)/shard_map/ppermute | solution.py:394
  669.0 15.7 %collective-permute-start.38 = (bf16[2,576,256]{2,1,0:T(8,128)(2,1)S(1)}, bf16[2,576,256]{2,1,0:T(8,128)(2,1)S(1)}, u32[]{:S(2)}, u32[]{:S(2)}) collective-permute-start(bf16[2,576,256]{2,1,0:T(8,128)(2,1)S(1)} %get-tuple-element.430), channel_id=1, source_target_pairs={{0,8},{4,12},{8,0},{12,4},{16,24},{20,28},{24,16},{28,20},{1,9},{5... | collective-permute-start | bytes 1769480 | tf_op jit(solution)/shard_map/ppermute | solution.py:394
  672.2 13.8 %collective-permute-start.39 = (bf16[2,576,256]{2,1,0:T(8,128)(2,1)S(1)}, bf16[2,576,256]{2,1,0:T(8,128)(2,1)S(1)}, u32[]{:S(2)}, u32[]{:S(2)}) collective-permute-start(bf16[2,576,256]{2,1,0:T(8,128)(2,1)S(1)} %get-tuple-element.428), channel_id=1, source_target_pairs={{0,16},{4,20},{8,24},{12,28},{16,0},{20,4},{24,8},{28,12},{1,17},{... | collective-permute-start | bytes 1769480 | tf_op jit(solution)/shard_map/ppermute | solution.py:394
  684.8 6.1 collective-permute-start.43
  693.8 9.1 %collective-permute-start.54 = (bf16[1,576,256]{2,1,0:T(8,128)(2,1)S(1)}, bf16[1,576,256]{2,1,0:T(8,128)(2,1)S(1)}, u32[]{:S(2)}, u32[]{:S(2)}) collective-permute-start(bf16[1,576,256]{2,1,0:T(8,128)(2,1)S(1)} %add_convert_fusion.24), channel_id=1, source_target_pairs={{0,16},{4,20},{8,24},{12,28},{16,0},{20,4},{24,8},{28,12},{1,17},{... | collective-permute-start | bytes 884744 | tf_op jit(solution)/shard_map/ppermute | solution.py:394
  695.4 9.8 %collective-permute-start.56 = (bf16[1,576,256]{2,1,0:T(8,128)(2,1)S(1)}, bf16[1,576,256]{2,1,0:T(8,128)(2,1)S(1)}, u32[]{:S(2)}, u32[]{:S(2)}) collective-permute-start(bf16[1,576,256]{2,1,0:T(8,128)(2,1)S(1)} %add_convert_fusion.21), channel_id=1, source_target_pairs={{0,8},{4,12},{8,0},{12,4},{16,24},{20,28},{24,16},{28,20},{1,9},{5... | collective-permute-start | bytes 884744 | tf_op jit(solution)/shard_map/ppermute | solution.py:394
  703.8 10.3 %collective-permute-start.55 = (bf16[1,576,256]{2,1,0:T(8,128)(2,1)}, bf16[1,576,256]{2,1,0:T(8,128)(2,1)}, u32[]{:S(2)}, u32[]{:S(2)}) collective-permute-start(bf16[1,576,256]{2,1,0:T(8,128)(2,1)} %add_convert_fusion.23.refs_0_), channel_id=1, source_target_pairs={{0,16},{4,20},{8,24},{12,28},{16,0},{20,4},{24,8},{28,12},{1,17},{... | collective-permute-start | bytes 884744 | tf_op jit(solution)/shard_map/ppermute | solution.py:394
  706.1 10.3 %collective-permute-start.57 = (bf16[1,576,256]{2,1,0:T(8,128)(2,1)}, bf16[1,576,256]{2,1,0:T(8,128)(2,1)}, u32[]{:S(2)}, u32[]{:S(2)}) collective-permute-start(bf16[1,576,256]{2,1,0:T(8,128)(2,1)} %add_convert_fusion.20.refs_8_), channel_id=1, source_target_pairs={{0,8},{4,12},{8,0},{12,4},{16,24},{20,28},{24,16},{28,20},{1,9},{5... | collective-permute-start | bytes 884744 | tf_op jit(solution)/shard_map/ppermute | solution.py:394
  707.4 29.0 %collective-permute-start.58 = (bf16[1,576,256]{2,1,0:T(8,128)(2,1)}, bf16[1,576,256]{2,1,0:T(8,128)(2,1)}, u32[]{:S(2)}, u32[]{:S(2)}) collective-permute-start(bf16[1,576,256]{2,1,0:T(8,128)(2,1)} %add_convert_fusion.23.refs_0_), channel_id=1, source_target_pairs={{0,8},{4,12},{8,0},{12,4},{16,24},{20,28},{24,16},{28,20},{1,9},{5... | collective-permute-start | bytes 884744 | tf_op jit(solution)/shard_map/ppermute | solution.py:394
  708.2 28.3 %collective-permute-start.60 = (bf16[1,576,256]{2,1,0:T(8,128)(2,1)}, bf16[1,576,256]{2,1,0:T(8,128)(2,1)}, u32[]{:S(2)}, u32[]{:S(2)}) collective-permute-start(bf16[1,576,256]{2,1,0:T(8,128)(2,1)} %add_convert_fusion.20.refs_8_), channel_id=1, source_target_pairs={{0,16},{4,20},{8,24},{12,28},{16,0},{20,4},{24,8},{28,12},{1,17},{... | collective-permute-start | bytes 884744 | tf_op jit(solution)/shard_map/ppermute | solution.py:394
  714.0 22.5 %collective-permute-start.59 = (bf16[1,576,256]{2,1,0:T(8,128)(2,1)}, bf16[1,576,256]{2,1,0:T(8,128)(2,1)}, u32[]{:S(2)}, u32[]{:S(2)}) collective-permute-start(bf16[1,576,256]{2,1,0:T(8,128)(2,1)} %collective-permute-done.55.refs_1_), channel_id=1, source_target_pairs={{0,8},{4,12},{8,0},{12,4},{16,24},{20,28},{24,16},{28,20},{1,9},{5... | collective-permute-start | bytes 884744 | tf_op jit(solution)/shard_map/ppermute | solution.py:394
  716.3 20.2 %collective-permute-start.61 = (bf16[1,576,256]{2,1,0:T(8,128)(2,1)}, bf16[1,576,256]{2,1,0:T(8,128)(2,1)}, u32[]{:S(2)}, u32[]{:S(2)}) collective-permute-start(bf16[1,576,256]{2,1,0:T(8,128)(2,1)} %collective-permute-done.57.refs_9_), channel_id=1, source_target_pairs={{0,16},{4,20},{8,24},{12,28},{16,0},{20,4},{24,8},{28,12},{1,17},{... | collective-permute-start | bytes 884744 | tf_op jit(solution)/shard_map/ppermute | solution.py:394
  739.1 8.5 %collective-permute-start.65 = (bf16[1,576,256]{2,1,0:T(8,128)(2,1)}, bf16[1,576,256]{2,1,0:T(8,128)(2,1)S(1)}, u32[]{:S(2)}, u32[]{:S(2)}) collective-permute-start(bf16[1,576,256]{2,1,0:T(8,128)(2,1)} %add_convert_fusion.23.refs_0_), channel_id=1, source_target_pairs={{0,4},{4,0},{8,12},{12,8},{16,20},{20,16},{24,28},{28,24},{1,5},{5... | collective-permute-start | bytes 884744 | tf_op jit(solution)/shard_map/ppermute | solution.py:394
  739.6 8.5 %collective-permute-start.66 = (bf16[1,576,256]{2,1,0:T(8,128)(2,1)}, bf16[1,576,256]{2,1,0:T(8,128)(2,1)S(1)}, u32[]{:S(2)}, u32[]{:S(2)}) collective-permute-start(bf16[1,576,256]{2,1,0:T(8,128)(2,1)} %collective-permute-done.55.refs_1_), channel_id=1, source_target_pairs={{0,4},{4,0},{8,12},{12,8},{16,20},{20,16},{24,28},{28,24},{1,5},{5... | collective-permute-start | bytes 884744 | tf_op jit(solution)/shard_map/ppermute | solution.py:394
  739.7 8.6 %collective-permute-start.67 = (bf16[1,576,256]{2,1,0:T(8,128)(2,1)}, bf16[1,576,256]{2,1,0:T(8,128)(2,1)S(1)}, u32[]{:S(2)}, u32[]{:S(2)}) collective-permute-start(bf16[1,576,256]{2,1,0:T(8,128)(2,1)} %collective-permute-done.58.refs_2_), channel_id=1, source_target_pairs={{0,4},{4,0},{8,12},{12,8},{16,20},{20,16},{24,28},{28,24},{1,5},{5... | collective-permute-start | bytes 884744 | tf_op jit(solution)/shard_map/ppermute | solution.py:394
  (146 other events, 1358.4 us)
Sparse Core Ops, SparseCore 0:
  9.6 83.5 all-gather.5
  245.6 44.3 all-gather.9
  292.2 44.6 all-gather.7
  339.6 42.5 reduce-scatter.4
  385.0 43.1 reduce-scatter.6
  440.9 45.2 all-gather.11
  490.1 44.5 all-gather.13
  537.6 75.4 reduce-scatter.8
  620.2 76.1 reduce-scatter.10

commit v3 on v2

--- a/solution.py
+++ b/solution.py
@@ -179,25 +179,35 @@
         dk_ref[...] = dk_acc[...]
 
 
-def pull_carry_body(k_ref, v_ref, tail_ref, sum_ref, norm_ref, dk_in_ref, dv_in_ref, table_ref, dk_ref, dv_ref, dk_acc):
+def thin_width(heads):
+    return -(-2 * heads * FEAT // HV) * HV
+
+
+def pull_carry_body(k_ref, v_ref, tail_ref, sum_ref, norm_ref, dq_ref, dk_ref, dv_ref, table_ref, out_ref, dk_acc):
     head = pl.program_id(0)
+    tokens, lanes = k_ref.shape
+    start = 2 * lanes + -2 * lanes % HV
 
     @pl.when(head == 0)
     def _():
-        dk_acc[...] = dk_in_ref[...]
+        dk_acc[...] = dk_ref[...]
 
     table = table_ref[...]
-    one, two = pickers(table, head, k_ref.shape[1])
+    one, two = pickers(table, head, lanes)
     left, right = factors(k_ref[...], table, one, two)
     scale = table[4:5, :] * tail_ref[...]
     state = pad_state(sum_ref[0].astype(LOW))
-    dv_ref[...] = (dv_in_ref[...] + nn((left * right * scale).astype(LOW), state)).astype(dv_ref.dtype)
+    dv = dv_ref[...] + nn((left * right * scale).astype(LOW), state)
+    out_ref[:, pl.ds(pl.multiple_of(start + head * HV, HV), HV)] = dv.astype(out_ref.dtype)
     pulled = (nt(v_ref[...], state) + norm_ref[0][0:1, :]) * scale
     dk_acc[...] += nt((pulled * right).astype(LOW), one) + nt((pulled * left).astype(LOW), two)
 
     @pl.when(head == pl.num_programs(0) - 1)
     def _():
-        dk_ref[...] = dk_acc[...].astype(dk_ref.dtype)
+        thin = [dq_ref[...], dk_acc[...].astype(out_ref.dtype)]
+        if start > 2 * lanes:
+            thin.append(jnp.zeros((tokens, start - 2 * lanes), out_ref.dtype))
+        out_ref[:, :start] = jnp.concatenate(thin, axis=1)
 
 
 def shape(dims, kind):
@@ -278,12 +288,13 @@
             [self.acc, self.acc], 20, q, k, v, segc, segr, wide, total, norm, opened, table,
         )
 
-    def pull_carry(self, k, v, tail, total, norm, dk, dv, table):
+    def pull_carry(self, k, v, tail, total, norm, dq, dk, dv, table):
+        width = thin_width(self.heads) + self.heads * HV
         return self.call(
             pull_carry_body, "mix_pull_carry",
-            [self.thin, self.head, self.column, self.sum, self.norm, self.thin, self.head, self.table],
-            [self.thin, self.head], [self.thin_shape(LOW), self.head_shape(LOW)], [self.acc], 6,
-            k, v, tail, total, norm, dk, dv, table,
+            [self.thin, self.head, self.column, self.sum, self.norm, self.thin, self.thin, self.head, self.table],
+            self.full(self.tokens, width), shape((self.tokens, width), LOW), [self.acc], 6,
+            k, v, tail, total, norm, dq, dk, dv, table,
         )
 
 
@@ -333,26 +344,51 @@
 BIG = pltpu.CompilerParams(dimension_semantics=("arbitrary",), vmem_limit_bytes=56 * 1024 * 1024)
 
 
-def grad_blocks_body(blocks, swap, *refs, groups):
-    out_a, out_b = refs[-2:]
-    refs = list(refs[:-2])
-    at = 0
+def grad_values(refs, groups):
+    values = []
     for rows, parts in groups:
         value = None
         for _ in range(parts):
             term = nn(refs[1][...], refs[0][...])
             refs = refs[2:]
             value = term if value is None else value + term
-        for n, out in enumerate((out_a, out_b)):
-            half = value[n * rows // 2 : (n + 1) * rows // 2].astype(LOW)
-            gap = padded(rows // 2) - rows // 2
-            if gap:
-                half = jnp.concatenate([half, jnp.zeros((gap, half.shape[1]), LOW)], axis=0)
-            out[0, at : at + padded(rows // 2), :] = half
-        at += padded(rows // 2)
-
-
-def grad_blocks(name, groups, far, micros):
+        values.append(value)
+    return values
+
+
+def grad_body(blocks, swap, *refs, groups, summed):
+    step = pl.program_id(0)
+    places = (step, swap[0, step])
+    middle = pl.num_programs(0) // 2
+    sources = 2 * sum(parts for _, parts in groups)
+    values = grad_values(list(refs[:sources]), groups)
+    outs = refs[-4:]
+    came = refs[sources:-4]
+    at = 0
+    for (rows, _), value in zip(groups, values):
+        size = padded(rows // 2)
+        for n in range(2):
+            half = value[n * rows // 2 : (n + 1) * rows // 2]
+            if size > rows // 2:
+                half = jnp.concatenate([half, jnp.zeros((size - rows // 2, half.shape[1]), F32)], axis=0)
+            span = slice(at, at + size)
+            if summed:
+                other = jnp.where(places[n] < middle, came[n][0, span, :], came[2 + n][0, span, :])
+                half = half + other.astype(F32)
+            half = half.astype(LOW)
+
+            @pl.when(places[n] < middle)
+            def _():
+                outs[n][0, span, :] = half
+
+            @pl.when(places[n] >= middle)
+            def _():
+                outs[2 + n][0, span, :] = half
+
+        at += size
+
+
+def grad_blocks(name, groups, far, came, micros):
     count = lax.axis_size("batch")
     split = count // 2
     width = groups[0][0][0].shape[1]
@@ -368,26 +404,27 @@
         kinds.append((parts[0][1].shape[0], len(parts)))
         rows += padded(parts[0][1].shape[0] // 2)
     size = (1, rows, columns)
-    return pl.pallas_call(
-        functools.partial(grad_blocks_body, groups=tuple(kinds)),
+    places = [p - base for p in places[base : base + split]]
+    table, specs = [places], []
+    for low in (0, split // 2):
+        for order in (list(range(split)), places):
+            uses = [(s, p - low) for s, p in enumerate(order) if low <= p < low + split // 2]
+            table.append([([at for when, at in uses if when <= s] or [uses[0][1]])[-1] for s in range(split)])
+            specs.append(pl.BlockSpec(size, lambda s, b, w, n=len(table) - 1: (w[n, s], 0, 0)))
+    if came:
+        in_specs += specs
+        operands += came
+    outs = pl.pallas_call(
+        functools.partial(grad_body, groups=tuple(kinds), summed=bool(came)),
         grid_spec=pltpu.PrefetchScalarGridSpec(
-            num_scalar_prefetch=2,
-            grid=(split,),
-            in_specs=in_specs,
-            out_specs=[
-                pl.BlockSpec(size, lambda s, b, w: (s, 0, 0)),
-                pl.BlockSpec(size, lambda s, b, w: (w[s], 0, 0)),
-            ],
+            num_scalar_prefetch=2, grid=(split,), in_specs=in_specs, out_specs=specs
         ),
-        out_shape=[shape((split, rows, columns), LOW)] * 2,
+        out_shape=[shape((split // 2, rows, columns), LOW)] * 4,
         name=name,
         compiler_params=BIG,
         cost_estimate=cost(micros),
-    )(
-        blocks[base : base + split],
-        jnp.asarray(np.array(places[base : base + split], np.int32) - base),
-        *operands,
-    )
+    )(blocks[base : base + split], jnp.asarray(np.array(table, np.int32)), *operands)
+    return outs[:2], outs[2:]
 
 
 def flip(value, bit):
@@ -402,7 +439,7 @@
     def __init__(self, far):
         self.orders = batch_orders()
         self.steps = len(self.orders[0])
-        self.away, self.near, self.came = [[f] for f in far], None, [[], []]
+        self.away, self.near, self.came = [list(f) for f in zip(*far)], None, [[], []]
         self.step = 0
 
     def get(self):
@@ -421,12 +458,19 @@
             last = len(self.away[half]) if limit is None else first + limit
             self.came[half] += [flip(a, bit) for a in self.away[half][first:last]]
 
+    def begin(self, name, groups, micros):
+        self.near, away = grad_blocks(name, groups, False, [c[n] for n in range(2) for c in self.came], micros)
+        self.away, self.came, self.step = [[a] for a in away], [[], []], 1
+
     def take(self):
         n = self.step
         if n == 2 * self.steps:
             return
         self.step += 1
-        if n < self.steps:
+        if n == 0:
+            self.near, away = [[added(b, c[m]) for b, c in zip(half, self.came)] for m, half in enumerate(self.near)]
+            self.away = [[a] for a in away]
+        elif n < self.steps:
             half = self.near[0].shape[0] // 2
             pairs = [(k, c[0]) for k, c in zip(self.near, self.came)]
             if half:
@@ -465,13 +509,15 @@
             results[index][...] = part.T if turned else part
 
 
-def place_blocks(name, pieces, outs, width, micros):
+def place_blocks(name, pieces, outs, width, micros, part=None):
     count = lax.axis_size("batch")
     columns = width // count
     blocks, places = block_order()
     table = np.array([list(range(count)), places], np.int32)
     size = pieces[0][0].shape[1:]
-    piece = pl.BlockSpec((1,) + size, lambda s, b, t: (0, 0, 0), pipeline_mode=pl.Buffered(1))
+    if part is not None:
+        size = (padded(outs[0][0] // 2), size[1])
+    piece = pl.BlockSpec((1,) + size, lambda s, b, t: (0, part or 0, 0), pipeline_mode=pl.Buffered(1))
     out_specs, out_shape, layout, start = [], [], [], 0
     for rows, targets in outs:
         listed = []
@@ -618,7 +664,7 @@
 
 
 def narrow(part):
-    return lax.psum_scatter(part, "tensor", scatter_dimension=1, tiled=True).astype(F32)
+    return lax.psum_scatter(part, "tensor", scatter_dimension=1, tiled=True)
 
 
 def project(left, right):
@@ -667,7 +713,9 @@
 
     x_full = widen(tokens)
     gains = lax.all_gather(jnp.stack([norm1_gain, norm2_gain]), "tensor", axis=1, tiled=True)
-    w_mix = jnp.concatenate([w_query, w_key, w_value], axis=1)
+    thin = thin_width(heads)
+    w_mix = [w_query, w_key, jnp.zeros((width, thin - 2 * lanes), LOW), w_value]
+    w_mix = jnp.concatenate([w for w in w_mix if w.shape[1]], axis=1)
     gather_c = Gather(cotangent)
     x_full, gains, w_mix = lock(x_full, gains, w_mix, gather_c)
 
@@ -675,8 +723,8 @@
     x_wide = x_full.astype(F32)
     scale_one = lax.rsqrt(row_sum(x_wide * x_wide) / width + EPSILON)
     normed_one = (x_wide * scale_one * gains[0:1]).astype(LOW)
-    mixed_in = project(normed_one, w_mix).astype(LOW)
-    q, k, v = mixed_in[:, :lanes], mixed_in[:, lanes : 2 * lanes], mixed_in[:, 2 * lanes :]
+    pair = project(normed_one, w_mix[:, :thin]).astype(LOW)
+    q, k, v = pair[:, :lanes], pair[:, lanes : 2 * lanes], project(normed_one, w_value).astype(LOW)
     carry = mixer.state(k, v, tail, table)
     prior = outside(carry, False)
     numer, denom = mixer.inner(q, k, v, segc, segr)
@@ -726,13 +774,13 @@
         [(normed_a, dup_a), (normed_b, dup_b)],
         [(ca_full, inner_a), (cb_full, inner_b)],
     ]
-    ffn = Exchange(grad_blocks("grad_ffn_far", groups, True, 16))
+    ffn = Exchange(grad_blocks("grad_ffn_far", groups, True, None, 16))
     back_a, scale_b, normed_b, inner_b, dgate_b, dup_b, part = lock(
         back_a, scale_b, normed_b, inner_b, dgate_b, dup_b, part, ffn
     )
 
     def turned(c, scale, back, hidden):
-        scaled = scale * back
+        scaled = scale * back.astype(F32)
         return c.astype(F32) + norm2_gain[None, :] * scaled, jnp.sum(scaled * hidden, axis=0)
 
     def spread(u, c, wide, scale, local_u, hidden):
@@ -750,7 +798,7 @@
         [(ca_full, inner_a), (cb_full, inner_b)],
     ]
     ffn.send()
-    ffn.near = grad_blocks("grad_ffn_near", groups, False, 16)
+    ffn.near = grad_blocks("grad_ffn_near", groups, False, None, 16)
     ffn.take()
     ffn.send()
     back_b, u_a, gain_a, low_a, ffn.away, ffn.near = lock(back_b, u_a, gain_a, low_a, ffn.away, ffn.near)
@@ -767,51 +815,61 @@
     dh_a, grad_hidden_a, dy_a = spread(wide_u, ca_full, wide_a, scale_a, u_a, hidden_a)
     ffn.take()
     ffn.send()
-    wide_v, dh_a, grad_hidden_a, dy_a = lock(wide_v, dh_a, grad_hidden_a, dy_a, ffn)
+    wide_v, dh_a, grad_hidden_a, dy_a, ffn.away, ffn.near = lock(
+        wide_v, dh_a, grad_hidden_a, dy_a, ffn.away, ffn.near
+    )
 
     down = narrow(join(*parts))
+    dh_b, grad_hidden_b, dy_b = spread(wide_v, cb_full, wide_b, scale_b, u_b, hidden_b)
+    wide, dsum, dnorm = mixer.pull_state(q, [dy_a, dy_b], y, total, opened, table)
     ffn.take()
     ffn.send(1)
-    dh_b, grad_hidden_b, dy_b = spread(wide_v, cb_full, wide_b, scale_b, u_b, hidden_b)
-    wide, dsum, dnorm = mixer.pull_state(q, [dy_a, dy_b], y, total, opened, table)
     wide, dsum, dnorm = lock(wide, dsum, dnorm, ffn)
     following = outside([dsum, dnorm], True)
     dq, dk, dv = mixer.pull_inner(q, k, v, segc, segr, wide, *prior, opened, table)
     following, dq, dk, dv = lock(following, dq, dk, dv, ffn)
     ffn.send()
-    dk, dv = mixer.pull_carry(k, v, tail, *following, dk, dv, table)
-    dmix = jnp.concatenate([dq, dk, dv], axis=1)
+    dmix = mixer.pull_carry(k, v, tail, *following, dq, dk, dv, table)
     part = project_back(dmix, w_mix).astype(LOW)
-    down, part, dmix, dh_b, grad_hidden_b = lock(down, part, dmix, dh_b, grad_hidden_b)
+    down, part, dmix, dh_b, grad_hidden_b = lock(down, part, dmix, dh_b, grad_hidden_b, ffn)
 
     back = narrow(part)
     y_a, y_b = cut(y)
     groups = [[(normed_one, dmix.T)], [(dh_a, y_a.T), (dh_b, y_b.T)]]
-    mix = Exchange(grad_blocks("grad_mix_far", groups, True, 5))
+    ffn.take()
+    ffn.send()
+    mix = Exchange(grad_blocks("grad_mix_far", groups, True, None, 5))
     mix.send()
-    mix.near = grad_blocks("grad_mix_near", groups, False, 5)
-    dots = Gather(row_sum(dmix.astype(F32) * mixed_in.astype(F32)).reshape(count // 128, 128)).run()
-    lock(mix, ffn)
+    mix.begin("grad_mix_near", groups, 5)
+    dot = row_sum(dmix[:, :thin].astype(F32) * pair.astype(F32))
+    dot = dot + row_sum(dmix[:, thin:].astype(F32) * v.astype(F32))
+    dots = Gather(dot.reshape(count // 128, 128))
+    lock(mix, dots, ffn)
+    mix.send()
+    dots.hop()
+    ffn.take()
+    final = ffn.run()
+
+    def ffn_weight(n):
+        return place_blocks(f"place_ffn_{n}", final, [(units, [(0, units, False)])], width, 7, n)[0]
+
+    grad_w_gate = lock(mix, dots, ffn_weight(0))[0]
     mix.take()
     mix.send()
-    ffn.take()
-    ffn.send()
-    output = (join(hidden_a, hidden_b) + down).astype(LOW)
-    output = lock(mix, ffn, output, dots)[0]
+    dots.hop()
+    grad_w_up = lock(mix, dots, ffn_weight(1))[0]
     mix.take()
     mix.send()
-    ffn.take()
-    grad_w_gate, grad_w_up, grad_w_down = place_blocks(
-        "place_ffn", ffn.run(), [(units, [(0, units, False)])] * 3, width, 20
-    )
+    dots.run()
+    output = (join(hidden_a, hidden_b) + down.astype(F32)).astype(LOW)
+    output = lock(mix, dots, output)[0]
     mix.take()
     mix.send()
+    grad_w_down = lock(mix, ffn_weight(2))[0]
     mix.take()
     mix.send()
-    back, grad_w_gate, grad_w_up, grad_w_down, output = lock(
-        back, grad_w_gate, grad_w_up, grad_w_down, output, mix
-    )
-    inputs = tokens.astype(F32)
+    back = lock(back, mix)[0]
+    inputs, back = tokens.astype(F32), back.astype(F32)
     gain_one = jnp.sum(back * inputs * scale_one, axis=0)
     gain_grads = batch_sum(jnp.stack([gain_one, gain_a + gain_b]))
     grad_tokens = (
@@ -824,7 +882,7 @@
         "place_mix",
         mix.run(),
         [
-            (2 * lanes + values, [(0, lanes, False), (lanes, lanes, False), (2 * lanes, values, True)]),
+            (thin + values, [(0, lanes, False), (lanes, lanes, False), (thin, values, True)]),
             (values, [(0, values, False)]),
         ],
         width,

time: 775 us -> 738 us (0.952)
  waiting for transfers between devices: 322 us -> 288 us
  Pallas kernels: 121 us -> 138 us
  local copies, waits for them, and re-layouts: 42.1 us -> 31.4 us
  other arithmetic: 93 us -> 82.4 us
    ppermute x43 -> x47, waiting for transfers between devices: 113 us -> 84.1 us  [flip(): lax.ppermute(value, 'batch', [(i, i ^ bit) for i in range(lax.axis_size('...]
    reduce_scatter x4, waiting for transfers between devices: 26.8 us -> 11.7 us  [narrow(): return lax.psum_scatter(part, 'tensor', scatter_dimension=1, tiled=True)]
    pallas_call x2 -> x4, Pallas kernels: 25.8 us -> 35.7 us  [place_blocks(): pl.pallas_call(functools.partial(place_body, outs=tuple(layout), count=co...]
    all_gather x5, waiting for transfers between devices: 101 us -> 110 us  [widen(): return lax.all_gather(part, 'tensor', axis=1, tiled=True)]
    convert_element_type x5 -> x1, other arithmetic: 10.1 us -> 1.33 us  [local(): output = (join(hidden_a, hidden_b) + down.astype(F32)).astype(LOW)]
    unnamed x258 -> x268, local copies, waits for them, and re-layouts: 22.8 us -> 18.4 us
    ppermute x43 -> x47, starting transfers between devices: 30.9 us -> 31.9 us  [flip(): lax.ppermute(value, 'batch', [(i, i ^ bit) for i in range(lax.axis_size('...]
  transfers between devices with their start and end apart: 82 -> 86, of which waited for: 39 -> 40; matrix products, arithmetic and copies ran while one was open for 22% -> 22% of each run, Pallas kernels for 14% -> 18%
where the time goes in v3:
time: 738 us; the launch traced here: 728 us
  waiting for transfers between devices  288 us (39%)
  Pallas kernels  138 us (19%)
  matrix products  84.2 us (11%)
  other arithmetic  82.4 us (11%)
  starting transfers between devices  72.5 us (10%)
  local copies, waits for them, and re-layouts  31.4 us (4%)
  between operations  16.7 us (2%)
  blocking collectives  14.9 us (2%)
    all_gather x5, waiting for transfers between devices, widen(): return lax.all_gather(part, 'tensor', axis=1, tiled=True)  110 us
    ppermute x47, waiting for transfers between devices, flip(): lax.ppermute(value, 'batch', [(i, i ^ bit) for i in range(lax.axis_size('...  84.1 us
    pallas_call x4, Pallas kernels, grad_blocks(): pl.pallas_call(functools.partial(grad_body, groups=tuple(kinds), summed=b...  53.9 us
    dot_general x9, matrix products, project_back(): return jnp.einsum('ti,ji->tj', left, right, preferred_element_type=F32)  45 us
    ppermute x3, waiting for transfers between devices, hop(): lax.ppermute(sends[0], 'tensor', [(k, k + 1) for k in range(0, count - se...  44.1 us
    pallas_call x6, Pallas kernels, call(): pl.pallas_call(body, grid=(self.heads,), in_specs=in_specs, out_specs=out...  42.7 us
    pallas_call x4, Pallas kernels, place_blocks(): pl.pallas_call(functools.partial(place_body, outs=tuple(layout), count=co...  35.7 us
    ppermute x47, starting transfers between devices, flip(): lax.ppermute(value, 'batch', [(i, i ^ bit) for i in range(lax.axis_size('...  31.9 us
  transfers between devices with their start and end apart: 86, of which 40 were waited for; matrix products, arithmetic and copies ran while one was open for 22% of the time, Pallas kernels for 18%

profile of v3, /device:TPU:0, one launch (start us, length us, event | category | flops | bytes accessed | tf_op | source)
XLA Modules:
  0.0 728.1 jit_solution(10894130530454964867)
XLA Ops:
  15.0 14.9 %all_gather.19 = f32[2,2048]{1,0:T(2,128)S(1)} all-gather(f32[2,512]{1,0:T(2,128)S(1)} %pad_maximum_fusion.3), channel_id=1, replica_groups=mesh['batch'=8,'tensor'=4] {'tensor'}, dimensions={1}, use_global_device_ids=true | all-gather | bytes 20480 | tf_op jit(solution)/shard_map/all_gather | solution.py:715
  32.2 4.1 pad_maximum_fusion.2
  36.3 56.9 %all-gather.6.cloned.1.call-done = bf16[1024,2048]{1,0:T(8,128)(2,1)} async-done(((bf16[1024,512]{1,0:T(8,128)(2,1)}), bf16[1024,2048]{1,0:T(8,128)(2,1)}) %all-gather.6.cloned.1.call-update) | async-done | bytes 4194320 | tf_op jit(solution)/shard_map/all_gather | solution.py:663
  93.2 3.2 fusion
  100.6 2.7 convolution_convert_fusion.4
  104.1 3.3 mix_state.1
  117.0 5.8 mix_inner.1
  128.5 3.1 collective-permute-done.2
  131.6 5.8 mix_merge.1
  140.7 5.2 collective-permute-start.8
  152.8 13.5 %collective-permute-done.8 = bf16[1024,512]{1,0:T(8,128)(2,1)} collective-permute-done((bf16[1024,512]{1,0:T(8,128)(2,1)}, bf16[1024,512]{1,0:T(8,128)(2,1)}, u32[]{:S(2)}, u32[]{:S(2)}) %collective-permute-start.8) | collective-permute-done | bytes 1048608 | tf_op jit(solution)/shard_map/ppermute | solution.py:629
  166.4 9.4 %collective-permute-done.11 = bf16[1024,512]{1,0:T(8,128)(2,1)} collective-permute-done((bf16[1024,512]{1,0:T(8,128)(2,1)}, bf16[1024,512]{1,0:T(8,128)(2,1)}, u32[]{:S(2)}, u32[]{:S(2)}) %collective-permute-start.11) | collective-permute-done | bytes 1048608 | tf_op jit(solution)/shard_map/ppermute | solution.py:587
  183.2 16.8 %collective-permute-done.12 = bf16[1024,512]{1,0:T(8,128)(2,1)S(1)} collective-permute-done((bf16[1024,512]{1,0:T(8,128)(2,1)S(1)}, bf16[1024,512]{1,0:T(8,128)(2,1)S(1)}, u32[]{:S(2)}, u32[]{:S(2)}) %collective-permute-start.12) | collective-permute-done | bytes 1048608 | tf_op jit(solution)/shard_map/ppermute | solution.py:629
  200.1 5.9 collective-permute-done.15
  207.3 2.6 collective-permute-start.16
  214.0 13.7 %collective-permute-done.16 = bf16[1024,512]{1,0:T(8,128)(2,1)} collective-permute-done((bf16[1024,512]{1,0:T(8,128)(2,1)}, bf16[1024,512]{1,0:T(8,128)(2,1)}, u32[]{:S(2)}, u32[]{:S(2)}) %collective-permute-start.16) | collective-permute-done | bytes 1048608 | tf_op jit(solution)/shard_map/ppermute | solution.py:629
  227.7 6.5 collective-permute-done.17
  244.7 5.6 straighten.1
  250.3 8.1 %convolution_bitcast_fusion.5 = f32[1376,512]{1,0:T(8,128)} fusion(bf16[1376,2048]{1,0:T(8,128)(2,1)} %param.39, bf16[1024,2048]{1,0:T(8,128)(2,1)} %straighten.1), kind=kOutput, calls=%fused_computation.41 | convolution fusion | flops 2885681152 | bytes 10551296 | tf_op jit(solution)/shard_map/ti,ji->tj/dot_general | solution.py:675
  258.4 4.7 convolution_bitcast_fusion.4
  263.4 19.8 %all-gather.10.cloned.1.call-done = bf16[512,2048]{1,0:T(8,128)(2,1)} async-done(((bf16[512,512]{1,0:T(8,128)(2,1)}), bf16[512,2048]{1,0:T(8,128)(2,1)}) %all-gather.10.cloned.1.call-update) | async-done | bytes 2097168 | tf_op jit(solution)/shard_map/all_gather | solution.py:663
  286.0 6.2 convolution_bitcast_fusion.2
  292.3 5.5 multiply_convert_fusion.3
  297.8 3.5 fusion.60
  301.4 4.6 add_convert_fusion.5
  306.0 24.0 %all-gather.8.cloned.1.call-done = bf16[512,2048]{1,0:T(8,128)(2,1)} async-done(((bf16[512,512]{1,0:T(8,128)(2,1)}), bf16[512,2048]{1,0:T(8,128)(2,1)}) %all-gather.8.cloned.1.call-update) | async-done | bytes 2097168 | tf_op jit(solution)/shard_map/all_gather | solution.py:663
  333.1 6.4 convolution_bitcast_fusion
  342.6 5.5 multiply_convert_fusion
  348.1 3.5 fusion.61
  351.7 4.6 add_convert_fusion.4
  356.3 18.0 %grad_ffn_far.1 = (bf16[2,2064,256]{2,1,0:T(8,128)(2,1)}, bf16[2,2064,256]{2,1,0:T(8,128)(2,1)}, bf16[2,2064,256]{2,1,0:T(8,128)(2,1)}, bf16[2,2064,256]{2,1,0:T(8,128)(2,1)}) custom-call(s32[4]{0:T(128)} %get-tuple-element.519.blocks, s32[5,4]{1,0:T(8,128)} %constant.83.clone.swap, bf16[512,2048]{1,0:T(8,128)(2,1)} %copy-done.75, ...), custom_call_target="tpu_custom_call" | custom-call | flops 16000000000 | bytes 1048576 | tf_op jit(solution)/shard_map/grad_ffn_far/pallas_call | solution.py:417
  376.9 18.2 %grad_ffn_near.1 = (bf16[2,2064,256]{2,1,0:T(8,128)(2,1)}, bf16[2,2064,256]{2,1,0:T(8,128)(2,1)}, bf16[2,2064,256]{2,1,0:T(8,128)(2,1)}, bf16[2,2064,256]{2,1,0:T(8,128)(2,1)}) custom-call(s32[4]{0:T(128)} %get-tuple-element.520.blocks, s32[5,4]{1,0:T(8,128)} %constant.83.clone.swap, bf16[512,2048]{1,0:T(8,128)(2,1)} %copy-done.75, ...), custom_call_target="tpu_custom_call" | custom-call | flops 16000000000 | bytes 1048576 | tf_op jit(solution)/shard_map/grad_ffn_near/pallas_call | solution.py:417
  397.3 3.7 add_convert_fusion.3
  400.9 3.7 add_convert_fusion.2
  404.6 3.6 add_convert_fusion.1
  410.1 10.7 %reduce-scatter.7.cloned.1.call-done = bf16[512,512]{1,0:T(8,128)(2,1)} async-done(((bf16[512,2048]{1,0:T(8,128)(2,1)}), bf16[512,512]{1,0:T(8,128)(2,1)}) %reduce-scatter.7.cloned.1.call-update) | async-done | bytes 524304 | tf_op jit(solution)/shard_map/reduce_scatter | solution.py:667
  423.9 7.8 %convolution_convert_fusion.2 = bf16[512,2048]{1,0:T(8,128)(2,1)} fusion(bf16[1376,512]{1,0:T(8,128)(2,1)} %get-tuple-element.304.refs_9_, bf16[1376,2048]{1,0:T(8,128)(2,1)} %param.39), kind=kOutput, calls=%fused_computation.46 | convolution fusion | flops 2886729728 | bytes 9142272 | tf_op jit(solution)/shard_map/it,ij->tj/dot_general | solution.py:679
  431.7 7.4 %convolution_convert_fusion.1 = bf16[512,2048]{1,0:T(8,128)(2,1)} fusion(bf16[1376,512]{1,0:T(8,128)(2,1)S(1)} %copy-done.120, bf16[1376,2048]{1,0:T(8,128)(2,1)} %param.39), kind=kOutput, calls=%fused_computation.45 | convolution fusion | flops 2886729728 | bytes 9142272 | tf_op jit(solution)/shard_map/it,ij->tj/dot_general | solution.py:679
  440.6 28.2 %collective-permute-done.22 = bf16[2,2064,256]{2,1,0:T(8,128)(2,1)} collective-permute-done((bf16[2,2064,256]{2,1,0:T(8,128)(2,1)}, bf16[2,2064,256]{2,1,0:T(8,128)(2,1)}, u32[]{:S(2)}, u32[]{:S(2)}) %collective-permute-start.22) | collective-permute-done | bytes 2113568 | tf_op jit(solution)/shard_map/ppermute | solution.py:431
  470.3 3.0 add_convert_fusion.10
  474.7 2.9 add_convert_fusion.7
  478.1 2.7 fusion.8
  480.8 2.6 pad_maximum_fusion.1
  483.5 2.9 fusion.3.refs_2_
  490.1 7.2 collective-permute-done.24
  497.3 3.0 add_convert_fusion.9.refs_0_
  501.8 3.1 add_convert_fusion.6.refs_8_
  505.8 9.1 %all-gather.14.cloned.1.call-done = bf16[512,2048]{1,0:T(8,128)(2,1)} async-done(((bf16[512,512]{1,0:T(8,128)(2,1)}), bf16[512,2048]{1,0:T(8,128)(2,1)}) %all-gather.14.cloned.1.call-update) | async-done | bytes 2097168 | tf_op jit(solution)/shard_map/all_gather | solution.py:663
  517.8 3.7 fusion.12
  524.6 6.0 mix_pull_state.1
  531.5 18.8 %collective-permute-done.28.refs_2_ = bf16[1,2064,256]{2,1,0:T(8,128)(2,1)S(1)} collective-permute-done((bf16[1,2064,256]{2,1,0:T(8,128)(2,1)}, bf16[1,2064,256]{2,1,0:T(8,128)(2,1)S(1)}, u32[]{:S(2)}, u32[]{:S(2)}) %collective-permute-start.28) | collective-permute-done | bytes 1056800 | tf_op jit(solution)/shard_map/ppermute | solution.py:431
  555.5 16.0 %mix_pull_inner.1 = (bf16[1024,64]{1,0:T(8,128)(2,1)S(1)}, f32[1024,64]{1,0:T(8,128)S(1)}, f32[1024,512]{1,0:T(8,128)S(1)}) custom-call(bf16[1024,64]{1,0:T(8,128)(2,1)S(1)} %copy-done.19, bf16[1024,64]{1,0:T(8,128)(2,1)S(1)} %copy-done.17, bf16[1024,512]{1,0:T(8,128)(2,1)S(1)} %copy-done.7, s32[1024,1]{1,0:T(8,128)S(1)} %copy-done.4, ...), custom_call_target="tpu_custom_call" | custom-call | flops 20000000000 | bytes 1048576 | tf_op jit(solution)/shard_map/mix_pull_inner/pallas_call | solution.py:236
  582.1 6.0 mix_pull_carry.1
  589.1 5.0 convolution_convert_fusion
  594.1 9.7 %collective-permute-done.36.refs_3_ = bf16[1,2064,256]{2,1,0:T(8,128)(2,1)} collective-permute-done((bf16[1,2064,256]{2,1,0:T(8,128)(2,1)}, bf16[1,2064,256]{2,1,0:T(8,128)(2,1)}, u32[]{:S(2)}, u32[]{:S(2)}) %collective-permute-start.36) | collective-permute-done | bytes 1056800 | tf_op jit(solution)/shard_map/ppermute | solution.py:431
  609.8 8.6 %grad_mix_far.1 = (bf16[2,576,256]{2,1,0:T(8,128)(2,1)}, bf16[2,576,256]{2,1,0:T(8,128)(2,1)}, bf16[2,576,256]{2,1,0:T(8,128)(2,1)}, bf16[2,576,256]{2,1,0:T(8,128)(2,1)}) custom-call(s32[4]{0:T(128)} %get-tuple-element.519.blocks, s32[5,4]{1,0:T(8,128)} %constant.83.clone.swap, bf16[1024,2048]{1,0:T(8,128)(2,1)} %copy-done.58, bf16[640,1024]{1,0:T(8,128)(2,1)} %bitcast.91, ...), custom_call_target="tpu_custom_call" | custom-call | flops 5000000000 | bytes 1048576 | tf_op jit(solution)/shard_map/grad_mix_far/pallas_call | solution.py:417
  621.6 5.2 collective-permute-done.40.refs_8_
  631.1 9.1 %grad_mix_near.1 = (bf16[2,576,256]{2,1,0:T(8,128)(2,1)}, bf16[2,576,256]{2,1,0:T(8,128)(2,1)}, bf16[2,576,256]{2,1,0:T(8,128)(2,1)}, bf16[2,576,256]{2,1,0:T(8,128)(2,1)}) custom-call(s32[4]{0:T(128)} %get-tuple-element.520.blocks, s32[5,4]{1,0:T(8,128)} %constant.83.clone.swap, bf16[1024,2048]{1,0:T(8,128)(2,1)} %copy-done.58, bf16[640,1024]{1,0:T(8,128)(2,1)} %bitcast.92, ...), custom_call_target="tpu_custom_call" | custom-call | flops 5000000000 | bytes 1048576 | tf_op jit(solution)/shard_map/grad_mix_near/pallas_call | solution.py:417
  645.6 9.1 %place_ffn_0.1 = f32[1376,2048]{1,0:T(8,128)} custom-call(s32[8]{0:T(128)} %copy-done.96, s32[2,8]{1,0:T(2,128)} %constant.84.clone.table, bf16[1,2064,256]{2,1,0:T(8,128)(2,1)} %add_convert_fusion.9.refs_0_, bf16[1,2064,256]{2,1,0:T(8,128)(2,1)} %collective-permute-done.26.refs_1_, bf16[1,2064,256]{2,1,0:T(8,128)(2,1)} %copy-done.45, ...), custom_call_target="tpu_custom_call" | custom-call | flops 7000000000 | bytes 1048576 | tf_op jit(solution)/shard_map/place_ffn_0/pallas_call | solution.py:534
  661.9 9.4 %place_ffn_1.1 = f32[1376,2048]{1,0:T(8,128)} custom-call(s32[8]{0:T(128)} %copy-done.96, s32[2,8]{1,0:T(2,128)} %constant.84.clone.table, bf16[1,2064,256]{2,1,0:T(8,128)(2,1)} %add_convert_fusion.9.refs_0_, bf16[1,2064,256]{2,1,0:T(8,128)(2,1)} %collective-permute-done.26.refs_1_, bf16[1,2064,256]{2,1,0:T(8,128)(2,1)} %copy-done.45, ...), custom_call_target="tpu_custom_call" | custom-call | flops 7000000000 | bytes 1048576 | tf_op jit(solution)/shard_map/place_ffn_1/pallas_call | solution.py:534
  676.4 6.2 collective-permute-done.61
  686.8 9.1 %place_ffn_2.1 = f32[1376,2048]{1,0:T(8,128)} custom-call(s32[8]{0:T(128)} %copy-done.96, s32[2,8]{1,0:T(2,128)} %constant.84.clone.table, bf16[1,2064,256]{2,1,0:T(8,128)(2,1)} %add_convert_fusion.9.refs_0_, bf16[1,2064,256]{2,1,0:T(8,128)(2,1)} %collective-permute-done.26.refs_1_, bf16[1,2064,256]{2,1,0:T(8,128)(2,1)} %copy-done.45, ...), custom_call_target="tpu_custom_call" | custom-call | flops 7000000000 | bytes 1048576 | tf_op jit(solution)/shard_map/place_ffn_2/pallas_call | solution.py:534
  702.2 3.9 fusion.18
  712.5 8.0 %place_mix.1 = (f32[64,2048]{1,0:T(8,128)}, f32[64,2048]{1,0:T(8,128)}, f32[2048,512]{1,0:T(8,128)}, f32[512,2048]{1,0:T(8,128)}) custom-call(s32[8]{0:T(128)} %copy-done.96, s32[2,8]{1,0:T(2,128)} %constant.84.clone.table, bf16[1,576,256]{2,1,0:T(8,128)(2,1)} %copy-done.88, bf16[1,576,256]{2,1,0:T(8,128)(2,1)} %copy-done.103, ...), custom_call_target="tpu_custom_call" | custom-call | flops 5000000000 | bytes 1048576 | tf_op jit(solution)/shard_map/place_mix/pallas_call | solution.py:534
  (515 shorter events, 164.0 us)
Async XLA Ops:
  7.2 86.0 %all-gather.6.cloned.1.call-start = ((), (), s32[]{:S(2)}) async-start(), calls=%async_computation.4 | async-start | bytes 5242880 | tf_op jit(solution)/shard_map/all_gather | solution.py:663
  8.0 275.2 %all-gather.10.cloned.1.call-start = ((), (), s32[]{:S(2)}) async-start(), calls=%async_computation.6 | async-start | bytes 2621440 | tf_op jit(solution)/shard_map/all_gather | solution.py:663
  108.0 31.5 %collective-permute-start.6 = (bf16[1024,512]{1,0:T(8,128)(2,1)}, bf16[1024,512]{1,0:T(8,128)(2,1)}, u32[]{:S(2)}, u32[]{:S(2)}) collective-permute-start(bf16[1024,512]{1,0:T(8,128)(2,1)} %param.40), channel_id=1, source_target_pairs={{0,1},{1,2},{2,3},{4,5},{5,6},{6,7},{8,9},{9,10},{10,11},{12,13},{... | collective-permute-start | bytes 3145736 | tf_op jit(solution)/shard_map/ppermute | solution.py:586
  110.4 29.1 %collective-permute-start.7 = (bf16[1024,512]{1,0:T(8,128)(2,1)}, bf16[1024,512]{1,0:T(8,128)(2,1)}, u32[]{:S(2)}, u32[]{:S(2)}) collective-permute-start(bf16[1024,512]{1,0:T(8,128)(2,1)} %param.40), channel_id=1, source_target_pairs={{1,0},{2,1},{3,2},{5,4},{6,5},{7,6},{9,8},{10,9},{11,10},{13,12},{... | collective-permute-start | bytes 3145736 | tf_op jit(solution)/shard_map/ppermute | solution.py:587
  111.7 12.4 %collective-permute-start.4 = (f32[4,8,256]{2,1,0:T(8,128)S(1)}, f32[4,8,256]{2,1,0:T(8,128)S(1)}, u32[]{:S(2)}, u32[]{:S(2)}) collective-permute-start(f32[4,8,256]{2,1,0:T(8,128)S(1)} %add.320), channel_id=1, source_target_pairs={{0,8},{4,12},{8,0},{12,4},{16,24},{20,28},{24,16},{28,20},{1,9},{5... | collective-permute-start | bytes 98312 | tf_op jit(solution)/shard_map/ppermute | solution.py:309
  113.3 12.4 %collective-permute-start.1 = (bf16[4,160,128]{2,1,0:T(8,128)(2,1)S(1)}, bf16[4,160,128]{2,1,0:T(8,128)(2,1)S(1)}, u32[]{:S(2)}, u32[]{:S(2)}) collective-permute-start(bf16[4,160,128]{2,1,0:T(8,128)(2,1)S(1)} %fusion.37), channel_id=1, source_target_pairs={{0,8},{4,12},{8,0},{12,4},{16,24},{20,28},{24,16},{28,20},{1,9},{5... | collective-permute-start | bytes 491528 | tf_op jit(solution)/shard_map/ppermute | solution.py:309
  140.7 25.6 %collective-permute-start.8 = (bf16[1024,512]{1,0:T(8,128)(2,1)}, bf16[1024,512]{1,0:T(8,128)(2,1)}, u32[]{:S(2)}, u32[]{:S(2)}) collective-permute-start(bf16[1024,512]{1,0:T(8,128)(2,1)} %convert_element_type.376), channel_id=1, source_target_pairs={{0,1},{4,5},{8,9},{12,13},{16,17},{20,21},{24,25},{28,29}} | collective-permute-start | bytes 3145736 | tf_op jit(solution)/shard_map/ppermute | solution.py:629
  147.1 19.3 %collective-permute-start.9 = (bf16[1024,512]{1,0:T(8,128)(2,1)}, bf16[1024,512]{1,0:T(8,128)(2,1)}, u32[]{:S(2)}, u32[]{:S(2)}) collective-permute-start(bf16[1024,512]{1,0:T(8,128)(2,1)} %convert_element_type.377), channel_id=1, source_target_pairs={{3,2},{7,6},{11,10},{15,14},{19,18},{23,22},{27,26},{31,30}} | collective-permute-start | bytes 3145736 | tf_op jit(solution)/shard_map/ppermute | solution.py:630
  148.7 17.7 %collective-permute-start.10 = (bf16[1024,512]{1,0:T(8,128)(2,1)}, bf16[1024,512]{1,0:T(8,128)(2,1)}, u32[]{:S(2)}, u32[]{:S(2)}) collective-permute-start(bf16[1024,512]{1,0:T(8,128)(2,1)} %collective-permute-done.6), channel_id=1, source_target_pairs={{1,2},{2,3},{5,6},{6,7},{9,10},{10,11},{13,14},{14,15},{17,18},{18... | collective-permute-start | bytes 3145736 | tf_op jit(solution)/shard_map/ppermute | solution.py:586
  150.3 25.5 %collective-permute-start.11 = (bf16[1024,512]{1,0:T(8,128)(2,1)}, bf16[1024,512]{1,0:T(8,128)(2,1)}, u32[]{:S(2)}, u32[]{:S(2)}) collective-permute-start(bf16[1024,512]{1,0:T(8,128)(2,1)} %collective-permute-done.7), channel_id=1, source_target_pairs={{1,0},{2,1},{5,4},{6,5},{9,8},{10,9},{13,12},{14,13},{17,16},{18,1... | collective-permute-start | bytes 3145736 | tf_op jit(solution)/shard_map/ppermute | solution.py:587
  178.0 22.1 %collective-permute-start.12 = (bf16[1024,512]{1,0:T(8,128)(2,1)S(1)}, bf16[1024,512]{1,0:T(8,128)(2,1)S(1)}, u32[]{:S(2)}, u32[]{:S(2)}) collective-permute-start(bf16[1024,512]{1,0:T(8,128)(2,1)S(1)} %get-tuple-element.498), channel_id=1, source_target_pairs={{0,1},{1,2},{4,5},{5,6},{8,9},{9,10},{12,13},{13,14},{16,17},{17,1... | collective-permute-start | bytes 3145736 | tf_op jit(solution)/shard_map/ppermute | solution.py:629
  180.5 19.6 %collective-permute-start.13 = (bf16[1024,512]{1,0:T(8,128)(2,1)S(1)}, bf16[1024,512]{1,0:T(8,128)(2,1)S(1)}, u32[]{:S(2)}, u32[]{:S(2)}) collective-permute-start(bf16[1024,512]{1,0:T(8,128)(2,1)S(1)} %get-tuple-element.497), channel_id=1, source_target_pairs={{2,1},{3,2},{6,5},{7,6},{10,9},{11,10},{14,13},{15,14},{18,17},{19... | collective-permute-start | bytes 3145736 | tf_op jit(solution)/shard_map/ppermute | solution.py:630
  181.2 18.8 %collective-permute-start.14 = (bf16[1024,512]{1,0:T(8,128)(2,1)}, bf16[1024,512]{1,0:T(8,128)(2,1)S(1)}, u32[]{:S(2)}, u32[]{:S(2)}) collective-permute-start(bf16[1024,512]{1,0:T(8,128)(2,1)} %collective-permute-done.10), channel_id=1, source_target_pairs={{2,3},{6,7},{10,11},{14,15},{18,19},{22,23},{26,27},{30,31}} | collective-permute-start | bytes 3145736 | tf_op jit(solution)/shard_map/ppermute | solution.py:586
  181.9 24.0 %collective-permute-start.15 = (bf16[1024,512]{1,0:T(8,128)(2,1)}, bf16[1024,512]{1,0:T(8,128)(2,1)S(1)}, u32[]{:S(2)}, u32[]{:S(2)}) collective-permute-start(bf16[1024,512]{1,0:T(8,128)(2,1)} %collective-permute-done.11), channel_id=1, source_target_pairs={{1,0},{5,4},{9,8},{13,12},{17,16},{21,20},{25,24},{29,28}} | collective-permute-start | bytes 3145736 | tf_op jit(solution)/shard_map/ppermute | solution.py:587
  207.3 20.5 %collective-permute-start.16 = (bf16[1024,512]{1,0:T(8,128)(2,1)}, bf16[1024,512]{1,0:T(8,128)(2,1)}, u32[]{:S(2)}, u32[]{:S(2)}) collective-permute-start(bf16[1024,512]{1,0:T(8,128)(2,1)} %add_convert_fusion.13), channel_id=1, source_target_pairs={{0,1},{1,2},{2,3},{4,5},{5,6},{6,7},{8,9},{9,10},{10,11},{12,13},{... | collective-permute-start | bytes 3145736 | tf_op jit(solution)/shard_map/ppermute | solution.py:629
  211.3 22.9 %collective-permute-start.17 = (bf16[1024,512]{1,0:T(8,128)(2,1)}, bf16[1024,512]{1,0:T(8,128)(2,1)}, u32[]{:S(2)}, u32[]{:S(2)}) collective-permute-start(bf16[1024,512]{1,0:T(8,128)(2,1)} %add_convert_fusion.12), channel_id=1, source_target_pairs={{1,0},{2,1},{3,2},{5,4},{6,5},{7,6},{9,8},{10,9},{11,10},{13,12},{... | collective-permute-start | bytes 3145736 | tf_op jit(solution)/shard_map/ppermute | solution.py:630
  238.9 91.1 %all-gather.8.cloned.1.call-start = ((), (), s32[]{:S(2)}) async-start(), calls=%async_computation.5 | async-start | bytes 2621440 | tf_op jit(solution)/shard_map/all_gather | solution.py:663
  263.1 112.2 %reduce-scatter.5.cloned.1.call-start = ((), (), s32[]{:S(2)}) async-start(), calls=%async_computation.7 | async-start | bytes 2621440 | tf_op jit(solution)/shard_map/reduce_scatter | solution.py:667
  330.0 90.8 %reduce-scatter.7.cloned.1.call-start = ((), (), s32[]{:S(2)}) async-start(), calls=%async_computation.8 | async-start | bytes 2621440 | tf_op jit(solution)/shard_map/reduce_scatter | solution.py:667
  375.3 21.3 %collective-permute-start.18 = (bf16[2,2064,256]{2,1,0:T(8,128)(2,1)}, bf16[2,2064,256]{2,1,0:T(8,128)(2,1)}, u32[]{:S(2)}, u32[]{:S(2)}) collective-permute-start(bf16[2,2064,256]{2,1,0:T(8,128)(2,1)} %get-tuple-element.318), channel_id=1, source_target_pairs={{0,4},{4,0},{8,12},{12,8},{16,20},{20,16},{24,28},{28,24},{1,5},{5... | collective-permute-start | bytes 6340616 | tf_op jit(solution)/shard_map/ppermute | solution.py:431
  375.3 94.7 %all-gather.12.cloned.1.call-start = ((), (), s32[]{:S(2)}) async-start(), calls=%async_computation.9 | async-start | bytes 2621440 | tf_op jit(solution)/shard_map/all_gather | solution.py:663
  375.8 25.1 %collective-permute-start.19 = (bf16[2,2064,256]{2,1,0:T(8,128)(2,1)}, bf16[2,2064,256]{2,1,0:T(8,128)(2,1)}, u32[]{:S(2)}, u32[]{:S(2)}) collective-permute-start(bf16[2,2064,256]{2,1,0:T(8,128)(2,1)} %get-tuple-element.320), channel_id=1, source_target_pairs={{0,4},{4,0},{8,12},{12,8},{16,20},{20,16},{24,28},{28,24},{1,5},{5... | collective-permute-start | bytes 6340616 | tf_op jit(solution)/shard_map/ppermute | solution.py:431
  376.4 28.2 %collective-permute-start.20 = (bf16[2,2064,256]{2,1,0:T(8,128)(2,1)}, bf16[2,2064,256]{2,1,0:T(8,128)(2,1)}, u32[]{:S(2)}, u32[]{:S(2)}) collective-permute-start(bf16[2,2064,256]{2,1,0:T(8,128)(2,1)} %get-tuple-element.322), channel_id=1, source_target_pairs={{0,4},{4,0},{8,12},{12,8},{16,20},{20,16},{24,28},{28,24},{1,5},{5... | collective-permute-start | bytes 6340616 | tf_op jit(solution)/shard_map/ppermute | solution.py:431
  376.5 31.8 %collective-permute-start.21 = (bf16[2,2064,256]{2,1,0:T(8,128)(2,1)}, bf16[2,2064,256]{2,1,0:T(8,128)(2,1)S(1)}, u32[]{:S(2)}, u32[]{:S(2)}) collective-permute-start(bf16[2,2064,256]{2,1,0:T(8,128)(2,1)} %get-tuple-element.324), channel_id=1, source_target_pairs={{0,4},{4,0},{8,12},{12,8},{16,20},{20,16},{24,28},{28,24},{1,5},{5... | collective-permute-start | bytes 6340616 | tf_op jit(solution)/shard_map/ppermute | solution.py:431
  420.8 94.1 %all-gather.14.cloned.1.call-start = ((), (), s32[]{:S(2)}) async-start(), calls=%async_computation.11 | async-start | bytes 2621440 | tf_op jit(solution)/shard_map/all_gather | solution.py:663
  420.9 47.9 %collective-permute-start.22 = (bf16[2,2064,256]{2,1,0:T(8,128)(2,1)}, bf16[2,2064,256]{2,1,0:T(8,128)(2,1)}, u32[]{:S(2)}, u32[]{:S(2)}) collective-permute-start(bf16[2,2064,256]{2,1,0:T(8,128)(2,1)} %add_convert_fusion.3), channel_id=1, source_target_pairs={{0,8},{4,12},{8,0},{12,4},{16,24},{20,28},{24,16},{28,20},{1,9},{5... | collective-permute-start | bytes 6340616 | tf_op jit(solution)/shard_map/ppermute | solution.py:431
  422.4 47.6 %collective-permute-start.23 = (bf16[2,2064,256]{2,1,0:T(8,128)(2,1)}, bf16[2,2064,256]{2,1,0:T(8,128)(2,1)}, u32[]{:S(2)}, u32[]{:S(2)}) collective-permute-start(bf16[2,2064,256]{2,1,0:T(8,128)(2,1)} %add_convert_fusion.2), channel_id=1, source_target_pairs={{0,16},{4,20},{8,24},{12,28},{16,0},{20,4},{24,8},{28,12},{1,17},{... | collective-permute-start | bytes 6340616 | tf_op jit(solution)/shard_map/ppermute | solution.py:431
  470.0 134.6 %reduce-scatter.9.cloned.1.call-start = ((), (), s32[]{:S(2)}) async-start(), calls=%async_computation.10 | async-start | bytes 5242880 | tf_op jit(solution)/shard_map/reduce_scatter | solution.py:667
  473.2 24.0 %collective-permute-start.24 = (bf16[1,2064,256]{2,1,0:T(8,128)(2,1)}, bf16[1,2064,256]{2,1,0:T(8,128)(2,1)}, u32[]{:S(2)}, u32[]{:S(2)}) collective-permute-start(bf16[1,2064,256]{2,1,0:T(8,128)(2,1)} %add_convert_fusion.10), channel_id=1, source_target_pairs={{0,16},{4,20},{8,24},{12,28},{16,0},{20,4},{24,8},{28,12},{1,17},{... | collective-permute-start | bytes 3170312 | tf_op jit(solution)/shard_map/ppermute | solution.py:431
  477.6 24.2 %collective-permute-start.25 = (bf16[1,2064,256]{2,1,0:T(8,128)(2,1)}, bf16[1,2064,256]{2,1,0:T(8,128)(2,1)}, u32[]{:S(2)}, u32[]{:S(2)}) collective-permute-start(bf16[1,2064,256]{2,1,0:T(8,128)(2,1)} %add_convert_fusion.7), channel_id=1, source_target_pairs={{0,8},{4,12},{8,0},{12,4},{16,24},{20,28},{24,16},{28,20},{1,9},{5... | collective-permute-start | bytes 3170312 | tf_op jit(solution)/shard_map/ppermute | solution.py:431
  483.4 218.7 %reduce-scatter.11.cloned.1.call-start = ((), (), s32[]{:S(2)}) async-start(), calls=%async_computation.12 | async-start | bytes 5242880 | tf_op jit(solution)/shard_map/reduce_scatter | solution.py:667
  500.3 30.3 %collective-permute-start.26 = (bf16[1,2064,256]{2,1,0:T(8,128)(2,1)}, bf16[1,2064,256]{2,1,0:T(8,128)(2,1)}, u32[]{:S(2)}, u32[]{:S(2)}) collective-permute-start(bf16[1,2064,256]{2,1,0:T(8,128)(2,1)} %add_convert_fusion.9.refs_0_), channel_id=1, source_target_pairs={{0,16},{4,20},{8,24},{12,28},{16,0},{20,4},{24,8},{28,12},{1,17},{... | collective-permute-start | bytes 3170312 | tf_op jit(solution)/shard_map/ppermute | solution.py:431
  505.0 26.6 %collective-permute-start.27 = (bf16[1,2064,256]{2,1,0:T(8,128)(2,1)}, bf16[1,2064,256]{2,1,0:T(8,128)(2,1)}, u32[]{:S(2)}, u32[]{:S(2)}) collective-permute-start(bf16[1,2064,256]{2,1,0:T(8,128)(2,1)} %add_convert_fusion.6.refs_8_), channel_id=1, source_target_pairs={{0,8},{4,12},{8,0},{12,4},{16,24},{20,28},{24,16},{28,20},{1,9},{5... | collective-permute-start | bytes 3170312 | tf_op jit(solution)/shard_map/ppermute | solution.py:431
  514.9 35.4 %collective-permute-start.28 = (bf16[1,2064,256]{2,1,0:T(8,128)(2,1)}, bf16[1,2064,256]{2,1,0:T(8,128)(2,1)S(1)}, u32[]{:S(2)}, u32[]{:S(2)}) collective-permute-start(bf16[1,2064,256]{2,1,0:T(8,128)(2,1)} %add_convert_fusion.9.refs_0_), channel_id=1, source_target_pairs={{0,8},{4,12},{8,0},{12,4},{16,24},{20,28},{24,16},{28,20},{1,9},{5... | collective-permute-start | bytes 3170312 | tf_op jit(solution)/shard_map/ppermute | solution.py:431
  516.4 34.0 %collective-permute-start.29 = (bf16[1,2064,256]{2,1,0:T(8,128)(2,1)}, bf16[1,2064,256]{2,1,0:T(8,128)(2,1)S(1)}, u32[]{:S(2)}, u32[]{:S(2)}) collective-permute-start(bf16[1,2064,256]{2,1,0:T(8,128)(2,1)} %add_convert_fusion.6.refs_8_), channel_id=1, source_target_pairs={{0,16},{4,20},{8,24},{12,28},{16,0},{20,4},{24,8},{28,12},{1,17},{... | collective-permute-start | bytes 3170312 | tf_op jit(solution)/shard_map/ppermute | solution.py:431
  553.3 19.6 %collective-permute-start.34 = (f32[4,8,256]{2,1,0:T(8,128)S(1)}, f32[4,8,256]{2,1,0:T(8,128)S(1)}, u32[]{:S(2)}, u32[]{:S(2)}) collective-permute-start(f32[4,8,256]{2,1,0:T(8,128)S(1)} %add.367), channel_id=1, source_target_pairs={{0,8},{4,12},{8,0},{12,4},{16,24},{20,28},{24,16},{28,20},{1,9},{5... | collective-permute-start | bytes 98312 | tf_op jit(solution)/shard_map/ppermute | solution.py:309
  554.5 19.0 %collective-permute-start.31 = (bf16[4,160,128]{2,1,0:T(8,128)(2,1)S(1)}, bf16[4,160,128]{2,1,0:T(8,128)(2,1)S(1)}, u32[]{:S(2)}, u32[]{:S(2)}) collective-permute-start(bf16[4,160,128]{2,1,0:T(8,128)(2,1)S(1)} %fusion.38), channel_id=1, source_target_pairs={{0,8},{4,12},{8,0},{12,4},{16,24},{20,28},{24,16},{28,20},{1,9},{5... | collective-permute-start | bytes 491528 | tf_op jit(solution)/shard_map/ppermute | solution.py:309
  579.4 24.4 %collective-permute-start.36 = (bf16[1,2064,256]{2,1,0:T(8,128)(2,1)}, bf16[1,2064,256]{2,1,0:T(8,128)(2,1)}, u32[]{:S(2)}, u32[]{:S(2)}) collective-permute-start(bf16[1,2064,256]{2,1,0:T(8,128)(2,1)} %collective-permute-done.26.refs_1_), channel_id=1, source_target_pairs={{0,8},{4,12},{8,0},{12,4},{16,24},{20,28},{24,16},{28,20},{1,9},{5... | collective-permute-start | bytes 3170312 | tf_op jit(solution)/shard_map/ppermute | solution.py:431
  580.6 24.0 %collective-permute-start.37 = (bf16[1,2064,256]{2,1,0:T(8,128)(2,1)}, bf16[1,2064,256]{2,1,0:T(8,128)(2,1)}, u32[]{:S(2)}, u32[]{:S(2)}) collective-permute-start(bf16[1,2064,256]{2,1,0:T(8,128)(2,1)} %collective-permute-done.27.refs_9_), channel_id=1, source_target_pairs={{0,16},{4,20},{8,24},{12,28},{16,0},{20,4},{24,8},{28,12},{1,17},{... | collective-permute-start | bytes 3170312 | tf_op jit(solution)/shard_map/ppermute | solution.py:431
  619.0 8.9 %collective-permute-start.42 = (bf16[1,2064,256]{2,1,0:T(8,128)(2,1)}, bf16[1,2064,256]{2,1,0:T(8,128)(2,1)S(1)}, u32[]{:S(2)}, u32[]{:S(2)}) collective-permute-start(bf16[1,2064,256]{2,1,0:T(8,128)(2,1)} %add_convert_fusion.9.refs_0_), channel_id=1, source_target_pairs={{0,4},{4,0},{8,12},{12,8},{16,20},{20,16},{24,28},{28,24},{1,5},{5... | collective-permute-start | bytes 3170312 | tf_op jit(solution)/shard_map/ppermute | solution.py:431
  619.0 9.2 %collective-permute-start.43 = (bf16[1,2064,256]{2,1,0:T(8,128)(2,1)}, bf16[1,2064,256]{2,1,0:T(8,128)(2,1)S(1)}, u32[]{:S(2)}, u32[]{:S(2)}) collective-permute-start(bf16[1,2064,256]{2,1,0:T(8,128)(2,1)} %collective-permute-done.26.refs_1_), channel_id=1, source_target_pairs={{0,4},{4,0},{8,12},{12,8},{16,20},{20,16},{24,28},{28,24},{1,5},{5... | collective-permute-start | bytes 3170312 | tf_op jit(solution)/shard_map/ppermute | solution.py:431
  619.5 9.0 %collective-permute-start.44 = (bf16[1,2064,256]{2,1,0:T(8,128)(2,1)S(1)}, bf16[1,2064,256]{2,1,0:T(8,128)(2,1)S(1)}, u32[]{:S(2)}, u32[]{:S(2)}) collective-permute-start(bf16[1,2064,256]{2,1,0:T(8,128)(2,1)S(1)} %copy-done.46), channel_id=1, source_target_pairs={{0,4},{4,0},{8,12},{12,8},{16,20},{20,16},{24,28},{28,24},{1,5},{5... | collective-permute-start | bytes 3170312 | tf_op jit(solution)/shard_map/ppermute | solution.py:431
  621.5 6.2 collective-permute-start.41
  626.9 13.3 %collective-permute-start.45 = (bf16[1,2064,256]{2,1,0:T(8,128)(2,1)}, bf16[1,2064,256]{2,1,0:T(8,128)(2,1)}, u32[]{:S(2)}, u32[]{:S(2)}) collective-permute-start(bf16[1,2064,256]{2,1,0:T(8,128)(2,1)} %collective-permute-done.36.refs_3_), channel_id=1, source_target_pairs={{0,4},{4,0},{8,12},{12,8},{16,20},{20,16},{24,28},{28,24},{1,5},{5... | collective-permute-start | bytes 3170312 | tf_op jit(solution)/shard_map/ppermute | solution.py:431
  627.7 12.5 %collective-permute-start.46 = (bf16[1,2064,256]{2,1,0:T(8,128)(2,1)}, bf16[1,2064,256]{2,1,0:T(8,128)(2,1)}, u32[]{:S(2)}, u32[]{:S(2)}) collective-permute-start(bf16[1,2064,256]{2,1,0:T(8,128)(2,1)} %add_convert_fusion.6.refs_8_), channel_id=1, source_target_pairs={{0,4},{4,0},{8,12},{12,8},{16,20},{20,16},{24,28},{28,24},{1,5},{5... | collective-permute-start | bytes 3170312 | tf_op jit(solution)/shard_map/ppermute | solution.py:431
  627.9 12.4 %collective-permute-start.47 = (bf16[1,2064,256]{2,1,0:T(8,128)(2,1)}, bf16[1,2064,256]{2,1,0:T(8,128)(2,1)}, u32[]{:S(2)}, u32[]{:S(2)}) collective-permute-start(bf16[1,2064,256]{2,1,0:T(8,128)(2,1)} %collective-permute-done.27.refs_9_), channel_id=1, source_target_pairs={{0,4},{4,0},{8,12},{12,8},{16,20},{20,16},{24,28},{28,24},{1,5},{5... | collective-permute-start | bytes 3170312 | tf_op jit(solution)/shard_map/ppermute | solution.py:431
  628.3 12.0 %collective-permute-start.48 = (bf16[1,2064,256]{2,1,0:T(8,128)(2,1)S(1)}, bf16[1,2064,256]{2,1,0:T(8,128)(2,1)}, u32[]{:S(2)}, u32[]{:S(2)}) collective-permute-start(bf16[1,2064,256]{2,1,0:T(8,128)(2,1)S(1)} %copy-done.48), channel_id=1, source_target_pairs={{0,4},{4,0},{8,12},{12,8},{16,20},{20,16},{24,28},{28,24},{1,5},{5... | collective-permute-start | bytes 3170312 | tf_op jit(solution)/shard_map/ppermute | solution.py:431
  630.3 10.0 %collective-permute-start.49 = (bf16[1,2064,256]{2,1,0:T(8,128)(2,1)}, bf16[1,2064,256]{2,1,0:T(8,128)(2,1)S(1)}, u32[]{:S(2)}, u32[]{:S(2)}) collective-permute-start(bf16[1,2064,256]{2,1,0:T(8,128)(2,1)} %collective-permute-done.37.refs_11_), channel_id=1, source_target_pairs={{0,4},{4,0},{8,12},{12,8},{16,20},{20,16},{24,28},{28,24},{1,5},{5... | collective-permute-start | bytes 3170312 | tf_op jit(solution)/shard_map/ppermute | solution.py:431
  640.3 15.8 %collective-permute-start.50 = (bf16[2,576,256]{2,1,0:T(8,128)(2,1)}, bf16[2,576,256]{2,1,0:T(8,128)(2,1)S(1)}, u32[]{:S(2)}, u32[]{:S(2)}) collective-permute-start(bf16[2,576,256]{2,1,0:T(8,128)(2,1)} %get-tuple-element.391), channel_id=1, source_target_pairs={{0,8},{4,12},{8,0},{12,4},{16,24},{20,28},{24,16},{28,20},{1,9},{5... | collective-permute-start | bytes 1769480 | tf_op jit(solution)/shard_map/ppermute | solution.py:431
  641.6 15.4 %collective-permute-start.51 = (bf16[2,576,256]{2,1,0:T(8,128)(2,1)}, bf16[2,576,256]{2,1,0:T(8,128)(2,1)S(1)}, u32[]{:S(2)}, u32[]{:S(2)}) collective-permute-start(bf16[2,576,256]{2,1,0:T(8,128)(2,1)} %get-tuple-element.392), channel_id=1, source_target_pairs={{0,16},{4,20},{8,24},{12,28},{16,0},{20,4},{24,8},{28,12},{1,17},{... | collective-permute-start | bytes 1769480 | tf_op jit(solution)/shard_map/ppermute | solution.py:431
  643.0 11.7 %collective-permute-start.52 = (f32[8,128]{1,0:T(8,128)S(1)}, f32[8,128]{1,0:T(8,128)S(1)}, u32[]{:S(2)}, u32[]{:S(2)}) collective-permute-start(f32[8,128]{1,0:T(8,128)S(1)} %add_bitcast_fusion), channel_id=1, source_target_pairs={{0,1},{1,2},{2,3},{4,5},{5,6},{6,7},{8,9},{9,10},{10,11},{12,13},{... | collective-permute-start | bytes 12296 | tf_op jit(solution)/shard_map/ppermute | solution.py:586
  644.3 10.5 %collective-permute-start.53 = (f32[8,128]{1,0:T(8,128)S(1)}, f32[8,128]{1,0:T(8,128)S(1)}, u32[]{:S(2)}, u32[]{:S(2)}) collective-permute-start(f32[8,128]{1,0:T(8,128)S(1)} %add_bitcast_fusion), channel_id=1, source_target_pairs={{1,0},{2,1},{3,2},{5,4},{6,5},{7,6},{9,8},{10,9},{11,10},{13,12},{... | collective-permute-start | bytes 12296 | tf_op jit(solution)/shard_map/ppermute | solution.py:587
  657.1 14.2 %collective-permute-start.54 = (bf16[1,576,256]{2,1,0:T(8,128)(2,1)S(1)}, bf16[1,576,256]{2,1,0:T(8,128)(2,1)S(1)}, u32[]{:S(2)}, u32[]{:S(2)}) collective-permute-start(bf16[1,576,256]{2,1,0:T(8,128)(2,1)S(1)} %get-tuple-element.502), channel_id=1, source_target_pairs={{0,16},{4,20},{8,24},{12,28},{16,0},{20,4},{24,8},{28,12},{1,17},{... | collective-permute-start | bytes 884744 | tf_op jit(solution)/shard_map/ppermute | solution.py:431
  658.8 12.5 %collective-permute-start.55 = (bf16[1,576,256]{2,1,0:T(8,128)(2,1)S(1)}, bf16[1,576,256]{2,1,0:T(8,128)(2,1)S(1)}, u32[]{:S(2)}, u32[]{:S(2)}) collective-permute-start(bf16[1,576,256]{2,1,0:T(8,128)(2,1)S(1)} %get-tuple-element.500), channel_id=1, source_target_pairs={{0,8},{4,12},{8,0},{12,4},{16,24},{20,28},{24,16},{28,20},{1,9},{5... | collective-permute-start | bytes 884744 | tf_op jit(solution)/shard_map/ppermute | solution.py:431
  659.9 11.4 %collective-permute-start.56 = (f32[8,128]{1,0:T(8,128)S(1)}, f32[8,128]{1,0:T(8,128)S(1)}, u32[]{:S(2)}, u32[]{:S(2)}) collective-permute-start(f32[8,128]{1,0:T(8,128)S(1)} %collective-permute-done.52), channel_id=1, source_target_pairs={{1,2},{2,3},{5,6},{6,7},{9,10},{10,11},{13,14},{14,15},{17,18},{18... | collective-permute-start | bytes 12296 | tf_op jit(solution)/shard_map/ppermute | solution.py:586
  660.6 10.7 %collective-permute-start.57 = (f32[8,128]{1,0:T(8,128)S(1)}, f32[8,128]{1,0:T(8,128)S(1)}, u32[]{:S(2)}, u32[]{:S(2)}) collective-permute-start(f32[8,128]{1,0:T(8,128)S(1)} %collective-permute-done.53), channel_id=1, source_target_pairs={{1,0},{2,1},{5,4},{6,5},{9,8},{10,9},{13,12},{14,13},{17,16},{18,1... | collective-permute-start | bytes 12296 | tf_op jit(solution)/shard_map/ppermute | solution.py:587
  671.4 11.3 %collective-permute-start.58 = (bf16[1,576,256]{2,1,0:T(8,128)(2,1)S(1)}, bf16[1,576,256]{2,1,0:T(8,128)(2,1)S(1)}, u32[]{:S(2)}, u32[]{:S(2)}) collective-permute-start(bf16[1,576,256]{2,1,0:T(8,128)(2,1)S(1)} %add_convert_fusion.17.refs_0_), channel_id=1, source_target_pairs={{0,16},{4,20},{8,24},{12,28},{16,0},{20,4},{24,8},{28,12},{1,17},{... | collective-permute-start | bytes 884744 | tf_op jit(solution)/shard_map/ppermute | solution.py:431
  671.8 10.8 %collective-permute-start.59 = (bf16[1,576,256]{2,1,0:T(8,128)(2,1)S(1)}, bf16[1,576,256]{2,1,0:T(8,128)(2,1)S(1)}, u32[]{:S(2)}, u32[]{:S(2)}) collective-permute-start(bf16[1,576,256]{2,1,0:T(8,128)(2,1)S(1)} %add_convert_fusion.16.refs_8_), channel_id=1, source_target_pairs={{0,8},{4,12},{8,0},{12,4},{16,24},{20,28},{24,16},{28,20},{1,9},{5... | collective-permute-start | bytes 884744 | tf_op jit(solution)/shard_map/ppermute | solution.py:431
  673.7 8.9 %collective-permute-start.61 = (f32[8,128]{1,0:T(8,128)S(1)}, f32[8,128]{1,0:T(8,128)S(1)}, u32[]{:S(2)}, u32[]{:S(2)}) collective-permute-start(f32[8,128]{1,0:T(8,128)S(1)} %collective-permute-done.57), channel_id=1, source_target_pairs={{1,0},{5,4},{9,8},{13,12},{17,16},{21,20},{25,24},{29,28}} | collective-permute-start | bytes 12296 | tf_op jit(solution)/shard_map/ppermute | solution.py:587
  682.7 13.3 %collective-permute-start.62 = (bf16[1,576,256]{2,1,0:T(8,128)(2,1)S(1)}, bf16[1,576,256]{2,1,0:T(8,128)(2,1)S(1)}, u32[]{:S(2)}, u32[]{:S(2)}) collective-permute-start(bf16[1,576,256]{2,1,0:T(8,128)(2,1)S(1)} %add_convert_fusion.17.refs_0_), channel_id=1, source_target_pairs={{0,8},{4,12},{8,0},{12,4},{16,24},{20,28},{24,16},{28,20},{1,9},{5... | collective-permute-start | bytes 884744 | tf_op jit(solution)/shard_map/ppermute | solution.py:431
  683.4 12.6 %collective-permute-start.63 = (bf16[1,576,256]{2,1,0:T(8,128)(2,1)S(1)}, bf16[1,576,256]{2,1,0:T(8,128)(2,1)S(1)}, u32[]{:S(2)}, u32[]{:S(2)}) collective-permute-start(bf16[1,576,256]{2,1,0:T(8,128)(2,1)S(1)} %collective-permute-done.58.refs_1_), channel_id=1, source_target_pairs={{0,8},{4,12},{8,0},{12,4},{16,24},{20,28},{24,16},{28,20},{1,9},{5... | collective-permute-start | bytes 884744 | tf_op jit(solution)/shard_map/ppermute | solution.py:431
  684.8 11.2 %collective-permute-start.64 = (bf16[1,576,256]{2,1,0:T(8,128)(2,1)S(1)}, bf16[1,576,256]{2,1,0:T(8,128)(2,1)S(1)}, u32[]{:S(2)}, u32[]{:S(2)}) collective-permute-start(bf16[1,576,256]{2,1,0:T(8,128)(2,1)S(1)} %add_convert_fusion.16.refs_8_), channel_id=1, source_target_pairs={{0,16},{4,20},{8,24},{12,28},{16,0},{20,4},{24,8},{28,12},{1,17},{... | collective-permute-start | bytes 884744 | tf_op jit(solution)/shard_map/ppermute | solution.py:431
  685.6 11.3 %collective-permute-start.65 = (bf16[1,576,256]{2,1,0:T(8,128)(2,1)S(1)}, bf16[1,576,256]{2,1,0:T(8,128)(2,1)S(1)}, u32[]{:S(2)}, u32[]{:S(2)}) collective-permute-start(bf16[1,576,256]{2,1,0:T(8,128)(2,1)S(1)} %collective-permute-done.59.refs_9_), channel_id=1, source_target_pairs={{0,16},{4,20},{8,24},{12,28},{16,0},{20,4},{24,8},{28,12},{1,17},{... | collective-permute-start | bytes 884744 | tf_op jit(solution)/shard_map/ppermute | solution.py:431
  711.1 9.4 %collective-permute-start.76 = (f32[2,512]{1,0:T(2,128)S(1)}, f32[2,512]{1,0:T(2,128)S(1)}, u32[]{:S(2)}, u32[]{:S(2)}) collective-permute-start(f32[2,512]{1,0:T(2,128)S(1)} %fusion.99), channel_id=1, source_target_pairs={{0,16},{4,20},{8,24},{12,28},{16,0},{20,4},{24,8},{28,12},{1,17},{... | collective-permute-start | bytes 12296 | tf_op jit(solution)/shard_map/ppermute | solution.py:431
  (155 other events, 1435.3 us)
Sparse Core Ops, SparseCore 0:
  9.6 83.5 all-gather.5
  239.0 44.1 all-gather.9
  285.3 44.6 all-gather.7
  332.7 42.5 reduce-scatter.4
  377.6 43.1 reduce-scatter.6
  422.8 45.2 all-gather.11
  470.2 44.6 all-gather.13
  517.8 75.4 reduce-scatter.8
  604.8 76.3 reduce-scatter.10

commit v4 on v3

--- a/solution.py
+++ b/solution.py
@@ -546,12 +546,15 @@
     )(blocks, jnp.asarray(table), *pieces[0], *pieces[1])
 
 
+def line_sum(value):
+    count = lax.axis_size("tensor")
+    turned = [lax.ppermute(value, "tensor", [(i, (i + n) % count) for i in range(count)]) for n in range(1, count)]
+    return [value] + turned
+
+
 def batch_sum(value):
-    bit = 1
-    while bit < lax.axis_size("batch"):
-        value = value + flip(value, bit)
-        bit *= 2
-    return value
+    value = value + flip(value, 1)
+    return value + sum(flip(value, mask) for mask in range(2, lax.axis_size("batch"), 2))
 
 
 def after(values, *others):
@@ -831,7 +834,10 @@
     ffn.send()
     dmix = mixer.pull_carry(k, v, tail, *following, dq, dk, dv, table)
     part = project_back(dmix, w_mix).astype(LOW)
-    down, part, dmix, dh_b, grad_hidden_b = lock(down, part, dmix, dh_b, grad_hidden_b, ffn)
+    dot = row_sum(dmix[:, :thin].astype(F32) * pair.astype(F32))
+    dot = dot + row_sum(dmix[:, thin:].astype(F32) * v.astype(F32))
+    dots = line_sum(dot.reshape(count // 128, 128))
+    down, part, dmix, dh_b, grad_hidden_b, dots = lock(down, part, dmix, dh_b, grad_hidden_b, dots, ffn)
 
     back = narrow(part)
     y_a, y_b = cut(y)
@@ -841,28 +847,22 @@
     mix = Exchange(grad_blocks("grad_mix_far", groups, True, None, 5))
     mix.send()
     mix.begin("grad_mix_near", groups, 5)
-    dot = row_sum(dmix[:, :thin].astype(F32) * pair.astype(F32))
-    dot = dot + row_sum(dmix[:, thin:].astype(F32) * v.astype(F32))
-    dots = Gather(dot.reshape(count // 128, 128))
-    lock(mix, dots, ffn)
+    lock(mix, ffn)
     mix.send()
-    dots.hop()
     ffn.take()
     final = ffn.run()
 
     def ffn_weight(n):
         return place_blocks(f"place_ffn_{n}", final, [(units, [(0, units, False)])], width, 7, n)[0]
 
-    grad_w_gate = lock(mix, dots, ffn_weight(0))[0]
+    grad_w_gate = lock(mix, ffn_weight(0))[0]
     mix.take()
     mix.send()
-    dots.hop()
-    grad_w_up = lock(mix, dots, ffn_weight(1))[0]
+    grad_w_up = lock(mix, ffn_weight(1))[0]
     mix.take()
     mix.send()
-    dots.run()
     output = (join(hidden_a, hidden_b) + down.astype(F32)).astype(LOW)
-    output = lock(mix, dots, output)[0]
+    output = lock(mix, output)[0]
     mix.take()
     mix.send()
     grad_w_down = lock(mix, ffn_weight(2))[0]
@@ -875,7 +875,7 @@
     grad_tokens = (
         join(grad_hidden_a, grad_hidden_b)
         + scale_one * norm1_gain[None, :] * back
-        - inputs * (scale_one * scale_one * dots.total().reshape(count, 1) / width)
+        - inputs * (scale_one * scale_one * sum(dots).reshape(count, 1) / width)
     )
     values = heads * HV
     grad_w_query, grad_w_key, grad_w_value, grad_w_out = place_blocks(

time: 738 us -> 729 us (0.988)
    ppermute x6 -> x3, waiting for transfers between devices: 21.5 us -> 15.3 us  [hop(): lax.ppermute(a, 'tensor', to_left)]
    unnamed x268 -> x266, local copies, waits for them, and re-layouts: 18.4 us -> 16.7 us
    ppermute x47 -> x48, starting transfers between devices: 31.9 us -> 32.8 us  [flip(): lax.ppermute(value, 'batch', [(i, i ^ bit) for i in range(lax.axis_size('...]
    ppermute x47 -> x48, waiting for transfers between devices: 84.1 us -> 84.4 us  [flip(): lax.ppermute(value, 'batch', [(i, i ^ bit) for i in range(lax.axis_size('...]
  transfers between devices with their start and end apart: 86 -> 84, of which waited for: 40 -> 40; matrix products, arithmetic and copies ran while one was open for 22% -> 22% of each run, Pallas kernels for 18% -> 19%
where the time goes in v4:
time: 729 us; the launch traced here: 719 us
  waiting for transfers between devices  282 us (39%)
  Pallas kernels  137 us (19%)
  matrix products  84.5 us (12%)
  other arithmetic  82.4 us (11%)
  starting transfers between devices  71.8 us (10%)
  local copies, waits for them, and re-layouts  29.8 us (4%)
  between operations  16.6 us (2%)
  blocking collectives  14.9 us (2%)
    all_gather x5, waiting for transfers between devices, widen(): return lax.all_gather(part, 'tensor', axis=1, tiled=True)  110 us
    ppermute x48, waiting for transfers between devices, flip(): lax.ppermute(value, 'batch', [(i, i ^ bit) for i in range(lax.axis_size('...  84.4 us
    pallas_call x4, Pallas kernels, grad_blocks(): pl.pallas_call(functools.partial(grad_body, groups=tuple(kinds), summed=b...  53.2 us
    dot_general x9, matrix products, project_back(): return jnp.einsum('ti,ji->tj', left, right, preferred_element_type=F32)  45.2 us
    ppermute x3, waiting for transfers between devices, hop(): lax.ppermute(sends[0], 'tensor', [(k, k + 1) for k in range(0, count - se...  44 us
    pallas_call x6, Pallas kernels, call(): pl.pallas_call(body, grid=(self.heads,), in_specs=in_specs, out_specs=out...  42.7 us
    pallas_call x4, Pallas kernels, place_blocks(): pl.pallas_call(functools.partial(place_body, outs=tuple(layout), count=co...  35.6 us
    ppermute x48, starting transfers between devices, flip(): lax.ppermute(value, 'batch', [(i, i ^ bit) for i in range(lax.axis_size('...  32.8 us
  transfers between devices with their start and end apart: 84, of which 40 were waited for; matrix products, arithmetic and copies ran while one was open for 22% of the time, Pallas kernels for 19%

profile of v4, /device:TPU:0, one launch (start us, length us, event | category | flops | bytes accessed | tf_op | source)
XLA Modules:
  0.0 719.1 jit_solution(2959780856435062380)
XLA Ops:
  15.0 14.9 %all_gather.19 = f32[2,2048]{1,0:T(2,128)S(1)} all-gather(f32[2,512]{1,0:T(2,128)S(1)} %pad_maximum_fusion.3), channel_id=1, replica_groups=mesh['batch'=8,'tensor'=4] {'tensor'}, dimensions={1}, use_global_device_ids=true | all-gather | bytes 20480 | tf_op jit(solution)/shard_map/all_gather | solution.py:718
  32.2 4.1 pad_maximum_fusion.2
  36.3 56.9 %all-gather.6.cloned.1.call-done = bf16[1024,2048]{1,0:T(8,128)(2,1)} async-done(((bf16[1024,512]{1,0:T(8,128)(2,1)}), bf16[1024,2048]{1,0:T(8,128)(2,1)}) %all-gather.6.cloned.1.call-update) | async-done | bytes 4194320 | tf_op jit(solution)/shard_map/all_gather | solution.py:666
  93.2 3.2 fusion
  100.6 2.7 convolution_convert_fusion.4
  104.1 3.2 mix_state.1
  117.0 5.8 mix_inner.1
  128.5 3.1 collective-permute-done.2
  131.7 5.8 mix_merge.1
  140.7 5.2 collective-permute-start.8
  152.9 13.5 %collective-permute-done.8 = bf16[1024,512]{1,0:T(8,128)(2,1)} collective-permute-done((bf16[1024,512]{1,0:T(8,128)(2,1)}, bf16[1024,512]{1,0:T(8,128)(2,1)}, u32[]{:S(2)}, u32[]{:S(2)}) %collective-permute-start.8) | collective-permute-done | bytes 1048608 | tf_op jit(solution)/shard_map/ppermute | solution.py:632
  166.4 9.5 %collective-permute-done.11 = bf16[1024,512]{1,0:T(8,128)(2,1)} collective-permute-done((bf16[1024,512]{1,0:T(8,128)(2,1)}, bf16[1024,512]{1,0:T(8,128)(2,1)}, u32[]{:S(2)}, u32[]{:S(2)}) %collective-permute-start.11) | collective-permute-done | bytes 1048608 | tf_op jit(solution)/shard_map/ppermute | solution.py:590
  183.3 16.8 %collective-permute-done.12 = bf16[1024,512]{1,0:T(8,128)(2,1)S(1)} collective-permute-done((bf16[1024,512]{1,0:T(8,128)(2,1)S(1)}, bf16[1024,512]{1,0:T(8,128)(2,1)S(1)}, u32[]{:S(2)}, u32[]{:S(2)}) %collective-permute-start.12) | collective-permute-done | bytes 1048608 | tf_op jit(solution)/shard_map/ppermute | solution.py:632
  200.1 5.9 collective-permute-done.15
  207.3 2.7 collective-permute-start.16
  214.1 13.6 %collective-permute-done.16 = bf16[1024,512]{1,0:T(8,128)(2,1)} collective-permute-done((bf16[1024,512]{1,0:T(8,128)(2,1)}, bf16[1024,512]{1,0:T(8,128)(2,1)}, u32[]{:S(2)}, u32[]{:S(2)}) %collective-permute-start.16) | collective-permute-done | bytes 1048608 | tf_op jit(solution)/shard_map/ppermute | solution.py:632
  227.7 6.5 collective-permute-done.17
  244.7 5.6 straighten.1
  250.3 8.1 %convolution_bitcast_fusion.5 = f32[1376,512]{1,0:T(8,128)} fusion(bf16[1376,2048]{1,0:T(8,128)(2,1)} %param.39, bf16[1024,2048]{1,0:T(8,128)(2,1)} %straighten.1), kind=kOutput, calls=%fused_computation.41 | convolution fusion | flops 2885681152 | bytes 10551296 | tf_op jit(solution)/shard_map/ti,ji->tj/dot_general | solution.py:678
  258.4 4.7 convolution_bitcast_fusion.4
  263.4 19.8 %all-gather.10.cloned.1.call-done = bf16[512,2048]{1,0:T(8,128)(2,1)} async-done(((bf16[512,512]{1,0:T(8,128)(2,1)}), bf16[512,2048]{1,0:T(8,128)(2,1)}) %all-gather.10.cloned.1.call-update) | async-done | bytes 2097168 | tf_op jit(solution)/shard_map/all_gather | solution.py:666
  286.0 6.2 convolution_bitcast_fusion.2
  292.3 5.5 multiply_convert_fusion.3
  297.9 3.5 fusion.60
  301.4 4.6 add_convert_fusion.5
  306.0 24.0 %all-gather.8.cloned.1.call-done = bf16[512,2048]{1,0:T(8,128)(2,1)} async-done(((bf16[512,512]{1,0:T(8,128)(2,1)}), bf16[512,2048]{1,0:T(8,128)(2,1)}) %all-gather.8.cloned.1.call-update) | async-done | bytes 2097168 | tf_op jit(solution)/shard_map/all_gather | solution.py:666
  333.1 6.4 convolution_bitcast_fusion
  342.6 5.5 multiply_convert_fusion
  348.1 3.5 fusion.61
  351.7 4.7 add_convert_fusion.4
  356.4 18.0 %grad_ffn_far.1 = (bf16[2,2064,256]{2,1,0:T(8,128)(2,1)}, bf16[2,2064,256]{2,1,0:T(8,128)(2,1)}, bf16[2,2064,256]{2,1,0:T(8,128)(2,1)}, bf16[2,2064,256]{2,1,0:T(8,128)(2,1)}) custom-call(s32[4]{0:T(128)} %get-tuple-element.493.blocks, s32[5,4]{1,0:T(8,128)} %constant.83.clone.swap, bf16[512,2048]{1,0:T(8,128)(2,1)} %copy-done.74, ...), custom_call_target="tpu_custom_call" | custom-call | flops 16000000000 | bytes 1048576 | tf_op jit(solution)/shard_map/grad_ffn_far/pallas_call | solution.py:417
  376.9 18.1 %grad_ffn_near.1 = (bf16[2,2064,256]{2,1,0:T(8,128)(2,1)}, bf16[2,2064,256]{2,1,0:T(8,128)(2,1)}, bf16[2,2064,256]{2,1,0:T(8,128)(2,1)}, bf16[2,2064,256]{2,1,0:T(8,128)(2,1)}) custom-call(s32[4]{0:T(128)} %get-tuple-element.494.blocks, s32[5,4]{1,0:T(8,128)} %constant.83.clone.swap, bf16[512,2048]{1,0:T(8,128)(2,1)} %copy-done.74, ...), custom_call_target="tpu_custom_call" | custom-call | flops 16000000000 | bytes 1048576 | tf_op jit(solution)/shard_map/grad_ffn_near/pallas_call | solution.py:417
  397.2 3.7 add_convert_fusion.3
  400.9 3.7 add_convert_fusion.2
  404.6 3.6 add_convert_fusion.1
  410.1 10.7 %reduce-scatter.7.cloned.1.call-done = bf16[512,512]{1,0:T(8,128)(2,1)} async-done(((bf16[512,2048]{1,0:T(8,128)(2,1)}), bf16[512,512]{1,0:T(8,128)(2,1)}) %reduce-scatter.7.cloned.1.call-update) | async-done | bytes 524304 | tf_op jit(solution)/shard_map/reduce_scatter | solution.py:670
  423.9 7.8 %convolution_convert_fusion.2 = bf16[512,2048]{1,0:T(8,128)(2,1)} fusion(bf16[1376,512]{1,0:T(8,128)(2,1)} %get-tuple-element.291.refs_9_, bf16[1376,2048]{1,0:T(8,128)(2,1)} %param.39), kind=kOutput, calls=%fused_computation.46 | convolution fusion | flops 2886729728 | bytes 9142272 | tf_op jit(solution)/shard_map/it,ij->tj/dot_general | solution.py:682
  431.7 7.4 %convolution_convert_fusion.1 = bf16[512,2048]{1,0:T(8,128)(2,1)} fusion(bf16[1376,512]{1,0:T(8,128)(2,1)S(1)} %copy-done.119, bf16[1376,2048]{1,0:T(8,128)(2,1)} %param.39), kind=kOutput, calls=%fused_computation.45 | convolution fusion | flops 2886729728 | bytes 9142272 | tf_op jit(solution)/shard_map/it,ij->tj/dot_general | solution.py:682
  440.6 28.2 %collective-permute-done.22 = bf16[2,2064,256]{2,1,0:T(8,128)(2,1)} collective-permute-done((bf16[2,2064,256]{2,1,0:T(8,128)(2,1)}, bf16[2,2064,256]{2,1,0:T(8,128)(2,1)}, u32[]{:S(2)}, u32[]{:S(2)}) %collective-permute-start.22) | collective-permute-done | bytes 2113568 | tf_op jit(solution)/shard_map/ppermute | solution.py:431
  470.3 2.9 add_convert_fusion.10
  474.7 2.9 add_convert_fusion.7
  478.0 2.7 fusion.8
  483.4 2.9 fusion.3.refs_2_
  490.1 7.2 collective-permute-done.24
  497.2 3.0 add_convert_fusion.9.refs_0_
  501.8 3.1 add_convert_fusion.6.refs_8_
  505.8 9.2 %all-gather.14.cloned.1.call-done = bf16[512,2048]{1,0:T(8,128)(2,1)} async-done(((bf16[512,512]{1,0:T(8,128)(2,1)}), bf16[512,2048]{1,0:T(8,128)(2,1)}) %all-gather.14.cloned.1.call-update) | async-done | bytes 2097168 | tf_op jit(solution)/shard_map/all_gather | solution.py:666
  517.9 3.7 fusion.12
  524.6 6.0 mix_pull_state.1
  531.5 18.8 %collective-permute-done.28.refs_2_ = bf16[1,2064,256]{2,1,0:T(8,128)(2,1)S(1)} collective-permute-done((bf16[1,2064,256]{2,1,0:T(8,128)(2,1)}, bf16[1,2064,256]{2,1,0:T(8,128)(2,1)S(1)}, u32[]{:S(2)}, u32[]{:S(2)}) %collective-permute-start.28) | collective-permute-done | bytes 1056800 | tf_op jit(solution)/shard_map/ppermute | solution.py:431
  555.4 16.0 %mix_pull_inner.1 = (bf16[1024,64]{1,0:T(8,128)(2,1)S(1)}, f32[1024,64]{1,0:T(8,128)S(1)}, f32[1024,512]{1,0:T(8,128)S(1)}) custom-call(bf16[1024,64]{1,0:T(8,128)(2,1)S(1)} %copy-done.18, bf16[1024,64]{1,0:T(8,128)(2,1)S(1)} %copy-done.16, bf16[1024,512]{1,0:T(8,128)(2,1)S(1)} %copy-done.7, s32[1024,1]{1,0:T(8,128)S(1)} %copy-done.4, ...), custom_call_target="tpu_custom_call" | custom-call | flops 20000000000 | bytes 1048576 | tf_op jit(solution)/shard_map/mix_pull_inner/pallas_call | solution.py:236
  582.0 6.0 mix_pull_carry.1
  593.4 5.2 convolution_convert_fusion
  598.7 5.1 collective-permute-done.39.refs_3_
  609.8 8.1 %grad_mix_far.1 = (bf16[2,576,256]{2,1,0:T(8,128)(2,1)}, bf16[2,576,256]{2,1,0:T(8,128)(2,1)}, bf16[2,576,256]{2,1,0:T(8,128)(2,1)}, bf16[2,576,256]{2,1,0:T(8,128)(2,1)}) custom-call(s32[4]{0:T(128)} %get-tuple-element.493.blocks, s32[5,4]{1,0:T(8,128)} %constant.83.clone.swap, bf16[1024,2048]{1,0:T(8,128)(2,1)} %copy-done.57, bf16[640,1024]{1,0:T(8,128)(2,1)} %bitcast.91, ...), custom_call_target="tpu_custom_call" | custom-call | flops 5000000000 | bytes 1048576 | tf_op jit(solution)/shard_map/grad_mix_far/pallas_call | solution.py:417
  621.1 5.2 collective-permute-done.43.refs_8_
  629.4 8.9 %grad_mix_near.1 = (bf16[2,576,256]{2,1,0:T(8,128)(2,1)}, bf16[2,576,256]{2,1,0:T(8,128)(2,1)}, bf16[2,576,256]{2,1,0:T(8,128)(2,1)}, bf16[2,576,256]{2,1,0:T(8,128)(2,1)}) custom-call(s32[4]{0:T(128)} %get-tuple-element.494.blocks, s32[5,4]{1,0:T(8,128)} %constant.83.clone.swap, bf16[1024,2048]{1,0:T(8,128)(2,1)} %copy-done.57, bf16[640,1024]{1,0:T(8,128)(2,1)} %bitcast.92, ...), custom_call_target="tpu_custom_call" | custom-call | flops 5000000000 | bytes 1048576 | tf_op jit(solution)/shard_map/grad_mix_near/pallas_call | solution.py:417
  641.2 9.1 %place_ffn_0.1 = f32[1376,2048]{1,0:T(8,128)} custom-call(s32[8]{0:T(128)} %copy-done.95, s32[2,8]{1,0:T(2,128)} %constant.84.clone.table, bf16[1,2064,256]{2,1,0:T(8,128)(2,1)} %add_convert_fusion.9.refs_0_, bf16[1,2064,256]{2,1,0:T(8,128)(2,1)} %collective-permute-done.26.refs_1_, bf16[1,2064,256]{2,1,0:T(8,128)(2,1)} %copy-done.44, ...), custom_call_target="tpu_custom_call" | custom-call | flops 7000000000 | bytes 1048576 | tf_op jit(solution)/shard_map/place_ffn_0/pallas_call | solution.py:534
  650.3 3.8 collective-permute-done.53
  657.9 9.3 %place_ffn_1.1 = f32[1376,2048]{1,0:T(8,128)} custom-call(s32[8]{0:T(128)} %copy-done.95, s32[2,8]{1,0:T(2,128)} %constant.84.clone.table, bf16[1,2064,256]{2,1,0:T(8,128)(2,1)} %add_convert_fusion.9.refs_0_, bf16[1,2064,256]{2,1,0:T(8,128)(2,1)} %collective-permute-done.26.refs_1_, bf16[1,2064,256]{2,1,0:T(8,128)(2,1)} %copy-done.44, ...), custom_call_target="tpu_custom_call" | custom-call | flops 7000000000 | bytes 1048576 | tf_op jit(solution)/shard_map/place_ffn_1/pallas_call | solution.py:534
  670.5 4.4 collective-permute-done.57.refs_1_
  679.2 9.2 %place_ffn_2.1 = f32[1376,2048]{1,0:T(8,128)} custom-call(s32[8]{0:T(128)} %copy-done.95, s32[2,8]{1,0:T(2,128)} %constant.84.clone.table, bf16[1,2064,256]{2,1,0:T(8,128)(2,1)} %add_convert_fusion.9.refs_0_, bf16[1,2064,256]{2,1,0:T(8,128)(2,1)} %collective-permute-done.26.refs_1_, bf16[1,2064,256]{2,1,0:T(8,128)(2,1)} %copy-done.44, ...), custom_call_target="tpu_custom_call" | custom-call | flops 7000000000 | bytes 1048576 | tf_op jit(solution)/shard_map/place_ffn_2/pallas_call | solution.py:534
  694.7 3.9 fusion.18
  703.5 8.0 %place_mix.1 = (f32[64,2048]{1,0:T(8,128)}, f32[64,2048]{1,0:T(8,128)}, f32[2048,512]{1,0:T(8,128)}, f32[512,2048]{1,0:T(8,128)}) custom-call(s32[8]{0:T(128)} %copy-done.95, s32[2,8]{1,0:T(2,128)} %constant.84.clone.table, bf16[1,576,256]{2,1,0:T(8,128)(2,1)} %copy-done.87, bf16[1,576,256]{2,1,0:T(8,128)(2,1)} %copy-done.102, ...), custom_call_target="tpu_custom_call" | custom-call | flops 5000000000 | bytes 1048576 | tf_op jit(solution)/shard_map/place_mix/pallas_call | solution.py:534
  (508 shorter events, 161.0 us)
Async XLA Ops:
  7.2 86.0 %all-gather.6.cloned.1.call-start = ((), (), s32[]{:S(2)}) async-start(), calls=%async_computation.4 | async-start | bytes 5242880 | tf_op jit(solution)/shard_map/all_gather | solution.py:666
  8.0 275.2 %all-gather.10.cloned.1.call-start = ((), (), s32[]{:S(2)}) async-start(), calls=%async_computation.6 | async-start | bytes 2621440 | tf_op jit(solution)/shard_map/all_gather | solution.py:666
  108.0 31.5 %collective-permute-start.6 = (bf16[1024,512]{1,0:T(8,128)(2,1)}, bf16[1024,512]{1,0:T(8,128)(2,1)}, u32[]{:S(2)}, u32[]{:S(2)}) collective-permute-start(bf16[1024,512]{1,0:T(8,128)(2,1)} %param.40), channel_id=1, source_target_pairs={{0,1},{1,2},{2,3},{4,5},{5,6},{6,7},{8,9},{9,10},{10,11},{12,13},{... | collective-permute-start | bytes 3145736 | tf_op jit(solution)/shard_map/ppermute | solution.py:589
  110.4 29.1 %collective-permute-start.7 = (bf16[1024,512]{1,0:T(8,128)(2,1)}, bf16[1024,512]{1,0:T(8,128)(2,1)}, u32[]{:S(2)}, u32[]{:S(2)}) collective-permute-start(bf16[1024,512]{1,0:T(8,128)(2,1)} %param.40), channel_id=1, source_target_pairs={{1,0},{2,1},{3,2},{5,4},{6,5},{7,6},{9,8},{10,9},{11,10},{13,12},{... | collective-permute-start | bytes 3145736 | tf_op jit(solution)/shard_map/ppermute | solution.py:590
  111.7 12.4 %collective-permute-start.4 = (f32[4,8,256]{2,1,0:T(8,128)S(1)}, f32[4,8,256]{2,1,0:T(8,128)S(1)}, u32[]{:S(2)}, u32[]{:S(2)}) collective-permute-start(f32[4,8,256]{2,1,0:T(8,128)S(1)} %add.314), channel_id=1, source_target_pairs={{0,8},{4,12},{8,0},{12,4},{16,24},{20,28},{24,16},{28,20},{1,9},{5... | collective-permute-start | bytes 98312 | tf_op jit(solution)/shard_map/ppermute | solution.py:309
  113.3 12.4 %collective-permute-start.1 = (bf16[4,160,128]{2,1,0:T(8,128)(2,1)S(1)}, bf16[4,160,128]{2,1,0:T(8,128)(2,1)S(1)}, u32[]{:S(2)}, u32[]{:S(2)}) collective-permute-start(bf16[4,160,128]{2,1,0:T(8,128)(2,1)S(1)} %fusion.37), channel_id=1, source_target_pairs={{0,8},{4,12},{8,0},{12,4},{16,24},{20,28},{24,16},{28,20},{1,9},{5... | collective-permute-start | bytes 491528 | tf_op jit(solution)/shard_map/ppermute | solution.py:309
  140.7 25.6 %collective-permute-start.8 = (bf16[1024,512]{1,0:T(8,128)(2,1)}, bf16[1024,512]{1,0:T(8,128)(2,1)}, u32[]{:S(2)}, u32[]{:S(2)}) collective-permute-start(bf16[1024,512]{1,0:T(8,128)(2,1)} %convert_element_type.376), channel_id=1, source_target_pairs={{0,1},{4,5},{8,9},{12,13},{16,17},{20,21},{24,25},{28,29}} | collective-permute-start | bytes 3145736 | tf_op jit(solution)/shard_map/ppermute | solution.py:632
  147.1 19.3 %collective-permute-start.9 = (bf16[1024,512]{1,0:T(8,128)(2,1)}, bf16[1024,512]{1,0:T(8,128)(2,1)}, u32[]{:S(2)}, u32[]{:S(2)}) collective-permute-start(bf16[1024,512]{1,0:T(8,128)(2,1)} %convert_element_type.377), channel_id=1, source_target_pairs={{3,2},{7,6},{11,10},{15,14},{19,18},{23,22},{27,26},{31,30}} | collective-permute-start | bytes 3145736 | tf_op jit(solution)/shard_map/ppermute | solution.py:633
  148.7 17.6 %collective-permute-start.10 = (bf16[1024,512]{1,0:T(8,128)(2,1)}, bf16[1024,512]{1,0:T(8,128)(2,1)}, u32[]{:S(2)}, u32[]{:S(2)}) collective-permute-start(bf16[1024,512]{1,0:T(8,128)(2,1)} %collective-permute-done.6), channel_id=1, source_target_pairs={{1,2},{2,3},{5,6},{6,7},{9,10},{10,11},{13,14},{14,15},{17,18},{18... | collective-permute-start | bytes 3145736 | tf_op jit(solution)/shard_map/ppermute | solution.py:589
  150.3 25.5 %collective-permute-start.11 = (bf16[1024,512]{1,0:T(8,128)(2,1)}, bf16[1024,512]{1,0:T(8,128)(2,1)}, u32[]{:S(2)}, u32[]{:S(2)}) collective-permute-start(bf16[1024,512]{1,0:T(8,128)(2,1)} %collective-permute-done.7), channel_id=1, source_target_pairs={{1,0},{2,1},{5,4},{6,5},{9,8},{10,9},{13,12},{14,13},{17,16},{18,1... | collective-permute-start | bytes 3145736 | tf_op jit(solution)/shard_map/ppermute | solution.py:590
  178.0 22.1 %collective-permute-start.12 = (bf16[1024,512]{1,0:T(8,128)(2,1)S(1)}, bf16[1024,512]{1,0:T(8,128)(2,1)S(1)}, u32[]{:S(2)}, u32[]{:S(2)}) collective-permute-start(bf16[1024,512]{1,0:T(8,128)(2,1)S(1)} %get-tuple-element.472), channel_id=1, source_target_pairs={{0,1},{1,2},{4,5},{5,6},{8,9},{9,10},{12,13},{13,14},{16,17},{17,1... | collective-permute-start | bytes 3145736 | tf_op jit(solution)/shard_map/ppermute | solution.py:632
  180.5 19.6 %collective-permute-start.13 = (bf16[1024,512]{1,0:T(8,128)(2,1)S(1)}, bf16[1024,512]{1,0:T(8,128)(2,1)S(1)}, u32[]{:S(2)}, u32[]{:S(2)}) collective-permute-start(bf16[1024,512]{1,0:T(8,128)(2,1)S(1)} %get-tuple-element.471), channel_id=1, source_target_pairs={{2,1},{3,2},{6,5},{7,6},{10,9},{11,10},{14,13},{15,14},{18,17},{19... | collective-permute-start | bytes 3145736 | tf_op jit(solution)/shard_map/ppermute | solution.py:633
  181.2 18.8 %collective-permute-start.14 = (bf16[1024,512]{1,0:T(8,128)(2,1)}, bf16[1024,512]{1,0:T(8,128)(2,1)S(1)}, u32[]{:S(2)}, u32[]{:S(2)}) collective-permute-start(bf16[1024,512]{1,0:T(8,128)(2,1)} %collective-permute-done.10), channel_id=1, source_target_pairs={{2,3},{6,7},{10,11},{14,15},{18,19},{22,23},{26,27},{30,31}} | collective-permute-start | bytes 3145736 | tf_op jit(solution)/shard_map/ppermute | solution.py:589
  182.0 24.0 %collective-permute-start.15 = (bf16[1024,512]{1,0:T(8,128)(2,1)}, bf16[1024,512]{1,0:T(8,128)(2,1)S(1)}, u32[]{:S(2)}, u32[]{:S(2)}) collective-permute-start(bf16[1024,512]{1,0:T(8,128)(2,1)} %collective-permute-done.11), channel_id=1, source_target_pairs={{1,0},{5,4},{9,8},{13,12},{17,16},{21,20},{25,24},{29,28}} | collective-permute-start | bytes 3145736 | tf_op jit(solution)/shard_map/ppermute | solution.py:590
  207.3 20.5 %collective-permute-start.16 = (bf16[1024,512]{1,0:T(8,128)(2,1)}, bf16[1024,512]{1,0:T(8,128)(2,1)}, u32[]{:S(2)}, u32[]{:S(2)}) collective-permute-start(bf16[1024,512]{1,0:T(8,128)(2,1)} %add_convert_fusion.13), channel_id=1, source_target_pairs={{0,1},{1,2},{2,3},{4,5},{5,6},{6,7},{8,9},{9,10},{10,11},{12,13},{... | collective-permute-start | bytes 3145736 | tf_op jit(solution)/shard_map/ppermute | solution.py:632
  211.3 22.9 %collective-permute-start.17 = (bf16[1024,512]{1,0:T(8,128)(2,1)}, bf16[1024,512]{1,0:T(8,128)(2,1)}, u32[]{:S(2)}, u32[]{:S(2)}) collective-permute-start(bf16[1024,512]{1,0:T(8,128)(2,1)} %add_convert_fusion.12), channel_id=1, source_target_pairs={{1,0},{2,1},{3,2},{5,4},{6,5},{7,6},{9,8},{10,9},{11,10},{13,12},{... | collective-permute-start | bytes 3145736 | tf_op jit(solution)/shard_map/ppermute | solution.py:633
  238.9 91.1 %all-gather.8.cloned.1.call-start = ((), (), s32[]{:S(2)}) async-start(), calls=%async_computation.5 | async-start | bytes 2621440 | tf_op jit(solution)/shard_map/all_gather | solution.py:666
  263.2 112.2 %reduce-scatter.5.cloned.1.call-start = ((), (), s32[]{:S(2)}) async-start(), calls=%async_computation.7 | async-start | bytes 2621440 | tf_op jit(solution)/shard_map/reduce_scatter | solution.py:670
  330.0 90.7 %reduce-scatter.7.cloned.1.call-start = ((), (), s32[]{:S(2)}) async-start(), calls=%async_computation.8 | async-start | bytes 2621440 | tf_op jit(solution)/shard_map/reduce_scatter | solution.py:670
  375.3 21.2 %collective-permute-start.18 = (bf16[2,2064,256]{2,1,0:T(8,128)(2,1)}, bf16[2,2064,256]{2,1,0:T(8,128)(2,1)}, u32[]{:S(2)}, u32[]{:S(2)}) collective-permute-start(bf16[2,2064,256]{2,1,0:T(8,128)(2,1)} %get-tuple-element.305), channel_id=1, source_target_pairs={{0,4},{4,0},{8,12},{12,8},{16,20},{20,16},{24,28},{28,24},{1,5},{5... | collective-permute-start | bytes 6340616 | tf_op jit(solution)/shard_map/ppermute | solution.py:431
  375.4 94.6 %all-gather.12.cloned.1.call-start = ((), (), s32[]{:S(2)}) async-start(), calls=%async_computation.9 | async-start | bytes 2621440 | tf_op jit(solution)/shard_map/all_gather | solution.py:666
  375.8 25.1 %collective-permute-start.19 = (bf16[2,2064,256]{2,1,0:T(8,128)(2,1)}, bf16[2,2064,256]{2,1,0:T(8,128)(2,1)}, u32[]{:S(2)}, u32[]{:S(2)}) collective-permute-start(bf16[2,2064,256]{2,1,0:T(8,128)(2,1)} %get-tuple-element.307), channel_id=1, source_target_pairs={{0,4},{4,0},{8,12},{12,8},{16,20},{20,16},{24,28},{28,24},{1,5},{5... | collective-permute-start | bytes 6340616 | tf_op jit(solution)/shard_map/ppermute | solution.py:431
  376.4 28.2 %collective-permute-start.20 = (bf16[2,2064,256]{2,1,0:T(8,128)(2,1)}, bf16[2,2064,256]{2,1,0:T(8,128)(2,1)}, u32[]{:S(2)}, u32[]{:S(2)}) collective-permute-start(bf16[2,2064,256]{2,1,0:T(8,128)(2,1)} %get-tuple-element.309), channel_id=1, source_target_pairs={{0,4},{4,0},{8,12},{12,8},{16,20},{20,16},{24,28},{28,24},{1,5},{5... | collective-permute-start | bytes 6340616 | tf_op jit(solution)/shard_map/ppermute | solution.py:431
  376.5 31.8 %collective-permute-start.21 = (bf16[2,2064,256]{2,1,0:T(8,128)(2,1)}, bf16[2,2064,256]{2,1,0:T(8,128)(2,1)S(1)}, u32[]{:S(2)}, u32[]{:S(2)}) collective-permute-start(bf16[2,2064,256]{2,1,0:T(8,128)(2,1)} %get-tuple-element.311), channel_id=1, source_target_pairs={{0,4},{4,0},{8,12},{12,8},{16,20},{20,16},{24,28},{28,24},{1,5},{5... | collective-permute-start | bytes 6340616 | tf_op jit(solution)/shard_map/ppermute | solution.py:431
  420.8 94.1 %all-gather.14.cloned.1.call-start = ((), (), s32[]{:S(2)}) async-start(), calls=%async_computation.11 | async-start | bytes 2621440 | tf_op jit(solution)/shard_map/all_gather | solution.py:666
  420.9 48.0 %collective-permute-start.22 = (bf16[2,2064,256]{2,1,0:T(8,128)(2,1)}, bf16[2,2064,256]{2,1,0:T(8,128)(2,1)}, u32[]{:S(2)}, u32[]{:S(2)}) collective-permute-start(bf16[2,2064,256]{2,1,0:T(8,128)(2,1)} %add_convert_fusion.3), channel_id=1, source_target_pairs={{0,8},{4,12},{8,0},{12,4},{16,24},{20,28},{24,16},{28,20},{1,9},{5... | collective-permute-start | bytes 6340616 | tf_op jit(solution)/shard_map/ppermute | solution.py:431
  422.4 47.6 %collective-permute-start.23 = (bf16[2,2064,256]{2,1,0:T(8,128)(2,1)}, bf16[2,2064,256]{2,1,0:T(8,128)(2,1)}, u32[]{:S(2)}, u32[]{:S(2)}) collective-permute-start(bf16[2,2064,256]{2,1,0:T(8,128)(2,1)} %add_convert_fusion.2), channel_id=1, source_target_pairs={{0,16},{4,20},{8,24},{12,28},{16,0},{20,4},{24,8},{28,12},{1,17},{... | collective-permute-start | bytes 6340616 | tf_op jit(solution)/shard_map/ppermute | solution.py:431
  470.0 134.6 %reduce-scatter.9.cloned.1.call-start = ((), (), s32[]{:S(2)}) async-start(), calls=%async_computation.10 | async-start | bytes 5242880 | tf_op jit(solution)/shard_map/reduce_scatter | solution.py:670
  473.2 24.0 %collective-permute-start.24 = (bf16[1,2064,256]{2,1,0:T(8,128)(2,1)}, bf16[1,2064,256]{2,1,0:T(8,128)(2,1)}, u32[]{:S(2)}, u32[]{:S(2)}) collective-permute-start(bf16[1,2064,256]{2,1,0:T(8,128)(2,1)} %add_convert_fusion.10), channel_id=1, source_target_pairs={{0,16},{4,20},{8,24},{12,28},{16,0},{20,4},{24,8},{28,12},{1,17},{... | collective-permute-start | bytes 3170312 | tf_op jit(solution)/shard_map/ppermute | solution.py:431
  477.6 24.2 %collective-permute-start.25 = (bf16[1,2064,256]{2,1,0:T(8,128)(2,1)}, bf16[1,2064,256]{2,1,0:T(8,128)(2,1)}, u32[]{:S(2)}, u32[]{:S(2)}) collective-permute-start(bf16[1,2064,256]{2,1,0:T(8,128)(2,1)} %add_convert_fusion.7), channel_id=1, source_target_pairs={{0,8},{4,12},{8,0},{12,4},{16,24},{20,28},{24,16},{28,20},{1,9},{5... | collective-permute-start | bytes 3170312 | tf_op jit(solution)/shard_map/ppermute | solution.py:431
  483.4 211.3 %reduce-scatter.11.cloned.1.call-start = ((), (), s32[]{:S(2)}) async-start(), calls=%async_computation.12 | async-start | bytes 5242880 | tf_op jit(solution)/shard_map/reduce_scatter | solution.py:670
  500.3 30.3 %collective-permute-start.26 = (bf16[1,2064,256]{2,1,0:T(8,128)(2,1)}, bf16[1,2064,256]{2,1,0:T(8,128)(2,1)}, u32[]{:S(2)}, u32[]{:S(2)}) collective-permute-start(bf16[1,2064,256]{2,1,0:T(8,128)(2,1)} %add_convert_fusion.9.refs_0_), channel_id=1, source_target_pairs={{0,16},{4,20},{8,24},{12,28},{16,0},{20,4},{24,8},{28,12},{1,17},{... | collective-permute-start | bytes 3170312 | tf_op jit(solution)/shard_map/ppermute | solution.py:431
  504.9 26.6 %collective-permute-start.27 = (bf16[1,2064,256]{2,1,0:T(8,128)(2,1)}, bf16[1,2064,256]{2,1,0:T(8,128)(2,1)}, u32[]{:S(2)}, u32[]{:S(2)}) collective-permute-start(bf16[1,2064,256]{2,1,0:T(8,128)(2,1)} %add_convert_fusion.6.refs_8_), channel_id=1, source_target_pairs={{0,8},{4,12},{8,0},{12,4},{16,24},{20,28},{24,16},{28,20},{1,9},{5... | collective-permute-start | bytes 3170312 | tf_op jit(solution)/shard_map/ppermute | solution.py:431
  514.9 35.3 %collective-permute-start.28 = (bf16[1,2064,256]{2,1,0:T(8,128)(2,1)}, bf16[1,2064,256]{2,1,0:T(8,128)(2,1)S(1)}, u32[]{:S(2)}, u32[]{:S(2)}) collective-permute-start(bf16[1,2064,256]{2,1,0:T(8,128)(2,1)} %add_convert_fusion.9.refs_0_), channel_id=1, source_target_pairs={{0,8},{4,12},{8,0},{12,4},{16,24},{20,28},{24,16},{28,20},{1,9},{5... | collective-permute-start | bytes 3170312 | tf_op jit(solution)/shard_map/ppermute | solution.py:431
  516.4 33.9 %collective-permute-start.29 = (bf16[1,2064,256]{2,1,0:T(8,128)(2,1)}, bf16[1,2064,256]{2,1,0:T(8,128)(2,1)S(1)}, u32[]{:S(2)}, u32[]{:S(2)}) collective-permute-start(bf16[1,2064,256]{2,1,0:T(8,128)(2,1)} %add_convert_fusion.6.refs_8_), channel_id=1, source_target_pairs={{0,16},{4,20},{8,24},{12,28},{16,0},{20,4},{24,8},{28,12},{1,17},{... | collective-permute-start | bytes 3170312 | tf_op jit(solution)/shard_map/ppermute | solution.py:431
  553.2 19.6 %collective-permute-start.34 = (f32[4,8,256]{2,1,0:T(8,128)S(1)}, f32[4,8,256]{2,1,0:T(8,128)S(1)}, u32[]{:S(2)}, u32[]{:S(2)}) collective-permute-start(f32[4,8,256]{2,1,0:T(8,128)S(1)} %add.361), channel_id=1, source_target_pairs={{0,8},{4,12},{8,0},{12,4},{16,24},{20,28},{24,16},{28,20},{1,9},{5... | collective-permute-start | bytes 98312 | tf_op jit(solution)/shard_map/ppermute | solution.py:309
  554.4 19.0 %collective-permute-start.31 = (bf16[4,160,128]{2,1,0:T(8,128)(2,1)S(1)}, bf16[4,160,128]{2,1,0:T(8,128)(2,1)S(1)}, u32[]{:S(2)}, u32[]{:S(2)}) collective-permute-start(bf16[4,160,128]{2,1,0:T(8,128)(2,1)S(1)} %fusion.38), channel_id=1, source_target_pairs={{0,8},{4,12},{8,0},{12,4},{16,24},{20,28},{24,16},{28,20},{1,9},{5... | collective-permute-start | bytes 491528 | tf_op jit(solution)/shard_map/ppermute | solution.py:309
  579.3 24.4 %collective-permute-start.39 = (bf16[1,2064,256]{2,1,0:T(8,128)(2,1)}, bf16[1,2064,256]{2,1,0:T(8,128)(2,1)}, u32[]{:S(2)}, u32[]{:S(2)}) collective-permute-start(bf16[1,2064,256]{2,1,0:T(8,128)(2,1)} %collective-permute-done.26.refs_1_), channel_id=1, source_target_pairs={{0,8},{4,12},{8,0},{12,4},{16,24},{20,28},{24,16},{28,20},{1,9},{5... | collective-permute-start | bytes 3170312 | tf_op jit(solution)/shard_map/ppermute | solution.py:431
  580.6 24.0 %collective-permute-start.40 = (bf16[1,2064,256]{2,1,0:T(8,128)(2,1)}, bf16[1,2064,256]{2,1,0:T(8,128)(2,1)}, u32[]{:S(2)}, u32[]{:S(2)}) collective-permute-start(bf16[1,2064,256]{2,1,0:T(8,128)(2,1)} %collective-permute-done.27.refs_9_), channel_id=1, source_target_pairs={{0,16},{4,20},{8,24},{12,28},{16,0},{20,4},{24,8},{28,12},{1,17},{... | collective-permute-start | bytes 3170312 | tf_op jit(solution)/shard_map/ppermute | solution.py:431
  588.6 10.1 %collective-permute-start.36 = (f32[8,128]{1,0:T(8,128)S(1)}, f32[8,128]{1,0:T(8,128)S(1)}, u32[]{:S(2)}, u32[]{:S(2)}) collective-permute-start(f32[8,128]{1,0:T(8,128)S(1)} %add_bitcast_fusion), channel_id=1, source_target_pairs={{0,1},{1,2},{2,3},{3,0},{4,5},{5,6},{6,7},{7,4},{8,9},{9,10},{10,1... | collective-permute-start | bytes 12296 | tf_op jit(solution)/shard_map/ppermute | solution.py:551
  588.7 9.9 %collective-permute-start.37 = (f32[8,128]{1,0:T(8,128)S(1)}, f32[8,128]{1,0:T(8,128)S(1)}, u32[]{:S(2)}, u32[]{:S(2)}) collective-permute-start(f32[8,128]{1,0:T(8,128)S(1)} %add_bitcast_fusion), channel_id=1, source_target_pairs={{0,2},{1,3},{2,0},{3,1},{4,6},{5,7},{6,4},{7,5},{8,10},{9,11},{10,... | collective-permute-start | bytes 12296 | tf_op jit(solution)/shard_map/ppermute | solution.py:551
  591.0 7.7 %collective-permute-start.38 = (f32[8,128]{1,0:T(8,128)S(1)}, f32[8,128]{1,0:T(8,128)S(1)}, u32[]{:S(2)}, u32[]{:S(2)}) collective-permute-start(f32[8,128]{1,0:T(8,128)S(1)} %add_bitcast_fusion), channel_id=1, source_target_pairs={{0,3},{1,0},{2,1},{3,2},{4,7},{5,4},{6,5},{7,6},{8,11},{9,8},{10,9... | collective-permute-start | bytes 12296 | tf_op jit(solution)/shard_map/ppermute | solution.py:551
  618.4 8.9 %collective-permute-start.45 = (bf16[1,2064,256]{2,1,0:T(8,128)(2,1)}, bf16[1,2064,256]{2,1,0:T(8,128)(2,1)S(1)}, u32[]{:S(2)}, u32[]{:S(2)}) collective-permute-start(bf16[1,2064,256]{2,1,0:T(8,128)(2,1)} %add_convert_fusion.9.refs_0_), channel_id=1, source_target_pairs={{0,4},{4,0},{8,12},{12,8},{16,20},{20,16},{24,28},{28,24},{1,5},{5... | collective-permute-start | bytes 3170312 | tf_op jit(solution)/shard_map/ppermute | solution.py:431
  618.5 9.2 %collective-permute-start.46 = (bf16[1,2064,256]{2,1,0:T(8,128)(2,1)}, bf16[1,2064,256]{2,1,0:T(8,128)(2,1)S(1)}, u32[]{:S(2)}, u32[]{:S(2)}) collective-permute-start(bf16[1,2064,256]{2,1,0:T(8,128)(2,1)} %collective-permute-done.26.refs_1_), channel_id=1, source_target_pairs={{0,4},{4,0},{8,12},{12,8},{16,20},{20,16},{24,28},{28,24},{1,5},{5... | collective-permute-start | bytes 3170312 | tf_op jit(solution)/shard_map/ppermute | solution.py:431
  619.0 9.0 %collective-permute-start.47 = (bf16[1,2064,256]{2,1,0:T(8,128)(2,1)S(1)}, bf16[1,2064,256]{2,1,0:T(8,128)(2,1)S(1)}, u32[]{:S(2)}, u32[]{:S(2)}) collective-permute-start(bf16[1,2064,256]{2,1,0:T(8,128)(2,1)S(1)} %copy-done.45), channel_id=1, source_target_pairs={{0,4},{4,0},{8,12},{12,8},{16,20},{20,16},{24,28},{28,24},{1,5},{5... | collective-permute-start | bytes 3170312 | tf_op jit(solution)/shard_map/ppermute | solution.py:431
  620.2 6.2 collective-permute-start.43
  626.4 12.0 %collective-permute-start.48 = (bf16[1,2064,256]{2,1,0:T(8,128)(2,1)}, bf16[1,2064,256]{2,1,0:T(8,128)(2,1)}, u32[]{:S(2)}, u32[]{:S(2)}) collective-permute-start(bf16[1,2064,256]{2,1,0:T(8,128)(2,1)} %collective-permute-done.39.refs_3_), channel_id=1, source_target_pairs={{0,4},{4,0},{8,12},{12,8},{16,20},{20,16},{24,28},{28,24},{1,5},{5... | collective-permute-start | bytes 3170312 | tf_op jit(solution)/shard_map/ppermute | solution.py:431
  627.2 11.1 %collective-permute-start.49 = (bf16[1,2064,256]{2,1,0:T(8,128)(2,1)}, bf16[1,2064,256]{2,1,0:T(8,128)(2,1)}, u32[]{:S(2)}, u32[]{:S(2)}) collective-permute-start(bf16[1,2064,256]{2,1,0:T(8,128)(2,1)} %add_convert_fusion.6.refs_8_), channel_id=1, source_target_pairs={{0,4},{4,0},{8,12},{12,8},{16,20},{20,16},{24,28},{28,24},{1,5},{5... | collective-permute-start | bytes 3170312 | tf_op jit(solution)/shard_map/ppermute | solution.py:431
  627.4 11.0 %collective-permute-start.50 = (bf16[1,2064,256]{2,1,0:T(8,128)(2,1)}, bf16[1,2064,256]{2,1,0:T(8,128)(2,1)}, u32[]{:S(2)}, u32[]{:S(2)}) collective-permute-start(bf16[1,2064,256]{2,1,0:T(8,128)(2,1)} %collective-permute-done.27.refs_9_), channel_id=1, source_target_pairs={{0,4},{4,0},{8,12},{12,8},{16,20},{20,16},{24,28},{28,24},{1,5},{5... | collective-permute-start | bytes 3170312 | tf_op jit(solution)/shard_map/ppermute | solution.py:431
  627.7 10.6 %collective-permute-start.51 = (bf16[1,2064,256]{2,1,0:T(8,128)(2,1)S(1)}, bf16[1,2064,256]{2,1,0:T(8,128)(2,1)}, u32[]{:S(2)}, u32[]{:S(2)}) collective-permute-start(bf16[1,2064,256]{2,1,0:T(8,128)(2,1)S(1)} %copy-done.47), channel_id=1, source_target_pairs={{0,4},{4,0},{8,12},{12,8},{16,20},{20,16},{24,28},{28,24},{1,5},{5... | collective-permute-start | bytes 3170312 | tf_op jit(solution)/shard_map/ppermute | solution.py:431
  629.1 9.3 %collective-permute-start.52 = (bf16[1,2064,256]{2,1,0:T(8,128)(2,1)}, bf16[1,2064,256]{2,1,0:T(8,128)(2,1)S(1)}, u32[]{:S(2)}, u32[]{:S(2)}) collective-permute-start(bf16[1,2064,256]{2,1,0:T(8,128)(2,1)} %collective-permute-done.40.refs_11_), channel_id=1, source_target_pairs={{0,4},{4,0},{8,12},{12,8},{16,20},{20,16},{24,28},{28,24},{1,5},{5... | collective-permute-start | bytes 3170312 | tf_op jit(solution)/shard_map/ppermute | solution.py:431
  638.4 15.7 %collective-permute-start.53 = (bf16[2,576,256]{2,1,0:T(8,128)(2,1)}, bf16[2,576,256]{2,1,0:T(8,128)(2,1)S(1)}, u32[]{:S(2)}, u32[]{:S(2)}) collective-permute-start(bf16[2,576,256]{2,1,0:T(8,128)(2,1)} %get-tuple-element.378), channel_id=1, source_target_pairs={{0,8},{4,12},{8,0},{12,4},{16,24},{20,28},{24,16},{28,20},{1,9},{5... | collective-permute-start | bytes 1769480 | tf_op jit(solution)/shard_map/ppermute | solution.py:431
  639.7 15.3 %collective-permute-start.54 = (bf16[2,576,256]{2,1,0:T(8,128)(2,1)}, bf16[2,576,256]{2,1,0:T(8,128)(2,1)S(1)}, u32[]{:S(2)}, u32[]{:S(2)}) collective-permute-start(bf16[2,576,256]{2,1,0:T(8,128)(2,1)} %get-tuple-element.379), channel_id=1, source_target_pairs={{0,16},{4,20},{8,24},{12,28},{16,0},{20,4},{24,8},{28,12},{1,17},{... | collective-permute-start | bytes 1769480 | tf_op jit(solution)/shard_map/ppermute | solution.py:431
  655.2 12.0 %collective-permute-start.55 = (bf16[1,576,256]{2,1,0:T(8,128)(2,1)S(1)}, bf16[1,576,256]{2,1,0:T(8,128)(2,1)S(1)}, u32[]{:S(2)}, u32[]{:S(2)}) collective-permute-start(bf16[1,576,256]{2,1,0:T(8,128)(2,1)S(1)} %get-tuple-element.476), channel_id=1, source_target_pairs={{0,16},{4,20},{8,24},{12,28},{16,0},{20,4},{24,8},{28,12},{1,17},{... | collective-permute-start | bytes 884744 | tf_op jit(solution)/shard_map/ppermute | solution.py:431
  656.9 10.3 %collective-permute-start.56 = (bf16[1,576,256]{2,1,0:T(8,128)(2,1)S(1)}, bf16[1,576,256]{2,1,0:T(8,128)(2,1)S(1)}, u32[]{:S(2)}, u32[]{:S(2)}) collective-permute-start(bf16[1,576,256]{2,1,0:T(8,128)(2,1)S(1)} %get-tuple-element.474), channel_id=1, source_target_pairs={{0,8},{4,12},{8,0},{12,4},{16,24},{20,28},{24,16},{28,20},{1,9},{5... | collective-permute-start | bytes 884744 | tf_op jit(solution)/shard_map/ppermute | solution.py:431
  667.3 7.5 %collective-permute-start.57 = (bf16[1,576,256]{2,1,0:T(8,128)(2,1)S(1)}, bf16[1,576,256]{2,1,0:T(8,128)(2,1)S(1)}, u32[]{:S(2)}, u32[]{:S(2)}) collective-permute-start(bf16[1,576,256]{2,1,0:T(8,128)(2,1)S(1)} %add_convert_fusion.17.refs_0_), channel_id=1, source_target_pairs={{0,16},{4,20},{8,24},{12,28},{16,0},{20,4},{24,8},{28,12},{1,17},{... | collective-permute-start | bytes 884744 | tf_op jit(solution)/shard_map/ppermute | solution.py:431
  667.9 7.3 %collective-permute-start.58 = (bf16[1,576,256]{2,1,0:T(8,128)(2,1)S(1)}, bf16[1,576,256]{2,1,0:T(8,128)(2,1)S(1)}, u32[]{:S(2)}, u32[]{:S(2)}) collective-permute-start(bf16[1,576,256]{2,1,0:T(8,128)(2,1)S(1)} %add_convert_fusion.16.refs_8_), channel_id=1, source_target_pairs={{0,8},{4,12},{8,0},{12,4},{16,24},{20,28},{24,16},{28,20},{1,9},{5... | collective-permute-start | bytes 884744 | tf_op jit(solution)/shard_map/ppermute | solution.py:431
  675.1 13.3 %collective-permute-start.59 = (bf16[1,576,256]{2,1,0:T(8,128)(2,1)S(1)}, bf16[1,576,256]{2,1,0:T(8,128)(2,1)S(1)}, u32[]{:S(2)}, u32[]{:S(2)}) collective-permute-start(bf16[1,576,256]{2,1,0:T(8,128)(2,1)S(1)} %add_convert_fusion.17.refs_0_), channel_id=1, source_target_pairs={{0,8},{4,12},{8,0},{12,4},{16,24},{20,28},{24,16},{28,20},{1,9},{5... | collective-permute-start | bytes 884744 | tf_op jit(solution)/shard_map/ppermute | solution.py:431
  676.3 12.1 %collective-permute-start.60 = (bf16[1,576,256]{2,1,0:T(8,128)(2,1)S(1)}, bf16[1,576,256]{2,1,0:T(8,128)(2,1)S(1)}, u32[]{:S(2)}, u32[]{:S(2)}) collective-permute-start(bf16[1,576,256]{2,1,0:T(8,128)(2,1)S(1)} %collective-permute-done.57.refs_1_), channel_id=1, source_target_pairs={{0,8},{4,12},{8,0},{12,4},{16,24},{20,28},{24,16},{28,20},{1,9},{5... | collective-permute-start | bytes 884744 | tf_op jit(solution)/shard_map/ppermute | solution.py:431
  677.1 11.3 %collective-permute-start.61 = (bf16[1,576,256]{2,1,0:T(8,128)(2,1)S(1)}, bf16[1,576,256]{2,1,0:T(8,128)(2,1)S(1)}, u32[]{:S(2)}, u32[]{:S(2)}) collective-permute-start(bf16[1,576,256]{2,1,0:T(8,128)(2,1)S(1)} %add_convert_fusion.16.refs_8_), channel_id=1, source_target_pairs={{0,16},{4,20},{8,24},{12,28},{16,0},{20,4},{24,8},{28,12},{1,17},{... | collective-permute-start | bytes 884744 | tf_op jit(solution)/shard_map/ppermute | solution.py:431
  678.8 10.6 %collective-permute-start.62 = (bf16[1,576,256]{2,1,0:T(8,128)(2,1)S(1)}, bf16[1,576,256]{2,1,0:T(8,128)(2,1)S(1)}, u32[]{:S(2)}, u32[]{:S(2)}) collective-permute-start(bf16[1,576,256]{2,1,0:T(8,128)(2,1)S(1)} %collective-permute-done.58.refs_9_), channel_id=1, source_target_pairs={{0,16},{4,20},{8,24},{12,28},{16,0},{20,4},{24,8},{28,12},{1,17},{... | collective-permute-start | bytes 884744 | tf_op jit(solution)/shard_map/ppermute | solution.py:431
  699.9 11.6 %collective-permute-start.74 = (f32[2,512]{1,0:T(2,128)S(1)}, f32[2,512]{1,0:T(2,128)S(1)}, u32[]{:S(2)}, u32[]{:S(2)}) collective-permute-start(f32[2,512]{1,0:T(2,128)S(1)} %fusion.48), channel_id=1, source_target_pairs={{0,24},{4,28},{8,16},{12,20},{16,8},{20,12},{24,0},{28,4},{1,25},{... | collective-permute-start | bytes 12296 | tf_op jit(solution)/shard_map/ppermute | solution.py:431
  702.0 9.5 %collective-permute-start.72 = (f32[2,512]{1,0:T(2,128)S(1)}, f32[2,512]{1,0:T(2,128)S(1)}, u32[]{:S(2)}, u32[]{:S(2)}) collective-permute-start(f32[2,512]{1,0:T(2,128)S(1)} %fusion.48), channel_id=1, source_target_pairs={{0,8},{4,12},{8,0},{12,4},{16,24},{20,28},{24,16},{28,20},{1,9},{5... | collective-permute-start | bytes 12296 | tf_op jit(solution)/shard_map/ppermute | solution.py:431
  703.0 8.5 %collective-permute-start.73 = (f32[2,512]{1,0:T(2,128)S(1)}, f32[2,512]{1,0:T(2,128)S(1)}, u32[]{:S(2)}, u32[]{:S(2)}) collective-permute-start(f32[2,512]{1,0:T(2,128)S(1)} %fusion.48), channel_id=1, source_target_pairs={{0,16},{4,20},{8,24},{12,28},{16,0},{20,4},{24,8},{28,12},{1,17},{... | collective-permute-start | bytes 12296 | tf_op jit(solution)/shard_map/ppermute | solution.py:431
  (152 other events, 1387.0 us)
Sparse Core Ops, SparseCore 0:
  9.6 83.5 all-gather.5
  239.0 44.1 all-gather.9
  285.3 44.6 all-gather.7
  332.7 42.5 reduce-scatter.4
  377.6 43.1 reduce-scatter.6
  422.8 45.2 all-gather.11
  470.2 44.6 all-gather.13
  517.8 75.5 reduce-scatter.8
  604.8 76.0 reduce-scatter.10

commit v5 on v4

--- a/solution.py
+++ b/solution.py
@@ -810,7 +810,8 @@
     u_b, gain_b = turned(c_b, scale_b, back_b, hidden_b)
     low_b = u_b.astype(LOW)
     parts = [across(m, w_down).astype(LOW) for m in (inner_a, inner_b)]
-    wide_u, u_b, gain_b, low_b, parts = lock(wide_u, u_b, gain_b, low_b, parts, ffn)
+    y_turned = [p.T for p in cut(y)]
+    wide_u, u_b, gain_b, low_b, parts, y_turned = lock(wide_u, u_b, gain_b, low_b, parts, y_turned, ffn)
 
     wide_v = widen(low_b)
     ffn.take()
@@ -840,8 +841,7 @@
     down, part, dmix, dh_b, grad_hidden_b, dots = lock(down, part, dmix, dh_b, grad_hidden_b, dots, ffn)
 
     back = narrow(part)
-    y_a, y_b = cut(y)
-    groups = [[(normed_one, dmix.T)], [(dh_a, y_a.T), (dh_b, y_b.T)]]
+    groups = [[(normed_one, dmix.T)], [(dh_a, y_turned[0]), (dh_b, y_turned[1])]]
     ffn.take()
     ffn.send()
     mix = Exchange(grad_blocks("grad_mix_far", groups, True, None, 5))

time: 729 us -> 726 us (level)
    unnamed x266 -> x262, local copies, waits for them, and re-layouts: 16.7 us -> 16.7 us
where the time goes in v5:
time: 726 us; the launch traced here: 716 us
  waiting for transfers between devices  279 us (38%)
  Pallas kernels  137 us (19%)
  matrix products  85.1 us (12%)
  other arithmetic  82.4 us (11%)
  starting transfers between devices  71.7 us (10%)
  local copies, waits for them, and re-layouts  29.7 us (4%)
  between operations  16.6 us (2%)
  blocking collectives  14.9 us (2%)
    all_gather x5, waiting for transfers between devices, widen(): return lax.all_gather(part, 'tensor', axis=1, tiled=True)  110 us
    ppermute x48, waiting for transfers between devices, flip(): lax.ppermute(value, 'batch', [(i, i ^ bit) for i in range(lax.axis_size('...  80.9 us
    pallas_call x4, Pallas kernels, grad_blocks(): pl.pallas_call(functools.partial(grad_body, groups=tuple(kinds), summed=b...  53.3 us
    dot_general x9, matrix products, project_back(): return jnp.einsum('ti,ji->tj', left, right, preferred_element_type=F32)  45.2 us
    ppermute x3, waiting for transfers between devices, hop(): lax.ppermute(sends[0], 'tensor', [(k, k + 1) for k in range(0, count - se...  44 us
    pallas_call x6, Pallas kernels, call(): pl.pallas_call(body, grid=(self.heads,), in_specs=in_specs, out_specs=out...  42.7 us
    pallas_call x4, Pallas kernels, place_blocks(): pl.pallas_call(functools.partial(place_body, outs=tuple(layout), count=co...  35.7 us
    ppermute x48, starting transfers between devices, flip(): lax.ppermute(value, 'batch', [(i, i ^ bit) for i in range(lax.axis_size('...  32 us
  transfers between devices with their start and end apart: 84, of which 40 were waited for; matrix products, arithmetic and copies ran while one was open for 22% of the time, Pallas kernels for 19%

profile of v5, /device:TPU:0, one launch (start us, length us, event | category | flops | bytes accessed | tf_op | source)
XLA Modules:
  0.0 716.4 jit_solution(17324276098681601930)
XLA Ops:
  15.0 14.9 %all_gather.19 = f32[2,2048]{1,0:T(2,128)S(1)} all-gather(f32[2,512]{1,0:T(2,128)S(1)} %pad_maximum_fusion.3), channel_id=1, replica_groups=mesh['batch'=8,'tensor'=4] {'tensor'}, dimensions={1}, use_global_device_ids=true | all-gather | bytes 20480 | tf_op jit(solution)/shard_map/all_gather | solution.py:718
  32.2 4.1 pad_maximum_fusion.2
  36.3 56.9 %all-gather.6.cloned.1.call-done = bf16[1024,2048]{1,0:T(8,128)(2,1)} async-done(((bf16[1024,512]{1,0:T(8,128)(2,1)}), bf16[1024,2048]{1,0:T(8,128)(2,1)}) %all-gather.6.cloned.1.call-update) | async-done | bytes 4194320 | tf_op jit(solution)/shard_map/all_gather | solution.py:666
  93.2 3.2 fusion
  100.6 2.7 convolution_convert_fusion.4
  104.1 3.2 mix_state.1
  117.0 5.8 mix_inner.1
  128.5 3.1 collective-permute-done.2
  131.6 5.8 mix_merge.1
  140.7 5.2 collective-permute-start.8
  152.8 13.5 %collective-permute-done.8 = bf16[1024,512]{1,0:T(8,128)(2,1)} collective-permute-done((bf16[1024,512]{1,0:T(8,128)(2,1)}, bf16[1024,512]{1,0:T(8,128)(2,1)}, u32[]{:S(2)}, u32[]{:S(2)}) %collective-permute-start.8) | collective-permute-done | bytes 1048608 | tf_op jit(solution)/shard_map/ppermute | solution.py:632
  166.4 9.4 %collective-permute-done.11 = bf16[1024,512]{1,0:T(8,128)(2,1)} collective-permute-done((bf16[1024,512]{1,0:T(8,128)(2,1)}, bf16[1024,512]{1,0:T(8,128)(2,1)}, u32[]{:S(2)}, u32[]{:S(2)}) %collective-permute-start.11) | collective-permute-done | bytes 1048608 | tf_op jit(solution)/shard_map/ppermute | solution.py:590
  183.3 16.8 %collective-permute-done.12 = bf16[1024,512]{1,0:T(8,128)(2,1)S(1)} collective-permute-done((bf16[1024,512]{1,0:T(8,128)(2,1)S(1)}, bf16[1024,512]{1,0:T(8,128)(2,1)S(1)}, u32[]{:S(2)}, u32[]{:S(2)}) %collective-permute-start.12) | collective-permute-done | bytes 1048608 | tf_op jit(solution)/shard_map/ppermute | solution.py:632
  200.1 5.9 collective-permute-done.15
  214.1 13.7 %collective-permute-done.16 = bf16[1024,512]{1,0:T(8,128)(2,1)} collective-permute-done((bf16[1024,512]{1,0:T(8,128)(2,1)}, bf16[1024,512]{1,0:T(8,128)(2,1)}, u32[]{:S(2)}, u32[]{:S(2)}) %collective-permute-start.16) | collective-permute-done | bytes 1048608 | tf_op jit(solution)/shard_map/ppermute | solution.py:632
  227.7 6.5 collective-permute-done.17
  244.7 5.6 straighten.1
  250.3 8.1 %convolution_bitcast_fusion.5 = f32[1376,512]{1,0:T(8,128)} fusion(bf16[1376,2048]{1,0:T(8,128)(2,1)} %param.39, bf16[1024,2048]{1,0:T(8,128)(2,1)} %straighten.1), kind=kOutput, calls=%fused_computation.41 | convolution fusion | flops 2885681152 | bytes 10551296 | tf_op jit(solution)/shard_map/ti,ji->tj/dot_general | solution.py:678
  258.4 4.7 convolution_bitcast_fusion.4
  263.4 19.8 %all-gather.10.cloned.1.call-done = bf16[512,2048]{1,0:T(8,128)(2,1)} async-done(((bf16[512,512]{1,0:T(8,128)(2,1)}), bf16[512,2048]{1,0:T(8,128)(2,1)}) %all-gather.10.cloned.1.call-update) | async-done | bytes 2097168 | tf_op jit(solution)/shard_map/all_gather | solution.py:666
  286.0 6.2 convolution_bitcast_fusion.2
  292.3 5.5 multiply_convert_fusion.3
  297.9 3.5 fusion.60
  301.4 4.6 add_convert_fusion.5
  306.0 24.0 %all-gather.8.cloned.1.call-done = bf16[512,2048]{1,0:T(8,128)(2,1)} async-done(((bf16[512,512]{1,0:T(8,128)(2,1)}), bf16[512,2048]{1,0:T(8,128)(2,1)}) %all-gather.8.cloned.1.call-update) | async-done | bytes 2097168 | tf_op jit(solution)/shard_map/all_gather | solution.py:666
  333.1 6.4 convolution_bitcast_fusion
  342.6 5.5 multiply_convert_fusion
  348.1 3.5 fusion.61
  351.7 4.7 add_convert_fusion.4
  356.4 18.0 %grad_ffn_far.1 = (bf16[2,2064,256]{2,1,0:T(8,128)(2,1)}, bf16[2,2064,256]{2,1,0:T(8,128)(2,1)}, bf16[2,2064,256]{2,1,0:T(8,128)(2,1)}, bf16[2,2064,256]{2,1,0:T(8,128)(2,1)}) custom-call(s32[4]{0:T(128)} %get-tuple-element.497.blocks, s32[5,4]{1,0:T(8,128)} %constant.83.clone.swap, bf16[512,2048]{1,0:T(8,128)(2,1)} %copy-done.72, ...), custom_call_target="tpu_custom_call" | custom-call | flops 16000000000 | bytes 1048576 | tf_op jit(solution)/shard_map/grad_ffn_far/pallas_call | solution.py:417
  376.9 18.1 %grad_ffn_near.1 = (bf16[2,2064,256]{2,1,0:T(8,128)(2,1)}, bf16[2,2064,256]{2,1,0:T(8,128)(2,1)}, bf16[2,2064,256]{2,1,0:T(8,128)(2,1)}, bf16[2,2064,256]{2,1,0:T(8,128)(2,1)}) custom-call(s32[4]{0:T(128)} %get-tuple-element.498.blocks, s32[5,4]{1,0:T(8,128)} %constant.83.clone.swap, bf16[512,2048]{1,0:T(8,128)(2,1)} %copy-done.72, ...), custom_call_target="tpu_custom_call" | custom-call | flops 16000000000 | bytes 1048576 | tf_op jit(solution)/shard_map/grad_ffn_near/pallas_call | solution.py:417
  397.2 3.6 add_convert_fusion.3
  400.9 3.7 add_convert_fusion.2
  404.6 3.6 add_convert_fusion.1
  410.1 10.7 %reduce-scatter.7.cloned.1.call-done = bf16[512,512]{1,0:T(8,128)(2,1)} async-done(((bf16[512,2048]{1,0:T(8,128)(2,1)}), bf16[512,512]{1,0:T(8,128)(2,1)}) %reduce-scatter.7.cloned.1.call-update) | async-done | bytes 524304 | tf_op jit(solution)/shard_map/reduce_scatter | solution.py:670
  427.4 8.3 %convolution_convert_fusion.2 = bf16[512,2048]{1,0:T(8,128)(2,1)} fusion(bf16[1376,512]{1,0:T(8,128)(2,1)} %get-tuple-element.293.refs_9_, bf16[1376,2048]{1,0:T(8,128)(2,1)} %param.39), kind=kOutput, calls=%fused_computation.46 | convolution fusion | flops 2886729728 | bytes 9142272 | tf_op jit(solution)/shard_map/it,ij->tj/dot_general | solution.py:682
  435.7 7.4 %convolution_convert_fusion.1 = bf16[512,2048]{1,0:T(8,128)(2,1)} fusion(bf16[1376,512]{1,0:T(8,128)(2,1)S(1)} %copy-done.117, bf16[1376,2048]{1,0:T(8,128)(2,1)} %param.39), kind=kOutput, calls=%fused_computation.45 | convolution fusion | flops 2886729728 | bytes 9142272 | tf_op jit(solution)/shard_map/it,ij->tj/dot_general | solution.py:682
  444.6 25.4 %collective-permute-done.22 = bf16[2,2064,256]{2,1,0:T(8,128)(2,1)} collective-permute-done((bf16[2,2064,256]{2,1,0:T(8,128)(2,1)}, bf16[2,2064,256]{2,1,0:T(8,128)(2,1)}, u32[]{:S(2)}, u32[]{:S(2)}) %collective-permute-start.22) | collective-permute-done | bytes 2113568 | tf_op jit(solution)/shard_map/ppermute | solution.py:431
  471.5 2.9 add_convert_fusion.10
  475.9 2.9 add_convert_fusion.7
  479.3 2.7 fusion.8
  484.7 2.9 fusion.3.refs_2_
  491.3 7.2 %collective-permute-done.24 = bf16[1,2064,256]{2,1,0:T(8,128)(2,1)} collective-permute-done((bf16[1,2064,256]{2,1,0:T(8,128)(2,1)}, bf16[1,2064,256]{2,1,0:T(8,128)(2,1)}, u32[]{:S(2)}, u32[]{:S(2)}) %collective-permute-start.24) | collective-permute-done | bytes 1056800 | tf_op jit(solution)/shard_map/ppermute | solution.py:431
  498.5 3.0 add_convert_fusion.9.refs_0_
  503.0 3.1 add_convert_fusion.6.refs_8_
  506.7 9.3 %all-gather.14.cloned.1.call-done = bf16[512,2048]{1,0:T(8,128)(2,1)} async-done(((bf16[512,512]{1,0:T(8,128)(2,1)}), bf16[512,2048]{1,0:T(8,128)(2,1)}) %all-gather.14.cloned.1.call-update) | async-done | bytes 2097168 | tf_op jit(solution)/shard_map/all_gather | solution.py:666
  518.9 3.7 fusion.12
  525.7 6.0 mix_pull_state.1
  532.7 18.8 %collective-permute-done.28.refs_2_ = bf16[1,2064,256]{2,1,0:T(8,128)(2,1)S(1)} collective-permute-done((bf16[1,2064,256]{2,1,0:T(8,128)(2,1)}, bf16[1,2064,256]{2,1,0:T(8,128)(2,1)S(1)}, u32[]{:S(2)}, u32[]{:S(2)}) %collective-permute-start.28) | collective-permute-done | bytes 1056800 | tf_op jit(solution)/shard_map/ppermute | solution.py:431
  556.6 16.0 %mix_pull_inner.1 = (bf16[1024,64]{1,0:T(8,128)(2,1)S(1)}, f32[1024,64]{1,0:T(8,128)S(1)}, f32[1024,512]{1,0:T(8,128)S(1)}) custom-call(bf16[1024,64]{1,0:T(8,128)(2,1)S(1)} %copy-done.16, bf16[1024,64]{1,0:T(8,128)(2,1)S(1)} %copy-done.14, bf16[1024,512]{1,0:T(8,128)(2,1)S(1)} %copy-done.5, s32[1024,1]{1,0:T(8,128)S(1)} %copy-done.2, ...), custom_call_target="tpu_custom_call" | custom-call | flops 20000000000 | bytes 1048576 | tf_op jit(solution)/shard_map/mix_pull_inner/pallas_call | solution.py:236
  582.6 6.0 mix_pull_carry.1
  589.3 3.0 collective-permute-start.37
  594.8 5.2 convolution_convert_fusion
  600.0 4.9 collective-permute-done.39.refs_3_
  606.8 8.3 %grad_mix_far.1 = (bf16[2,576,256]{2,1,0:T(8,128)(2,1)}, bf16[2,576,256]{2,1,0:T(8,128)(2,1)}, bf16[2,576,256]{2,1,0:T(8,128)(2,1)}, bf16[2,576,256]{2,1,0:T(8,128)(2,1)}) custom-call(s32[4]{0:T(128)} %get-tuple-element.497.blocks, s32[5,4]{1,0:T(8,128)} %constant.83.clone.swap, bf16[1024,2048]{1,0:T(8,128)(2,1)} %copy-done.55, bf16[640,1024]{1,0:T(8,128)(2,1)} %bitcast.91, ...), custom_call_target="tpu_custom_call" | custom-call | flops 5000000000 | bytes 1048576 | tf_op jit(solution)/shard_map/grad_mix_far/pallas_call | solution.py:417
  618.3 5.2 collective-permute-done.43.refs_8_
  626.6 8.9 %grad_mix_near.1 = (bf16[2,576,256]{2,1,0:T(8,128)(2,1)}, bf16[2,576,256]{2,1,0:T(8,128)(2,1)}, bf16[2,576,256]{2,1,0:T(8,128)(2,1)}, bf16[2,576,256]{2,1,0:T(8,128)(2,1)}) custom-call(s32[4]{0:T(128)} %get-tuple-element.498.blocks, s32[5,4]{1,0:T(8,128)} %constant.83.clone.swap, bf16[1024,2048]{1,0:T(8,128)(2,1)} %copy-done.55, bf16[640,1024]{1,0:T(8,128)(2,1)} %bitcast.92, ...), custom_call_target="tpu_custom_call" | custom-call | flops 5000000000 | bytes 1048576 | tf_op jit(solution)/shard_map/grad_mix_near/pallas_call | solution.py:417
  638.5 9.2 %place_ffn_0.1 = f32[1376,2048]{1,0:T(8,128)} custom-call(s32[8]{0:T(128)} %copy-done.93, s32[2,8]{1,0:T(2,128)} %constant.84.clone.table, bf16[1,2064,256]{2,1,0:T(8,128)(2,1)} %add_convert_fusion.9.refs_0_, bf16[1,2064,256]{2,1,0:T(8,128)(2,1)} %collective-permute-done.26.refs_1_, bf16[1,2064,256]{2,1,0:T(8,128)(2,1)} %copy-done.42, ...), custom_call_target="tpu_custom_call" | custom-call | flops 7000000000 | bytes 1048576 | tf_op jit(solution)/shard_map/place_ffn_0/pallas_call | solution.py:534
  647.7 3.6 collective-permute-done.53
  654.8 9.4 %place_ffn_1.1 = f32[1376,2048]{1,0:T(8,128)} custom-call(s32[8]{0:T(128)} %copy-done.93, s32[2,8]{1,0:T(2,128)} %constant.84.clone.table, bf16[1,2064,256]{2,1,0:T(8,128)(2,1)} %add_convert_fusion.9.refs_0_, bf16[1,2064,256]{2,1,0:T(8,128)(2,1)} %collective-permute-done.26.refs_1_, bf16[1,2064,256]{2,1,0:T(8,128)(2,1)} %copy-done.42, ...), custom_call_target="tpu_custom_call" | custom-call | flops 7000000000 | bytes 1048576 | tf_op jit(solution)/shard_map/place_ffn_1/pallas_call | solution.py:534
  667.8 3.9 collective-permute-done.57.refs_1_
  676.4 9.1 %place_ffn_2.1 = f32[1376,2048]{1,0:T(8,128)} custom-call(s32[8]{0:T(128)} %copy-done.93, s32[2,8]{1,0:T(2,128)} %constant.84.clone.table, bf16[1,2064,256]{2,1,0:T(8,128)(2,1)} %add_convert_fusion.9.refs_0_, bf16[1,2064,256]{2,1,0:T(8,128)(2,1)} %collective-permute-done.26.refs_1_, bf16[1,2064,256]{2,1,0:T(8,128)(2,1)} %copy-done.42, ...), custom_call_target="tpu_custom_call" | custom-call | flops 7000000000 | bytes 1048576 | tf_op jit(solution)/shard_map/place_ffn_2/pallas_call | solution.py:534
  692.0 3.9 fusion.18
  700.7 8.0 %place_mix.1 = (f32[64,2048]{1,0:T(8,128)}, f32[64,2048]{1,0:T(8,128)}, f32[2048,512]{1,0:T(8,128)}, f32[512,2048]{1,0:T(8,128)}) custom-call(s32[8]{0:T(128)} %copy-done.93, s32[2,8]{1,0:T(2,128)} %constant.84.clone.table, bf16[1,576,256]{2,1,0:T(8,128)(2,1)} %copy-done.85, bf16[1,576,256]{2,1,0:T(8,128)(2,1)} %copy-done.100, ...), custom_call_target="tpu_custom_call" | custom-call | flops 5000000000 | bytes 1048576 | tf_op jit(solution)/shard_map/place_mix/pallas_call | solution.py:534
  (504 shorter events, 160.7 us)
Async XLA Ops:
  7.2 86.0 %all-gather.6.cloned.1.call-start = ((), (), s32[]{:S(2)}) async-start(), calls=%async_computation.4 | async-start | bytes 5242880 | tf_op jit(solution)/shard_map/all_gather | solution.py:666
  8.0 275.2 %all-gather.10.cloned.1.call-start = ((), (), s32[]{:S(2)}) async-start(), calls=%async_computation.6 | async-start | bytes 2621440 | tf_op jit(solution)/shard_map/all_gather | solution.py:666
  108.0 31.5 %collective-permute-start.6 = (bf16[1024,512]{1,0:T(8,128)(2,1)}, bf16[1024,512]{1,0:T(8,128)(2,1)}, u32[]{:S(2)}, u32[]{:S(2)}) collective-permute-start(bf16[1024,512]{1,0:T(8,128)(2,1)} %param.40), channel_id=1, source_target_pairs={{0,1},{1,2},{2,3},{4,5},{5,6},{6,7},{8,9},{9,10},{10,11},{12,13},{... | collective-permute-start | bytes 3145736 | tf_op jit(solution)/shard_map/ppermute | solution.py:589
  110.4 29.1 %collective-permute-start.7 = (bf16[1024,512]{1,0:T(8,128)(2,1)}, bf16[1024,512]{1,0:T(8,128)(2,1)}, u32[]{:S(2)}, u32[]{:S(2)}) collective-permute-start(bf16[1024,512]{1,0:T(8,128)(2,1)} %param.40), channel_id=1, source_target_pairs={{1,0},{2,1},{3,2},{5,4},{6,5},{7,6},{9,8},{10,9},{11,10},{13,12},{... | collective-permute-start | bytes 3145736 | tf_op jit(solution)/shard_map/ppermute | solution.py:590
  111.7 12.4 %collective-permute-start.4 = (f32[4,8,256]{2,1,0:T(8,128)S(1)}, f32[4,8,256]{2,1,0:T(8,128)S(1)}, u32[]{:S(2)}, u32[]{:S(2)}) collective-permute-start(f32[4,8,256]{2,1,0:T(8,128)S(1)} %add.314), channel_id=1, source_target_pairs={{0,8},{4,12},{8,0},{12,4},{16,24},{20,28},{24,16},{28,20},{1,9},{5... | collective-permute-start | bytes 98312 | tf_op jit(solution)/shard_map/ppermute | solution.py:309
  113.3 12.4 %collective-permute-start.1 = (bf16[4,160,128]{2,1,0:T(8,128)(2,1)S(1)}, bf16[4,160,128]{2,1,0:T(8,128)(2,1)S(1)}, u32[]{:S(2)}, u32[]{:S(2)}) collective-permute-start(bf16[4,160,128]{2,1,0:T(8,128)(2,1)S(1)} %fusion.37), channel_id=1, source_target_pairs={{0,8},{4,12},{8,0},{12,4},{16,24},{20,28},{24,16},{28,20},{1,9},{5... | collective-permute-start | bytes 491528 | tf_op jit(solution)/shard_map/ppermute | solution.py:309
  140.7 25.6 %collective-permute-start.8 = (bf16[1024,512]{1,0:T(8,128)(2,1)}, bf16[1024,512]{1,0:T(8,128)(2,1)}, u32[]{:S(2)}, u32[]{:S(2)}) collective-permute-start(bf16[1024,512]{1,0:T(8,128)(2,1)} %convert_element_type.376), channel_id=1, source_target_pairs={{0,1},{4,5},{8,9},{12,13},{16,17},{20,21},{24,25},{28,29}} | collective-permute-start | bytes 3145736 | tf_op jit(solution)/shard_map/ppermute | solution.py:632
  147.1 19.3 %collective-permute-start.9 = (bf16[1024,512]{1,0:T(8,128)(2,1)}, bf16[1024,512]{1,0:T(8,128)(2,1)}, u32[]{:S(2)}, u32[]{:S(2)}) collective-permute-start(bf16[1024,512]{1,0:T(8,128)(2,1)} %convert_element_type.377), channel_id=1, source_target_pairs={{3,2},{7,6},{11,10},{15,14},{19,18},{23,22},{27,26},{31,30}} | collective-permute-start | bytes 3145736 | tf_op jit(solution)/shard_map/ppermute | solution.py:633
  148.7 17.7 %collective-permute-start.10 = (bf16[1024,512]{1,0:T(8,128)(2,1)}, bf16[1024,512]{1,0:T(8,128)(2,1)}, u32[]{:S(2)}, u32[]{:S(2)}) collective-permute-start(bf16[1024,512]{1,0:T(8,128)(2,1)} %collective-permute-done.6), channel_id=1, source_target_pairs={{1,2},{2,3},{5,6},{6,7},{9,10},{10,11},{13,14},{14,15},{17,18},{18... | collective-permute-start | bytes 3145736 | tf_op jit(solution)/shard_map/ppermute | solution.py:589
  150.3 25.5 %collective-permute-start.11 = (bf16[1024,512]{1,0:T(8,128)(2,1)}, bf16[1024,512]{1,0:T(8,128)(2,1)}, u32[]{:S(2)}, u32[]{:S(2)}) collective-permute-start(bf16[1024,512]{1,0:T(8,128)(2,1)} %collective-permute-done.7), channel_id=1, source_target_pairs={{1,0},{2,1},{5,4},{6,5},{9,8},{10,9},{13,12},{14,13},{17,16},{18,1... | collective-permute-start | bytes 3145736 | tf_op jit(solution)/shard_map/ppermute | solution.py:590
  178.0 22.1 %collective-permute-start.12 = (bf16[1024,512]{1,0:T(8,128)(2,1)S(1)}, bf16[1024,512]{1,0:T(8,128)(2,1)S(1)}, u32[]{:S(2)}, u32[]{:S(2)}) collective-permute-start(bf16[1024,512]{1,0:T(8,128)(2,1)S(1)} %get-tuple-element.476), channel_id=1, source_target_pairs={{0,1},{1,2},{4,5},{5,6},{8,9},{9,10},{12,13},{13,14},{16,17},{17,1... | collective-permute-start | bytes 3145736 | tf_op jit(solution)/shard_map/ppermute | solution.py:632
  180.5 19.6 %collective-permute-start.13 = (bf16[1024,512]{1,0:T(8,128)(2,1)S(1)}, bf16[1024,512]{1,0:T(8,128)(2,1)S(1)}, u32[]{:S(2)}, u32[]{:S(2)}) collective-permute-start(bf16[1024,512]{1,0:T(8,128)(2,1)S(1)} %get-tuple-element.475), channel_id=1, source_target_pairs={{2,1},{3,2},{6,5},{7,6},{10,9},{11,10},{14,13},{15,14},{18,17},{19... | collective-permute-start | bytes 3145736 | tf_op jit(solution)/shard_map/ppermute | solution.py:633
  181.2 18.8 %collective-permute-start.14 = (bf16[1024,512]{1,0:T(8,128)(2,1)}, bf16[1024,512]{1,0:T(8,128)(2,1)S(1)}, u32[]{:S(2)}, u32[]{:S(2)}) collective-permute-start(bf16[1024,512]{1,0:T(8,128)(2,1)} %collective-permute-done.10), channel_id=1, source_target_pairs={{2,3},{6,7},{10,11},{14,15},{18,19},{22,23},{26,27},{30,31}} | collective-permute-start | bytes 3145736 | tf_op jit(solution)/shard_map/ppermute | solution.py:589
  182.0 24.0 %collective-permute-start.15 = (bf16[1024,512]{1,0:T(8,128)(2,1)}, bf16[1024,512]{1,0:T(8,128)(2,1)S(1)}, u32[]{:S(2)}, u32[]{:S(2)}) collective-permute-start(bf16[1024,512]{1,0:T(8,128)(2,1)} %collective-permute-done.11), channel_id=1, source_target_pairs={{1,0},{5,4},{9,8},{13,12},{17,16},{21,20},{25,24},{29,28}} | collective-permute-start | bytes 3145736 | tf_op jit(solution)/shard_map/ppermute | solution.py:590
  207.3 20.5 %collective-permute-start.16 = (bf16[1024,512]{1,0:T(8,128)(2,1)}, bf16[1024,512]{1,0:T(8,128)(2,1)}, u32[]{:S(2)}, u32[]{:S(2)}) collective-permute-start(bf16[1024,512]{1,0:T(8,128)(2,1)} %add_convert_fusion.13), channel_id=1, source_target_pairs={{0,1},{1,2},{2,3},{4,5},{5,6},{6,7},{8,9},{9,10},{10,11},{12,13},{... | collective-permute-start | bytes 3145736 | tf_op jit(solution)/shard_map/ppermute | solution.py:632
  211.3 22.9 %collective-permute-start.17 = (bf16[1024,512]{1,0:T(8,128)(2,1)}, bf16[1024,512]{1,0:T(8,128)(2,1)}, u32[]{:S(2)}, u32[]{:S(2)}) collective-permute-start(bf16[1024,512]{1,0:T(8,128)(2,1)} %add_convert_fusion.12), channel_id=1, source_target_pairs={{1,0},{2,1},{3,2},{5,4},{6,5},{7,6},{9,8},{10,9},{11,10},{13,12},{... | collective-permute-start | bytes 3145736 | tf_op jit(solution)/shard_map/ppermute | solution.py:633
  238.9 91.1 %all-gather.8.cloned.1.call-start = ((), (), s32[]{:S(2)}) async-start(), calls=%async_computation.5 | async-start | bytes 2621440 | tf_op jit(solution)/shard_map/all_gather | solution.py:666
  263.1 112.2 %reduce-scatter.5.cloned.1.call-start = ((), (), s32[]{:S(2)}) async-start(), calls=%async_computation.7 | async-start | bytes 2621440 | tf_op jit(solution)/shard_map/reduce_scatter | solution.py:670
  330.0 90.8 %reduce-scatter.7.cloned.1.call-start = ((), (), s32[]{:S(2)}) async-start(), calls=%async_computation.8 | async-start | bytes 2621440 | tf_op jit(solution)/shard_map/reduce_scatter | solution.py:670
  375.3 21.2 %collective-permute-start.18 = (bf16[2,2064,256]{2,1,0:T(8,128)(2,1)}, bf16[2,2064,256]{2,1,0:T(8,128)(2,1)}, u32[]{:S(2)}, u32[]{:S(2)}) collective-permute-start(bf16[2,2064,256]{2,1,0:T(8,128)(2,1)} %get-tuple-element.307), channel_id=1, source_target_pairs={{0,4},{4,0},{8,12},{12,8},{16,20},{20,16},{24,28},{28,24},{1,5},{5... | collective-permute-start | bytes 6340616 | tf_op jit(solution)/shard_map/ppermute | solution.py:431
  375.4 95.9 %all-gather.12.cloned.1.call-start = ((), (), s32[]{:S(2)}) async-start(), calls=%async_computation.9 | async-start | bytes 2621440 | tf_op jit(solution)/shard_map/all_gather | solution.py:666
  375.8 25.1 %collective-permute-start.19 = (bf16[2,2064,256]{2,1,0:T(8,128)(2,1)}, bf16[2,2064,256]{2,1,0:T(8,128)(2,1)}, u32[]{:S(2)}, u32[]{:S(2)}) collective-permute-start(bf16[2,2064,256]{2,1,0:T(8,128)(2,1)} %get-tuple-element.309), channel_id=1, source_target_pairs={{0,4},{4,0},{8,12},{12,8},{16,20},{20,16},{24,28},{28,24},{1,5},{5... | collective-permute-start | bytes 6340616 | tf_op jit(solution)/shard_map/ppermute | solution.py:431
  376.4 28.2 %collective-permute-start.20 = (bf16[2,2064,256]{2,1,0:T(8,128)(2,1)}, bf16[2,2064,256]{2,1,0:T(8,128)(2,1)}, u32[]{:S(2)}, u32[]{:S(2)}) collective-permute-start(bf16[2,2064,256]{2,1,0:T(8,128)(2,1)} %get-tuple-element.311), channel_id=1, source_target_pairs={{0,4},{4,0},{8,12},{12,8},{16,20},{20,16},{24,28},{28,24},{1,5},{5... | collective-permute-start | bytes 6340616 | tf_op jit(solution)/shard_map/ppermute | solution.py:431
  376.5 31.7 %collective-permute-start.21 = (bf16[2,2064,256]{2,1,0:T(8,128)(2,1)}, bf16[2,2064,256]{2,1,0:T(8,128)(2,1)S(1)}, u32[]{:S(2)}, u32[]{:S(2)}) collective-permute-start(bf16[2,2064,256]{2,1,0:T(8,128)(2,1)} %get-tuple-element.313), channel_id=1, source_target_pairs={{0,4},{4,0},{8,12},{12,8},{16,20},{20,16},{24,28},{28,24},{1,5},{5... | collective-permute-start | bytes 6340616 | tf_op jit(solution)/shard_map/ppermute | solution.py:431
  420.8 95.2 %all-gather.14.cloned.1.call-start = ((), (), s32[]{:S(2)}) async-start(), calls=%async_computation.11 | async-start | bytes 2621440 | tf_op jit(solution)/shard_map/all_gather | solution.py:666
  422.2 47.9 %collective-permute-start.22 = (bf16[2,2064,256]{2,1,0:T(8,128)(2,1)}, bf16[2,2064,256]{2,1,0:T(8,128)(2,1)}, u32[]{:S(2)}, u32[]{:S(2)}) collective-permute-start(bf16[2,2064,256]{2,1,0:T(8,128)(2,1)} %add_convert_fusion.3), channel_id=1, source_target_pairs={{0,8},{4,12},{8,0},{12,4},{16,24},{20,28},{24,16},{28,20},{1,9},{5... | collective-permute-start | bytes 6340616 | tf_op jit(solution)/shard_map/ppermute | solution.py:431
  423.6 47.6 %collective-permute-start.23 = (bf16[2,2064,256]{2,1,0:T(8,128)(2,1)}, bf16[2,2064,256]{2,1,0:T(8,128)(2,1)}, u32[]{:S(2)}, u32[]{:S(2)}) collective-permute-start(bf16[2,2064,256]{2,1,0:T(8,128)(2,1)} %add_convert_fusion.2), channel_id=1, source_target_pairs={{0,16},{4,20},{8,24},{12,28},{16,0},{20,4},{24,8},{28,12},{1,17},{... | collective-permute-start | bytes 6340616 | tf_op jit(solution)/shard_map/ppermute | solution.py:431
  471.3 134.0 %reduce-scatter.9.cloned.1.call-start = ((), (), s32[]{:S(2)}) async-start(), calls=%async_computation.10 | async-start | bytes 5242880 | tf_op jit(solution)/shard_map/reduce_scatter | solution.py:670
  474.4 24.0 %collective-permute-start.24 = (bf16[1,2064,256]{2,1,0:T(8,128)(2,1)}, bf16[1,2064,256]{2,1,0:T(8,128)(2,1)}, u32[]{:S(2)}, u32[]{:S(2)}) collective-permute-start(bf16[1,2064,256]{2,1,0:T(8,128)(2,1)} %add_convert_fusion.10), channel_id=1, source_target_pairs={{0,16},{4,20},{8,24},{12,28},{16,0},{20,4},{24,8},{28,12},{1,17},{... | collective-permute-start | bytes 3170312 | tf_op jit(solution)/shard_map/ppermute | solution.py:431
  478.9 24.1 %collective-permute-start.25 = (bf16[1,2064,256]{2,1,0:T(8,128)(2,1)}, bf16[1,2064,256]{2,1,0:T(8,128)(2,1)}, u32[]{:S(2)}, u32[]{:S(2)}) collective-permute-start(bf16[1,2064,256]{2,1,0:T(8,128)(2,1)} %add_convert_fusion.7), channel_id=1, source_target_pairs={{0,8},{4,12},{8,0},{12,4},{16,24},{20,28},{24,16},{28,20},{1,9},{5... | collective-permute-start | bytes 3170312 | tf_op jit(solution)/shard_map/ppermute | solution.py:431
  484.7 207.3 %reduce-scatter.11.cloned.1.call-start = ((), (), s32[]{:S(2)}) async-start(), calls=%async_computation.12 | async-start | bytes 5242880 | tf_op jit(solution)/shard_map/reduce_scatter | solution.py:670
  501.5 30.1 %collective-permute-start.26 = (bf16[1,2064,256]{2,1,0:T(8,128)(2,1)}, bf16[1,2064,256]{2,1,0:T(8,128)(2,1)}, u32[]{:S(2)}, u32[]{:S(2)}) collective-permute-start(bf16[1,2064,256]{2,1,0:T(8,128)(2,1)} %add_convert_fusion.9.refs_0_), channel_id=1, source_target_pairs={{0,16},{4,20},{8,24},{12,28},{16,0},{20,4},{24,8},{28,12},{1,17},{... | collective-permute-start | bytes 3170312 | tf_op jit(solution)/shard_map/ppermute | solution.py:431
  506.1 26.6 %collective-permute-start.27 = (bf16[1,2064,256]{2,1,0:T(8,128)(2,1)}, bf16[1,2064,256]{2,1,0:T(8,128)(2,1)}, u32[]{:S(2)}, u32[]{:S(2)}) collective-permute-start(bf16[1,2064,256]{2,1,0:T(8,128)(2,1)} %add_convert_fusion.6.refs_8_), channel_id=1, source_target_pairs={{0,8},{4,12},{8,0},{12,4},{16,24},{20,28},{24,16},{28,20},{1,9},{5... | collective-permute-start | bytes 3170312 | tf_op jit(solution)/shard_map/ppermute | solution.py:431
  516.0 35.5 %collective-permute-start.28 = (bf16[1,2064,256]{2,1,0:T(8,128)(2,1)}, bf16[1,2064,256]{2,1,0:T(8,128)(2,1)S(1)}, u32[]{:S(2)}, u32[]{:S(2)}) collective-permute-start(bf16[1,2064,256]{2,1,0:T(8,128)(2,1)} %add_convert_fusion.9.refs_0_), channel_id=1, source_target_pairs={{0,8},{4,12},{8,0},{12,4},{16,24},{20,28},{24,16},{28,20},{1,9},{5... | collective-permute-start | bytes 3170312 | tf_op jit(solution)/shard_map/ppermute | solution.py:431
  517.5 34.0 %collective-permute-start.29 = (bf16[1,2064,256]{2,1,0:T(8,128)(2,1)}, bf16[1,2064,256]{2,1,0:T(8,128)(2,1)S(1)}, u32[]{:S(2)}, u32[]{:S(2)}) collective-permute-start(bf16[1,2064,256]{2,1,0:T(8,128)(2,1)} %add_convert_fusion.6.refs_8_), channel_id=1, source_target_pairs={{0,16},{4,20},{8,24},{12,28},{16,0},{20,4},{24,8},{28,12},{1,17},{... | collective-permute-start | bytes 3170312 | tf_op jit(solution)/shard_map/ppermute | solution.py:431
  554.3 19.6 %collective-permute-start.34 = (f32[4,8,256]{2,1,0:T(8,128)S(1)}, f32[4,8,256]{2,1,0:T(8,128)S(1)}, u32[]{:S(2)}, u32[]{:S(2)}) collective-permute-start(f32[4,8,256]{2,1,0:T(8,128)S(1)} %add.361), channel_id=1, source_target_pairs={{0,8},{4,12},{8,0},{12,4},{16,24},{20,28},{24,16},{28,20},{1,9},{5... | collective-permute-start | bytes 98312 | tf_op jit(solution)/shard_map/ppermute | solution.py:309
  555.1 19.5 %collective-permute-start.31 = (bf16[4,160,128]{2,1,0:T(8,128)(2,1)S(1)}, bf16[4,160,128]{2,1,0:T(8,128)(2,1)S(1)}, u32[]{:S(2)}, u32[]{:S(2)}) collective-permute-start(bf16[4,160,128]{2,1,0:T(8,128)(2,1)S(1)} %fusion.38), channel_id=1, source_target_pairs={{0,8},{4,12},{8,0},{12,4},{16,24},{20,28},{24,16},{28,20},{1,9},{5... | collective-permute-start | bytes 491528 | tf_op jit(solution)/shard_map/ppermute | solution.py:309
  580.6 24.4 %collective-permute-start.39 = (bf16[1,2064,256]{2,1,0:T(8,128)(2,1)}, bf16[1,2064,256]{2,1,0:T(8,128)(2,1)}, u32[]{:S(2)}, u32[]{:S(2)}) collective-permute-start(bf16[1,2064,256]{2,1,0:T(8,128)(2,1)} %collective-permute-done.26.refs_1_), channel_id=1, source_target_pairs={{0,8},{4,12},{8,0},{12,4},{16,24},{20,28},{24,16},{28,20},{1,9},{5... | collective-permute-start | bytes 3170312 | tf_op jit(solution)/shard_map/ppermute | solution.py:431
  581.2 24.0 %collective-permute-start.40 = (bf16[1,2064,256]{2,1,0:T(8,128)(2,1)}, bf16[1,2064,256]{2,1,0:T(8,128)(2,1)}, u32[]{:S(2)}, u32[]{:S(2)}) collective-permute-start(bf16[1,2064,256]{2,1,0:T(8,128)(2,1)} %collective-permute-done.27.refs_9_), channel_id=1, source_target_pairs={{0,16},{4,20},{8,24},{12,28},{16,0},{20,4},{24,8},{28,12},{1,17},{... | collective-permute-start | bytes 3170312 | tf_op jit(solution)/shard_map/ppermute | solution.py:431
  589.2 10.8 %collective-permute-start.36 = (f32[8,128]{1,0:T(8,128)S(1)}, f32[8,128]{1,0:T(8,128)S(1)}, u32[]{:S(2)}, u32[]{:S(2)}) collective-permute-start(f32[8,128]{1,0:T(8,128)S(1)} %add_bitcast_fusion), channel_id=1, source_target_pairs={{0,1},{1,2},{2,3},{3,0},{4,5},{5,6},{6,7},{7,4},{8,9},{9,10},{10,1... | collective-permute-start | bytes 12296 | tf_op jit(solution)/shard_map/ppermute | solution.py:551
  589.3 10.7 %collective-permute-start.37 = (f32[8,128]{1,0:T(8,128)S(1)}, f32[8,128]{1,0:T(8,128)S(1)}, u32[]{:S(2)}, u32[]{:S(2)}) collective-permute-start(f32[8,128]{1,0:T(8,128)S(1)} %add_bitcast_fusion), channel_id=1, source_target_pairs={{0,2},{1,3},{2,0},{3,1},{4,6},{5,7},{6,4},{7,5},{8,10},{9,11},{10,... | collective-permute-start | bytes 12296 | tf_op jit(solution)/shard_map/ppermute | solution.py:551
  592.3 7.7 %collective-permute-start.38 = (f32[8,128]{1,0:T(8,128)S(1)}, f32[8,128]{1,0:T(8,128)S(1)}, u32[]{:S(2)}, u32[]{:S(2)}) collective-permute-start(f32[8,128]{1,0:T(8,128)S(1)} %add_bitcast_fusion), channel_id=1, source_target_pairs={{0,3},{1,0},{2,1},{3,2},{4,7},{5,4},{6,5},{7,6},{8,11},{9,8},{10,9... | collective-permute-start | bytes 12296 | tf_op jit(solution)/shard_map/ppermute | solution.py:551
  615.6 8.9 %collective-permute-start.45 = (bf16[1,2064,256]{2,1,0:T(8,128)(2,1)}, bf16[1,2064,256]{2,1,0:T(8,128)(2,1)S(1)}, u32[]{:S(2)}, u32[]{:S(2)}) collective-permute-start(bf16[1,2064,256]{2,1,0:T(8,128)(2,1)} %add_convert_fusion.9.refs_0_), channel_id=1, source_target_pairs={{0,4},{4,0},{8,12},{12,8},{16,20},{20,16},{24,28},{28,24},{1,5},{5... | collective-permute-start | bytes 3170312 | tf_op jit(solution)/shard_map/ppermute | solution.py:431
  615.7 9.2 %collective-permute-start.46 = (bf16[1,2064,256]{2,1,0:T(8,128)(2,1)}, bf16[1,2064,256]{2,1,0:T(8,128)(2,1)S(1)}, u32[]{:S(2)}, u32[]{:S(2)}) collective-permute-start(bf16[1,2064,256]{2,1,0:T(8,128)(2,1)} %collective-permute-done.26.refs_1_), channel_id=1, source_target_pairs={{0,4},{4,0},{8,12},{12,8},{16,20},{20,16},{24,28},{28,24},{1,5},{5... | collective-permute-start | bytes 3170312 | tf_op jit(solution)/shard_map/ppermute | solution.py:431
  616.1 9.0 %collective-permute-start.47 = (bf16[1,2064,256]{2,1,0:T(8,128)(2,1)S(1)}, bf16[1,2064,256]{2,1,0:T(8,128)(2,1)S(1)}, u32[]{:S(2)}, u32[]{:S(2)}) collective-permute-start(bf16[1,2064,256]{2,1,0:T(8,128)(2,1)S(1)} %copy-done.43), channel_id=1, source_target_pairs={{0,4},{4,0},{8,12},{12,8},{16,20},{20,16},{24,28},{28,24},{1,5},{5... | collective-permute-start | bytes 3170312 | tf_op jit(solution)/shard_map/ppermute | solution.py:431
  617.3 6.2 collective-permute-start.43
  623.5 11.9 %collective-permute-start.48 = (bf16[1,2064,256]{2,1,0:T(8,128)(2,1)}, bf16[1,2064,256]{2,1,0:T(8,128)(2,1)}, u32[]{:S(2)}, u32[]{:S(2)}) collective-permute-start(bf16[1,2064,256]{2,1,0:T(8,128)(2,1)} %collective-permute-done.39.refs_3_), channel_id=1, source_target_pairs={{0,4},{4,0},{8,12},{12,8},{16,20},{20,16},{24,28},{28,24},{1,5},{5... | collective-permute-start | bytes 3170312 | tf_op jit(solution)/shard_map/ppermute | solution.py:431
  624.4 11.1 %collective-permute-start.49 = (bf16[1,2064,256]{2,1,0:T(8,128)(2,1)}, bf16[1,2064,256]{2,1,0:T(8,128)(2,1)}, u32[]{:S(2)}, u32[]{:S(2)}) collective-permute-start(bf16[1,2064,256]{2,1,0:T(8,128)(2,1)} %add_convert_fusion.6.refs_8_), channel_id=1, source_target_pairs={{0,4},{4,0},{8,12},{12,8},{16,20},{20,16},{24,28},{28,24},{1,5},{5... | collective-permute-start | bytes 3170312 | tf_op jit(solution)/shard_map/ppermute | solution.py:431
  624.5 10.9 %collective-permute-start.50 = (bf16[1,2064,256]{2,1,0:T(8,128)(2,1)}, bf16[1,2064,256]{2,1,0:T(8,128)(2,1)}, u32[]{:S(2)}, u32[]{:S(2)}) collective-permute-start(bf16[1,2064,256]{2,1,0:T(8,128)(2,1)} %collective-permute-done.27.refs_9_), channel_id=1, source_target_pairs={{0,4},{4,0},{8,12},{12,8},{16,20},{20,16},{24,28},{28,24},{1,5},{5... | collective-permute-start | bytes 3170312 | tf_op jit(solution)/shard_map/ppermute | solution.py:431
  624.9 10.6 %collective-permute-start.51 = (bf16[1,2064,256]{2,1,0:T(8,128)(2,1)S(1)}, bf16[1,2064,256]{2,1,0:T(8,128)(2,1)}, u32[]{:S(2)}, u32[]{:S(2)}) collective-permute-start(bf16[1,2064,256]{2,1,0:T(8,128)(2,1)S(1)} %copy-done.45), channel_id=1, source_target_pairs={{0,4},{4,0},{8,12},{12,8},{16,20},{20,16},{24,28},{28,24},{1,5},{5... | collective-permute-start | bytes 3170312 | tf_op jit(solution)/shard_map/ppermute | solution.py:431
  626.2 9.2 %collective-permute-start.52 = (bf16[1,2064,256]{2,1,0:T(8,128)(2,1)}, bf16[1,2064,256]{2,1,0:T(8,128)(2,1)S(1)}, u32[]{:S(2)}, u32[]{:S(2)}) collective-permute-start(bf16[1,2064,256]{2,1,0:T(8,128)(2,1)} %collective-permute-done.40.refs_11_), channel_id=1, source_target_pairs={{0,4},{4,0},{8,12},{12,8},{16,20},{20,16},{24,28},{28,24},{1,5},{5... | collective-permute-start | bytes 3170312 | tf_op jit(solution)/shard_map/ppermute | solution.py:431
  635.5 15.7 %collective-permute-start.53 = (bf16[2,576,256]{2,1,0:T(8,128)(2,1)}, bf16[2,576,256]{2,1,0:T(8,128)(2,1)S(1)}, u32[]{:S(2)}, u32[]{:S(2)}) collective-permute-start(bf16[2,576,256]{2,1,0:T(8,128)(2,1)} %get-tuple-element.382), channel_id=1, source_target_pairs={{0,8},{4,12},{8,0},{12,4},{16,24},{20,28},{24,16},{28,20},{1,9},{5... | collective-permute-start | bytes 1769480 | tf_op jit(solution)/shard_map/ppermute | solution.py:431
  637.0 15.3 %collective-permute-start.54 = (bf16[2,576,256]{2,1,0:T(8,128)(2,1)}, bf16[2,576,256]{2,1,0:T(8,128)(2,1)S(1)}, u32[]{:S(2)}, u32[]{:S(2)}) collective-permute-start(bf16[2,576,256]{2,1,0:T(8,128)(2,1)} %get-tuple-element.383), channel_id=1, source_target_pairs={{0,16},{4,20},{8,24},{12,28},{16,0},{20,4},{24,8},{28,12},{1,17},{... | collective-permute-start | bytes 1769480 | tf_op jit(solution)/shard_map/ppermute | solution.py:431
  652.5 11.7 %collective-permute-start.55 = (bf16[1,576,256]{2,1,0:T(8,128)(2,1)S(1)}, bf16[1,576,256]{2,1,0:T(8,128)(2,1)S(1)}, u32[]{:S(2)}, u32[]{:S(2)}) collective-permute-start(bf16[1,576,256]{2,1,0:T(8,128)(2,1)S(1)} %get-tuple-element.480), channel_id=1, source_target_pairs={{0,16},{4,20},{8,24},{12,28},{16,0},{20,4},{24,8},{28,12},{1,17},{... | collective-permute-start | bytes 884744 | tf_op jit(solution)/shard_map/ppermute | solution.py:431
  654.2 10.0 %collective-permute-start.56 = (bf16[1,576,256]{2,1,0:T(8,128)(2,1)S(1)}, bf16[1,576,256]{2,1,0:T(8,128)(2,1)S(1)}, u32[]{:S(2)}, u32[]{:S(2)}) collective-permute-start(bf16[1,576,256]{2,1,0:T(8,128)(2,1)S(1)} %get-tuple-element.478), channel_id=1, source_target_pairs={{0,8},{4,12},{8,0},{12,4},{16,24},{20,28},{24,16},{28,20},{1,9},{5... | collective-permute-start | bytes 884744 | tf_op jit(solution)/shard_map/ppermute | solution.py:431
  664.3 7.5 %collective-permute-start.57 = (bf16[1,576,256]{2,1,0:T(8,128)(2,1)S(1)}, bf16[1,576,256]{2,1,0:T(8,128)(2,1)S(1)}, u32[]{:S(2)}, u32[]{:S(2)}) collective-permute-start(bf16[1,576,256]{2,1,0:T(8,128)(2,1)S(1)} %add_convert_fusion.17.refs_0_), channel_id=1, source_target_pairs={{0,16},{4,20},{8,24},{12,28},{16,0},{20,4},{24,8},{28,12},{1,17},{... | collective-permute-start | bytes 884744 | tf_op jit(solution)/shard_map/ppermute | solution.py:431
  665.0 7.3 %collective-permute-start.58 = (bf16[1,576,256]{2,1,0:T(8,128)(2,1)S(1)}, bf16[1,576,256]{2,1,0:T(8,128)(2,1)S(1)}, u32[]{:S(2)}, u32[]{:S(2)}) collective-permute-start(bf16[1,576,256]{2,1,0:T(8,128)(2,1)S(1)} %add_convert_fusion.16.refs_8_), channel_id=1, source_target_pairs={{0,8},{4,12},{8,0},{12,4},{16,24},{20,28},{24,16},{28,20},{1,9},{5... | collective-permute-start | bytes 884744 | tf_op jit(solution)/shard_map/ppermute | solution.py:431
  672.4 13.2 %collective-permute-start.59 = (bf16[1,576,256]{2,1,0:T(8,128)(2,1)S(1)}, bf16[1,576,256]{2,1,0:T(8,128)(2,1)S(1)}, u32[]{:S(2)}, u32[]{:S(2)}) collective-permute-start(bf16[1,576,256]{2,1,0:T(8,128)(2,1)S(1)} %add_convert_fusion.17.refs_0_), channel_id=1, source_target_pairs={{0,8},{4,12},{8,0},{12,4},{16,24},{20,28},{24,16},{28,20},{1,9},{5... | collective-permute-start | bytes 884744 | tf_op jit(solution)/shard_map/ppermute | solution.py:431
  673.7 11.9 %collective-permute-start.60 = (bf16[1,576,256]{2,1,0:T(8,128)(2,1)S(1)}, bf16[1,576,256]{2,1,0:T(8,128)(2,1)S(1)}, u32[]{:S(2)}, u32[]{:S(2)}) collective-permute-start(bf16[1,576,256]{2,1,0:T(8,128)(2,1)S(1)} %collective-permute-done.57.refs_1_), channel_id=1, source_target_pairs={{0,8},{4,12},{8,0},{12,4},{16,24},{20,28},{24,16},{28,20},{1,9},{5... | collective-permute-start | bytes 884744 | tf_op jit(solution)/shard_map/ppermute | solution.py:431
  674.4 11.2 %collective-permute-start.61 = (bf16[1,576,256]{2,1,0:T(8,128)(2,1)S(1)}, bf16[1,576,256]{2,1,0:T(8,128)(2,1)S(1)}, u32[]{:S(2)}, u32[]{:S(2)}) collective-permute-start(bf16[1,576,256]{2,1,0:T(8,128)(2,1)S(1)} %add_convert_fusion.16.refs_8_), channel_id=1, source_target_pairs={{0,16},{4,20},{8,24},{12,28},{16,0},{20,4},{24,8},{28,12},{1,17},{... | collective-permute-start | bytes 884744 | tf_op jit(solution)/shard_map/ppermute | solution.py:431
  675.7 10.9 %collective-permute-start.62 = (bf16[1,576,256]{2,1,0:T(8,128)(2,1)S(1)}, bf16[1,576,256]{2,1,0:T(8,128)(2,1)S(1)}, u32[]{:S(2)}, u32[]{:S(2)}) collective-permute-start(bf16[1,576,256]{2,1,0:T(8,128)(2,1)S(1)} %collective-permute-done.58.refs_9_), channel_id=1, source_target_pairs={{0,16},{4,20},{8,24},{12,28},{16,0},{20,4},{24,8},{28,12},{1,17},{... | collective-permute-start | bytes 884744 | tf_op jit(solution)/shard_map/ppermute | solution.py:431
  697.2 11.6 %collective-permute-start.74 = (f32[2,512]{1,0:T(2,128)S(1)}, f32[2,512]{1,0:T(2,128)S(1)}, u32[]{:S(2)}, u32[]{:S(2)}) collective-permute-start(f32[2,512]{1,0:T(2,128)S(1)} %fusion.48), channel_id=1, source_target_pairs={{0,24},{4,28},{8,16},{12,20},{16,8},{20,12},{24,0},{28,4},{1,25},{... | collective-permute-start | bytes 12296 | tf_op jit(solution)/shard_map/ppermute | solution.py:431
  699.3 9.5 %collective-permute-start.72 = (f32[2,512]{1,0:T(2,128)S(1)}, f32[2,512]{1,0:T(2,128)S(1)}, u32[]{:S(2)}, u32[]{:S(2)}) collective-permute-start(f32[2,512]{1,0:T(2,128)S(1)} %fusion.48), channel_id=1, source_target_pairs={{0,8},{4,12},{8,0},{12,4},{16,24},{20,28},{24,16},{28,20},{1,9},{5... | collective-permute-start | bytes 12296 | tf_op jit(solution)/shard_map/ppermute | solution.py:431
  699.9 8.9 %collective-permute-start.73 = (f32[2,512]{1,0:T(2,128)S(1)}, f32[2,512]{1,0:T(2,128)S(1)}, u32[]{:S(2)}, u32[]{:S(2)}) collective-permute-start(f32[2,512]{1,0:T(2,128)S(1)} %fusion.48), channel_id=1, source_target_pairs={{0,16},{4,20},{8,24},{12,28},{16,0},{20,4},{24,8},{28,12},{1,17},{... | collective-permute-start | bytes 12296 | tf_op jit(solution)/shard_map/ppermute | solution.py:431
  (150 other events, 1378.3 us)
Sparse Core Ops, SparseCore 0:
  9.6 83.5 all-gather.5
  239.0 44.1 all-gather.9
  285.3 44.6 all-gather.7
  332.7 42.5 reduce-scatter.4
  377.6 43.1 reduce-scatter.6
  422.8 45.2 all-gather.11
  471.4 44.5 all-gather.13
  518.9 75.5 reduce-scatter.8
  605.4 76.7 reduce-scatter.10

commit v6 on v5

--- a/solution.py
+++ b/solution.py
@@ -493,6 +493,16 @@
 def place_body(blocks, table, *refs, outs, count):
     step = pl.program_id(0)
     pieces = count
+    if len(outs) == 1 and len(outs[0][2]) == 1 and not outs[0][2][0][3]:
+        used = outs[0][1] // 2
+        for n in range(2):
+            for m in range(pieces):
+
+                @pl.when(table[n, step] == m)
+                def _():
+                    refs[-1][n * used : (n + 1) * used, :] = refs[n * pieces + m][0, :used, :].astype(F32)
+
+        return
     chosen = []
     for n in range(2):
         which = table[n, step]

time: 726 us -> 726 us (level)
  no operation moved by 1% of the time
where the time goes in v6:
time: 726 us; the launch traced here: 716 us
  waiting for transfers between devices  279 us (38%)
  Pallas kernels  137 us (19%)
  matrix products  85.1 us (12%)
  other arithmetic  82.4 us (11%)
  starting transfers between devices  71.7 us (10%)
  local copies, waits for them, and re-layouts  29.7 us (4%)
  between operations  16.6 us (2%)
  blocking collectives  14.9 us (2%)
    all_gather x5, waiting for transfers between devices, widen(): return lax.all_gather(part, 'tensor', axis=1, tiled=True)  110 us
    ppermute x48, waiting for transfers between devices, flip(): lax.ppermute(value, 'batch', [(i, i ^ bit) for i in range(lax.axis_size('...  81.4 us
    pallas_call x4, Pallas kernels, grad_blocks(): pl.pallas_call(functools.partial(grad_body, groups=tuple(kinds), summed=b...  53.3 us
    dot_general x9, matrix products, project_back(): return jnp.einsum('ti,ji->tj', left, right, preferred_element_type=F32)  45.2 us
    ppermute x3, waiting for transfers between devices, hop(): lax.ppermute(sends[0], 'tensor', [(k, k + 1) for k in range(0, count - se...  44 us
    pallas_call x6, Pallas kernels, call(): pl.pallas_call(body, grid=(self.heads,), in_specs=in_specs, out_specs=out...  42.7 us
    pallas_call x4, Pallas kernels, place_blocks(): pl.pallas_call(functools.partial(place_body, outs=tuple(layout), count=co...  34.9 us
    ppermute x48, starting transfers between devices, flip(): lax.ppermute(value, 'batch', [(i, i ^ bit) for i in range(lax.axis_size('...  32 us
  transfers between devices with their start and end apart: 84, of which 40 were waited for; matrix products, arithmetic and copies ran while one was open for 22% of the time, Pallas kernels for 19%

profile of v6, /device:TPU:0, one launch (start us, length us, event | category | flops | bytes accessed | tf_op | source)
XLA Modules:
  0.0 716.1 jit_solution(3418905893725673651)
XLA Ops:
  15.0 14.9 %all_gather.19 = f32[2,2048]{1,0:T(2,128)S(1)} all-gather(f32[2,512]{1,0:T(2,128)S(1)} %pad_maximum_fusion.3), channel_id=1, replica_groups=mesh['batch'=8,'tensor'=4] {'tensor'}, dimensions={1}, use_global_device_ids=true | all-gather | bytes 20480 | tf_op jit(solution)/shard_map/all_gather | solution.py:728
  32.2 4.1 pad_maximum_fusion.2
  36.3 56.9 %all-gather.6.cloned.1.call-done = bf16[1024,2048]{1,0:T(8,128)(2,1)} async-done(((bf16[1024,512]{1,0:T(8,128)(2,1)}), bf16[1024,2048]{1,0:T(8,128)(2,1)}) %all-gather.6.cloned.1.call-update) | async-done | bytes 4194320 | tf_op jit(solution)/shard_map/all_gather | solution.py:676
  93.2 3.2 fusion
  100.6 2.7 convolution_convert_fusion.4
  104.1 3.2 mix_state.1
  117.0 5.8 mix_inner.1
  128.5 3.1 collective-permute-done.2
  131.6 5.8 mix_merge.1
  140.7 5.2 collective-permute-start.8
  152.8 13.5 %collective-permute-done.8 = bf16[1024,512]{1,0:T(8,128)(2,1)} collective-permute-done((bf16[1024,512]{1,0:T(8,128)(2,1)}, bf16[1024,512]{1,0:T(8,128)(2,1)}, u32[]{:S(2)}, u32[]{:S(2)}) %collective-permute-start.8) | collective-permute-done | bytes 1048608 | tf_op jit(solution)/shard_map/ppermute | solution.py:642
  166.4 9.4 %collective-permute-done.11 = bf16[1024,512]{1,0:T(8,128)(2,1)} collective-permute-done((bf16[1024,512]{1,0:T(8,128)(2,1)}, bf16[1024,512]{1,0:T(8,128)(2,1)}, u32[]{:S(2)}, u32[]{:S(2)}) %collective-permute-start.11) | collective-permute-done | bytes 1048608 | tf_op jit(solution)/shard_map/ppermute | solution.py:600
  183.3 16.8 %collective-permute-done.12 = bf16[1024,512]{1,0:T(8,128)(2,1)S(1)} collective-permute-done((bf16[1024,512]{1,0:T(8,128)(2,1)S(1)}, bf16[1024,512]{1,0:T(8,128)(2,1)S(1)}, u32[]{:S(2)}, u32[]{:S(2)}) %collective-permute-start.12) | collective-permute-done | bytes 1048608 | tf_op jit(solution)/shard_map/ppermute | solution.py:642
  200.1 5.9 collective-permute-done.15
  214.1 13.7 %collective-permute-done.16 = bf16[1024,512]{1,0:T(8,128)(2,1)} collective-permute-done((bf16[1024,512]{1,0:T(8,128)(2,1)}, bf16[1024,512]{1,0:T(8,128)(2,1)}, u32[]{:S(2)}, u32[]{:S(2)}) %collective-permute-start.16) | collective-permute-done | bytes 1048608 | tf_op jit(solution)/shard_map/ppermute | solution.py:642
  227.7 6.5 collective-permute-done.17
  244.7 5.6 straighten.1
  250.3 8.1 %convolution_bitcast_fusion.5 = f32[1376,512]{1,0:T(8,128)} fusion(bf16[1376,2048]{1,0:T(8,128)(2,1)} %param.39, bf16[1024,2048]{1,0:T(8,128)(2,1)} %straighten.1), kind=kOutput, calls=%fused_computation.41 | convolution fusion | flops 2885681152 | bytes 10551296 | tf_op jit(solution)/shard_map/ti,ji->tj/dot_general | solution.py:688
  258.4 4.7 convolution_bitcast_fusion.4
  263.4 19.8 %all-gather.10.cloned.1.call-done = bf16[512,2048]{1,0:T(8,128)(2,1)} async-done(((bf16[512,512]{1,0:T(8,128)(2,1)}), bf16[512,2048]{1,0:T(8,128)(2,1)}) %all-gather.10.cloned.1.call-update) | async-done | bytes 2097168 | tf_op jit(solution)/shard_map/all_gather | solution.py:676
  286.0 6.2 convolution_bitcast_fusion.2
  292.3 5.5 multiply_convert_fusion.3
  297.9 3.5 fusion.60
  301.4 4.6 add_convert_fusion.5
  306.0 24.0 %all-gather.8.cloned.1.call-done = bf16[512,2048]{1,0:T(8,128)(2,1)} async-done(((bf16[512,512]{1,0:T(8,128)(2,1)}), bf16[512,2048]{1,0:T(8,128)(2,1)}) %all-gather.8.cloned.1.call-update) | async-done | bytes 2097168 | tf_op jit(solution)/shard_map/all_gather | solution.py:676
  333.1 6.4 convolution_bitcast_fusion
  342.6 5.5 multiply_convert_fusion
  348.1 3.5 fusion.61
  351.7 4.7 add_convert_fusion.4
  356.4 18.0 %grad_ffn_far.1 = (bf16[2,2064,256]{2,1,0:T(8,128)(2,1)}, bf16[2,2064,256]{2,1,0:T(8,128)(2,1)}, bf16[2,2064,256]{2,1,0:T(8,128)(2,1)}, bf16[2,2064,256]{2,1,0:T(8,128)(2,1)}) custom-call(s32[4]{0:T(128)} %get-tuple-element.497.blocks, s32[5,4]{1,0:T(8,128)} %constant.83.clone.swap, bf16[512,2048]{1,0:T(8,128)(2,1)} %copy-done.72, ...), custom_call_target="tpu_custom_call" | custom-call | flops 16000000000 | bytes 1048576 | tf_op jit(solution)/shard_map/grad_ffn_far/pallas_call | solution.py:417
  376.9 18.1 %grad_ffn_near.1 = (bf16[2,2064,256]{2,1,0:T(8,128)(2,1)}, bf16[2,2064,256]{2,1,0:T(8,128)(2,1)}, bf16[2,2064,256]{2,1,0:T(8,128)(2,1)}, bf16[2,2064,256]{2,1,0:T(8,128)(2,1)}) custom-call(s32[4]{0:T(128)} %get-tuple-element.498.blocks, s32[5,4]{1,0:T(8,128)} %constant.83.clone.swap, bf16[512,2048]{1,0:T(8,128)(2,1)} %copy-done.72, ...), custom_call_target="tpu_custom_call" | custom-call | flops 16000000000 | bytes 1048576 | tf_op jit(solution)/shard_map/grad_ffn_near/pallas_call | solution.py:417
  397.2 3.6 add_convert_fusion.3
  400.9 3.7 add_convert_fusion.2
  404.6 3.6 add_convert_fusion.1
  410.1 10.7 %reduce-scatter.7.cloned.1.call-done = bf16[512,512]{1,0:T(8,128)(2,1)} async-done(((bf16[512,2048]{1,0:T(8,128)(2,1)}), bf16[512,512]{1,0:T(8,128)(2,1)}) %reduce-scatter.7.cloned.1.call-update) | async-done | bytes 524304 | tf_op jit(solution)/shard_map/reduce_scatter | solution.py:680
  427.4 8.3 %convolution_convert_fusion.2 = bf16[512,2048]{1,0:T(8,128)(2,1)} fusion(bf16[1376,512]{1,0:T(8,128)(2,1)} %get-tuple-element.293.refs_9_, bf16[1376,2048]{1,0:T(8,128)(2,1)} %param.39), kind=kOutput, calls=%fused_computation.46 | convolution fusion | flops 2886729728 | bytes 9142272 | tf_op jit(solution)/shard_map/it,ij->tj/dot_general | solution.py:692
  435.7 7.4 %convolution_convert_fusion.1 = bf16[512,2048]{1,0:T(8,128)(2,1)} fusion(bf16[1376,512]{1,0:T(8,128)(2,1)S(1)} %copy-done.117, bf16[1376,2048]{1,0:T(8,128)(2,1)} %param.39), kind=kOutput, calls=%fused_computation.45 | convolution fusion | flops 2886729728 | bytes 9142272 | tf_op jit(solution)/shard_map/it,ij->tj/dot_general | solution.py:692
  444.6 25.4 %collective-permute-done.22 = bf16[2,2064,256]{2,1,0:T(8,128)(2,1)} collective-permute-done((bf16[2,2064,256]{2,1,0:T(8,128)(2,1)}, bf16[2,2064,256]{2,1,0:T(8,128)(2,1)}, u32[]{:S(2)}, u32[]{:S(2)}) %collective-permute-start.22) | collective-permute-done | bytes 2113568 | tf_op jit(solution)/shard_map/ppermute | solution.py:431
  471.5 2.9 add_convert_fusion.10
  475.9 2.9 add_convert_fusion.7
  479.3 2.7 fusion.8
  484.7 2.9 fusion.3.refs_2_
  491.3 7.2 %collective-permute-done.24 = bf16[1,2064,256]{2,1,0:T(8,128)(2,1)} collective-permute-done((bf16[1,2064,256]{2,1,0:T(8,128)(2,1)}, bf16[1,2064,256]{2,1,0:T(8,128)(2,1)}, u32[]{:S(2)}, u32[]{:S(2)}) %collective-permute-start.24) | collective-permute-done | bytes 1056800 | tf_op jit(solution)/shard_map/ppermute | solution.py:431
  498.5 3.0 add_convert_fusion.9.refs_0_
  503.0 3.1 add_convert_fusion.6.refs_8_
  506.7 9.3 %all-gather.14.cloned.1.call-done = bf16[512,2048]{1,0:T(8,128)(2,1)} async-done(((bf16[512,512]{1,0:T(8,128)(2,1)}), bf16[512,2048]{1,0:T(8,128)(2,1)}) %all-gather.14.cloned.1.call-update) | async-done | bytes 2097168 | tf_op jit(solution)/shard_map/all_gather | solution.py:676
  518.9 3.7 fusion.12
  525.7 6.0 mix_pull_state.1
  532.7 18.8 %collective-permute-done.28.refs_2_ = bf16[1,2064,256]{2,1,0:T(8,128)(2,1)S(1)} collective-permute-done((bf16[1,2064,256]{2,1,0:T(8,128)(2,1)}, bf16[1,2064,256]{2,1,0:T(8,128)(2,1)S(1)}, u32[]{:S(2)}, u32[]{:S(2)}) %collective-permute-start.28) | collective-permute-done | bytes 1056800 | tf_op jit(solution)/shard_map/ppermute | solution.py:431
  556.6 16.0 %mix_pull_inner.1 = (bf16[1024,64]{1,0:T(8,128)(2,1)S(1)}, f32[1024,64]{1,0:T(8,128)S(1)}, f32[1024,512]{1,0:T(8,128)S(1)}) custom-call(bf16[1024,64]{1,0:T(8,128)(2,1)S(1)} %copy-done.16, bf16[1024,64]{1,0:T(8,128)(2,1)S(1)} %copy-done.14, bf16[1024,512]{1,0:T(8,128)(2,1)S(1)} %copy-done.5, s32[1024,1]{1,0:T(8,128)S(1)} %copy-done.2, ...), custom_call_target="tpu_custom_call" | custom-call | flops 20000000000 | bytes 1048576 | tf_op jit(solution)/shard_map/mix_pull_inner/pallas_call | solution.py:236
  582.6 6.0 mix_pull_carry.1
  589.3 3.0 collective-permute-start.37
  594.8 5.2 convolution_convert_fusion
  600.0 4.9 collective-permute-done.39.refs_3_
  606.8 8.3 %grad_mix_far.1 = (bf16[2,576,256]{2,1,0:T(8,128)(2,1)}, bf16[2,576,256]{2,1,0:T(8,128)(2,1)}, bf16[2,576,256]{2,1,0:T(8,128)(2,1)}, bf16[2,576,256]{2,1,0:T(8,128)(2,1)}) custom-call(s32[4]{0:T(128)} %get-tuple-element.497.blocks, s32[5,4]{1,0:T(8,128)} %constant.83.clone.swap, bf16[1024,2048]{1,0:T(8,128)(2,1)} %copy-done.55, bf16[640,1024]{1,0:T(8,128)(2,1)} %bitcast.91, ...), custom_call_target="tpu_custom_call" | custom-call | flops 5000000000 | bytes 1048576 | tf_op jit(solution)/shard_map/grad_mix_far/pallas_call | solution.py:417
  618.3 5.2 collective-permute-done.43.refs_8_
  626.6 8.9 %grad_mix_near.1 = (bf16[2,576,256]{2,1,0:T(8,128)(2,1)}, bf16[2,576,256]{2,1,0:T(8,128)(2,1)}, bf16[2,576,256]{2,1,0:T(8,128)(2,1)}, bf16[2,576,256]{2,1,0:T(8,128)(2,1)}) custom-call(s32[4]{0:T(128)} %get-tuple-element.498.blocks, s32[5,4]{1,0:T(8,128)} %constant.83.clone.swap, bf16[1024,2048]{1,0:T(8,128)(2,1)} %copy-done.55, bf16[640,1024]{1,0:T(8,128)(2,1)} %bitcast.92, ...), custom_call_target="tpu_custom_call" | custom-call | flops 5000000000 | bytes 1048576 | tf_op jit(solution)/shard_map/grad_mix_near/pallas_call | solution.py:417
  638.5 9.0 %place_ffn_0.1 = f32[1376,2048]{1,0:T(8,128)} custom-call(s32[8]{0:T(128)} %copy-done.93, s32[2,8]{1,0:T(2,128)} %constant.84.clone.table, bf16[1,2064,256]{2,1,0:T(8,128)(2,1)} %add_convert_fusion.9.refs_0_, bf16[1,2064,256]{2,1,0:T(8,128)(2,1)} %collective-permute-done.26.refs_1_, bf16[1,2064,256]{2,1,0:T(8,128)(2,1)} %copy-done.42, ...), custom_call_target="tpu_custom_call" | custom-call | flops 7000000000 | bytes 1048576 | tf_op jit(solution)/shard_map/place_ffn_0/pallas_call | solution.py:544
  647.4 3.8 collective-permute-done.53
  654.8 9.1 %place_ffn_1.1 = f32[1376,2048]{1,0:T(8,128)} custom-call(s32[8]{0:T(128)} %copy-done.93, s32[2,8]{1,0:T(2,128)} %constant.84.clone.table, bf16[1,2064,256]{2,1,0:T(8,128)(2,1)} %add_convert_fusion.9.refs_0_, bf16[1,2064,256]{2,1,0:T(8,128)(2,1)} %collective-permute-done.26.refs_1_, bf16[1,2064,256]{2,1,0:T(8,128)(2,1)} %copy-done.42, ...), custom_call_target="tpu_custom_call" | custom-call | flops 7000000000 | bytes 1048576 | tf_op jit(solution)/shard_map/place_ffn_1/pallas_call | solution.py:544
  667.6 3.9 collective-permute-done.57.refs_1_
  676.2 8.9 %place_ffn_2.1 = f32[1376,2048]{1,0:T(8,128)} custom-call(s32[8]{0:T(128)} %copy-done.93, s32[2,8]{1,0:T(2,128)} %constant.84.clone.table, bf16[1,2064,256]{2,1,0:T(8,128)(2,1)} %add_convert_fusion.9.refs_0_, bf16[1,2064,256]{2,1,0:T(8,128)(2,1)} %collective-permute-done.26.refs_1_, bf16[1,2064,256]{2,1,0:T(8,128)(2,1)} %copy-done.42, ...), custom_call_target="tpu_custom_call" | custom-call | flops 7000000000 | bytes 1048576 | tf_op jit(solution)/shard_map/place_ffn_2/pallas_call | solution.py:544
  691.7 3.9 fusion.18
  700.5 8.0 %place_mix.1 = (f32[64,2048]{1,0:T(8,128)}, f32[64,2048]{1,0:T(8,128)}, f32[2048,512]{1,0:T(8,128)}, f32[512,2048]{1,0:T(8,128)}) custom-call(s32[8]{0:T(128)} %copy-done.93, s32[2,8]{1,0:T(2,128)} %constant.84.clone.table, bf16[1,576,256]{2,1,0:T(8,128)(2,1)} %copy-done.85, bf16[1,576,256]{2,1,0:T(8,128)(2,1)} %copy-done.100, ...), custom_call_target="tpu_custom_call" | custom-call | flops 5000000000 | bytes 1048576 | tf_op jit(solution)/shard_map/place_mix/pallas_call | solution.py:544
  (504 shorter events, 161.0 us)
Async XLA Ops:
  7.2 86.0 %all-gather.6.cloned.1.call-start = ((), (), s32[]{:S(2)}) async-start(), calls=%async_computation.4 | async-start | bytes 5242880 | tf_op jit(solution)/shard_map/all_gather | solution.py:676
  8.0 275.2 %all-gather.10.cloned.1.call-start = ((), (), s32[]{:S(2)}) async-start(), calls=%async_computation.6 | async-start | bytes 2621440 | tf_op jit(solution)/shard_map/all_gather | solution.py:676
  108.0 31.5 %collective-permute-start.6 = (bf16[1024,512]{1,0:T(8,128)(2,1)}, bf16[1024,512]{1,0:T(8,128)(2,1)}, u32[]{:S(2)}, u32[]{:S(2)}) collective-permute-start(bf16[1024,512]{1,0:T(8,128)(2,1)} %param.40), channel_id=1, source_target_pairs={{0,1},{1,2},{2,3},{4,5},{5,6},{6,7},{8,9},{9,10},{10,11},{12,13},{... | collective-permute-start | bytes 3145736 | tf_op jit(solution)/shard_map/ppermute | solution.py:599
  110.4 29.1 %collective-permute-start.7 = (bf16[1024,512]{1,0:T(8,128)(2,1)}, bf16[1024,512]{1,0:T(8,128)(2,1)}, u32[]{:S(2)}, u32[]{:S(2)}) collective-permute-start(bf16[1024,512]{1,0:T(8,128)(2,1)} %param.40), channel_id=1, source_target_pairs={{1,0},{2,1},{3,2},{5,4},{6,5},{7,6},{9,8},{10,9},{11,10},{13,12},{... | collective-permute-start | bytes 3145736 | tf_op jit(solution)/shard_map/ppermute | solution.py:600
  111.7 12.4 %collective-permute-start.4 = (f32[4,8,256]{2,1,0:T(8,128)S(1)}, f32[4,8,256]{2,1,0:T(8,128)S(1)}, u32[]{:S(2)}, u32[]{:S(2)}) collective-permute-start(f32[4,8,256]{2,1,0:T(8,128)S(1)} %add.314), channel_id=1, source_target_pairs={{0,8},{4,12},{8,0},{12,4},{16,24},{20,28},{24,16},{28,20},{1,9},{5... | collective-permute-start | bytes 98312 | tf_op jit(solution)/shard_map/ppermute | solution.py:309
  113.3 12.4 %collective-permute-start.1 = (bf16[4,160,128]{2,1,0:T(8,128)(2,1)S(1)}, bf16[4,160,128]{2,1,0:T(8,128)(2,1)S(1)}, u32[]{:S(2)}, u32[]{:S(2)}) collective-permute-start(bf16[4,160,128]{2,1,0:T(8,128)(2,1)S(1)} %fusion.37), channel_id=1, source_target_pairs={{0,8},{4,12},{8,0},{12,4},{16,24},{20,28},{24,16},{28,20},{1,9},{5... | collective-permute-start | bytes 491528 | tf_op jit(solution)/shard_map/ppermute | solution.py:309
  140.7 25.6 %collective-permute-start.8 = (bf16[1024,512]{1,0:T(8,128)(2,1)}, bf16[1024,512]{1,0:T(8,128)(2,1)}, u32[]{:S(2)}, u32[]{:S(2)}) collective-permute-start(bf16[1024,512]{1,0:T(8,128)(2,1)} %convert_element_type.376), channel_id=1, source_target_pairs={{0,1},{4,5},{8,9},{12,13},{16,17},{20,21},{24,25},{28,29}} | collective-permute-start | bytes 3145736 | tf_op jit(solution)/shard_map/ppermute | solution.py:642
  147.1 19.3 %collective-permute-start.9 = (bf16[1024,512]{1,0:T(8,128)(2,1)}, bf16[1024,512]{1,0:T(8,128)(2,1)}, u32[]{:S(2)}, u32[]{:S(2)}) collective-permute-start(bf16[1024,512]{1,0:T(8,128)(2,1)} %convert_element_type.377), channel_id=1, source_target_pairs={{3,2},{7,6},{11,10},{15,14},{19,18},{23,22},{27,26},{31,30}} | collective-permute-start | bytes 3145736 | tf_op jit(solution)/shard_map/ppermute | solution.py:643
  148.7 17.7 %collective-permute-start.10 = (bf16[1024,512]{1,0:T(8,128)(2,1)}, bf16[1024,512]{1,0:T(8,128)(2,1)}, u32[]{:S(2)}, u32[]{:S(2)}) collective-permute-start(bf16[1024,512]{1,0:T(8,128)(2,1)} %collective-permute-done.6), channel_id=1, source_target_pairs={{1,2},{2,3},{5,6},{6,7},{9,10},{10,11},{13,14},{14,15},{17,18},{18... | collective-permute-start | bytes 3145736 | tf_op jit(solution)/shard_map/ppermute | solution.py:599
  150.3 25.5 %collective-permute-start.11 = (bf16[1024,512]{1,0:T(8,128)(2,1)}, bf16[1024,512]{1,0:T(8,128)(2,1)}, u32[]{:S(2)}, u32[]{:S(2)}) collective-permute-start(bf16[1024,512]{1,0:T(8,128)(2,1)} %collective-permute-done.7), channel_id=1, source_target_pairs={{1,0},{2,1},{5,4},{6,5},{9,8},{10,9},{13,12},{14,13},{17,16},{18,1... | collective-permute-start | bytes 3145736 | tf_op jit(solution)/shard_map/ppermute | solution.py:600
  178.0 22.1 %collective-permute-start.12 = (bf16[1024,512]{1,0:T(8,128)(2,1)S(1)}, bf16[1024,512]{1,0:T(8,128)(2,1)S(1)}, u32[]{:S(2)}, u32[]{:S(2)}) collective-permute-start(bf16[1024,512]{1,0:T(8,128)(2,1)S(1)} %get-tuple-element.476), channel_id=1, source_target_pairs={{0,1},{1,2},{4,5},{5,6},{8,9},{9,10},{12,13},{13,14},{16,17},{17,1... | collective-permute-start | bytes 3145736 | tf_op jit(solution)/shard_map/ppermute | solution.py:642
  180.5 19.6 %collective-permute-start.13 = (bf16[1024,512]{1,0:T(8,128)(2,1)S(1)}, bf16[1024,512]{1,0:T(8,128)(2,1)S(1)}, u32[]{:S(2)}, u32[]{:S(2)}) collective-permute-start(bf16[1024,512]{1,0:T(8,128)(2,1)S(1)} %get-tuple-element.475), channel_id=1, source_target_pairs={{2,1},{3,2},{6,5},{7,6},{10,9},{11,10},{14,13},{15,14},{18,17},{19... | collective-permute-start | bytes 3145736 | tf_op jit(solution)/shard_map/ppermute | solution.py:643
  181.2 18.8 %collective-permute-start.14 = (bf16[1024,512]{1,0:T(8,128)(2,1)}, bf16[1024,512]{1,0:T(8,128)(2,1)S(1)}, u32[]{:S(2)}, u32[]{:S(2)}) collective-permute-start(bf16[1024,512]{1,0:T(8,128)(2,1)} %collective-permute-done.10), channel_id=1, source_target_pairs={{2,3},{6,7},{10,11},{14,15},{18,19},{22,23},{26,27},{30,31}} | collective-permute-start | bytes 3145736 | tf_op jit(solution)/shard_map/ppermute | solution.py:599
  182.0 24.0 %collective-permute-start.15 = (bf16[1024,512]{1,0:T(8,128)(2,1)}, bf16[1024,512]{1,0:T(8,128)(2,1)S(1)}, u32[]{:S(2)}, u32[]{:S(2)}) collective-permute-start(bf16[1024,512]{1,0:T(8,128)(2,1)} %collective-permute-done.11), channel_id=1, source_target_pairs={{1,0},{5,4},{9,8},{13,12},{17,16},{21,20},{25,24},{29,28}} | collective-permute-start | bytes 3145736 | tf_op jit(solution)/shard_map/ppermute | solution.py:600
  207.3 20.5 %collective-permute-start.16 = (bf16[1024,512]{1,0:T(8,128)(2,1)}, bf16[1024,512]{1,0:T(8,128)(2,1)}, u32[]{:S(2)}, u32[]{:S(2)}) collective-permute-start(bf16[1024,512]{1,0:T(8,128)(2,1)} %add_convert_fusion.13), channel_id=1, source_target_pairs={{0,1},{1,2},{2,3},{4,5},{5,6},{6,7},{8,9},{9,10},{10,11},{12,13},{... | collective-permute-start | bytes 3145736 | tf_op jit(solution)/shard_map/ppermute | solution.py:642
  211.3 22.9 %collective-permute-start.17 = (bf16[1024,512]{1,0:T(8,128)(2,1)}, bf16[1024,512]{1,0:T(8,128)(2,1)}, u32[]{:S(2)}, u32[]{:S(2)}) collective-permute-start(bf16[1024,512]{1,0:T(8,128)(2,1)} %add_convert_fusion.12), channel_id=1, source_target_pairs={{1,0},{2,1},{3,2},{5,4},{6,5},{7,6},{9,8},{10,9},{11,10},{13,12},{... | collective-permute-start | bytes 3145736 | tf_op jit(solution)/shard_map/ppermute | solution.py:643
  238.9 91.1 %all-gather.8.cloned.1.call-start = ((), (), s32[]{:S(2)}) async-start(), calls=%async_computation.5 | async-start | bytes 2621440 | tf_op jit(solution)/shard_map/all_gather | solution.py:676
  263.1 112.2 %reduce-scatter.5.cloned.1.call-start = ((), (), s32[]{:S(2)}) async-start(), calls=%async_computation.7 | async-start | bytes 2621440 | tf_op jit(solution)/shard_map/reduce_scatter | solution.py:680
  330.0 90.8 %reduce-scatter.7.cloned.1.call-start = ((), (), s32[]{:S(2)}) async-start(), calls=%async_computation.8 | async-start | bytes 2621440 | tf_op jit(solution)/shard_map/reduce_scatter | solution.py:680
  375.3 21.2 %collective-permute-start.18 = (bf16[2,2064,256]{2,1,0:T(8,128)(2,1)}, bf16[2,2064,256]{2,1,0:T(8,128)(2,1)}, u32[]{:S(2)}, u32[]{:S(2)}) collective-permute-start(bf16[2,2064,256]{2,1,0:T(8,128)(2,1)} %get-tuple-element.307), channel_id=1, source_target_pairs={{0,4},{4,0},{8,12},{12,8},{16,20},{20,16},{24,28},{28,24},{1,5},{5... | collective-permute-start | bytes 6340616 | tf_op jit(solution)/shard_map/ppermute | solution.py:431
  375.4 95.9 %all-gather.12.cloned.1.call-start = ((), (), s32[]{:S(2)}) async-start(), calls=%async_computation.9 | async-start | bytes 2621440 | tf_op jit(solution)/shard_map/all_gather | solution.py:676
  375.8 25.1 %collective-permute-start.19 = (bf16[2,2064,256]{2,1,0:T(8,128)(2,1)}, bf16[2,2064,256]{2,1,0:T(8,128)(2,1)}, u32[]{:S(2)}, u32[]{:S(2)}) collective-permute-start(bf16[2,2064,256]{2,1,0:T(8,128)(2,1)} %get-tuple-element.309), channel_id=1, source_target_pairs={{0,4},{4,0},{8,12},{12,8},{16,20},{20,16},{24,28},{28,24},{1,5},{5... | collective-permute-start | bytes 6340616 | tf_op jit(solution)/shard_map/ppermute | solution.py:431
  376.4 28.2 %collective-permute-start.20 = (bf16[2,2064,256]{2,1,0:T(8,128)(2,1)}, bf16[2,2064,256]{2,1,0:T(8,128)(2,1)}, u32[]{:S(2)}, u32[]{:S(2)}) collective-permute-start(bf16[2,2064,256]{2,1,0:T(8,128)(2,1)} %get-tuple-element.311), channel_id=1, source_target_pairs={{0,4},{4,0},{8,12},{12,8},{16,20},{20,16},{24,28},{28,24},{1,5},{5... | collective-permute-start | bytes 6340616 | tf_op jit(solution)/shard_map/ppermute | solution.py:431
  376.5 31.7 %collective-permute-start.21 = (bf16[2,2064,256]{2,1,0:T(8,128)(2,1)}, bf16[2,2064,256]{2,1,0:T(8,128)(2,1)S(1)}, u32[]{:S(2)}, u32[]{:S(2)}) collective-permute-start(bf16[2,2064,256]{2,1,0:T(8,128)(2,1)} %get-tuple-element.313), channel_id=1, source_target_pairs={{0,4},{4,0},{8,12},{12,8},{16,20},{20,16},{24,28},{28,24},{1,5},{5... | collective-permute-start | bytes 6340616 | tf_op jit(solution)/shard_map/ppermute | solution.py:431
  420.8 95.2 %all-gather.14.cloned.1.call-start = ((), (), s32[]{:S(2)}) async-start(), calls=%async_computation.11 | async-start | bytes 2621440 | tf_op jit(solution)/shard_map/all_gather | solution.py:676
  422.2 47.9 %collective-permute-start.22 = (bf16[2,2064,256]{2,1,0:T(8,128)(2,1)}, bf16[2,2064,256]{2,1,0:T(8,128)(2,1)}, u32[]{:S(2)}, u32[]{:S(2)}) collective-permute-start(bf16[2,2064,256]{2,1,0:T(8,128)(2,1)} %add_convert_fusion.3), channel_id=1, source_target_pairs={{0,8},{4,12},{8,0},{12,4},{16,24},{20,28},{24,16},{28,20},{1,9},{5... | collective-permute-start | bytes 6340616 | tf_op jit(solution)/shard_map/ppermute | solution.py:431
  423.6 47.6 %collective-permute-start.23 = (bf16[2,2064,256]{2,1,0:T(8,128)(2,1)}, bf16[2,2064,256]{2,1,0:T(8,128)(2,1)}, u32[]{:S(2)}, u32[]{:S(2)}) collective-permute-start(bf16[2,2064,256]{2,1,0:T(8,128)(2,1)} %add_convert_fusion.2), channel_id=1, source_target_pairs={{0,16},{4,20},{8,24},{12,28},{16,0},{20,4},{24,8},{28,12},{1,17},{... | collective-permute-start | bytes 6340616 | tf_op jit(solution)/shard_map/ppermute | solution.py:431
  471.3 134.0 %reduce-scatter.9.cloned.1.call-start = ((), (), s32[]{:S(2)}) async-start(), calls=%async_computation.10 | async-start | bytes 5242880 | tf_op jit(solution)/shard_map/reduce_scatter | solution.py:680
  474.4 24.0 %collective-permute-start.24 = (bf16[1,2064,256]{2,1,0:T(8,128)(2,1)}, bf16[1,2064,256]{2,1,0:T(8,128)(2,1)}, u32[]{:S(2)}, u32[]{:S(2)}) collective-permute-start(bf16[1,2064,256]{2,1,0:T(8,128)(2,1)} %add_convert_fusion.10), channel_id=1, source_target_pairs={{0,16},{4,20},{8,24},{12,28},{16,0},{20,4},{24,8},{28,12},{1,17},{... | collective-permute-start | bytes 3170312 | tf_op jit(solution)/shard_map/ppermute | solution.py:431
  478.9 24.1 %collective-permute-start.25 = (bf16[1,2064,256]{2,1,0:T(8,128)(2,1)}, bf16[1,2064,256]{2,1,0:T(8,128)(2,1)}, u32[]{:S(2)}, u32[]{:S(2)}) collective-permute-start(bf16[1,2064,256]{2,1,0:T(8,128)(2,1)} %add_convert_fusion.7), channel_id=1, source_target_pairs={{0,8},{4,12},{8,0},{12,4},{16,24},{20,28},{24,16},{28,20},{1,9},{5... | collective-permute-start | bytes 3170312 | tf_op jit(solution)/shard_map/ppermute | solution.py:431
  484.7 207.0 %reduce-scatter.11.cloned.1.call-start = ((), (), s32[]{:S(2)}) async-start(), calls=%async_computation.12 | async-start | bytes 5242880 | tf_op jit(solution)/shard_map/reduce_scatter | solution.py:680
  501.5 30.1 %collective-permute-start.26 = (bf16[1,2064,256]{2,1,0:T(8,128)(2,1)}, bf16[1,2064,256]{2,1,0:T(8,128)(2,1)}, u32[]{:S(2)}, u32[]{:S(2)}) collective-permute-start(bf16[1,2064,256]{2,1,0:T(8,128)(2,1)} %add_convert_fusion.9.refs_0_), channel_id=1, source_target_pairs={{0,16},{4,20},{8,24},{12,28},{16,0},{20,4},{24,8},{28,12},{1,17},{... | collective-permute-start | bytes 3170312 | tf_op jit(solution)/shard_map/ppermute | solution.py:431
  506.1 26.6 %collective-permute-start.27 = (bf16[1,2064,256]{2,1,0:T(8,128)(2,1)}, bf16[1,2064,256]{2,1,0:T(8,128)(2,1)}, u32[]{:S(2)}, u32[]{:S(2)}) collective-permute-start(bf16[1,2064,256]{2,1,0:T(8,128)(2,1)} %add_convert_fusion.6.refs_8_), channel_id=1, source_target_pairs={{0,8},{4,12},{8,0},{12,4},{16,24},{20,28},{24,16},{28,20},{1,9},{5... | collective-permute-start | bytes 3170312 | tf_op jit(solution)/shard_map/ppermute | solution.py:431
  516.0 35.5 %collective-permute-start.28 = (bf16[1,2064,256]{2,1,0:T(8,128)(2,1)}, bf16[1,2064,256]{2,1,0:T(8,128)(2,1)S(1)}, u32[]{:S(2)}, u32[]{:S(2)}) collective-permute-start(bf16[1,2064,256]{2,1,0:T(8,128)(2,1)} %add_convert_fusion.9.refs_0_), channel_id=1, source_target_pairs={{0,8},{4,12},{8,0},{12,4},{16,24},{20,28},{24,16},{28,20},{1,9},{5... | collective-permute-start | bytes 3170312 | tf_op jit(solution)/shard_map/ppermute | solution.py:431
  517.5 34.0 %collective-permute-start.29 = (bf16[1,2064,256]{2,1,0:T(8,128)(2,1)}, bf16[1,2064,256]{2,1,0:T(8,128)(2,1)S(1)}, u32[]{:S(2)}, u32[]{:S(2)}) collective-permute-start(bf16[1,2064,256]{2,1,0:T(8,128)(2,1)} %add_convert_fusion.6.refs_8_), channel_id=1, source_target_pairs={{0,16},{4,20},{8,24},{12,28},{16,0},{20,4},{24,8},{28,12},{1,17},{... | collective-permute-start | bytes 3170312 | tf_op jit(solution)/shard_map/ppermute | solution.py:431
  554.3 19.6 %collective-permute-start.34 = (f32[4,8,256]{2,1,0:T(8,128)S(1)}, f32[4,8,256]{2,1,0:T(8,128)S(1)}, u32[]{:S(2)}, u32[]{:S(2)}) collective-permute-start(f32[4,8,256]{2,1,0:T(8,128)S(1)} %add.361), channel_id=1, source_target_pairs={{0,8},{4,12},{8,0},{12,4},{16,24},{20,28},{24,16},{28,20},{1,9},{5... | collective-permute-start | bytes 98312 | tf_op jit(solution)/shard_map/ppermute | solution.py:309
  555.1 19.5 %collective-permute-start.31 = (bf16[4,160,128]{2,1,0:T(8,128)(2,1)S(1)}, bf16[4,160,128]{2,1,0:T(8,128)(2,1)S(1)}, u32[]{:S(2)}, u32[]{:S(2)}) collective-permute-start(bf16[4,160,128]{2,1,0:T(8,128)(2,1)S(1)} %fusion.38), channel_id=1, source_target_pairs={{0,8},{4,12},{8,0},{12,4},{16,24},{20,28},{24,16},{28,20},{1,9},{5... | collective-permute-start | bytes 491528 | tf_op jit(solution)/shard_map/ppermute | solution.py:309
  580.6 24.4 %collective-permute-start.39 = (bf16[1,2064,256]{2,1,0:T(8,128)(2,1)}, bf16[1,2064,256]{2,1,0:T(8,128)(2,1)}, u32[]{:S(2)}, u32[]{:S(2)}) collective-permute-start(bf16[1,2064,256]{2,1,0:T(8,128)(2,1)} %collective-permute-done.26.refs_1_), channel_id=1, source_target_pairs={{0,8},{4,12},{8,0},{12,4},{16,24},{20,28},{24,16},{28,20},{1,9},{5... | collective-permute-start | bytes 3170312 | tf_op jit(solution)/shard_map/ppermute | solution.py:431
  581.2 24.0 %collective-permute-start.40 = (bf16[1,2064,256]{2,1,0:T(8,128)(2,1)}, bf16[1,2064,256]{2,1,0:T(8,128)(2,1)}, u32[]{:S(2)}, u32[]{:S(2)}) collective-permute-start(bf16[1,2064,256]{2,1,0:T(8,128)(2,1)} %collective-permute-done.27.refs_9_), channel_id=1, source_target_pairs={{0,16},{4,20},{8,24},{12,28},{16,0},{20,4},{24,8},{28,12},{1,17},{... | collective-permute-start | bytes 3170312 | tf_op jit(solution)/shard_map/ppermute | solution.py:431
  589.2 10.8 %collective-permute-start.36 = (f32[8,128]{1,0:T(8,128)S(1)}, f32[8,128]{1,0:T(8,128)S(1)}, u32[]{:S(2)}, u32[]{:S(2)}) collective-permute-start(f32[8,128]{1,0:T(8,128)S(1)} %add_bitcast_fusion), channel_id=1, source_target_pairs={{0,1},{1,2},{2,3},{3,0},{4,5},{5,6},{6,7},{7,4},{8,9},{9,10},{10,1... | collective-permute-start | bytes 12296 | tf_op jit(solution)/shard_map/ppermute | solution.py:561
  589.3 10.7 %collective-permute-start.37 = (f32[8,128]{1,0:T(8,128)S(1)}, f32[8,128]{1,0:T(8,128)S(1)}, u32[]{:S(2)}, u32[]{:S(2)}) collective-permute-start(f32[8,128]{1,0:T(8,128)S(1)} %add_bitcast_fusion), channel_id=1, source_target_pairs={{0,2},{1,3},{2,0},{3,1},{4,6},{5,7},{6,4},{7,5},{8,10},{9,11},{10,... | collective-permute-start | bytes 12296 | tf_op jit(solution)/shard_map/ppermute | solution.py:561
  592.3 7.7 %collective-permute-start.38 = (f32[8,128]{1,0:T(8,128)S(1)}, f32[8,128]{1,0:T(8,128)S(1)}, u32[]{:S(2)}, u32[]{:S(2)}) collective-permute-start(f32[8,128]{1,0:T(8,128)S(1)} %add_bitcast_fusion), channel_id=1, source_target_pairs={{0,3},{1,0},{2,1},{3,2},{4,7},{5,4},{6,5},{7,6},{8,11},{9,8},{10,9... | collective-permute-start | bytes 12296 | tf_op jit(solution)/shard_map/ppermute | solution.py:561
  615.6 8.9 %collective-permute-start.45 = (bf16[1,2064,256]{2,1,0:T(8,128)(2,1)}, bf16[1,2064,256]{2,1,0:T(8,128)(2,1)S(1)}, u32[]{:S(2)}, u32[]{:S(2)}) collective-permute-start(bf16[1,2064,256]{2,1,0:T(8,128)(2,1)} %add_convert_fusion.9.refs_0_), channel_id=1, source_target_pairs={{0,4},{4,0},{8,12},{12,8},{16,20},{20,16},{24,28},{28,24},{1,5},{5... | collective-permute-start | bytes 3170312 | tf_op jit(solution)/shard_map/ppermute | solution.py:431
  615.7 9.2 %collective-permute-start.46 = (bf16[1,2064,256]{2,1,0:T(8,128)(2,1)}, bf16[1,2064,256]{2,1,0:T(8,128)(2,1)S(1)}, u32[]{:S(2)}, u32[]{:S(2)}) collective-permute-start(bf16[1,2064,256]{2,1,0:T(8,128)(2,1)} %collective-permute-done.26.refs_1_), channel_id=1, source_target_pairs={{0,4},{4,0},{8,12},{12,8},{16,20},{20,16},{24,28},{28,24},{1,5},{5... | collective-permute-start | bytes 3170312 | tf_op jit(solution)/shard_map/ppermute | solution.py:431
  616.1 9.0 %collective-permute-start.47 = (bf16[1,2064,256]{2,1,0:T(8,128)(2,1)S(1)}, bf16[1,2064,256]{2,1,0:T(8,128)(2,1)S(1)}, u32[]{:S(2)}, u32[]{:S(2)}) collective-permute-start(bf16[1,2064,256]{2,1,0:T(8,128)(2,1)S(1)} %copy-done.43), channel_id=1, source_target_pairs={{0,4},{4,0},{8,12},{12,8},{16,20},{20,16},{24,28},{28,24},{1,5},{5... | collective-permute-start | bytes 3170312 | tf_op jit(solution)/shard_map/ppermute | solution.py:431
  617.3 6.2 collective-permute-start.43
  623.5 11.9 %collective-permute-start.48 = (bf16[1,2064,256]{2,1,0:T(8,128)(2,1)}, bf16[1,2064,256]{2,1,0:T(8,128)(2,1)}, u32[]{:S(2)}, u32[]{:S(2)}) collective-permute-start(bf16[1,2064,256]{2,1,0:T(8,128)(2,1)} %collective-permute-done.39.refs_3_), channel_id=1, source_target_pairs={{0,4},{4,0},{8,12},{12,8},{16,20},{20,16},{24,28},{28,24},{1,5},{5... | collective-permute-start | bytes 3170312 | tf_op jit(solution)/shard_map/ppermute | solution.py:431
  624.4 11.1 %collective-permute-start.49 = (bf16[1,2064,256]{2,1,0:T(8,128)(2,1)}, bf16[1,2064,256]{2,1,0:T(8,128)(2,1)}, u32[]{:S(2)}, u32[]{:S(2)}) collective-permute-start(bf16[1,2064,256]{2,1,0:T(8,128)(2,1)} %add_convert_fusion.6.refs_8_), channel_id=1, source_target_pairs={{0,4},{4,0},{8,12},{12,8},{16,20},{20,16},{24,28},{28,24},{1,5},{5... | collective-permute-start | bytes 3170312 | tf_op jit(solution)/shard_map/ppermute | solution.py:431
  624.5 10.9 %collective-permute-start.50 = (bf16[1,2064,256]{2,1,0:T(8,128)(2,1)}, bf16[1,2064,256]{2,1,0:T(8,128)(2,1)}, u32[]{:S(2)}, u32[]{:S(2)}) collective-permute-start(bf16[1,2064,256]{2,1,0:T(8,128)(2,1)} %collective-permute-done.27.refs_9_), channel_id=1, source_target_pairs={{0,4},{4,0},{8,12},{12,8},{16,20},{20,16},{24,28},{28,24},{1,5},{5... | collective-permute-start | bytes 3170312 | tf_op jit(solution)/shard_map/ppermute | solution.py:431
  624.9 10.6 %collective-permute-start.51 = (bf16[1,2064,256]{2,1,0:T(8,128)(2,1)S(1)}, bf16[1,2064,256]{2,1,0:T(8,128)(2,1)}, u32[]{:S(2)}, u32[]{:S(2)}) collective-permute-start(bf16[1,2064,256]{2,1,0:T(8,128)(2,1)S(1)} %copy-done.45), channel_id=1, source_target_pairs={{0,4},{4,0},{8,12},{12,8},{16,20},{20,16},{24,28},{28,24},{1,5},{5... | collective-permute-start | bytes 3170312 | tf_op jit(solution)/shard_map/ppermute | solution.py:431
  626.2 9.2 %collective-permute-start.52 = (bf16[1,2064,256]{2,1,0:T(8,128)(2,1)}, bf16[1,2064,256]{2,1,0:T(8,128)(2,1)S(1)}, u32[]{:S(2)}, u32[]{:S(2)}) collective-permute-start(bf16[1,2064,256]{2,1,0:T(8,128)(2,1)} %collective-permute-done.40.refs_11_), channel_id=1, source_target_pairs={{0,4},{4,0},{8,12},{12,8},{16,20},{20,16},{24,28},{28,24},{1,5},{5... | collective-permute-start | bytes 3170312 | tf_op jit(solution)/shard_map/ppermute | solution.py:431
  635.5 15.7 %collective-permute-start.53 = (bf16[2,576,256]{2,1,0:T(8,128)(2,1)}, bf16[2,576,256]{2,1,0:T(8,128)(2,1)S(1)}, u32[]{:S(2)}, u32[]{:S(2)}) collective-permute-start(bf16[2,576,256]{2,1,0:T(8,128)(2,1)} %get-tuple-element.382), channel_id=1, source_target_pairs={{0,8},{4,12},{8,0},{12,4},{16,24},{20,28},{24,16},{28,20},{1,9},{5... | collective-permute-start | bytes 1769480 | tf_op jit(solution)/shard_map/ppermute | solution.py:431
  637.0 15.3 %collective-permute-start.54 = (bf16[2,576,256]{2,1,0:T(8,128)(2,1)}, bf16[2,576,256]{2,1,0:T(8,128)(2,1)S(1)}, u32[]{:S(2)}, u32[]{:S(2)}) collective-permute-start(bf16[2,576,256]{2,1,0:T(8,128)(2,1)} %get-tuple-element.383), channel_id=1, source_target_pairs={{0,16},{4,20},{8,24},{12,28},{16,0},{20,4},{24,8},{28,12},{1,17},{... | collective-permute-start | bytes 1769480 | tf_op jit(solution)/shard_map/ppermute | solution.py:431
  652.5 11.4 %collective-permute-start.55 = (bf16[1,576,256]{2,1,0:T(8,128)(2,1)S(1)}, bf16[1,576,256]{2,1,0:T(8,128)(2,1)S(1)}, u32[]{:S(2)}, u32[]{:S(2)}) collective-permute-start(bf16[1,576,256]{2,1,0:T(8,128)(2,1)S(1)} %get-tuple-element.480), channel_id=1, source_target_pairs={{0,16},{4,20},{8,24},{12,28},{16,0},{20,4},{24,8},{28,12},{1,17},{... | collective-permute-start | bytes 884744 | tf_op jit(solution)/shard_map/ppermute | solution.py:431
  654.2 9.7 %collective-permute-start.56 = (bf16[1,576,256]{2,1,0:T(8,128)(2,1)S(1)}, bf16[1,576,256]{2,1,0:T(8,128)(2,1)S(1)}, u32[]{:S(2)}, u32[]{:S(2)}) collective-permute-start(bf16[1,576,256]{2,1,0:T(8,128)(2,1)S(1)} %get-tuple-element.478), channel_id=1, source_target_pairs={{0,8},{4,12},{8,0},{12,4},{16,24},{20,28},{24,16},{28,20},{1,9},{5... | collective-permute-start | bytes 884744 | tf_op jit(solution)/shard_map/ppermute | solution.py:431
  664.0 7.5 %collective-permute-start.57 = (bf16[1,576,256]{2,1,0:T(8,128)(2,1)S(1)}, bf16[1,576,256]{2,1,0:T(8,128)(2,1)S(1)}, u32[]{:S(2)}, u32[]{:S(2)}) collective-permute-start(bf16[1,576,256]{2,1,0:T(8,128)(2,1)S(1)} %add_convert_fusion.17.refs_0_), channel_id=1, source_target_pairs={{0,16},{4,20},{8,24},{12,28},{16,0},{20,4},{24,8},{28,12},{1,17},{... | collective-permute-start | bytes 884744 | tf_op jit(solution)/shard_map/ppermute | solution.py:431
  664.8 7.3 %collective-permute-start.58 = (bf16[1,576,256]{2,1,0:T(8,128)(2,1)S(1)}, bf16[1,576,256]{2,1,0:T(8,128)(2,1)S(1)}, u32[]{:S(2)}, u32[]{:S(2)}) collective-permute-start(bf16[1,576,256]{2,1,0:T(8,128)(2,1)S(1)} %add_convert_fusion.16.refs_8_), channel_id=1, source_target_pairs={{0,8},{4,12},{8,0},{12,4},{16,24},{20,28},{24,16},{28,20},{1,9},{5... | collective-permute-start | bytes 884744 | tf_op jit(solution)/shard_map/ppermute | solution.py:431
  672.1 12.9 %collective-permute-start.59 = (bf16[1,576,256]{2,1,0:T(8,128)(2,1)S(1)}, bf16[1,576,256]{2,1,0:T(8,128)(2,1)S(1)}, u32[]{:S(2)}, u32[]{:S(2)}) collective-permute-start(bf16[1,576,256]{2,1,0:T(8,128)(2,1)S(1)} %add_convert_fusion.17.refs_0_), channel_id=1, source_target_pairs={{0,8},{4,12},{8,0},{12,4},{16,24},{20,28},{24,16},{28,20},{1,9},{5... | collective-permute-start | bytes 884744 | tf_op jit(solution)/shard_map/ppermute | solution.py:431
  673.4 11.6 %collective-permute-start.60 = (bf16[1,576,256]{2,1,0:T(8,128)(2,1)S(1)}, bf16[1,576,256]{2,1,0:T(8,128)(2,1)S(1)}, u32[]{:S(2)}, u32[]{:S(2)}) collective-permute-start(bf16[1,576,256]{2,1,0:T(8,128)(2,1)S(1)} %collective-permute-done.57.refs_1_), channel_id=1, source_target_pairs={{0,8},{4,12},{8,0},{12,4},{16,24},{20,28},{24,16},{28,20},{1,9},{5... | collective-permute-start | bytes 884744 | tf_op jit(solution)/shard_map/ppermute | solution.py:431
  674.1 10.9 %collective-permute-start.61 = (bf16[1,576,256]{2,1,0:T(8,128)(2,1)S(1)}, bf16[1,576,256]{2,1,0:T(8,128)(2,1)S(1)}, u32[]{:S(2)}, u32[]{:S(2)}) collective-permute-start(bf16[1,576,256]{2,1,0:T(8,128)(2,1)S(1)} %add_convert_fusion.16.refs_8_), channel_id=1, source_target_pairs={{0,16},{4,20},{8,24},{12,28},{16,0},{20,4},{24,8},{28,12},{1,17},{... | collective-permute-start | bytes 884744 | tf_op jit(solution)/shard_map/ppermute | solution.py:431
  675.5 10.9 %collective-permute-start.62 = (bf16[1,576,256]{2,1,0:T(8,128)(2,1)S(1)}, bf16[1,576,256]{2,1,0:T(8,128)(2,1)S(1)}, u32[]{:S(2)}, u32[]{:S(2)}) collective-permute-start(bf16[1,576,256]{2,1,0:T(8,128)(2,1)S(1)} %collective-permute-done.58.refs_9_), channel_id=1, source_target_pairs={{0,16},{4,20},{8,24},{12,28},{16,0},{20,4},{24,8},{28,12},{1,17},{... | collective-permute-start | bytes 884744 | tf_op jit(solution)/shard_map/ppermute | solution.py:431
  696.9 11.6 %collective-permute-start.74 = (f32[2,512]{1,0:T(2,128)S(1)}, f32[2,512]{1,0:T(2,128)S(1)}, u32[]{:S(2)}, u32[]{:S(2)}) collective-permute-start(f32[2,512]{1,0:T(2,128)S(1)} %fusion.48), channel_id=1, source_target_pairs={{0,24},{4,28},{8,16},{12,20},{16,8},{20,12},{24,0},{28,4},{1,25},{... | collective-permute-start | bytes 12296 | tf_op jit(solution)/shard_map/ppermute | solution.py:431
  699.0 9.5 %collective-permute-start.72 = (f32[2,512]{1,0:T(2,128)S(1)}, f32[2,512]{1,0:T(2,128)S(1)}, u32[]{:S(2)}, u32[]{:S(2)}) collective-permute-start(f32[2,512]{1,0:T(2,128)S(1)} %fusion.48), channel_id=1, source_target_pairs={{0,8},{4,12},{8,0},{12,4},{16,24},{20,28},{24,16},{28,20},{1,9},{5... | collective-permute-start | bytes 12296 | tf_op jit(solution)/shard_map/ppermute | solution.py:431
  699.6 8.9 %collective-permute-start.73 = (f32[2,512]{1,0:T(2,128)S(1)}, f32[2,512]{1,0:T(2,128)S(1)}, u32[]{:S(2)}, u32[]{:S(2)}) collective-permute-start(f32[2,512]{1,0:T(2,128)S(1)} %fusion.48), channel_id=1, source_target_pairs={{0,16},{4,20},{8,24},{12,28},{16,0},{20,4},{24,8},{28,12},{1,17},{... | collective-permute-start | bytes 12296 | tf_op jit(solution)/shard_map/ppermute | solution.py:431
  (150 other events, 1378.8 us)
Sparse Core Ops, SparseCore 0:
  9.6 83.5 all-gather.5
  239.0 44.1 all-gather.9
  285.3 44.6 all-gather.7
  332.7 42.5 reduce-scatter.4
  377.6 43.1 reduce-scatter.6
  422.8 45.2 all-gather.11
  471.4 44.5 all-gather.13
  518.9 75.5 reduce-scatter.8
  605.4 76.7 reduce-scatter.10
